TPU v7x, 256 devices: a whole 4x4x8 slice. The times are simulated.
256 devices in a mesh: cells: 16 (over x, z_hi), vel: 16 (over y, z_lo, core).
Axes of the slice: x: 4, y: 4, z: 8 (z_hi: 4, z_lo: 2; z = z_hi * 2 + z_lo), core: 2. Of those that a mesh axis runs over, the one named last changes fastest.
Arguments:
- dist: float32 [32768, 64, 128], P('vel', 'cells'), may hold values from 0.05 to 2
- basis: float32 [512, 32768], P(None, 'vel'), may hold values from -0.03125 to 0.03125
- left_factor: float32 [2048, 512], P('vel'), may hold values from -0.25 to 0.25
- right_factor: float32 [2048, 512], P('vel'), may hold values from -0.25 to 0.25
- mixing: float32 [512, 2048], P(None, 'vel'), may hold values from -0.125 to 0.125
- next_cell: int32 [64, 128], P('cells'), may hold values from 0 to 127, as said below
- prev_cell: int32 [64, 128], P('cells'), may hold values from 0 to 127, as said below
- cell_kind: int32 [64, 128], P('cells'), may hold values 0 or 1
Outputs:
- relaxed: float32 [32768, 64, 128], P('vel', 'cells')
Inputs may be any that keep to these rules, and one draw needn't show every extreme that they name: In each column x, following next_cell[x, y] from any row visits all 128 rows once before returning. prev_cell[x, next_cell[x, y]] = y for every cell.
All inputs are finite; a program needn't handle non-finite values. No bound on the sum of `cell_kind` on one device may be relied on, other than what follows from the above.
Results may differ from a plain program's by a relative error of at most 0.0003.
Values sent between devices are 32-bit elements; how exact they have to be, the bound alone decides.
No kernel may reach another device: no remote copies, remote signals or barrier semaphores. Data moves between devices by JAX's collectives and lax.ppermute only.
A program may use at most 64 MiB of HBM per device.

v0:
```python
import functools

import jax
import jax.numpy as jnp
from jax import lax
from jax.experimental import pallas as pl
from jax.experimental.pallas import tpu as pltpu
from jax.sharding import PartitionSpec as P

POINTS = 32
STEP = 6.4 / POINTS
MIDDLE = (POINTS - 1) * 0.5
RATIO_X = 0.2
RATIO_Y = 0.12
HALF_STEP = 0.5

COLUMNS = 4
ROWS = 128
PER_DEVICE = 2048
HALF = PER_DEVICE // 2
CHUNK = 256
MOMENTS = 512
CELLS = COLUMNS * ROWS
RANKS = 1024
GROUP = CELLS // 8
F32 = jnp.float32
BF16 = jnp.bfloat16
VMEM_LIMIT = 28 << 20


def shifted(x, by):
    size = lax.axis_size("cells")
    return lax.ppermute(x, "cells", [(i, (i + by) % size) for i in range(size)])


def exchanged(x, bit):
    return lax.ppermute(x, "vel", [(i, i ^ bit) for i in range(16)])


def along_y(x, by):
    return lax.ppermute(x, "vel", [(i, (i + 4 * by) % 16) for i in range(16)])


def halves(x):
    high = x.astype(BF16)
    return high, (x - high.astype(F32)).astype(BF16)


def minmod(a, b):
    return jnp.maximum(jnp.minimum(a, b), 0.0) + jnp.minimum(jnp.maximum(a, b), 0.0)


def dot(a, b):
    return jnp.dot(a, b, preferred_element_type=F32)


def dot_nt(a, b):
    return lax.dot_general(a, b, (((1,), (1,)), ((), ())), preferred_element_type=F32)


def column(ref, x, count=CHUNK):
    return ref[pl.ds(x, count, stride=COLUMNS), :]


def params(limit=VMEM_LIMIT):
    return pltpu.CompilerParams(vmem_limit_bytes=limit)


VM = pl.BlockSpec(memory_space=pltpu.VMEM)
SM = pl.BlockSpec(memory_space=pltpu.SMEM)


def pack_kernel(lower, upper, right, left):
    right[0] = column(upper, 3)
    right[1] = column(upper, 2)
    right[2] = column(lower, 3)
    left[0] = column(lower, 0)
    left[1] = column(lower, 1)
    left[2] = column(upper, 0)


def pack(flat):
    steps = HALF // CHUNK
    rows = CHUNK * COLUMNS
    out = jax.ShapeDtypeStruct((3, HALF, ROWS), F32)
    spec = pl.BlockSpec((3, CHUNK, ROWS), lambda i: (0, i, 0))
    return pl.pallas_call(
        pack_kernel,
        name="pack",
        grid=(steps,),
        in_specs=[
            pl.BlockSpec((rows, ROWS), lambda i: (i, 0)),
            pl.BlockSpec((rows, ROWS), lambda i: (i + steps, 0)),
        ],
        out_specs=[spec, spec],
        out_shape=[out, out],
        compiler_params=params(),
    )(flat, flat)


def local_kernel(speed, dist, kind, tables, out):
    step = pl.program_id(0)
    in_upper = step >= HALF // CHUNK
    line = lax.broadcasted_iota(jnp.int32, (CHUNK, ROWS), 0) + step * CHUNK
    along = (line // POINTS) % POINTS
    along = jnp.where(in_upper, POINTS - 1 - along, along)
    courant_y = jnp.abs((along.astype(F32) - MIDDLE) * STEP * RATIO_Y)
    slope_y = 0.5 * (1.0 - courant_y)
    courant_x = speed[0]
    slope_x = 0.5 * (1.0 - courant_x)
    fields = []
    for x in range(COLUMNS):
        here = column(dist, x)
        both = dot(jnp.concatenate(halves(here), axis=1), tables[0, x])
        face = here + slope_y * minmod(here - both[:, :ROWS], both[:, ROWS:] - here)
        behind = dot(jnp.concatenate(halves(face), axis=1), tables[0, x, :, :ROWS])
        fields.append((here, courant_y * (face - behind)))

    def finish(order):
        here = [fields[x][0] for x in order]
        change = [fields[x][1] for x in order]
        fluid = [(1 - kind[x : x + 1, :]).astype(F32) for x in order]
        face_1 = courant_x * (here[1] + slope_x * minmod(here[1] - here[0], here[2] - here[1]))
        face_2 = courant_x * (here[2] + slope_x * minmod(here[2] - here[1], here[3] - here[2]))
        out[order[0]] = here[0] - fluid[0] * change[0]
        out[order[1]] = here[1] - fluid[1] * (change[1] + face_1)
        out[order[2]] = here[2] - fluid[2] * (change[2] + (face_2 - face_1))
        out[order[3]] = here[3] - fluid[3] * (change[3] - face_2)

    @pl.when(in_upper)
    def _():
        finish((0, 1, 2, 3))

    @pl.when(jnp.logical_not(in_upper))
    def _():
        finish((3, 2, 1, 0))


def local_part(speed, flat, kind, tables):
    steps = PER_DEVICE // CHUNK
    quarter = steps // 4

    def against(i):
        return jnp.where((i >= quarter) & (i < 3 * quarter), 0, 1)

    return pl.pallas_call(
        local_kernel,
        name="local_transport",
        grid=(steps,),
        in_specs=[
            SM,
            pl.BlockSpec((CHUNK * COLUMNS, ROWS), lambda i: (i, 0)),
            VM,
            pl.BlockSpec((1, COLUMNS, 2 * ROWS, 2 * ROWS), lambda i: (against(i), 0, 0, 0)),
        ],
        out_specs=pl.BlockSpec((COLUMNS, CHUNK, ROWS), lambda i: (0, i, 0)),
        out_shape=jax.ShapeDtypeStruct((COLUMNS, PER_DEVICE, ROWS), F32),
        compiler_params=params(),
        cost_estimate=pl.CostEstimate(flops=4 << 30, bytes_accessed=10 << 20, transcendentals=0),
    )(speed, flat, kind, tables)


def row_tables(following, preceding):
    rows = jnp.arange(ROWS, dtype=jnp.int32)[None, :, None]
    after = (rows == following[:, None, :]).astype(BF16)
    before = (rows == preceding[:, None, :]).astype(BF16)
    forward = jnp.concatenate([before, after], axis=2)
    backward = jnp.concatenate([after, before], axis=2)
    forward = jnp.concatenate([forward, forward], axis=1)
    backward = jnp.concatenate([backward, backward], axis=1)
    return jnp.stack([forward, backward])


def basis_kernel(basis, high, low, turned_high, turned_low):
    values = basis[...]
    high[...], low[...] = halves(values)
    turned_high[...], turned_low[...] = halves(values.T)


def split_basis(basis):
    width = 256
    flat = pl.BlockSpec((MOMENTS, width), lambda i: (0, i))
    turned = pl.BlockSpec((width, MOMENTS), lambda i: (i, 0))
    return pl.pallas_call(
        basis_kernel,
        name="split_basis",
        grid=(PER_DEVICE // width,),
        in_specs=[flat],
        out_specs=[flat, flat, turned, turned],
        out_shape=[jax.ShapeDtypeStruct((MOMENTS, PER_DEVICE), BF16)] * 2
        + [jax.ShapeDtypeStruct((PER_DEVICE, MOMENTS), BF16)] * 2,
        compiler_params=params(),
        cost_estimate=pl.CostEstimate(flops=1 << 24, bytes_accessed=12 << 20, transcendentals=0),
    )(basis)


def factor_kernel(factors, high, low):
    high[...], low[...] = halves(factors[0])


def split_factors(factors):
    count = RANKS // 128
    out = jax.ShapeDtypeStruct((3, RANKS, MOMENTS), BF16)
    spec = pl.BlockSpec((3, 128, MOMENTS), lambda i: (0, i, 0))
    return pl.pallas_call(
        factor_kernel,
        name="split_factors",
        grid=(count,),
        in_specs=[pl.BlockSpec((1, 3, 128, MOMENTS), lambda i: (i, 0, 0, 0))],
        out_specs=[spec, spec],
        out_shape=[out, out],
        compiler_params=params(),
        cost_estimate=pl.CostEstimate(flops=1 << 24, bytes_accessed=12 << 20, transcendentals=0),
    )(factors)


def moments_kernel(
    speed, place, lower, upper, part_lower, part_upper, from_left, from_right, kind,
    high_lower, low_lower, high_upper, low_upper,
    moved_lower, moved_upper, kept, sent, total,
):
    step = pl.program_id(0)
    courant = speed[0]
    slope = 0.5 * (1.0 - courant)

    def half(dist, part, moved, order, behind, behind_two, ahead):
        first, second = column(dist, order[0]), column(dist, order[1])
        third, fourth = column(dist, order[2]), column(dist, order[3])
        fluid = [courant * (1 - kind[x : x + 1, :]).astype(F32) for x in order]
        face_in = behind + slope * minmod(behind - behind_two, first - behind)
        face_0 = first + slope * minmod(first - behind, second - first)
        face_3 = fourth + slope * minmod(fourth - third, ahead - fourth)
        values = [None] * COLUMNS
        values[order[0]] = part[order[0]] - fluid[0] * (face_0 - face_in)
        values[order[1]] = part[order[1]] + fluid[1] * face_0
        values[order[2]] = part[order[2]]
        values[order[3]] = part[order[3]] - fluid[3] * face_3
        for x in range(COLUMNS):
            moved[x] = values[x]
        return halves(jnp.concatenate(values, axis=1))

    def share(high, low, values):
        top, rest = values
        return dot(high[...], top) + (dot(high[...], rest) + dot(low[...], top))

    values_lower = half(
        lower, part_lower, moved_lower, (3, 2, 1, 0), from_right[0], from_right[1], from_left[2]
    )
    values_upper = half(
        upper, part_upper, moved_upper, (0, 1, 2, 3), from_left[0], from_left[1], from_right[2]
    )
    added = share(high_lower, low_lower, values_lower) + share(high_upper, low_upper, values_upper)

    @pl.when(step == 0)
    def _():
        total[...] = added

    @pl.when(step > 0)
    def _():
        total[...] += added

    @pl.when(step == pl.num_programs(0) - 1)
    def _():
        count = CELLS // 2
        core = place[0]
        first = total[:, :count].T
        second = total[:, count:].T
        kept[...] = jnp.where(core == 0, first, second)
        sent[...] = jnp.where(core == 0, second, first)


def moments_part(speed, place, flat, part, from_left, from_right, kind, high, low):
    steps = HALF // CHUNK
    rows = CHUNK * COLUMNS
    lower = pl.BlockSpec((COLUMNS, CHUNK, ROWS), lambda i: (0, i, 0))
    upper = pl.BlockSpec((COLUMNS, CHUNK, ROWS), lambda i: (0, i + steps, 0))
    halo = pl.BlockSpec((3, CHUNK, ROWS), lambda i: (0, i, 0))
    basis_lower = pl.BlockSpec((MOMENTS, CHUNK), lambda i: (0, i))
    basis_upper = pl.BlockSpec((MOMENTS, CHUNK), lambda i: (0, i + steps))
    moved = jax.ShapeDtypeStruct((COLUMNS, HALF, ROWS), F32)
    piece = jax.ShapeDtypeStruct((CELLS // 2, MOMENTS), F32)
    return pl.pallas_call(
        moments_kernel,
        name="faces_and_moments",
        grid=(steps,),
        in_specs=[
            SM,
            SM,
            pl.BlockSpec((rows, ROWS), lambda i: (i, 0)),
            pl.BlockSpec((rows, ROWS), lambda i: (i + steps, 0)),
            lower,
            upper,
            halo,
            halo,
            VM,
            basis_lower,
            basis_lower,
            basis_upper,
            basis_upper,
        ],
        out_specs=[lower, lower, VM, VM],
        out_shape=[moved, moved, piece, piece],
        scratch_shapes=[pltpu.VMEM((MOMENTS, CELLS), F32)],
        compiler_params=params(),
    )(speed, place, flat, flat, part, part, from_left, from_right, kind, high, low, high, low)


def small_call(kernel, name, count, shape, operands, smem=0, scratch=()):
    out = [jax.ShapeDtypeStruct(shape, F32)] * count
    return pl.pallas_call(
        kernel,
        name=name,
        in_specs=[SM] * smem + [VM] * (len(operands) - smem),
        out_specs=[VM] * count if count > 1 else VM,
        out_shape=out if count > 1 else out[0],
        scratch_shapes=scratch,
        compiler_params=params(),
    )(*operands)


def scatter_kernel(place, kept, received, own, to_one, to_two, to_three):
    for away, out in enumerate((own, to_one, to_two, to_three)):
        at = pl.multiple_of(((place[1] + away) % 4) * GROUP, GROUP)
        out[...] = kept[pl.ds(at, GROUP), :] + received[pl.ds(at, GROUP), :]


def add_four_kernel(a, b, c, d, out):
    out[...] = (a[...] + b[...]) + (c[...] + d[...])


def add_two_kernel(a, b, out):
    out[...] = a[...] + b[...]


def collision_kernel(mine, theirs, high, low, out):
    def times(values, which, product):
        top, rest = halves(values)
        both = product(jnp.concatenate([top, rest], axis=0), high[which])
        return both[:GROUP] + (both[GROUP:] + product(top, low[which]))

    moments = mine[...] + theirs[...]
    terms = times(moments, 0, dot_nt) * times(moments, 1, dot_nt)
    out[...] = times(terms, 2, dot)


def relax_kernel(
    place, own, y_1, y_2, y_3, other, z_1, z_2, z_3, kind, moved_lower, moved_upper,
    high, low, out, collision_high, collision_low,
):
    step = pl.program_id(0)

    @pl.when(step == 0)
    def _():
        pieces = (((own, y_1, y_2, y_3), place[0]), ((other, z_1, z_2, z_3), 1 - place[0]))
        for group, core in pieces:
            for away, piece in enumerate(group):
                at = core * 4 + (place[1] + (4 - away)) % 4
                at = pl.multiple_of(at * GROUP, GROUP)
                top, rest = halves(piece[...])
                collision_high[pl.ds(at, GROUP), :] = top
                collision_low[pl.ds(at, GROUP), :] = rest

    top = collision_high[...]
    gain = dot_nt(high[...], top) + (dot_nt(high[...], collision_low[...]) + dot_nt(low[...], top))
    in_upper = step >= HALF // CHUNK
    for x in range(COLUMNS):
        fluid = HALF_STEP * (1 - kind[x : x + 1, :]).astype(F32)
        moved = jnp.where(in_upper, moved_upper[x], moved_lower[x])
        out[pl.ds(x, CHUNK, stride=COLUMNS), :] = (
            moved + fluid * gain[:, x * ROWS : (x + 1) * ROWS]
        )


def relax(place, pieces, kind, moved_lower, moved_upper, high, low):
    steps = PER_DEVICE // CHUNK
    last = steps // 2 - 1
    turned = pl.BlockSpec((CHUNK, MOMENTS), lambda i: (i, 0))
    return pl.pallas_call(
        relax_kernel,
        name="relax",
        grid=(steps,),
        in_specs=[SM]
        + [VM] * 9
        + [
            pl.BlockSpec((COLUMNS, CHUNK, ROWS), lambda i: (0, jnp.minimum(i, last), 0)),
            pl.BlockSpec((COLUMNS, CHUNK, ROWS), lambda i: (0, jnp.maximum(i - last - 1, 0), 0)),
            turned,
            turned,
        ],
        out_specs=pl.BlockSpec((CHUNK * COLUMNS, ROWS), lambda i: (i, 0)),
        out_shape=jax.ShapeDtypeStruct((PER_DEVICE * COLUMNS, ROWS), F32),
        scratch_shapes=[pltpu.VMEM((CELLS, MOMENTS), BF16)] * 2,
        compiler_params=params(),
    )(place, *pieces, kind, moved_lower, moved_upper, high, low)


def on_device(dist, basis, left_factor, right_factor, mixing, next_cell, prev_cell, cell_kind):
    owner = lax.axis_index("vel")
    place = jnp.stack([owner % 2, owner // 4]).astype(jnp.int32)
    speed = ((MIDDLE - owner.astype(F32)) * STEP * RATIO_X).reshape(1)
    flat = dist.reshape(PER_DEVICE * COLUMNS, ROWS)
    to_right, to_left = pack(flat)
    from_left = shifted(to_right, 1)
    from_right = shifted(to_left, -1)

    mine = jnp.concatenate([left_factor, right_factor, mixing.T], axis=0)
    groups = [[4 * y + 2 * z + c for y in range(4) for c in range(2)] for z in range(2)]
    factors = lax.all_gather(mine, "vel", axis=0, tiled=True, axis_index_groups=groups)
    factor_high, factor_low = split_factors(factors.reshape(8, 3, 128, MOMENTS))
    high, low, turned_high, turned_low = split_basis(basis)
    part = local_part(speed, flat, cell_kind, row_tables(next_cell, prev_cell))

    moved_lower, moved_upper, kept, sent = moments_part(
        speed, place, flat, part, from_left, from_right, cell_kind, high, low
    )
    shape = (GROUP, MOMENTS)
    operands = (place, kept, exchanged(sent, 1))
    own, *others = small_call(scatter_kernel, "scatter", 4, shape, operands, 1)
    arrived = [along_y(piece, away + 1) for away, piece in enumerate(others)]
    summed = small_call(add_four_kernel, "add_four", 1, shape, (own, *arrived))
    operands = (summed, exchanged(summed, 2), factor_high, factor_low)
    share = small_call(collision_kernel, "collide", 1, shape, operands)
    whole = small_call(add_two_kernel, "add_two", 1, shape, (share, exchanged(share, 2)))
    pieces = [whole] + [along_y(whole, away) for away in (1, 2, 3)]
    pieces = pieces + [exchanged(piece, 1) for piece in pieces]
    out = relax(place, pieces, cell_kind, moved_lower, moved_upper, turned_high, turned_low)
    return out.reshape(dist.shape)


def solution(mesh):
    in_specs = (
        P("vel", "cells", None),
        P(None, "vel"),
        P("vel", None),
        P("vel", None),
        P(None, "vel"),
        P("cells", None),
        P("cells", None),
        P("cells", None),
    )
    out_specs = P("vel", "cells", None)
    return jax.shard_map(
        on_device, mesh=mesh, in_specs=in_specs, out_specs=out_specs, check_vma=False
    )
```

profile of v0, /device:TPU:1, one launch (start us, length us, event | category | flops | bytes accessed | tf_op | source)
XLA Modules:
  0.0 159.4 jit_solution(2466134328705326205)
XLA Ops:
  6.5 0.0 all-gather.2.cloned.1.call-start
  6.5 1.1 copy.10
  7.6 1.1 copy.9
  8.7 1.9 %pad_maximum_fusion.1 = f32[384,512]{0,1:T(8,128)} fusion(f32[128,512]{0,1:T(8,128)} %bitcast.17, f32[128,512]{0,1:T(8,128)S(1)} %copy.10, f32[128,512]{0,1:T(8,128)S(1)} %copy.9), kind=kLoop, calls=%fused_computation.1 | loop fusion | flops 393216 | bytes 1572864 | tf_op jit(solution)/shard_map/concatenate | solution.py:406
  10.6 0.0 all-gather.2.cloned.1.call-update
  10.6 0.0 copy-start
  10.6 2.2 %copy-done = f32[2048,4,128]{2,1,0:T(4,128)S(1)} copy-done((f32[2048,4,128]{2,1,0:T(4,128)S(1)}, f32[2048,4,128]{2,1,0:T(4,128)}, u32[]{:S(2)}) %copy-start) | copy-done | bytes 4194328
  12.8 2.2 %pack.1 = (f32[3,1024,128]{2,1,0:T(8,128)}, f32[3,1024,128]{2,1,0:T(8,128)}) custom-call(f32[8192,128]{1,0:T(8,128)S(1)} %bitcast.11, f32[8192,128]{1,0:T(8,128)S(1)} %bitcast.12), custom_call_target="tpu_custom_call" | custom-call | tf_op jit(solution)/shard_map/pack/pallas_call | solution.py:87
  15.0 3.8 %collective-permute-start = (f32[3,1024,128]{2,1,0:T(8,128)}, f32[3,1024,128]{2,1,0:T(8,128)}, u32[]{:S(2)}, u32[]{:S(2)}) collective-permute-start(f32[3,1024,128]{2,1,0:T(8,128)} %get-tuple-element.21), channel_id=1, source_target_pairs={{0,16},{16,32},{32,48},{48,64},{64,80},{80,96},{96,112},{112,128},... | collective-permute-start | bytes 4718600 | tf_op jit(solution)/shard_map/ppermute | solution.py:33
  18.8 5.2 %collective-permute-start.1 = (f32[3,1024,128]{2,1,0:T(8,128)}, f32[3,1024,128]{2,1,0:T(8,128)}, u32[]{:S(2)}, u32[]{:S(2)}) collective-permute-start(f32[3,1024,128]{2,1,0:T(8,128)} %get-tuple-element.22), channel_id=1, source_target_pairs={{0,240},{16,0},{32,16},{48,32},{64,48},{80,64},{96,80},{112,96},{1... | collective-permute-start | bytes 4718600 | tf_op jit(solution)/shard_map/ppermute | solution.py:33
  24.0 2.3 %copy-done.3 = f32[512,2048]{1,0:T(8,128)S(1)} copy-done((f32[512,2048]{1,0:T(8,128)S(1)}, f32[512,2048]{1,0:T(8,128)}, u32[]{:S(2)}) %copy-start.3) | copy-done | bytes 4194328
  26.3 2.5 %split_basis.1 = (bf16[512,2048]{1,0:T(8,128)(2,1)S(1)}, bf16[512,2048]{1,0:T(8,128)(2,1)S(1)}, bf16[2048,512]{1,0:T(8,128)(2,1)S(1)}, bf16[2048,512]{1,0:T(8,128)(2,1)S(1)}) custom-call(f32[512,2048]{1,0:T(8,128)S(1)} %copy-done.3), custom_call_target="tpu_custom_call" | custom-call | flops 16777216 | bytes 12582912 | tf_op jit(solution)/shard_map/split_basis/pallas_call | solution.py:184
  28.8 0.0 copy-start.4
  28.9 0.0 copy-start.10
  28.9 0.1 pad_add_fusion.place
  28.9 0.0 copy-done.11
  28.9 0.0 copy-done.12
  28.9 0.1 fusion
  29.0 0.1 maximum_bitcast_fusion
  29.1 0.1 pad_maximum_fusion.tables
  29.2 0.0 copy-done.1
  29.2 0.3 copy-done.10
  29.6 7.6 %local_transport.1.part_lower.part_upper = f32[4,2048,128]{2,1,0:T(8,128)S(1)} custom-call(f32[1]{0:T(128)} %bitcast.2.speed, f32[8192,128]{1,0:T(8,128)S(1)} %bitcast.13, s32[4,128]{1,0:T(4,128)S(1)} %copy-done.10, bf16[2,4,256,256]{3,2,1,0:T(8,128)(2,1)S(1)} %pad_maximum_fusion.tables), custom_call_target="tpu_custom_call" | custom-call | flops 4294967296 | bytes 10485760 | tf_op jit(solution)/shard_map/local_transport/pallas_call | solution.py:146
  37.2 0.0 copy-done.4
  37.2 34.5 %collective-permute-done.from_left = f32[3,1024,128]{2,1,0:T(8,128)} collective-permute-done((f32[3,1024,128]{2,1,0:T(8,128)}, f32[3,1024,128]{2,1,0:T(8,128)}, u32[]{:S(2)}, u32[]{:S(2)}) %collective-permute-start) | collective-permute-done | bytes 1572896 | tf_op jit(solution)/shard_map/ppermute | solution.py:33
  71.7 19.9 %collective-permute-done.1.from_right = f32[3,1024,128]{2,1,0:T(8,128)} collective-permute-done((f32[3,1024,128]{2,1,0:T(8,128)}, f32[3,1024,128]{2,1,0:T(8,128)}, u32[]{:S(2)}, u32[]{:S(2)}) %collective-permute-start.1) | collective-permute-done | bytes 1572896 | tf_op jit(solution)/shard_map/ppermute | solution.py:33
  91.6 7.3 %faces_and_moments.1 = (f32[4,1024,128]{2,1,0:T(8,128)S(1)}, f32[4,1024,128]{2,1,0:T(8,128)S(1)}, f32[256,512]{1,0:T(8,128)S(1)}, f32[256,512]{1,0:T(8,128)S(1)}) custom-call(f32[1]{0:T(128)} %bitcast.2.speed, s32[2]{0:T(128)S(1)} %pad_add_fusion.place, f32[8192,128]{1,0:T(8,128)S(1)} %bitcast.14, f32[8192,128]{1,0:T(8,128)S(1)} %bitcast.15, ...), custom_call_target="tpu_custom_call" | custom-call | tf_op jit(solution)/shard_map/faces_and_moments/pallas_call | solution.py:282
  98.9 0.0 copy-start.6
  98.9 1.3 copy-done.6
  100.2 1.3 copy-done.8
  101.5 1.0 collective-permute-start.2
  102.5 1.5 collective-permute-done.2.received
  104.0 0.6 scatter.1
  104.6 1.4 collective-permute-start.3
  106.0 2.6 %collective-permute-start.4 = (f32[64,512]{1,0:T(8,128)S(1)}, f32[64,512]{1,0:T(8,128)S(1)}, u32[]{:S(2)}, u32[]{:S(2)}) collective-permute-start(f32[64,512]{1,0:T(8,128)S(1)} %get-tuple-element.29), channel_id=1, source_target_pairs={{0,8},{1,9},{2,10},{3,11},{4,12},{5,13},{6,14},{7,15},{8,0},{9,1},... | collective-permute-start | bytes 393224 | tf_op jit(solution)/shard_map/ppermute | solution.py:41
  108.6 1.1 collective-permute-start.5
  109.7 1.1 collective-permute-done.3.b
  110.8 3.9 %collective-permute-done.4.c = f32[64,512]{1,0:T(8,128)S(1)} collective-permute-done((f32[64,512]{1,0:T(8,128)S(1)}, f32[64,512]{1,0:T(8,128)S(1)}, u32[]{:S(2)}, u32[]{:S(2)}) %collective-permute-start.4) | collective-permute-done | bytes 131104 | tf_op jit(solution)/shard_map/ppermute | solution.py:41
  114.7 0.0 collective-permute-done.5.d
  114.7 1.6 %collective-permute-start.6 = (f32[64,512]{1,0:T(8,128)S(1)}, f32[64,512]{1,0:T(8,128)S(1)}, u32[]{:S(2)}, u32[]{:S(2)}) collective-permute-start(f32[64,512]{1,0:T(8,128)S(1)} %add_four.1.mine), channel_id=1, source_target_pairs={{0,2},{1,3},{2,0},{3,1},{4,6},{5,7},{6,4},{7,5},{8,10},{9,11},{10,... | collective-permute-start | bytes 393224 | tf_op jit(solution)/shard_map/ppermute | solution.py:37
  116.4 6.6 %copy.11 = f32[3072,512]{1,0:T(8,128)} copy(f32[3072,512]{0,1:T(8,128)} %all-gather.2.cloned.1.call-done) | data formatting | bytes 12582912 | tf_op jit(solution)/shard_map/all_gather | solution.py:408
  122.9 2.8 %copy-done.2 = f32[3072,512]{1,0:T(8,128)S(1)} copy-done((f32[3072,512]{1,0:T(8,128)S(1)}, f32[3072,512]{1,0:T(8,128)}, u32[]{:S(2)}) %copy-start.2) | copy-done | bytes 6291480
  125.7 1.6 %split_factors.1 = (bf16[3,1024,512]{2,1,0:T(8,128)(2,1)S(1)}, bf16[3,1024,512]{2,1,0:T(8,128)(2,1)S(1)}) custom-call(f32[8,3,128,512]{3,2,1,0:T(8,128)S(1)} %bitcast.16), custom_call_target="tpu_custom_call" | custom-call | flops 16777216 | bytes 12582912 | tf_op jit(solution)/shard_map/split_factors/pallas_call | solution.py:205
  127.3 0.0 collective-permute-done.6.theirs
  127.3 0.0 copy-start.5
  127.4 0.0 copy-start.7
  127.4 1.8 %collide.1.a = f32[64,512]{1,0:T(8,128)S(1)} custom-call(f32[64,512]{1,0:T(8,128)S(1)} %add_four.1.mine, f32[64,512]{1,0:T(8,128)S(1)} %collective-permute-done.6.theirs, bf16[3,1024,512]{2,1,0:T(8,128)(2,1)S(1)} %get-tuple-element.31.high, bf16[3,1024,512]{2,1,0:T(8,128)(2,1)S(1)} %get-tuple-element.32.low), custom_call_target="tpu_custom_call" | custom-call | tf_op jit(solution)/shard_map/collide/pallas_call | solution.py:310
  129.1 0.1 collective-permute-start.7
  129.3 3.8 %collective-permute-done.7.b = f32[64,512]{1,0:T(8,128)S(1)} collective-permute-done((f32[64,512]{1,0:T(8,128)S(1)}, f32[64,512]{1,0:T(8,128)S(1)}, u32[]{:S(2)}, u32[]{:S(2)}) %collective-permute-start.7) | collective-permute-done | bytes 131104 | tf_op jit(solution)/shard_map/ppermute | solution.py:37
  133.1 1.0 collective-permute-start.8
  134.1 2.2 %collective-permute-start.9 = (f32[64,512]{1,0:T(8,128)S(1)}, f32[64,512]{1,0:T(8,128)S(1)}, u32[]{:S(2)}, u32[]{:S(2)}) collective-permute-start(f32[64,512]{1,0:T(8,128)S(1)} %add_two.1.own), channel_id=1, source_target_pairs={{0,8},{1,9},{2,10},{3,11},{4,12},{5,13},{6,14},{7,15},{8,0},{9,1},... | collective-permute-start | bytes 393224 | tf_op jit(solution)/shard_map/ppermute | solution.py:41
  136.3 0.9 collective-permute-start.10
  137.2 3.7 %collective-permute-start.11 = (f32[64,512]{1,0:T(8,128)S(1)}, f32[64,512]{1,0:T(8,128)S(1)}, u32[]{:S(2)}, u32[]{:S(2)}) collective-permute-start(f32[64,512]{1,0:T(8,128)S(1)} %add_two.1.own), channel_id=1, source_target_pairs={{0,1},{1,0},{2,3},{3,2},{4,5},{5,4},{6,7},{7,6},{8,9},{9,8},{10,11... | collective-permute-start | bytes 393224 | tf_op jit(solution)/shard_map/ppermute | solution.py:37
  141.0 0.0 collective-permute-done.8.y_1
  141.0 1.2 collective-permute-start.12
  142.2 0.0 collective-permute-done.9.y_2
  142.2 1.6 collective-permute-start.13
  143.7 0.0 collective-permute-done.10.y_3
  143.7 0.6 collective-permute-start.14
  144.4 0.0 collective-permute-done.11.other
  144.4 0.0 collective-permute-done.12.z_1
  144.4 0.4 collective-permute-done.13.z_2
  144.7 0.6 collective-permute-done.14.z_3
  145.4 7.2 %relax.1 = f32[8192,128]{1,0:T(8,128)} custom-call(s32[2]{0:T(128)S(1)} %pad_add_fusion.place, f32[64,512]{1,0:T(8,128)S(1)} %add_two.1.own, f32[64,512]{1,0:T(8,128)S(1)} %collective-permute-done.8.y_1, f32[64,512]{1,0:T(8,128)S(1)} %collective-permute-done.9.y_2, f32[64,512]{1,0:T(8,128)S(1)} %collective-permute-done.10.y_3, ...), custom_call_target="tpu_custom_call" | custom-call | tf_op jit(solution)/shard_map/relax/pallas_call | solution.py:378
  (13 shorter events, 0.1 us)
Async XLA Ops:
  6.5 109.8 %all-gather.2.cloned.1.call-start = ((), (), s32[]{:S(2)}) async-start(), calls=%async_computation | async-start | bytes 7077888 | tf_op jit(solution)/shard_map/all_gather | solution.py:408
  10.6 2.2 %copy-start = (f32[2048,4,128]{2,1,0:T(4,128)S(1)}, f32[2048,4,128]{2,1,0:T(4,128)}, u32[]{:S(2)}) copy-start(f32[2048,4,128]{2,1,0:T(4,128)} %param.8) | copy-start | bytes 12582916
  15.0 56.7 %collective-permute-start = (f32[3,1024,128]{2,1,0:T(8,128)}, f32[3,1024,128]{2,1,0:T(8,128)}, u32[]{:S(2)}, u32[]{:S(2)}) collective-permute-start(f32[3,1024,128]{2,1,0:T(8,128)} %get-tuple-element.21), channel_id=1, source_target_pairs={{0,16},{16,32},{32,48},{48,64},{64,80},{80,96},{96,112},{112,128},... | collective-permute-start | bytes 4718600 | tf_op jit(solution)/shard_map/ppermute | solution.py:33
  18.8 72.8 %collective-permute-start.1 = (f32[3,1024,128]{2,1,0:T(8,128)}, f32[3,1024,128]{2,1,0:T(8,128)}, u32[]{:S(2)}, u32[]{:S(2)}) collective-permute-start(f32[3,1024,128]{2,1,0:T(8,128)} %get-tuple-element.22), channel_id=1, source_target_pairs={{0,240},{16,0},{32,16},{48,32},{64,48},{80,64},{96,80},{112,96},{1... | collective-permute-start | bytes 4718600 | tf_op jit(solution)/shard_map/ppermute | solution.py:33
  24.0 2.3 %copy-start.3 = (f32[512,2048]{1,0:T(8,128)S(1)}, f32[512,2048]{1,0:T(8,128)}, u32[]{:S(2)}) copy-start(f32[512,2048]{1,0:T(8,128)} %basis.1) | copy-start | bytes 12582916
  26.3 2.7 %copy-start.11 = (s32[4,128]{1,0:T(4,128)S(1)}, s32[4,128]{1,0:T(4,128)}, u32[]{:S(2)}) copy-start(s32[4,128]{1,0:T(4,128)} %param.14) | copy-start | bytes 6148
  26.3 2.7 %copy-start.12 = (s32[4,128]{1,0:T(4,128)S(1)}, s32[4,128]{1,0:T(4,128)}, u32[]{:S(2)}) copy-start(s32[4,128]{1,0:T(4,128)} %param.13) | copy-start | bytes 6148
  26.3 2.9 %copy-start.1 = (f32[2048,4,128]{2,1,0:T(4,128)S(1)}, f32[2048,4,128]{2,1,0:T(4,128)}, u32[]{:S(2)}) copy-start(f32[2048,4,128]{2,1,0:T(4,128)} %param.8) | copy-start | bytes 12582916
  28.8 8.3 %copy-start.4 = (bf16[2048,512]{1,0:T(8,128)(2,1)}, bf16[2048,512]{1,0:T(8,128)(2,1)S(1)}, u32[]{:S(2)}) copy-start(bf16[2048,512]{1,0:T(8,128)(2,1)S(1)} %get-tuple-element.36.low) | copy-start | bytes 6291460
  28.9 0.7 copy-start.10
  98.9 1.3 copy-start.6
  100.2 1.3 copy-start.8
  101.5 2.6 %collective-permute-start.2 = (f32[256,512]{1,0:T(8,128)S(1)}, f32[256,512]{1,0:T(8,128)S(1)}, u32[]{:S(2)}, u32[]{:S(2)}) collective-permute-start(f32[256,512]{1,0:T(8,128)S(1)} %get-tuple-element.26), channel_id=1, source_target_pairs={{0,1},{1,0},{2,3},{3,2},{4,5},{5,4},{6,7},{7,6},{8,9},{9,8},{10,11... | collective-permute-start | bytes 1572872 | tf_op jit(solution)/shard_map/ppermute | solution.py:37
  104.6 6.1 %collective-permute-start.3 = (f32[64,512]{1,0:T(8,128)S(1)}, f32[64,512]{1,0:T(8,128)S(1)}, u32[]{:S(2)}, u32[]{:S(2)}) collective-permute-start(f32[64,512]{1,0:T(8,128)S(1)} %get-tuple-element.28), channel_id=1, source_target_pairs={{0,4},{1,5},{2,6},{3,7},{4,8},{5,9},{6,10},{7,11},{8,12},{9,13},{1... | collective-permute-start | bytes 393224 | tf_op jit(solution)/shard_map/ppermute | solution.py:41
  106.0 8.7 %collective-permute-start.4 = (f32[64,512]{1,0:T(8,128)S(1)}, f32[64,512]{1,0:T(8,128)S(1)}, u32[]{:S(2)}, u32[]{:S(2)}) collective-permute-start(f32[64,512]{1,0:T(8,128)S(1)} %get-tuple-element.29), channel_id=1, source_target_pairs={{0,8},{1,9},{2,10},{3,11},{4,12},{5,13},{6,14},{7,15},{8,0},{9,1},... | collective-permute-start | bytes 393224 | tf_op jit(solution)/shard_map/ppermute | solution.py:41
  108.6 6.1 %collective-permute-start.5 = (f32[64,512]{1,0:T(8,128)S(1)}, f32[64,512]{1,0:T(8,128)S(1)}, u32[]{:S(2)}, u32[]{:S(2)}) collective-permute-start(f32[64,512]{1,0:T(8,128)S(1)} %get-tuple-element.30), channel_id=1, source_target_pairs={{0,12},{1,13},{2,14},{3,15},{4,0},{5,1},{6,2},{7,3},{8,4},{9,5},{1... | collective-permute-start | bytes 393224 | tf_op jit(solution)/shard_map/ppermute | solution.py:41
  114.7 12.6 %collective-permute-start.6 = (f32[64,512]{1,0:T(8,128)S(1)}, f32[64,512]{1,0:T(8,128)S(1)}, u32[]{:S(2)}, u32[]{:S(2)}) collective-permute-start(f32[64,512]{1,0:T(8,128)S(1)} %add_four.1.mine), channel_id=1, source_target_pairs={{0,2},{1,3},{2,0},{3,1},{4,6},{5,7},{6,4},{7,5},{8,10},{9,11},{10,... | collective-permute-start | bytes 393224 | tf_op jit(solution)/shard_map/ppermute | solution.py:37
  122.9 2.8 %copy-start.2 = (f32[3072,512]{1,0:T(8,128)S(1)}, f32[3072,512]{1,0:T(8,128)}, u32[]{:S(2)}) copy-start(f32[3072,512]{1,0:T(8,128)} %copy.11) | copy-start | bytes 18874372
  127.3 18.0 %copy-start.5 = (bf16[2048,512]{1,0:T(8,128)(2,1)S(1)}, bf16[2048,512]{1,0:T(8,128)(2,1)}, u32[]{:S(2)}) copy-start(bf16[2048,512]{1,0:T(8,128)(2,1)} %copy-done.4) | copy-start | bytes 6291460
  127.4 18.0 %copy-start.7 = (f32[4,1024,128]{2,1,0:T(8,128)S(1)}, f32[4,1024,128]{2,1,0:T(8,128)}, u32[]{:S(2)}) copy-start(f32[4,1024,128]{2,1,0:T(8,128)} %copy-done.6) | copy-start | bytes 6291460
  127.4 18.0 %copy-start.9 = (f32[4,1024,128]{2,1,0:T(8,128)S(1)}, f32[4,1024,128]{2,1,0:T(8,128)}, u32[]{:S(2)}) copy-start(f32[4,1024,128]{2,1,0:T(8,128)} %copy-done.8) | copy-start | bytes 6291460
  129.1 3.9 %collective-permute-start.7 = (f32[64,512]{1,0:T(8,128)S(1)}, f32[64,512]{1,0:T(8,128)S(1)}, u32[]{:S(2)}, u32[]{:S(2)}) collective-permute-start(f32[64,512]{1,0:T(8,128)S(1)} %collide.1.a), channel_id=1, source_target_pairs={{0,2},{1,3},{2,0},{3,1},{4,6},{5,7},{6,4},{7,5},{8,10},{9,11},{10,... | collective-permute-start | bytes 393224 | tf_op jit(solution)/shard_map/ppermute | solution.py:37
  133.1 7.9 %collective-permute-start.8 = (f32[64,512]{1,0:T(8,128)S(1)}, f32[64,512]{1,0:T(8,128)S(1)}, u32[]{:S(2)}, u32[]{:S(2)}) collective-permute-start(f32[64,512]{1,0:T(8,128)S(1)} %add_two.1.own), channel_id=1, source_target_pairs={{0,4},{1,5},{2,6},{3,7},{4,8},{5,9},{6,10},{7,11},{8,12},{9,13},{1... | collective-permute-start | bytes 393224 | tf_op jit(solution)/shard_map/ppermute | solution.py:41
  134.1 8.1 %collective-permute-start.9 = (f32[64,512]{1,0:T(8,128)S(1)}, f32[64,512]{1,0:T(8,128)S(1)}, u32[]{:S(2)}, u32[]{:S(2)}) collective-permute-start(f32[64,512]{1,0:T(8,128)S(1)} %add_two.1.own), channel_id=1, source_target_pairs={{0,8},{1,9},{2,10},{3,11},{4,12},{5,13},{6,14},{7,15},{8,0},{9,1},... | collective-permute-start | bytes 393224 | tf_op jit(solution)/shard_map/ppermute | solution.py:41
  136.3 7.4 %collective-permute-start.10 = (f32[64,512]{1,0:T(8,128)S(1)}, f32[64,512]{1,0:T(8,128)S(1)}, u32[]{:S(2)}, u32[]{:S(2)}) collective-permute-start(f32[64,512]{1,0:T(8,128)S(1)} %add_two.1.own), channel_id=1, source_target_pairs={{0,12},{1,13},{2,14},{3,15},{4,0},{5,1},{6,2},{7,3},{8,4},{9,5},{1... | collective-permute-start | bytes 393224 | tf_op jit(solution)/shard_map/ppermute | solution.py:41
  137.2 7.1 %collective-permute-start.11 = (f32[64,512]{1,0:T(8,128)S(1)}, f32[64,512]{1,0:T(8,128)S(1)}, u32[]{:S(2)}, u32[]{:S(2)}) collective-permute-start(f32[64,512]{1,0:T(8,128)S(1)} %add_two.1.own), channel_id=1, source_target_pairs={{0,1},{1,0},{2,3},{3,2},{4,5},{5,4},{6,7},{7,6},{8,9},{9,8},{10,11... | collective-permute-start | bytes 393224 | tf_op jit(solution)/shard_map/ppermute | solution.py:37
  141.0 3.4 %collective-permute-start.12 = (f32[64,512]{1,0:T(8,128)S(1)}, f32[64,512]{1,0:T(8,128)S(1)}, u32[]{:S(2)}, u32[]{:S(2)}) collective-permute-start(f32[64,512]{1,0:T(8,128)S(1)} %collective-permute-done.8.y_1), channel_id=1, source_target_pairs={{0,1},{1,0},{2,3},{3,2},{4,5},{5,4},{6,7},{7,6},{8,9},{9,8},{10,11... | collective-permute-start | bytes 393224 | tf_op jit(solution)/shard_map/ppermute | solution.py:37
  142.2 2.6 %collective-permute-start.13 = (f32[64,512]{1,0:T(8,128)S(1)}, f32[64,512]{1,0:T(8,128)S(1)}, u32[]{:S(2)}, u32[]{:S(2)}) collective-permute-start(f32[64,512]{1,0:T(8,128)S(1)} %collective-permute-done.9.y_2), channel_id=1, source_target_pairs={{0,1},{1,0},{2,3},{3,2},{4,5},{5,4},{6,7},{7,6},{8,9},{9,8},{10,11... | collective-permute-start | bytes 393224 | tf_op jit(solution)/shard_map/ppermute | solution.py:37
  143.7 1.6 %collective-permute-start.14 = (f32[64,512]{1,0:T(8,128)S(1)}, f32[64,512]{1,0:T(8,128)S(1)}, u32[]{:S(2)}, u32[]{:S(2)}) collective-permute-start(f32[64,512]{1,0:T(8,128)S(1)} %collective-permute-done.10.y_3), channel_id=1, source_target_pairs={{0,1},{1,0},{2,3},{3,2},{4,5},{5,4},{6,7},{7,6},{8,9},{9,8},{10,11... | collective-permute-start | bytes 393224 | tf_op jit(solution)/shard_map/ppermute | solution.py:37
Sparse Core Ops, SparseCore 0:
  10.7 47.6 all-gather.1
where the time goes:
time: 160 us; the launch traced here: 159 us
  waiting for transfers between devices  65.7 us (41%)
  Pallas kernels  30.8 us (19%)
  starting transfers between devices  28.2 us (18%)
  local copies, waits for them, and re-layouts  19 us (12%)
  between operations  13.6 us (8%)
  other arithmetic  2.2 us (1%)
    ppermute x2, waiting for transfers between devices, shifted(): return lax.ppermute(x, 'cells', [(i, (i + by) % size) for i in range(size)])  54.4 us
    unnamed x28, local copies, waits for them, and re-layouts  12.4 us
    ppermute x7, starting transfers between devices, exchanged(): return lax.ppermute(x, 'vel', [(i, i ^ bit) for i in range(16)])  9.89 us
    ppermute x6, starting transfers between devices, along_y(): return lax.ppermute(x, 'vel', [(i, (i + 4 * by) % 16) for i in range(16)])  9.22 us
    ppermute x2, starting transfers between devices, shifted(): return lax.ppermute(x, 'cells', [(i, (i + by) % size) for i in range(size)])  9.05 us
    pallas_call x1, Pallas kernels, local_part(): pl.pallas_call(local_kernel, name='local_transport', grid=(steps,), in_sp...  7.6 us
    pallas_call x1, Pallas kernels, moments_part(): pl.pallas_call(moments_kernel, name='faces_and_moments', grid=(steps,), i...  7.29 us
    pallas_call x1, Pallas kernels, relax(): pl.pallas_call(relax_kernel, name='relax', grid=(steps,), in_specs=[SM] +...  7.19 us
  transfers between devices with their start and end apart: 16, of which 8 were waited for; matrix products, arithmetic and copies ran while one was open for 4% of the time, Pallas kernels for 14%

commit v1 on v0

v1 whole, which is shorter than its diff:
```python
import functools

import jax
import jax.numpy as jnp
from jax import lax
from jax.experimental import pallas as pl
from jax.experimental.pallas import tpu as pltpu
from jax.sharding import PartitionSpec as P

POINTS = 32
STEP = 6.4 / POINTS
MIDDLE = (POINTS - 1) * 0.5
RATIO_X = 0.2
RATIO_Y = 0.12
HALF_STEP = 0.5

COLUMNS = 4
ROWS = 128
PER_DEVICE = 2048
HALF = PER_DEVICE // 2
CHUNK = 256
MOMENTS = 512
RANKS = 1024
F32 = jnp.float32
BF16 = jnp.bfloat16
MIB = 1 << 20
UP = (0, 1, 2, 3)
DOWN = (3, 2, 1, 0)
EVERY = (0, 1, 2, 3)


def shifted(x, by):
    size = lax.axis_size("cells")
    return lax.ppermute(x, "cells", [(i, (i + by) % size) for i in range(size)])


def exchanged(x, bit):
    return lax.ppermute(x, "vel", [(i, i ^ bit) for i in range(16)])


def along_y(x, by):
    return lax.ppermute(x, "vel", [(i, (i + 4 * by) % 16) for i in range(16)])


def halves(x):
    high = x.astype(BF16)
    return high, (x - high.astype(F32)).astype(BF16)


def minmod(a, b):
    return jnp.maximum(jnp.minimum(a, b), 0.0) + jnp.minimum(jnp.maximum(a, b), 0.0)


def dot(a, b):
    return jnp.dot(a, b, preferred_element_type=F32)


def dot_nt(a, b):
    return lax.dot_general(a, b, (((1,), (1,)), ((), ())), preferred_element_type=F32)


def column(ref, x, count=CHUNK):
    return ref[pl.ds(x, count, stride=COLUMNS), :]


def params(mib):
    return pltpu.CompilerParams(vmem_limit_bytes=mib * MIB)


def cost(flops, size):
    return pl.CostEstimate(flops=flops, bytes_accessed=size, transcendentals=0)


VM = pl.BlockSpec(memory_space=pltpu.VMEM)
SM = pl.BlockSpec(memory_space=pltpu.SMEM)


def pack_kernel(flat, right, left):
    upper = flat.at[pl.ds(HALF * COLUMNS, HALF * COLUMNS)]
    right[0] = column(upper, 3, HALF)
    right[1] = column(upper, 2, HALF)
    right[2] = column(flat, 3, HALF)
    left[0] = column(flat, 0, HALF)
    left[1] = column(flat, 1, HALF)
    left[2] = column(upper, 0, HALF)


def pack(flat):
    out = jax.ShapeDtypeStruct((3, HALF, ROWS), F32)
    return pl.pallas_call(
        pack_kernel,
        name="pack",
        in_specs=[VM],
        out_specs=[VM, VM],
        out_shape=[out, out],
        compiler_params=params(12),
        cost_estimate=cost(1 << 20, 8 * MIB),
    )(flat)


def local_kernel(speed, dist, kind, tables, out):
    step = pl.program_id(0)
    in_upper = step >= HALF // CHUNK
    line = lax.broadcasted_iota(jnp.int32, (CHUNK, ROWS), 0) + step * CHUNK
    along = (line // POINTS) % POINTS
    along = jnp.where(in_upper, POINTS - 1 - along, along)
    courant_y = jnp.abs((along.astype(F32) - MIDDLE) * STEP * RATIO_Y)
    slope_y = 0.5 * (1.0 - courant_y)
    courant_x = speed[0]
    slope_x = 0.5 * (1.0 - courant_x)
    fields = []
    for x in range(COLUMNS):
        here = column(dist, x)
        both = dot(jnp.concatenate(halves(here), axis=1), tables[0, x])
        face = here + slope_y * minmod(here - both[:, :ROWS], both[:, ROWS:] - here)
        behind = dot(jnp.concatenate(halves(face), axis=1), tables[0, x, :, :ROWS])
        fields.append((here, courant_y * (face - behind)))

    def finish(order):
        here = [fields[x][0] for x in order]
        change = [fields[x][1] for x in order]
        fluid = [(1 - kind[x : x + 1, :]).astype(F32) for x in order]
        face_1 = courant_x * (here[1] + slope_x * minmod(here[1] - here[0], here[2] - here[1]))
        face_2 = courant_x * (here[2] + slope_x * minmod(here[2] - here[1], here[3] - here[2]))
        out[order[0]] = here[0] - fluid[0] * change[0]
        out[order[1]] = here[1] - fluid[1] * (change[1] + face_1)
        out[order[2]] = here[2] - fluid[2] * (change[2] + (face_2 - face_1))
        out[order[3]] = here[3] - fluid[3] * (change[3] - face_2)

    @pl.when(in_upper)
    def _():
        finish((0, 1, 2, 3))

    @pl.when(jnp.logical_not(in_upper))
    def _():
        finish((3, 2, 1, 0))


def local_part(speed, flat, kind, tables):
    steps = PER_DEVICE // CHUNK
    quarter = steps // 4

    def against(i):
        return jnp.where((i >= quarter) & (i < 3 * quarter), 0, 1)

    return pl.pallas_call(
        local_kernel,
        name="local_transport",
        grid=(steps,),
        in_specs=[
            SM,
            pl.BlockSpec((CHUNK * COLUMNS, ROWS), lambda i: (i, 0)),
            VM,
            pl.BlockSpec((1, COLUMNS, 2 * ROWS, 2 * ROWS), lambda i: (against(i), 0, 0, 0)),
        ],
        out_specs=pl.BlockSpec((COLUMNS, CHUNK, ROWS), lambda i: (0, i, 0)),
        out_shape=jax.ShapeDtypeStruct((COLUMNS, PER_DEVICE, ROWS), F32),
        compiler_params=params(12),
        cost_estimate=cost(4 << 30, 10 * MIB),
    )(speed, flat, kind, tables)


def row_tables(following, preceding):
    rows = jnp.arange(ROWS, dtype=jnp.int32)[None, :, None]
    after = (rows == following[:, None, :]).astype(BF16)
    before = (rows == preceding[:, None, :]).astype(BF16)
    forward = jnp.concatenate([before, after], axis=2)
    backward = jnp.concatenate([after, before], axis=2)
    forward = jnp.concatenate([forward, forward], axis=1)
    backward = jnp.concatenate([backward, backward], axis=1)
    return jnp.stack([forward, backward])


def basis_kernel(basis, high, low, turned_high, turned_low):
    values = basis[...]
    high[...], low[...] = halves(values)
    turned_high[...], turned_low[...] = halves(values.T)


def split_basis(basis):
    width = 256
    flat = pl.BlockSpec((MOMENTS, width), lambda i: (0, i))
    turned = pl.BlockSpec((width, MOMENTS), lambda i: (i, 0))
    return pl.pallas_call(
        basis_kernel,
        name="split_basis",
        grid=(PER_DEVICE // width,),
        in_specs=[flat],
        out_specs=[flat, flat, turned, turned],
        out_shape=[jax.ShapeDtypeStruct((MOMENTS, PER_DEVICE), BF16)] * 2
        + [jax.ShapeDtypeStruct((PER_DEVICE, MOMENTS), BF16)] * 2,
        compiler_params=params(8),
        cost_estimate=cost(1 << 24, 12 * MIB),
    )(basis)


def stack_kernel(left, right, mixing, out):
    out[:128] = left[...]
    out[128:256] = right[...]
    out[256:] = mixing[...].T


def split_kernel(given, high, low):
    for which in range(3):
        high[which], low[which] = halves(given[which * 128 : (which + 1) * 128])


def gathered_factors(left, right, mixing):
    own = pl.pallas_call(
        stack_kernel,
        name="stack_factors",
        in_specs=[VM] * 3,
        out_specs=VM,
        out_shape=jax.ShapeDtypeStruct((384, MOMENTS), F32),
        compiler_params=params(3),
        cost_estimate=cost(1 << 20, 2 * MIB),
    )(left, right, mixing)
    groups = [[4 * y + 2 * z + c for y in range(4) for c in range(2)] for z in range(2)]
    every = lax.all_gather(own, "vel", axis=0, tiled=True, axis_index_groups=groups)
    out = jax.ShapeDtypeStruct((3, RANKS, MOMENTS), BF16)
    spec = pl.BlockSpec((3, 128, MOMENTS), lambda i: (0, i, 0))
    return pl.pallas_call(
        split_kernel,
        name="split_factors",
        grid=(RANKS // 128,),
        in_specs=[pl.BlockSpec((384, MOMENTS), lambda i: (i, 0))],
        out_specs=[spec, spec],
        out_shape=[out, out],
        compiler_params=params(6),
        cost_estimate=cost(1 << 24, 12 * MIB),
    )(every)


def moments_kernel(
    columns, speed, place, lower, upper, part_lower, part_upper, from_left, from_right, kind,
    high_lower, low_lower, high_upper, low_upper, moved, kept, sent, total,
):
    step = pl.program_id(0)
    courant = speed[0]
    slope = 0.5 * (1.0 - courant)

    def half(dist, part, out, order, behind, behind_two, ahead):
        fluid = [courant * (1 - kind[x : x + 1, :]).astype(F32) for x in order]
        first, second = column(dist, order[0]), column(dist, order[1])
        face_0 = first + slope * minmod(first - behind, second - first)
        values = {order[2]: part[order[2]]}
        values[order[1]] = part[order[1]] + fluid[1] * face_0
        if order[0] in columns:
            third, fourth = column(dist, order[2]), column(dist, order[3])
            face_in = behind + slope * minmod(behind - behind_two, first - behind)
            face_3 = fourth + slope * minmod(fourth - third, ahead - fourth)
            values[order[0]] = part[order[0]] - fluid[0] * (face_0 - face_in)
            values[order[3]] = part[order[3]] - fluid[3] * face_3
        values = [values[x] for x in columns]
        for i, value in enumerate(values):
            moved[out, i] = value
        return halves(jnp.concatenate(values, axis=1))

    @pl.when(step == 0)
    def _():
        total[...] = jnp.zeros_like(total)

    top, rest = half(lower, part_lower, 0, DOWN, from_right[0], from_right[1], from_left[2])
    added = total[...] + dot(high_lower[...], top)
    added = added + dot(high_lower[...], rest)
    added = added + dot(low_lower[...], top)
    top, rest = half(upper, part_upper, 1, UP, from_left[0], from_left[1], from_right[2])
    added = added + dot(high_upper[...], top)
    added = added + dot(high_upper[...], rest)
    added = added + dot(low_upper[...], top)
    total[...] = added

    @pl.when(step == pl.num_programs(0) - 1)
    def _():
        count = total.shape[1] // 2
        core = place[0]
        first = total[:, :count].T
        second = total[:, count:].T
        kept[...] = jnp.where(core == 0, first, second)
        sent[...] = jnp.where(core == 0, second, first)


def moments_part(columns, speed, place, flat, part, from_left, from_right, kind, high, low):
    steps = HALF // CHUNK
    rows = CHUNK * COLUMNS
    count = len(columns)
    lower = pl.BlockSpec((COLUMNS, CHUNK, ROWS), lambda i: (0, i, 0))
    upper = pl.BlockSpec((COLUMNS, CHUNK, ROWS), lambda i: (0, i + steps, 0))
    halo = pl.BlockSpec((3, CHUNK, ROWS), lambda i: (0, i, 0))
    basis_lower = pl.BlockSpec((MOMENTS, CHUNK), lambda i: (0, i))
    basis_upper = pl.BlockSpec((MOMENTS, CHUNK), lambda i: (0, i + steps))
    piece = jax.ShapeDtypeStruct((count * ROWS // 2, MOMENTS), F32)
    return pl.pallas_call(
        functools.partial(moments_kernel, columns),
        name="faces_and_moments",
        grid=(steps,),
        in_specs=[
            SM,
            SM,
            pl.BlockSpec((rows, ROWS), lambda i: (i, 0)),
            pl.BlockSpec((rows, ROWS), lambda i: (i + steps, 0)),
            lower,
            upper,
            halo,
            halo,
            VM,
            basis_lower,
            basis_lower,
            basis_upper,
            basis_upper,
        ],
        out_specs=[pl.BlockSpec((2, count, CHUNK, ROWS), lambda i: (0, 0, i, 0)), VM, VM],
        out_shape=[jax.ShapeDtypeStruct((2, count, HALF, ROWS), F32), piece, piece],
        scratch_shapes=[pltpu.VMEM((MOMENTS, count * ROWS), F32)],
        compiler_params=params(18),
        cost_estimate=cost(8 << 30, 20 * MIB),
    )(speed, place, flat, flat, part, part, from_left, from_right, kind, high, low, high, low)


def small_call(kernel, name, count, shape, operands, smem=0, mib=3):
    out = [jax.ShapeDtypeStruct(shape, F32)] * count
    return pl.pallas_call(
        kernel,
        name=name,
        in_specs=[SM] * smem + [VM] * (len(operands) - smem),
        out_specs=[VM] * count if count > 1 else VM,
        out_shape=out if count > 1 else out[0],
        compiler_params=params(mib),
        cost_estimate=cost(1 << 20, 1 * MIB),
    )(*operands)


def scatter_kernel(place, kept, received, own, to_one, to_two, to_three):
    size = own.shape[0]
    for away, out in enumerate((own, to_one, to_two, to_three)):
        at = pl.multiple_of(((place[1] + away) % 4) * size, size)
        out[...] = kept[pl.ds(at, size), :] + received[pl.ds(at, size), :]


def add_four_kernel(a, b, c, d, out):
    out[...] = (a[...] + b[...]) + (c[...] + d[...])


def add_two_kernel(a, b, out):
    out[...] = a[...] + b[...]


def collision_kernel(mine, theirs, high, low, out):
    size = out.shape[0]

    def times(values, which, product):
        top, rest = halves(values)
        both = product(jnp.concatenate([top, rest], axis=0), high[which])
        return both[:size] + (both[size:] + product(top, low[which]))

    moments = mine[...] + theirs[...]
    terms = times(moments, 0, dot_nt) * times(moments, 1, dot_nt)
    out[...] = times(terms, 2, dot)


def collision_part(place, kept, sent, factor_high, factor_low):
    shape = (kept.shape[0] // 4, MOMENTS)
    operands = (place, kept, exchanged(sent, 1))
    own, *others = small_call(scatter_kernel, "scatter", 4, shape, operands, 1)
    arrived = [along_y(piece, away + 1) for away, piece in enumerate(others)]
    summed = small_call(add_four_kernel, "add_four", 1, shape, (own, *arrived))
    operands = (summed, exchanged(summed, 2), factor_high, factor_low)
    share = small_call(collision_kernel, "collide", 1, shape, operands, mib=10)
    whole = small_call(add_two_kernel, "add_two", 1, shape, (share, exchanged(share, 2)))
    pieces = [whole] + [along_y(whole, away) for away in (1, 2, 3)]
    return pieces + [exchanged(piece, 1) for piece in pieces]


def relax_kernel(
    columns, place, own, y_1, y_2, y_3, other, z_1, z_2, z_3, kind, moved,
    high, low, out, gathered, turned_high, turned_low,
):
    step = pl.program_id(0)
    size = own.shape[0]

    @pl.when(step == 0)
    def _():
        pieces = (((own, y_1, y_2, y_3), place[0]), ((other, z_1, z_2, z_3), 1 - place[0]))
        for group, core in pieces:
            for away, piece in enumerate(group):
                at = core * 4 + (place[1] + (4 - away)) % 4
                gathered[pl.ds(pl.multiple_of(at * size, size), size), :] = piece[...]
        turned_high[...], turned_low[...] = halves(gathered[...].T)

    gain = dot(high[...], turned_high[...])
    gain = gain + dot(high[...], turned_low[...])
    gain = gain + dot(low[...], turned_high[...])
    for i, x in enumerate(columns):
        fluid = HALF_STEP * (1 - kind[x : x + 1, :]).astype(F32)
        out[pl.ds(x, CHUNK, stride=COLUMNS), :] = (
            moved[0, i] + fluid * gain[:, i * ROWS : (i + 1) * ROWS]
        )


def relax(columns, place, pieces, kind, moved, high, low):
    steps = PER_DEVICE // CHUNK
    half = steps // 2
    count = len(columns)
    turned = pl.BlockSpec((CHUNK, MOMENTS), lambda i: (i, 0))
    return pl.pallas_call(
        functools.partial(relax_kernel, columns),
        name="relax",
        grid=(steps,),
        in_specs=[SM]
        + [VM] * 9
        + [
            pl.BlockSpec((1, count, CHUNK, ROWS), lambda i: (i // half, 0, i % half, 0)),
            turned,
            turned,
        ],
        out_specs=pl.BlockSpec((CHUNK * COLUMNS, ROWS), lambda i: (i, 0)),
        out_shape=jax.ShapeDtypeStruct((PER_DEVICE * COLUMNS, ROWS), F32),
        scratch_shapes=[
            pltpu.VMEM((count * ROWS, MOMENTS), F32),
            pltpu.VMEM((MOMENTS, count * ROWS), BF16),
            pltpu.VMEM((MOMENTS, count * ROWS), BF16),
        ],
        compiler_params=params(14),
        cost_estimate=cost(8 << 30, 16 * MIB),
    )(place, *pieces, kind, moved, high, low)


def on_device(dist, basis, left_factor, right_factor, mixing, next_cell, prev_cell, cell_kind):
    owner = lax.axis_index("vel")
    place = jnp.stack([owner % 2, owner // 4]).astype(jnp.int32)
    speed = ((MIDDLE - owner.astype(F32)) * STEP * RATIO_X).reshape(1)
    flat = dist.reshape(PER_DEVICE * COLUMNS, ROWS)
    to_right, to_left = pack(flat)
    from_left = shifted(to_right, 1)
    from_right = shifted(to_left, -1)

    given = (left_factor, right_factor, mixing)
    _, (left_factor, right_factor, mixing) = lax.optimization_barrier((to_left, given))
    factors = gathered_factors(left_factor, right_factor, mixing)
    high, low, turned_high, turned_low = split_basis(basis)
    part = local_part(speed, flat, cell_kind, row_tables(next_cell, prev_cell))
    halo = (from_left, from_right)
    (from_left, from_right), factors = lax.optimization_barrier((halo, factors))

    moved, kept, sent = moments_part(
        EVERY, speed, place, flat, part, from_left, from_right, cell_kind, high, low
    )
    pieces = collision_part(place, kept, sent, *factors)
    out = relax(EVERY, place, pieces, cell_kind, moved, turned_high, turned_low)
    return out.reshape(dist.shape)


def solution(mesh):
    in_specs = (
        P("vel", "cells", None),
        P(None, "vel"),
        P("vel", None),
        P("vel", None),
        P(None, "vel"),
        P("cells", None),
        P("cells", None),
        P("cells", None),
    )
    out_specs = P("vel", "cells", None)
    return jax.shard_map(
        on_device, mesh=mesh, in_specs=in_specs, out_specs=out_specs, check_vma=False
    )
```

time: 160 us -> 151 us (0.944)
  waiting for transfers between devices: 65.7 us -> 56.5 us
  starting transfers between devices: 28.2 us -> 32.1 us
  other arithmetic: 2.2 us -> 0.3 us
  local copies, waits for them, and re-layouts: 19 us -> 17.1 us
    ppermute x2, waiting for transfers between devices: 54.4 us -> 24.5 us  [shifted(): return lax.ppermute(x, 'cells', [(i, (i + by) % size) for i in range(size)])]
    all_gather x1, waiting for transfers between devices: 0.01 us -> 19.8 us  [gathered_factors(): lax.all_gather(own, 'vel', axis=0, tiled=True, axis_index_groups=groups)]
    all_gather x1 -> x0, local copies, waits for them, and re-layouts: 6.58 us -> none  [on_device(): lax.all_gather(mine, 'vel', axis=0, tiled=True, axis_index_groups=groups)]
    ppermute x7, starting transfers between devices: 9.89 us -> 14.8 us  [exchanged(): return lax.ppermute(x, 'vel', [(i, i ^ bit) for i in range(16)])]
    unnamed x28 -> x38, local copies, waits for them, and re-layouts: 12.4 us -> 17.1 us
    concatenate x1 -> x0, other arithmetic: 1.87 us -> none  [on_device(): mine = jnp.concatenate([left_factor, right_factor, mixing.T], axis=0)]
    pallas_call x4 -> x5, Pallas kernels: 18.2 us -> 18.7 us  [the longest x1 7.27 us: relax(): pl.pallas_call(functools.partial(relax_kernel, columns), name='relax', gr...]
  transfers between devices with their start and end apart: 16 -> 16, of which waited for: 8 -> 9; matrix products, arithmetic and copies ran while one was open for 4% -> 0% of each run, Pallas kernels for 14% -> 8%
where the time goes in v1:
time: 151 us
  waiting for transfers between devices  56.5 us (37%)
  starting transfers between devices  32.1 us (21%)
  Pallas kernels  31.2 us (21%)
  local copies, waits for them, and re-layouts  17.1 us (11%)
  between operations  13.6 us (9%)
    ppermute x2, waiting for transfers between devices, shifted(): return lax.ppermute(x, 'cells', [(i, (i + by) % size) for i in range(size)])  24.5 us
    all_gather x1, waiting for transfers between devices, gathered_factors(): lax.all_gather(own, 'vel', axis=0, tiled=True, axis_index_groups=groups)  19.8 us
    unnamed x38, local copies, waits for them, and re-layouts  17.1 us
    ppermute x7, starting transfers between devices, exchanged(): return lax.ppermute(x, 'vel', [(i, i ^ bit) for i in range(16)])  14.8 us
    ppermute x2, starting transfers between devices, shifted(): return lax.ppermute(x, 'cells', [(i, (i + by) % size) for i in range(size)])  9.21 us
    ppermute x6, starting transfers between devices, along_y(): return lax.ppermute(x, 'vel', [(i, (i + 4 * by) % 16) for i in range(16)])  8.03 us
    pallas_call x1, Pallas kernels, local_part(): pl.pallas_call(local_kernel, name='local_transport', grid=(steps,), in_sp...  7.62 us
    pallas_call x1, Pallas kernels, relax(): pl.pallas_call(functools.partial(relax_kernel, columns), name='relax', gr...  7.27 us
  transfers between devices with their start and end apart: 16, of which 9 were waited for; matrix products, arithmetic and copies ran while one was open for 0% of the time, Pallas kernels for 8%

profile of v1, /device:TPU:1, one launch (start us, length us, event | category | flops | bytes accessed | tf_op | source)
XLA Modules:
  0.0 150.8 jit_solution(16045984514276061345)
XLA Ops:
  6.5 0.0 all-gather.2.cloned.1.call-start
  6.5 2.2 %copy-done.2 = f32[2048,4,128]{2,1,0:T(4,128)S(1)} copy-done((f32[2048,4,128]{2,1,0:T(4,128)S(1)}, f32[2048,4,128]{2,1,0:T(4,128)}, u32[]{:S(2)}) %copy-start.2) | copy-done | bytes 4194328
  8.7 1.9 %pack.1 = (f32[3,1024,128]{2,1,0:T(8,128)}, f32[3,1024,128]{2,1,0:T(8,128)}) custom-call(f32[8192,128]{1,0:T(8,128)S(1)} %bitcast.9), custom_call_target="tpu_custom_call" | custom-call | flops 1048576 | bytes 8388608 | tf_op jit(solution)/shard_map/pack/pallas_call | solution.py:90
  10.6 0.0 copy-done.5
  10.6 0.0 copy-done.6
  10.6 0.0 copy-done.7
  10.6 0.0 copy-start.17
  10.6 0.0 copy-start.18
  10.7 1.0 stack_factors.1
  11.7 0.0 all-gather.2.cloned.1.call-update
  11.7 3.9 %collective-permute-start = (f32[3,1024,128]{2,1,0:T(8,128)}, f32[3,1024,128]{2,1,0:T(8,128)}, u32[]{:S(2)}, u32[]{:S(2)}) collective-permute-start(f32[3,1024,128]{2,1,0:T(8,128)} %get-tuple-element.27), channel_id=1, source_target_pairs={{0,16},{16,32},{32,48},{48,64},{64,80},{80,96},{96,112},{112,128},... | collective-permute-start | bytes 4718600 | tf_op jit(solution)/shard_map/ppermute | solution.py:34
  15.6 5.3 %collective-permute-start.1 = (f32[3,1024,128]{2,1,0:T(8,128)}, f32[3,1024,128]{2,1,0:T(8,128)}, u32[]{:S(2)}, u32[]{:S(2)}) collective-permute-start(f32[3,1024,128]{2,1,0:T(8,128)} %get-tuple-element.28), channel_id=1, source_target_pairs={{0,240},{16,0},{32,16},{48,32},{64,48},{80,64},{96,80},{112,96},{1... | collective-permute-start | bytes 4718600 | tf_op jit(solution)/shard_map/ppermute | solution.py:34
  20.9 2.2 %copy-done.1 = f32[512,2048]{1,0:T(8,128)S(1)} copy-done((f32[512,2048]{1,0:T(8,128)S(1)}, f32[512,2048]{1,0:T(8,128)}, u32[]{:S(2)}) %copy-start.1) | copy-done | bytes 4194328
  23.1 2.5 %split_basis.1 = (bf16[512,2048]{1,0:T(8,128)(2,1)S(1)}, bf16[512,2048]{1,0:T(8,128)(2,1)S(1)}, bf16[2048,512]{1,0:T(8,128)(2,1)S(1)}, bf16[2048,512]{1,0:T(8,128)(2,1)S(1)}) custom-call(f32[512,2048]{1,0:T(8,128)S(1)} %copy-done.1), custom_call_target="tpu_custom_call" | custom-call | flops 16777216 | bytes 12582912 | tf_op jit(solution)/shard_map/split_basis/pallas_call | solution.py:184
  25.7 0.0 copy-start.8
  25.7 1.4 copy-done.8
  27.1 1.4 copy-done.10
  28.4 1.4 copy-done.12
  29.8 0.1 pad_add_fusion.place
  29.9 0.0 copy-done.17
  29.9 0.0 copy-done.18
  29.9 0.1 fusion
  30.0 0.1 maximum_bitcast_fusion
  30.0 0.1 pad_maximum_fusion.tables
  30.2 7.6 %local_transport.1.part_lower.part_upper = f32[4,2048,128]{2,1,0:T(8,128)S(1)} custom-call(f32[1]{0:T(128)} %bitcast.2.speed, f32[8192,128]{1,0:T(8,128)S(1)} %bitcast.10, s32[4,128]{1,0:T(4,128)S(1)} %copy-done.14, bf16[2,4,256,256]{3,2,1,0:T(8,128)(2,1)S(1)} %pad_maximum_fusion.tables), custom_call_target="tpu_custom_call" | custom-call | flops 4294967296 | bytes 10485760 | tf_op jit(solution)/shard_map/local_transport/pallas_call | solution.py:146
  37.8 0.0 copy-start.15
  37.8 2.0 %copy-done.15 = f32[4,2048,128]{2,1,0:T(8,128)} copy-done((f32[4,2048,128]{2,1,0:T(8,128)}, f32[4,2048,128]{2,1,0:T(8,128)S(1)}, u32[]{:S(2)}) %copy-start.15) | copy-done | bytes 4194328
  39.8 19.8 %all-gather.2.cloned.1.call-done.given = f32[3072,512]{1,0:T(8,128)} async-done(((f32[384,512]{1,0:T(8,128)}), f32[3072,512]{1,0:T(8,128)}) %all-gather.2.cloned.1.call-update) | async-done | bytes 6291472 | tf_op jit(solution)/shard_map/all_gather | solution.py:219
  59.6 2.8 %copy-done = f32[3072,512]{1,0:T(8,128)S(1)} copy-done((f32[3072,512]{1,0:T(8,128)S(1)}, f32[3072,512]{1,0:T(8,128)}, u32[]{:S(2)}) %copy-start) | copy-done | bytes 6291480
  62.4 1.5 split_factors.1
  63.8 4.7 %collective-permute-done.from_left = f32[3,1024,128]{2,1,0:T(8,128)} collective-permute-done((f32[3,1024,128]{2,1,0:T(8,128)}, f32[3,1024,128]{2,1,0:T(8,128)}, u32[]{:S(2)}, u32[]{:S(2)}) %collective-permute-start) | collective-permute-done | bytes 1572896 | tf_op jit(solution)/shard_map/ppermute | solution.py:34
  68.6 19.8 %collective-permute-done.1.from_right = f32[3,1024,128]{2,1,0:T(8,128)} collective-permute-done((f32[3,1024,128]{2,1,0:T(8,128)}, f32[3,1024,128]{2,1,0:T(8,128)}, u32[]{:S(2)}, u32[]{:S(2)}) %collective-permute-start.1) | collective-permute-done | bytes 1572896 | tf_op jit(solution)/shard_map/ppermute | solution.py:34
  88.4 1.6 %copy-done.13 = bf16[512,2048]{1,0:T(8,128)(2,1)S(1)} copy-done((bf16[512,2048]{1,0:T(8,128)(2,1)S(1)}, bf16[512,2048]{1,0:T(8,128)(2,1)}, u32[]{:S(2)}) %copy-start.13) | copy-done | bytes 2097176
  90.0 2.2 %copy-done.16 = f32[4,2048,128]{2,1,0:T(8,128)S(1)} copy-done((f32[4,2048,128]{2,1,0:T(8,128)S(1)}, f32[4,2048,128]{2,1,0:T(8,128)}, u32[]{:S(2)}) %copy-start.16) | copy-done | bytes 4194328
  92.1 7.0 %faces_and_moments.1 = (f32[2,4,1024,128]{3,2,1,0:T(8,128)S(1)}, f32[256,512]{1,0:T(8,128)S(1)}, f32[256,512]{1,0:T(8,128)S(1)}) custom-call(f32[1]{0:T(128)} %bitcast.2.speed, s32[2]{0:T(128)S(1)} %pad_add_fusion.place, f32[8192,128]{1,0:T(8,128)S(1)} %bitcast.11, f32[8192,128]{1,0:T(8,128)S(1)} %bitcast.12, f32[4,2048,128]{2,1,0:T(8,128)S(1)} %copy-done.16, ...), custom_call_target="tpu_custom_call" | custom-call | flops 8589934592 | bytes 20971520 | tf_op jit(solution)/shard_map/faces_and_moments/pallas_call | solution.py:293
  99.1 1.1 collective-permute-start.2
  100.2 1.5 %collective-permute-done.2.received = f32[256,512]{1,0:T(8,128)S(1)} collective-permute-done((f32[256,512]{1,0:T(8,128)S(1)}, f32[256,512]{1,0:T(8,128)S(1)}, u32[]{:S(2)}, u32[]{:S(2)}) %collective-permute-start.2) | collective-permute-done | bytes 524320 | tf_op jit(solution)/shard_map/ppermute | solution.py:38
  101.7 0.6 scatter.1
  102.4 1.4 collective-permute-start.3
  103.7 2.6 %collective-permute-start.4 = (f32[64,512]{1,0:T(8,128)S(1)}, f32[64,512]{1,0:T(8,128)S(1)}, u32[]{:S(2)}, u32[]{:S(2)}) collective-permute-start(f32[64,512]{1,0:T(8,128)S(1)} %get-tuple-element.42), channel_id=1, source_target_pairs={{0,8},{1,9},{2,10},{3,11},{4,12},{5,13},{6,14},{7,15},{8,0},{9,1},... | collective-permute-start | bytes 393224 | tf_op jit(solution)/shard_map/ppermute | solution.py:42
  106.4 1.1 collective-permute-start.5
  107.4 1.1 collective-permute-done.3.b
  108.5 3.9 %collective-permute-done.4.c = f32[64,512]{1,0:T(8,128)S(1)} collective-permute-done((f32[64,512]{1,0:T(8,128)S(1)}, f32[64,512]{1,0:T(8,128)S(1)}, u32[]{:S(2)}, u32[]{:S(2)}) %collective-permute-start.4) | collective-permute-done | bytes 131104 | tf_op jit(solution)/shard_map/ppermute | solution.py:42
  112.4 0.0 collective-permute-done.5.d
  112.5 1.7 %collective-permute-start.6 = (f32[64,512]{1,0:T(8,128)S(1)}, f32[64,512]{1,0:T(8,128)S(1)}, u32[]{:S(2)}, u32[]{:S(2)}) collective-permute-start(f32[64,512]{1,0:T(8,128)S(1)} %add_four.1.mine), channel_id=1, source_target_pairs={{0,2},{1,3},{2,0},{3,1},{4,6},{5,7},{6,4},{7,5},{8,10},{9,11},{10,... | collective-permute-start | bytes 393224 | tf_op jit(solution)/shard_map/ppermute | solution.py:38
  114.2 2.4 %collective-permute-done.6.theirs = f32[64,512]{1,0:T(8,128)S(1)} collective-permute-done((f32[64,512]{1,0:T(8,128)S(1)}, f32[64,512]{1,0:T(8,128)S(1)}, u32[]{:S(2)}, u32[]{:S(2)}) %collective-permute-start.6) | collective-permute-done | bytes 131104 | tf_op jit(solution)/shard_map/ppermute | solution.py:38
  116.5 1.7 %collide.1.a = f32[64,512]{1,0:T(8,128)S(1)} custom-call(f32[64,512]{1,0:T(8,128)S(1)} %add_four.1.mine, f32[64,512]{1,0:T(8,128)S(1)} %collective-permute-done.6.theirs, bf16[3,1024,512]{2,1,0:T(8,128)(2,1)S(1)} %get-tuple-element.44.high, bf16[3,1024,512]{2,1,0:T(8,128)(2,1)S(1)} %get-tuple-element.45.low), custom_call_target="tpu_custom_call" | custom-call | flops 1048576 | bytes 1048576 | tf_op jit(solution)/shard_map/collide/pallas_call | solution.py:322
  118.3 1.5 %collective-permute-start.7 = (f32[64,512]{1,0:T(8,128)S(1)}, f32[64,512]{1,0:T(8,128)S(1)}, u32[]{:S(2)}, u32[]{:S(2)}) collective-permute-start(f32[64,512]{1,0:T(8,128)S(1)} %collide.1.a), channel_id=1, source_target_pairs={{0,2},{1,3},{2,0},{3,1},{4,6},{5,7},{6,4},{7,5},{8,10},{9,11},{10,... | collective-permute-start | bytes 393224 | tf_op jit(solution)/shard_map/ppermute | solution.py:38
  119.8 2.4 %collective-permute-done.7.b = f32[64,512]{1,0:T(8,128)S(1)} collective-permute-done((f32[64,512]{1,0:T(8,128)S(1)}, f32[64,512]{1,0:T(8,128)S(1)}, u32[]{:S(2)}, u32[]{:S(2)}) %collective-permute-start.7) | collective-permute-done | bytes 131104 | tf_op jit(solution)/shard_map/ppermute | solution.py:38
  122.2 2.1 %collective-permute-start.10 = (f32[64,512]{1,0:T(8,128)S(1)}, f32[64,512]{1,0:T(8,128)S(1)}, u32[]{:S(2)}, u32[]{:S(2)}) collective-permute-start(f32[64,512]{1,0:T(8,128)S(1)} %add_two.1.own), channel_id=1, source_target_pairs={{0,12},{1,13},{2,14},{3,15},{4,0},{5,1},{6,2},{7,3},{8,4},{9,5},{1... | collective-permute-start | bytes 393224 | tf_op jit(solution)/shard_map/ppermute | solution.py:42
  124.3 0.8 collective-permute-start.9
  125.0 0.1 collective-permute-start.8
  125.2 4.4 %collective-permute-start.11 = (f32[64,512]{1,0:T(8,128)S(1)}, f32[64,512]{1,0:T(8,128)S(1)}, u32[]{:S(2)}, u32[]{:S(2)}) collective-permute-start(f32[64,512]{1,0:T(8,128)S(1)} %add_two.1.own), channel_id=1, source_target_pairs={{0,1},{1,0},{2,3},{3,2},{4,5},{5,4},{6,7},{7,6},{8,9},{9,8},{10,11... | collective-permute-start | bytes 393224 | tf_op jit(solution)/shard_map/ppermute | solution.py:38
  129.6 0.0 collective-permute-done.10.y_3
  129.6 1.0 collective-permute-start.14
  130.6 0.0 collective-permute-done.9.y_2
  130.6 3.7 %collective-permute-start.13 = (f32[64,512]{1,0:T(8,128)S(1)}, f32[64,512]{1,0:T(8,128)S(1)}, u32[]{:S(2)}, u32[]{:S(2)}) collective-permute-start(f32[64,512]{1,0:T(8,128)S(1)} %collective-permute-done.9.y_2), channel_id=1, source_target_pairs={{0,1},{1,0},{2,3},{3,2},{4,5},{5,4},{6,7},{7,6},{8,9},{9,8},{10,11... | collective-permute-start | bytes 393224 | tf_op jit(solution)/shard_map/ppermute | solution.py:38
  134.4 0.0 collective-permute-done.8.y_1
  134.4 1.3 collective-permute-start.12
  135.7 0.0 collective-permute-done.11.other
  135.7 0.0 collective-permute-done.14.z_3
  135.7 0.0 collective-permute-done.13.z_2
  135.7 1.0 collective-permute-done.12.z_1
  136.7 7.3 %relax.1 = f32[8192,128]{1,0:T(8,128)} custom-call(s32[2]{0:T(128)S(1)} %pad_add_fusion.place, f32[64,512]{1,0:T(8,128)S(1)} %add_two.1.own, f32[64,512]{1,0:T(8,128)S(1)} %collective-permute-done.8.y_1, f32[64,512]{1,0:T(8,128)S(1)} %collective-permute-done.9.y_2, f32[64,512]{1,0:T(8,128)S(1)} %collective-permute-done.10.y_3, ...), custom_call_target="tpu_custom_call" | custom-call | flops 8589934592 | bytes 16777216 | tf_op jit(solution)/shard_map/relax/pallas_call | solution.py:405
  (22 shorter events, 0.1 us)
Async XLA Ops:
  6.5 53.0 %all-gather.2.cloned.1.call-start = ((), (), s32[]{:S(2)}) async-start(), calls=%async_computation | async-start | bytes 7077888 | tf_op jit(solution)/shard_map/all_gather | solution.py:219
  6.5 2.2 %copy-start.2 = (f32[2048,4,128]{2,1,0:T(4,128)S(1)}, f32[2048,4,128]{2,1,0:T(4,128)}, u32[]{:S(2)}) copy-start(f32[2048,4,128]{2,1,0:T(4,128)} %param.8) | copy-start | bytes 12582916
  8.7 1.9 %copy-start.5 = (f32[128,512]{1,0:T(8,128)S(1)}, f32[128,512]{1,0:T(8,128)}, u32[]{:S(2)}) copy-start(f32[128,512]{1,0:T(8,128)} %left) | copy-start | bytes 786436
  8.7 1.9 %copy-start.6 = (f32[128,512]{1,0:T(8,128)S(1)}, f32[128,512]{1,0:T(8,128)}, u32[]{:S(2)}) copy-start(f32[128,512]{1,0:T(8,128)} %right) | copy-start | bytes 786436
  8.7 1.9 %copy-start.7 = (f32[512,128]{1,0:T(8,128)S(1)}, f32[512,128]{1,0:T(8,128)}, u32[]{:S(2)}) copy-start(f32[512,128]{1,0:T(8,128)} %mixing) | copy-start | bytes 786436
  10.6 19.3 %copy-start.17 = (s32[4,128]{1,0:T(4,128)S(1)}, s32[4,128]{1,0:T(4,128)}, u32[]{:S(2)}) copy-start(s32[4,128]{1,0:T(4,128)} %param.14) | copy-start | bytes 6148
  10.6 19.3 %copy-start.18 = (s32[4,128]{1,0:T(4,128)S(1)}, s32[4,128]{1,0:T(4,128)}, u32[]{:S(2)}) copy-start(s32[4,128]{1,0:T(4,128)} %param.13) | copy-start | bytes 6148
  11.7 56.8 %collective-permute-start = (f32[3,1024,128]{2,1,0:T(8,128)}, f32[3,1024,128]{2,1,0:T(8,128)}, u32[]{:S(2)}, u32[]{:S(2)}) collective-permute-start(f32[3,1024,128]{2,1,0:T(8,128)} %get-tuple-element.27), channel_id=1, source_target_pairs={{0,16},{16,32},{32,48},{48,64},{64,80},{80,96},{96,112},{112,128},... | collective-permute-start | bytes 4718600 | tf_op jit(solution)/shard_map/ppermute | solution.py:34
  15.6 72.7 %collective-permute-start.1 = (f32[3,1024,128]{2,1,0:T(8,128)}, f32[3,1024,128]{2,1,0:T(8,128)}, u32[]{:S(2)}, u32[]{:S(2)}) collective-permute-start(f32[3,1024,128]{2,1,0:T(8,128)} %get-tuple-element.28), channel_id=1, source_target_pairs={{0,240},{16,0},{32,16},{48,32},{64,48},{80,64},{96,80},{112,96},{1... | collective-permute-start | bytes 4718600 | tf_op jit(solution)/shard_map/ppermute | solution.py:34
  20.9 2.2 %copy-start.1 = (f32[512,2048]{1,0:T(8,128)S(1)}, f32[512,2048]{1,0:T(8,128)}, u32[]{:S(2)}) copy-start(f32[512,2048]{1,0:T(8,128)} %basis.1) | copy-start | bytes 12582916
  23.1 7.0 %copy-start.3 = (f32[2048,4,128]{2,1,0:T(4,128)S(1)}, f32[2048,4,128]{2,1,0:T(4,128)}, u32[]{:S(2)}) copy-start(f32[2048,4,128]{2,1,0:T(4,128)} %param.8) | copy-start | bytes 12582916
  23.1 7.0 %copy-start.14 = (s32[4,128]{1,0:T(4,128)S(1)}, s32[4,128]{1,0:T(4,128)}, u32[]{:S(2)}) copy-start(s32[4,128]{1,0:T(4,128)} %kind.5) | copy-start | bytes 6148
  25.7 1.4 copy-start.8
  27.1 1.4 copy-start.10
  28.4 1.4 copy-start.12
  37.8 2.0 %copy-start.15 = (f32[4,2048,128]{2,1,0:T(8,128)}, f32[4,2048,128]{2,1,0:T(8,128)S(1)}, u32[]{:S(2)}) copy-start(f32[4,2048,128]{2,1,0:T(8,128)S(1)} %local_transport.1.part_lower.part_upper) | copy-start | bytes 12582916
  59.6 2.8 %copy-start = (f32[3072,512]{1,0:T(8,128)S(1)}, f32[3072,512]{1,0:T(8,128)}, u32[]{:S(2)}) copy-start(f32[3072,512]{1,0:T(8,128)} %all-gather.2.cloned.1.call-done.given) | copy-start | bytes 18874372
  62.4 26.0 %copy-start.4 = (f32[2048,4,128]{2,1,0:T(4,128)S(1)}, f32[2048,4,128]{2,1,0:T(4,128)}, u32[]{:S(2)}) copy-start(f32[2048,4,128]{2,1,0:T(4,128)} %param.8) | copy-start | bytes 12582916
  62.4 26.0 %copy-start.11 = (bf16[512,2048]{1,0:T(8,128)(2,1)S(1)}, bf16[512,2048]{1,0:T(8,128)(2,1)}, u32[]{:S(2)}) copy-start(bf16[512,2048]{1,0:T(8,128)(2,1)} %copy-done.10) | copy-start | bytes 6291460
  88.4 1.6 %copy-start.13 = (bf16[512,2048]{1,0:T(8,128)(2,1)S(1)}, bf16[512,2048]{1,0:T(8,128)(2,1)}, u32[]{:S(2)}) copy-start(bf16[512,2048]{1,0:T(8,128)(2,1)} %copy-done.12) | copy-start | bytes 6291460
  90.0 2.2 %copy-start.16 = (f32[4,2048,128]{2,1,0:T(8,128)S(1)}, f32[4,2048,128]{2,1,0:T(8,128)}, u32[]{:S(2)}) copy-start(f32[4,2048,128]{2,1,0:T(8,128)} %copy-done.15) | copy-start | bytes 12582916
  99.1 2.6 %collective-permute-start.2 = (f32[256,512]{1,0:T(8,128)S(1)}, f32[256,512]{1,0:T(8,128)S(1)}, u32[]{:S(2)}, u32[]{:S(2)}) collective-permute-start(f32[256,512]{1,0:T(8,128)S(1)} %get-tuple-element.39), channel_id=1, source_target_pairs={{0,1},{1,0},{2,3},{3,2},{4,5},{5,4},{6,7},{7,6},{8,9},{9,8},{10,11... | collective-permute-start | bytes 1572872 | tf_op jit(solution)/shard_map/ppermute | solution.py:38
  102.4 6.1 %collective-permute-start.3 = (f32[64,512]{1,0:T(8,128)S(1)}, f32[64,512]{1,0:T(8,128)S(1)}, u32[]{:S(2)}, u32[]{:S(2)}) collective-permute-start(f32[64,512]{1,0:T(8,128)S(1)} %get-tuple-element.41), channel_id=1, source_target_pairs={{0,4},{1,5},{2,6},{3,7},{4,8},{5,9},{6,10},{7,11},{8,12},{9,13},{1... | collective-permute-start | bytes 393224 | tf_op jit(solution)/shard_map/ppermute | solution.py:42
  103.7 8.7 %collective-permute-start.4 = (f32[64,512]{1,0:T(8,128)S(1)}, f32[64,512]{1,0:T(8,128)S(1)}, u32[]{:S(2)}, u32[]{:S(2)}) collective-permute-start(f32[64,512]{1,0:T(8,128)S(1)} %get-tuple-element.42), channel_id=1, source_target_pairs={{0,8},{1,9},{2,10},{3,11},{4,12},{5,13},{6,14},{7,15},{8,0},{9,1},... | collective-permute-start | bytes 393224 | tf_op jit(solution)/shard_map/ppermute | solution.py:42
  106.4 6.1 %collective-permute-start.5 = (f32[64,512]{1,0:T(8,128)S(1)}, f32[64,512]{1,0:T(8,128)S(1)}, u32[]{:S(2)}, u32[]{:S(2)}) collective-permute-start(f32[64,512]{1,0:T(8,128)S(1)} %get-tuple-element.43), channel_id=1, source_target_pairs={{0,12},{1,13},{2,14},{3,15},{4,0},{5,1},{6,2},{7,3},{8,4},{9,5},{1... | collective-permute-start | bytes 393224 | tf_op jit(solution)/shard_map/ppermute | solution.py:42
  112.5 24.2 %copy-start.9 = (bf16[2048,512]{1,0:T(8,128)(2,1)S(1)}, bf16[2048,512]{1,0:T(8,128)(2,1)}, u32[]{:S(2)}) copy-start(bf16[2048,512]{1,0:T(8,128)(2,1)} %copy-done.8) | copy-start | bytes 6291460
  112.5 4.1 %collective-permute-start.6 = (f32[64,512]{1,0:T(8,128)S(1)}, f32[64,512]{1,0:T(8,128)S(1)}, u32[]{:S(2)}, u32[]{:S(2)}) collective-permute-start(f32[64,512]{1,0:T(8,128)S(1)} %add_four.1.mine), channel_id=1, source_target_pairs={{0,2},{1,3},{2,0},{3,1},{4,6},{5,7},{6,4},{7,5},{8,10},{9,11},{10,... | collective-permute-start | bytes 393224 | tf_op jit(solution)/shard_map/ppermute | solution.py:38
  118.3 3.9 %collective-permute-start.7 = (f32[64,512]{1,0:T(8,128)S(1)}, f32[64,512]{1,0:T(8,128)S(1)}, u32[]{:S(2)}, u32[]{:S(2)}) collective-permute-start(f32[64,512]{1,0:T(8,128)S(1)} %collide.1.a), channel_id=1, source_target_pairs={{0,2},{1,3},{2,0},{3,1},{4,6},{5,7},{6,4},{7,5},{8,10},{9,11},{10,... | collective-permute-start | bytes 393224 | tf_op jit(solution)/shard_map/ppermute | solution.py:38
  122.2 7.4 %collective-permute-start.10 = (f32[64,512]{1,0:T(8,128)S(1)}, f32[64,512]{1,0:T(8,128)S(1)}, u32[]{:S(2)}, u32[]{:S(2)}) collective-permute-start(f32[64,512]{1,0:T(8,128)S(1)} %add_two.1.own), channel_id=1, source_target_pairs={{0,12},{1,13},{2,14},{3,15},{4,0},{5,1},{6,2},{7,3},{8,4},{9,5},{1... | collective-permute-start | bytes 393224 | tf_op jit(solution)/shard_map/ppermute | solution.py:42
  124.3 6.3 %collective-permute-start.9 = (f32[64,512]{1,0:T(8,128)S(1)}, f32[64,512]{1,0:T(8,128)S(1)}, u32[]{:S(2)}, u32[]{:S(2)}) collective-permute-start(f32[64,512]{1,0:T(8,128)S(1)} %add_two.1.own), channel_id=1, source_target_pairs={{0,8},{1,9},{2,10},{3,11},{4,12},{5,13},{6,14},{7,15},{8,0},{9,1},... | collective-permute-start | bytes 393224 | tf_op jit(solution)/shard_map/ppermute | solution.py:42
  125.0 9.3 %collective-permute-start.8 = (f32[64,512]{1,0:T(8,128)S(1)}, f32[64,512]{1,0:T(8,128)S(1)}, u32[]{:S(2)}, u32[]{:S(2)}) collective-permute-start(f32[64,512]{1,0:T(8,128)S(1)} %add_two.1.own), channel_id=1, source_target_pairs={{0,4},{1,5},{2,6},{3,7},{4,8},{5,9},{6,10},{7,11},{8,12},{9,13},{1... | collective-permute-start | bytes 393224 | tf_op jit(solution)/shard_map/ppermute | solution.py:42
  125.2 10.5 %collective-permute-start.11 = (f32[64,512]{1,0:T(8,128)S(1)}, f32[64,512]{1,0:T(8,128)S(1)}, u32[]{:S(2)}, u32[]{:S(2)}) collective-permute-start(f32[64,512]{1,0:T(8,128)S(1)} %add_two.1.own), channel_id=1, source_target_pairs={{0,1},{1,0},{2,3},{3,2},{4,5},{5,4},{6,7},{7,6},{8,9},{9,8},{10,11... | collective-permute-start | bytes 393224 | tf_op jit(solution)/shard_map/ppermute | solution.py:38
  129.6 6.1 %collective-permute-start.14 = (f32[64,512]{1,0:T(8,128)S(1)}, f32[64,512]{1,0:T(8,128)S(1)}, u32[]{:S(2)}, u32[]{:S(2)}) collective-permute-start(f32[64,512]{1,0:T(8,128)S(1)} %collective-permute-done.10.y_3), channel_id=1, source_target_pairs={{0,1},{1,0},{2,3},{3,2},{4,5},{5,4},{6,7},{7,6},{8,9},{9,8},{10,11... | collective-permute-start | bytes 393224 | tf_op jit(solution)/shard_map/ppermute | solution.py:38
  130.6 5.1 %collective-permute-start.13 = (f32[64,512]{1,0:T(8,128)S(1)}, f32[64,512]{1,0:T(8,128)S(1)}, u32[]{:S(2)}, u32[]{:S(2)}) collective-permute-start(f32[64,512]{1,0:T(8,128)S(1)} %collective-permute-done.9.y_2), channel_id=1, source_target_pairs={{0,1},{1,0},{2,3},{3,2},{4,5},{5,4},{6,7},{7,6},{8,9},{9,8},{10,11... | collective-permute-start | bytes 393224 | tf_op jit(solution)/shard_map/ppermute | solution.py:38
  134.4 2.3 %collective-permute-start.12 = (f32[64,512]{1,0:T(8,128)S(1)}, f32[64,512]{1,0:T(8,128)S(1)}, u32[]{:S(2)}, u32[]{:S(2)}) collective-permute-start(f32[64,512]{1,0:T(8,128)S(1)} %collective-permute-done.8.y_1), channel_id=1, source_target_pairs={{0,1},{1,0},{2,3},{3,2},{4,5},{5,4},{6,7},{7,6},{8,9},{9,8},{10,11... | collective-permute-start | bytes 393224 | tf_op jit(solution)/shard_map/ppermute | solution.py:38
Sparse Core Ops, SparseCore 0:
  11.8 47.6 all-gather.1

commit v2 on v1

--- a/solution.py
+++ b/solution.py
@@ -26,7 +26,8 @@
 MIB = 1 << 20
 UP = (0, 1, 2, 3)
 DOWN = (3, 2, 1, 0)
-EVERY = (0, 1, 2, 3)
+INNER = (1, 2)
+OUTER = (0, 3)
 
 
 def shifted(x, by):
@@ -75,27 +76,35 @@
 SM = pl.BlockSpec(memory_space=pltpu.SMEM)
 
 
-def pack_kernel(flat, right, left):
+def pack_kernel(flat, right_near, left_near, right_far, left_far):
     upper = flat.at[pl.ds(HALF * COLUMNS, HALF * COLUMNS)]
-    right[0] = column(upper, 3, HALF)
-    right[1] = column(upper, 2, HALF)
-    right[2] = column(flat, 3, HALF)
-    left[0] = column(flat, 0, HALF)
-    left[1] = column(flat, 1, HALF)
-    left[2] = column(upper, 0, HALF)
+    right_near[...] = column(upper, 3, HALF)
+    left_near[...] = column(flat, 0, HALF)
+    right_far[0] = column(upper, 2, HALF)
+    right_far[1] = column(flat, 3, HALF)
+    left_far[0] = column(flat, 1, HALF)
+    left_far[1] = column(upper, 0, HALF)
 
 
 def pack(flat):
-    out = jax.ShapeDtypeStruct((3, HALF, ROWS), F32)
+    near = jax.ShapeDtypeStruct((HALF, ROWS), F32)
+    far = jax.ShapeDtypeStruct((2, HALF, ROWS), F32)
     return pl.pallas_call(
         pack_kernel,
         name="pack",
         in_specs=[VM],
-        out_specs=[VM, VM],
-        out_shape=[out, out],
+        out_specs=[VM] * 4,
+        out_shape=[near, near, far, far],
         compiler_params=params(12),
         cost_estimate=cost(1 << 20, 8 * MIB),
     )(flat)
+
+
+def staged(stage, operands):
+    shapes = jax.eval_shape(stage, *operands)
+    blank = lambda *_: jax.tree.map(lambda x: jnp.zeros(x.shape, x.dtype), shapes)
+    taken = lax.optimization_barrier(jnp.array(True))
+    return lax.cond(taken, stage, blank, *operands)
 
 
 def local_kernel(speed, dist, kind, tables, out):
@@ -216,7 +225,10 @@
         cost_estimate=cost(1 << 20, 2 * MIB),
     )(left, right, mixing)
     groups = [[4 * y + 2 * z + c for y in range(4) for c in range(2)] for z in range(2)]
-    every = lax.all_gather(own, "vel", axis=0, tiled=True, axis_index_groups=groups)
+    return lax.all_gather(own, "vel", axis=0, tiled=True, axis_index_groups=groups)
+
+
+def split_factors(factors):
     out = jax.ShapeDtypeStruct((3, RANKS, MOMENTS), BF16)
     spec = pl.BlockSpec((3, 128, MOMENTS), lambda i: (0, i, 0))
     return pl.pallas_call(
@@ -228,29 +240,33 @@
         out_shape=[out, out],
         compiler_params=params(6),
         cost_estimate=cost(1 << 24, 12 * MIB),
-    )(every)
+    )(factors)
 
 
 def moments_kernel(
-    columns, speed, place, lower, upper, part_lower, part_upper, from_left, from_right, kind,
-    high_lower, low_lower, high_upper, low_upper, moved, kept, sent, total,
+    columns, speed, place, lower, upper, part_lower, part_upper, kind,
+    high_lower, low_lower, high_upper, low_upper, left_near, right_near, *rest,
 ):
+    *far, moved, kept, sent, total = rest
     step = pl.program_id(0)
     courant = speed[0]
     slope = 0.5 * (1.0 - courant)
 
-    def half(dist, part, out, order, behind, behind_two, ahead):
+    def half(dist, part, out, order, behind, outer):
         fluid = [courant * (1 - kind[x : x + 1, :]).astype(F32) for x in order]
         first, second = column(dist, order[0]), column(dist, order[1])
         face_0 = first + slope * minmod(first - behind, second - first)
-        values = {order[2]: part[order[2]]}
-        values[order[1]] = part[order[1]] + fluid[1] * face_0
-        if order[0] in columns:
+        if outer:
+            behind_two, ahead = outer
             third, fourth = column(dist, order[2]), column(dist, order[3])
             face_in = behind + slope * minmod(behind - behind_two, first - behind)
             face_3 = fourth + slope * minmod(fourth - third, ahead - fourth)
-            values[order[0]] = part[order[0]] - fluid[0] * (face_0 - face_in)
-            values[order[3]] = part[order[3]] - fluid[3] * face_3
+            values = {
+                order[0]: part[order[0]] - fluid[0] * (face_0 - face_in),
+                order[3]: part[order[3]] - fluid[3] * face_3,
+            }
+        else:
+            values = {order[1]: part[order[1]] + fluid[1] * face_0, order[2]: part[order[2]]}
         values = [values[x] for x in columns]
         for i, value in enumerate(values):
             moved[out, i] = value
@@ -260,11 +276,14 @@
     def _():
         total[...] = jnp.zeros_like(total)
 
-    top, rest = half(lower, part_lower, 0, DOWN, from_right[0], from_right[1], from_left[2])
+    outer = ((), ())
+    if far:
+        outer = ((far[1][0], far[0][1]), (far[0][0], far[1][1]))
+    top, rest = half(lower, part_lower, 0, DOWN, right_near[...], outer[0])
     added = total[...] + dot(high_lower[...], top)
     added = added + dot(high_lower[...], rest)
     added = added + dot(low_lower[...], top)
-    top, rest = half(upper, part_upper, 1, UP, from_left[0], from_left[1], from_right[2])
+    top, rest = half(upper, part_upper, 1, UP, left_near[...], outer[1])
     added = added + dot(high_upper[...], top)
     added = added + dot(high_upper[...], rest)
     added = added + dot(low_upper[...], top)
@@ -280,13 +299,12 @@
         sent[...] = jnp.where(core == 0, second, first)
 
 
-def moments_part(columns, speed, place, flat, part, from_left, from_right, kind, high, low):
+def moments_part(columns, speed, place, flat, part, kind, high, low, near, far=()):
     steps = HALF // CHUNK
     rows = CHUNK * COLUMNS
     count = len(columns)
     lower = pl.BlockSpec((COLUMNS, CHUNK, ROWS), lambda i: (0, i, 0))
     upper = pl.BlockSpec((COLUMNS, CHUNK, ROWS), lambda i: (0, i + steps, 0))
-    halo = pl.BlockSpec((3, CHUNK, ROWS), lambda i: (0, i, 0))
     basis_lower = pl.BlockSpec((MOMENTS, CHUNK), lambda i: (0, i))
     basis_upper = pl.BlockSpec((MOMENTS, CHUNK), lambda i: (0, i + steps))
     piece = jax.ShapeDtypeStruct((count * ROWS // 2, MOMENTS), F32)
@@ -301,20 +319,20 @@
             pl.BlockSpec((rows, ROWS), lambda i: (i + steps, 0)),
             lower,
             upper,
-            halo,
-            halo,
             VM,
             basis_lower,
             basis_lower,
             basis_upper,
             basis_upper,
-        ],
+        ]
+        + [pl.BlockSpec((CHUNK, ROWS), lambda i: (i, 0))] * 2
+        + [pl.BlockSpec((2, CHUNK, ROWS), lambda i: (0, i, 0))] * len(far),
         out_specs=[pl.BlockSpec((2, count, CHUNK, ROWS), lambda i: (0, 0, i, 0)), VM, VM],
         out_shape=[jax.ShapeDtypeStruct((2, count, HALF, ROWS), F32), piece, piece],
         scratch_shapes=[pltpu.VMEM((MOMENTS, count * ROWS), F32)],
-        compiler_params=params(18),
+        compiler_params=params(16),
         cost_estimate=cost(8 << 30, 20 * MIB),
-    )(speed, place, flat, flat, part, part, from_left, from_right, kind, high, low, high, low)
+    )(speed, place, flat, flat, part, part, kind, high, low, high, low, *near, *far)
 
 
 def small_call(kernel, name, count, shape, operands, smem=0, mib=3):
@@ -358,23 +376,37 @@
     out[...] = times(terms, 2, dot)
 
 
-def collision_part(place, kept, sent, factor_high, factor_low):
+def in_turn(sends, at_once):
+    done = []
+    for i, (send, piece, *rest) in enumerate(sends):
+        if i >= at_once:
+            piece, done[i - at_once] = lax.optimization_barrier((piece, done[i - at_once]))
+        done.append(send(piece, *rest))
+    return done
+
+
+def summed_moments(place, kept, sent, at_once):
     shape = (kept.shape[0] // 4, MOMENTS)
     operands = (place, kept, exchanged(sent, 1))
     own, *others = small_call(scatter_kernel, "scatter", 4, shape, operands, 1)
-    arrived = [along_y(piece, away + 1) for away, piece in enumerate(others)]
+    arrived = in_turn([(along_y, piece, i + 1) for i, piece in enumerate(others)], at_once)
     summed = small_call(add_four_kernel, "add_four", 1, shape, (own, *arrived))
-    operands = (summed, exchanged(summed, 2), factor_high, factor_low)
+    return summed, exchanged(summed, 2)
+
+
+def collision_part(moments, factor_high, factor_low, at_once):
+    shape = moments[0].shape
+    operands = (*moments, factor_high, factor_low)
     share = small_call(collision_kernel, "collide", 1, shape, operands, mib=10)
     whole = small_call(add_two_kernel, "add_two", 1, shape, (share, exchanged(share, 2)))
-    pieces = [whole] + [along_y(whole, away) for away in (1, 2, 3)]
-    return pieces + [exchanged(piece, 1) for piece in pieces]
+    pieces = [whole] + in_turn([(along_y, whole, away) for away in (1, 2, 3)], at_once)
+    return pieces + in_turn([(exchanged, piece, 1) for piece in pieces], at_once)
 
 
 def relax_kernel(
-    columns, place, own, y_1, y_2, y_3, other, z_1, z_2, z_3, kind, moved,
-    high, low, out, gathered, turned_high, turned_low,
+    columns, place, own, y_1, y_2, y_3, other, z_1, z_2, z_3, kind, moved, high, low, *rest
 ):
+    *finished, out, gathered, turned_high, turned_low = rest
     step = pl.program_id(0)
     size = own.shape[0]
 
@@ -392,37 +424,38 @@
     gain = gain + dot(low[...], turned_high[...])
     for i, x in enumerate(columns):
         fluid = HALF_STEP * (1 - kind[x : x + 1, :]).astype(F32)
-        out[pl.ds(x, CHUNK, stride=COLUMNS), :] = (
-            moved[0, i] + fluid * gain[:, i * ROWS : (i + 1) * ROWS]
-        )
-
-
-def relax(columns, place, pieces, kind, moved, high, low):
+        value = moved[0, i] + fluid * gain[:, i * ROWS : (i + 1) * ROWS]
+        if finished:
+            out[pl.ds(x, CHUNK, stride=COLUMNS), :] = value
+            there = INNER[i]
+            out[pl.ds(there, CHUNK, stride=COLUMNS), :] = finished[0][0, i]
+        else:
+            out[0, i] = value
+
+
+def relax(columns, place, pieces, kind, moved, high, low, finished=()):
     steps = PER_DEVICE // CHUNK
     half = steps // 2
     count = len(columns)
     turned = pl.BlockSpec((CHUNK, MOMENTS), lambda i: (i, 0))
+    planes = pl.BlockSpec((1, count, CHUNK, ROWS), lambda i: (i // half, 0, i % half, 0))
+    whole = pl.BlockSpec((CHUNK * COLUMNS, ROWS), lambda i: (i, 0))
+    shape = (PER_DEVICE * COLUMNS, ROWS) if finished else moved.shape
     return pl.pallas_call(
         functools.partial(relax_kernel, columns),
         name="relax",
         grid=(steps,),
-        in_specs=[SM]
-        + [VM] * 9
-        + [
-            pl.BlockSpec((1, count, CHUNK, ROWS), lambda i: (i // half, 0, i % half, 0)),
-            turned,
-            turned,
-        ],
-        out_specs=pl.BlockSpec((CHUNK * COLUMNS, ROWS), lambda i: (i, 0)),
-        out_shape=jax.ShapeDtypeStruct((PER_DEVICE * COLUMNS, ROWS), F32),
+        in_specs=[SM] + [VM] * 9 + [planes, turned, turned] + [planes] * len(finished),
+        out_specs=whole if finished else planes,
+        out_shape=jax.ShapeDtypeStruct(shape, F32),
         scratch_shapes=[
             pltpu.VMEM((count * ROWS, MOMENTS), F32),
             pltpu.VMEM((MOMENTS, count * ROWS), BF16),
             pltpu.VMEM((MOMENTS, count * ROWS), BF16),
         ],
         compiler_params=params(14),
-        cost_estimate=cost(8 << 30, 16 * MIB),
-    )(place, *pieces, kind, moved, high, low)
+        cost_estimate=cost(16 << 30, 1 * MIB),
+    )(place, *pieces, kind, moved, high, low, *finished)
 
 
 def on_device(dist, basis, left_factor, right_factor, mixing, next_cell, prev_cell, cell_kind):
@@ -430,23 +463,47 @@
     place = jnp.stack([owner % 2, owner // 4]).astype(jnp.int32)
     speed = ((MIDDLE - owner.astype(F32)) * STEP * RATIO_X).reshape(1)
     flat = dist.reshape(PER_DEVICE * COLUMNS, ROWS)
-    to_right, to_left = pack(flat)
-    from_left = shifted(to_right, 1)
-    from_right = shifted(to_left, -1)
-
+    right_near, left_near, right_far, left_far = pack(flat)
+    near = (shifted(right_near, 1), shifted(left_near, -1))
+    far = (shifted(right_far, 1), shifted(left_far, -1))
     given = (left_factor, right_factor, mixing)
-    _, (left_factor, right_factor, mixing) = lax.optimization_barrier((to_left, given))
-    factors = gathered_factors(left_factor, right_factor, mixing)
-    high, low, turned_high, turned_low = split_basis(basis)
-    part = local_part(speed, flat, cell_kind, row_tables(next_cell, prev_cell))
-    halo = (from_left, from_right)
-    (from_left, from_right), factors = lax.optimization_barrier((halo, factors))
-
-    moved, kept, sent = moments_part(
-        EVERY, speed, place, flat, part, from_left, from_right, cell_kind, high, low
+    _, given = lax.optimization_barrier((left_near, given))
+    factors = gathered_factors(*given)
+
+    def prepare(_, basis, speed, flat, kind, following, preceding):
+        part = local_part(speed, flat, kind, row_tables(following, preceding))
+        return split_basis(basis), part
+
+    given = (left_near[:8], basis, speed, flat, cell_kind, next_cell, prev_cell)
+    bases, part = staged(prepare, given)
+    high, low, turned_high, turned_low = bases
+
+    def inner_moments(speed, place, flat, part, kind, high, low, near):
+        moved, *pieces = moments_part(
+            INNER, speed, place, flat, part, kind, high, low, near
+        )
+        return moved, summed_moments(place, *pieces, 1)
+
+    given = (speed, place, flat, part, cell_kind, high, low, near)
+    moved, moments = staged(inner_moments, given)
+    moments, factors = lax.optimization_barrier((moments, factors))
+
+    def inner_collision(moments, factors):
+        factors = split_factors(factors)
+        pieces = collision_part(moments, *factors, 1)
+        return pieces, factors
+
+    pieces, factors = staged(inner_collision, (moments, factors))
+    finished = relax(INNER, place, pieces, cell_kind, moved, turned_high, turned_low)
+    finished, far = lax.optimization_barrier((finished, far))
+
+    moved, *pieces = moments_part(
+        OUTER, speed, place, flat, part, cell_kind, high, low, near, far
     )
-    pieces = collision_part(place, kept, sent, *factors)
-    out = relax(EVERY, place, pieces, cell_kind, moved, turned_high, turned_low)
+    pieces = collision_part(summed_moments(place, *pieces, 4), *factors, 4)
+    out = relax(
+        OUTER, place, pieces, cell_kind, moved, turned_high, turned_low, (finished,)
+    )
     return out.reshape(dist.shape)
 
 

time: 151 us -> 193 us (1.28)
  the two profiles are of different devices: /device:TPU:1 before, /device:TPU:67 now
where the time goes in v2:
time: 193 us; the launch traced here: 192 us
  Pallas kernels  67.5 us (35%)
  starting transfers between devices  56.6 us (29%)
  waiting for transfers between devices  54.3 us (28%)
  between operations  13.5 us (7%)
    ppermute x14, starting transfers between devices, exchanged(): return lax.ppermute(x, 'vel', [(i, i ^ bit) for i in range(16)])  30.9 us
    ppermute x4, waiting for transfers between devices, shifted(): return lax.ppermute(x, 'cells', [(i, (i + by) % size) for i in range(size)])  21.5 us
    ppermute x14, waiting for transfers between devices, exchanged(): return lax.ppermute(x, 'vel', [(i, i ^ bit) for i in range(16)])  18.5 us
    ppermute x12, starting transfers between devices, along_y(): return lax.ppermute(x, 'vel', [(i, (i + 4 * by) % 16) for i in range(16)])  17.9 us
    pallas_call x2, Pallas kernels, moments_part(): pl.pallas_call(functools.partial(moments_kernel, columns), name='faces_an...  14.4 us
    ppermute x12, waiting for transfers between devices, along_y(): return lax.ppermute(x, 'vel', [(i, (i + 4 * by) % 16) for i in range(16)])  14.3 us
    pallas_call x2, Pallas kernels, relax(): pl.pallas_call(functools.partial(relax_kernel, columns), name='relax', gr...  13.5 us
    pallas_call x8, Pallas kernels, small_call(): pl.pallas_call(kernel, name=name, in_specs=[SM] * smem + [VM] * (len(oper...  11.7 us
  transfers between devices with their start and end apart: 31, of which 18 were waited for; matrix products, arithmetic and copies ran while one was open for 0% of the time, Pallas kernels for 23%

profile of v2, /device:TPU:67, one launch (start us, length us, event | category | flops | bytes accessed | tf_op | source)
XLA Modules:
  0.0 192.4 jit_solution(2929113990499484471)
XLA Ops:
  6.5 3.3 %pack.1 = (f32[1024,128]{1,0:T(8,128)}, f32[1024,128]{1,0:T(8,128)}, f32[2,1024,128]{2,1,0:T(8,128)S(1)}, f32[2,1024,128]{2,1,0:T(8,128)S(1)}) custom-call(f32[8192,128]{1,0:T(8,128)} %bitcast.9), custom_call_target="tpu_custom_call" | custom-call | flops 1048576 | bytes 8388608 | tf_op jit(solution)/shard_map/pack/pallas_call | solution.py:92
  9.9 1.0 stack_factors.1
  10.9 4.3 %collective-permute-start.13 = (f32[1024,128]{1,0:T(8,128)}, f32[1024,128]{1,0:T(8,128)}, u32[]{:S(2)}, u32[]{:S(2)}) collective-permute-start(f32[1024,128]{1,0:T(8,128)} %get-tuple-element.127), channel_id=1, source_target_pairs={{0,16},{16,32},{32,48},{48,64},{64,80},{80,96},{96,112},{112,128},... | collective-permute-start | bytes 1572872 | tf_op jit(solution)/shard_map/ppermute | solution.py:35
  15.2 3.6 %collective-permute-start.15 = (f32[2,1024,128]{2,1,0:T(8,128)S(1)}, f32[2,1024,128]{2,1,0:T(8,128)S(1)}, u32[]{:S(2)}, u32[]{:S(2)}) collective-permute-start(f32[2,1024,128]{2,1,0:T(8,128)S(1)} %get-tuple-element.148), channel_id=1, source_target_pairs={{0,16},{16,32},{32,48},{48,64},{64,80},{80,96},{96,112},{112,128},... | collective-permute-start | bytes 3145736 | tf_op jit(solution)/shard_map/ppermute | solution.py:35
  18.8 15.6 %conditional.3 = (bf16[512,2048]{1,0:T(8,128)(2,1)}, bf16[512,2048]{1,0:T(8,128)(2,1)}, bf16[2048,512]{1,0:T(8,128)(2,1)}, bf16[2048,512]{1,0:T(8,128)(2,1)}, f32[4,2048,128]{2,1,0:T(8,128)}) conditional(s32[]{:T(128)} %convert_element_type.15, () %tuple.39, (f32[512,2048]{1,0:T(8,128)}, s32[4,128]{1,0:T(4,128)S(1)}, s32[4,128]{1,0:T(4,128)S(1)}, ...), branch_computations={%region_0.1_spmd, %region_1.2_spmd} | conditional | flops 4316725248 | bytes 43520068 | solution.py:107
  18.8 0.1 fusion
  18.9 0.1 maximum_bitcast_fusion
  19.0 0.1 pad_maximum_fusion.tables
  19.1 10.5 %local_transport.1 = f32[4,2048,128]{2,1,0:T(8,128)} custom-call(f32[1]{0:T(128)} %get-tuple-element.46.speed, f32[8192,128]{1,0:T(8,128)} %get-tuple-element.47.dist, s32[4,128]{1,0:T(4,128)S(1)} %get-tuple-element.48.kind, bf16[2,4,256,256]{3,2,1,0:T(8,128)(2,1)S(1)} %pad_maximum_fusion.tables), custom_call_target="tpu_custom_call" | custom-call | flops 4294967296 | bytes 10485760 | tf_op jit(solution)/shard_map/cond/branch_1_fun/local_transport/pallas_call | solution.py:155
  29.7 4.8 %split_basis.1 = (bf16[512,2048]{1,0:T(8,128)(2,1)}, bf16[512,2048]{1,0:T(8,128)(2,1)}, bf16[2048,512]{1,0:T(8,128)(2,1)}, bf16[2048,512]{1,0:T(8,128)(2,1)}) custom-call(f32[512,2048]{1,0:T(8,128)S(1)} %copy-done.3), custom_call_target="tpu_custom_call" | custom-call | flops 16777216 | bytes 12582912 | tf_op jit(solution)/shard_map/cond/branch_1_fun/split_basis/pallas_call | solution.py:193
  34.5 0.1 pad_add_fusion.place
  34.5 21.5 %collective-permute-done.14.right_near = f32[1024,128]{1,0:T(8,128)} collective-permute-done((f32[1024,128]{1,0:T(8,128)}, f32[1024,128]{1,0:T(8,128)}, u32[]{:S(2)}, u32[]{:S(2)}) %collective-permute-start.14) | collective-permute-done | bytes 524320 | tf_op jit(solution)/shard_map/ppermute | solution.py:35
  56.0 35.7 %conditional.4 = (f32[2,2,1024,128]{3,2,1,0:T(8,128)}, f32[32,512]{1,0:T(8,128)}, f32[32,512]{1,0:T(8,128)}) conditional(s32[]{:T(128)} %convert_element_type.15, () %tuple.42, (f32[1]{0:T(128)}, s32[2]{0:T(128)S(1)}, f32[8192,128]{1,0:T(8,128)}, f32[4,2048,128]{2,1,0:T(8,128)}, s32[4,128]{1,0:T(4,128)S(1)}, /*index=5*/bf16[512,2048]{1,0:T(8,128)(2,1)}, ...), branch_computations={%region_2.3_spmd, %region_3.4_spmd} | conditional | flops 8592031744 | bytes 25166048 | solution.py:107
  56.1 7.8 %faces_and_moments.2 = (f32[2,2,1024,128]{3,2,1,0:T(8,128)}, f32[128,512]{1,0:T(8,128)S(1)}, f32[128,512]{1,0:T(8,128)S(1)}) custom-call(f32[1]{0:T(128)} %get-tuple-element.51.speed, s32[2]{0:T(128)S(1)} %get-tuple-element.52.place, f32[8192,128]{1,0:T(8,128)} %get-tuple-element.53.lower.upper, f32[8192,128]{1,0:T(8,128)} %get-tuple-element.53.lower.upper, ...), custom_call_target="tpu_custom_call" | custom-call | flops 8589934592 | bytes 20971520 | tf_op jit(solution)/shard_map/cond/branch_1_fun/faces_and_moments/pallas_call | solution.py:311
  63.9 8.7 %collective-permute-start = (f32[128,512]{1,0:T(8,128)S(1)}, f32[128,512]{1,0:T(8,128)S(1)}, u32[]{:S(2)}, u32[]{:S(2)}) collective-permute-start(f32[128,512]{1,0:T(8,128)S(1)} %get-tuple-element.62), channel_id=1, source_target_pairs={{0,1},{1,0},{2,3},{3,2},{4,5},{5,4},{6,7},{7,6},{8,9},{9,8},{10,11... | collective-permute-start | bytes 786440 | tf_op jit(solution)/shard_map/cond/branch_1_fun/ppermute | solution.py:39
  72.6 1.2 collective-permute-done.received
  73.7 0.6 scatter.2
  74.3 1.4 collective-permute-start.1
  75.7 3.5 %collective-permute-done.1.b = f32[32,512]{1,0:T(8,128)S(1)} collective-permute-done((f32[32,512]{1,0:T(8,128)S(1)}, f32[32,512]{1,0:T(8,128)S(1)}, u32[]{:S(2)}, u32[]{:S(2)}) %collective-permute-start.1) | collective-permute-done | bytes 65568 | tf_op jit(solution)/shard_map/cond/branch_1_fun/ppermute | solution.py:43
  79.2 1.6 collective-permute-start.2
  80.8 3.4 %collective-permute-done.2.c = f32[32,512]{1,0:T(8,128)S(1)} collective-permute-done((f32[32,512]{1,0:T(8,128)S(1)}, f32[32,512]{1,0:T(8,128)S(1)}, u32[]{:S(2)}, u32[]{:S(2)}) %collective-permute-start.2) | collective-permute-done | bytes 65568 | tf_op jit(solution)/shard_map/cond/branch_1_fun/ppermute | solution.py:43
  84.2 1.5 collective-permute-start.3
  85.6 2.0 %collective-permute-done.3.d = f32[32,512]{1,0:T(8,128)S(1)} collective-permute-done((f32[32,512]{1,0:T(8,128)S(1)}, f32[32,512]{1,0:T(8,128)S(1)}, u32[]{:S(2)}, u32[]{:S(2)}) %collective-permute-start.3) | collective-permute-done | bytes 65568 | tf_op jit(solution)/shard_map/cond/branch_1_fun/ppermute | solution.py:43
  87.7 0.6 add_four.2
  88.3 3.4 %collective-permute-done.4 = f32[32,512]{1,0:T(8,128)} collective-permute-done((f32[32,512]{1,0:T(8,128)}, f32[32,512]{1,0:T(8,128)}, u32[]{:S(2)}, u32[]{:S(2)}) %collective-permute-start.4) | collective-permute-done | bytes 65568 | tf_op jit(solution)/shard_map/cond/branch_1_fun/ppermute | solution.py:39
  91.8 39.3 %conditional.5 = (f32[32,512]{1,0:T(8,128)}, f32[32,512]{1,0:T(8,128)}, f32[32,512]{1,0:T(8,128)}, f32[32,512]{1,0:T(8,128)}, f32[32,512]{1,0:T(8,128)}, /*index...) conditional(s32[]{:T(128)} %convert_element_type.15, () %tuple.41, ...), branch_computations={%region_4.5_spmd, %region_5.6_spmd} | conditional | flops 18874368 | bytes 16777616 | solution.py:107
  91.8 8.1 %split_factors.1 = (bf16[3,1024,512]{2,1,0:T(8,128)(2,1)}, bf16[3,1024,512]{2,1,0:T(8,128)(2,1)}) custom-call(f32[3072,512]{1,0:T(8,128)} %get-tuple-element.73.given), custom_call_target="tpu_custom_call" | custom-call | flops 16777216 | bytes 12582912 | tf_op jit(solution)/shard_map/cond/branch_1_fun/split_factors/pallas_call | solution.py:234
  99.9 4.6 %collide.2.a = f32[32,512]{1,0:T(8,128)S(1)} custom-call(f32[32,512]{1,0:T(8,128)} %get-tuple-element.71.mine, f32[32,512]{1,0:T(8,128)} %get-tuple-element.72.theirs, bf16[3,1024,512]{2,1,0:T(8,128)(2,1)} %get-tuple-element.206.high, bf16[3,1024,512]{2,1,0:T(8,128)(2,1)} %get-tuple-element.207.low), custom_call_target="tpu_custom_call" | custom-call | flops 1048576 | bytes 1048576 | tf_op jit(solution)/shard_map/cond/branch_1_fun/collide/pallas_call | solution.py:340
  104.5 3.1 %collective-permute-done.5.b = f32[32,512]{1,0:T(8,128)S(1)} collective-permute-done((f32[32,512]{1,0:T(8,128)S(1)}, f32[32,512]{1,0:T(8,128)S(1)}, u32[]{:S(2)}, u32[]{:S(2)}) %collective-permute-start.5) | collective-permute-done | bytes 65568 | tf_op jit(solution)/shard_map/cond/branch_1_fun/ppermute | solution.py:39
  107.6 0.6 add_two.2
  108.2 0.1 collective-permute-start.6
  108.3 5.2 %collective-permute-start.9 = (f32[32,512]{1,0:T(8,128)}, f32[32,512]{1,0:T(8,128)}, u32[]{:S(2)}, u32[]{:S(2)}) collective-permute-start(f32[32,512]{1,0:T(8,128)} %add_two.2), channel_id=1, source_target_pairs={{0,1},{1,0},{2,3},{3,2},{4,5},{5,4},{6,7},{7,6},{8,9},{9,8},{10,11... | collective-permute-start | bytes 196616 | tf_op jit(solution)/shard_map/cond/branch_1_fun/ppermute | solution.py:39
  113.5 3.8 %collective-permute-start.7 = (f32[32,512]{1,0:T(8,128)}, f32[32,512]{1,0:T(8,128)}, u32[]{:S(2)}, u32[]{:S(2)}) collective-permute-start(f32[32,512]{1,0:T(8,128)} %add_two.2), channel_id=1, source_target_pairs={{0,8},{1,9},{2,10},{3,11},{4,12},{5,13},{6,14},{7,15},{8,0},{9,1},... | collective-permute-start | bytes 196616 | tf_op jit(solution)/shard_map/cond/branch_1_fun/ppermute | solution.py:43
  117.3 2.9 %collective-permute-start.10 = (f32[32,512]{1,0:T(8,128)}, f32[32,512]{1,0:T(8,128)}, u32[]{:S(2)}, u32[]{:S(2)}) collective-permute-start(f32[32,512]{1,0:T(8,128)} %collective-permute-done.6), channel_id=1, source_target_pairs={{0,1},{1,0},{2,3},{3,2},{4,5},{5,4},{6,7},{7,6},{8,9},{9,8},{10,11... | collective-permute-start | bytes 196616 | tf_op jit(solution)/shard_map/cond/branch_1_fun/ppermute | solution.py:39
  120.2 1.2 collective-permute-done.10
  121.5 3.5 %collective-permute-start.11 = (f32[32,512]{1,0:T(8,128)}, f32[32,512]{1,0:T(8,128)}, u32[]{:S(2)}, u32[]{:S(2)}) collective-permute-start(f32[32,512]{1,0:T(8,128)} %collective-permute-done.7), channel_id=1, source_target_pairs={{0,1},{1,0},{2,3},{3,2},{4,5},{5,4},{6,7},{7,6},{8,9},{9,8},{10,11... | collective-permute-start | bytes 196616 | tf_op jit(solution)/shard_map/cond/branch_1_fun/ppermute | solution.py:39
  125.0 2.1 %collective-permute-start.8 = (f32[32,512]{1,0:T(8,128)}, f32[32,512]{1,0:T(8,128)}, u32[]{:S(2)}, u32[]{:S(2)}) collective-permute-start(f32[32,512]{1,0:T(8,128)} %add_two.2), channel_id=1, source_target_pairs={{0,12},{1,13},{2,14},{3,15},{4,0},{5,1},{6,2},{7,3},{8,4},{9,5},{1... | collective-permute-start | bytes 196616 | tf_op jit(solution)/shard_map/cond/branch_1_fun/ppermute | solution.py:43
  127.1 2.0 %collective-permute-done.8 = f32[32,512]{1,0:T(8,128)} collective-permute-done((f32[32,512]{1,0:T(8,128)}, f32[32,512]{1,0:T(8,128)}, u32[]{:S(2)}, u32[]{:S(2)}) %collective-permute-start.8) | collective-permute-done | bytes 65568 | tf_op jit(solution)/shard_map/cond/branch_1_fun/ppermute | solution.py:43
  129.0 0.8 collective-permute-start.12
  129.8 1.2 collective-permute-done.12
  131.1 7.4 %relax.2.rest_0_ = f32[2,2,1024,128]{3,2,1,0:T(8,128)S(1)} custom-call(s32[2]{0:T(128)S(1)} %pad_add_fusion.place, f32[32,512]{1,0:T(8,128)} %get-tuple-element.137.own, f32[32,512]{1,0:T(8,128)} %get-tuple-element.138.y_1, f32[32,512]{1,0:T(8,128)} %get-tuple-element.139.y_2, f32[32,512]{1,0:T(8,128)} %get-tuple-element.140.y_3, ...), custom_call_target="tpu_custom_call" | custom-call | flops 17179869184 | bytes 1048576 | tf_op jit(solution)/shard_map/relax/pallas_call | solution.py:444
  138.5 6.6 %faces_and_moments.3 = (f32[2,2,1024,128]{3,2,1,0:T(8,128)S(1)}, f32[128,512]{1,0:T(8,128)S(1)}, f32[128,512]{1,0:T(8,128)S(1)}) custom-call(f32[1]{0:T(128)} %bitcast.4.speed, s32[2]{0:T(128)S(1)} %pad_add_fusion.place, f32[8192,128]{1,0:T(8,128)S(1)} %bitcast.12, f32[8192,128]{1,0:T(8,128)S(1)} %bitcast.13, ...), custom_call_target="tpu_custom_call" | custom-call | flops 8589934592 | bytes 20971520 | tf_op jit(solution)/shard_map/faces_and_moments/pallas_call | solution.py:311
  145.1 0.5 collective-permute-start.17
  145.6 1.2 collective-permute-done.17.received
  146.8 0.6 scatter.3
  147.4 0.1 collective-permute-start.18
  147.4 4.4 %collective-permute-start.19 = (f32[32,512]{1,0:T(8,128)S(1)}, f32[32,512]{1,0:T(8,128)S(1)}, u32[]{:S(2)}, u32[]{:S(2)}) collective-permute-start(f32[32,512]{1,0:T(8,128)S(1)} %get-tuple-element.156), channel_id=1, source_target_pairs={{0,8},{1,9},{2,10},{3,11},{4,12},{5,13},{6,14},{7,15},{8,0},{9,1},... | collective-permute-start | bytes 196616 | tf_op jit(solution)/shard_map/ppermute | solution.py:43
  151.9 1.0 collective-permute-done.18.b
  152.9 2.0 %collective-permute-done.19.c = f32[32,512]{1,0:T(8,128)S(1)} collective-permute-done((f32[32,512]{1,0:T(8,128)S(1)}, f32[32,512]{1,0:T(8,128)S(1)}, u32[]{:S(2)}, u32[]{:S(2)}) %collective-permute-start.19) | collective-permute-done | bytes 65568 | tf_op jit(solution)/shard_map/ppermute | solution.py:43
  154.8 0.5 collective-permute-done.20.d
  155.3 0.1 collective-permute-start.21
  155.4 3.1 %collective-permute-done.21.theirs = f32[32,512]{1,0:T(8,128)S(1)} collective-permute-done((f32[32,512]{1,0:T(8,128)S(1)}, f32[32,512]{1,0:T(8,128)S(1)}, u32[]{:S(2)}, u32[]{:S(2)}) %collective-permute-start.21) | collective-permute-done | bytes 65568 | tf_op jit(solution)/shard_map/ppermute | solution.py:39
  158.5 4.7 %collide.3.a = f32[32,512]{1,0:T(8,128)S(1)} custom-call(f32[32,512]{1,0:T(8,128)S(1)} %add_four.3.mine, f32[32,512]{1,0:T(8,128)S(1)} %collective-permute-done.21.theirs, bf16[3,1024,512]{2,1,0:T(8,128)(2,1)} %get-tuple-element.158.high, bf16[3,1024,512]{2,1,0:T(8,128)(2,1)} %get-tuple-element.159.low), custom_call_target="tpu_custom_call" | custom-call | flops 1048576 | bytes 1048576 | tf_op jit(solution)/shard_map/collide/pallas_call | solution.py:340
  163.2 0.0 collective-permute-start.22
  163.2 3.1 %collective-permute-done.22.b = f32[32,512]{1,0:T(8,128)S(1)} collective-permute-done((f32[32,512]{1,0:T(8,128)S(1)}, f32[32,512]{1,0:T(8,128)S(1)}, u32[]{:S(2)}, u32[]{:S(2)}) %collective-permute-start.22) | collective-permute-done | bytes 65568 | tf_op jit(solution)/shard_map/ppermute | solution.py:39
  166.3 2.3 %collective-permute-start.25 = (f32[32,512]{1,0:T(8,128)S(1)}, f32[32,512]{1,0:T(8,128)S(1)}, u32[]{:S(2)}, u32[]{:S(2)}) collective-permute-start(f32[32,512]{1,0:T(8,128)S(1)} %add_two.3.own), channel_id=1, source_target_pairs={{0,12},{1,13},{2,14},{3,15},{4,0},{5,1},{6,2},{7,3},{8,4},{9,5},{1... | collective-permute-start | bytes 196616 | tf_op jit(solution)/shard_map/ppermute | solution.py:43
  168.6 0.7 collective-permute-start.23
  169.3 4.2 %collective-permute-start.26 = (f32[32,512]{1,0:T(8,128)S(1)}, f32[32,512]{1,0:T(8,128)S(1)}, u32[]{:S(2)}, u32[]{:S(2)}) collective-permute-start(f32[32,512]{1,0:T(8,128)S(1)} %add_two.3.own), channel_id=1, source_target_pairs={{0,1},{1,0},{2,3},{3,2},{4,5},{5,4},{6,7},{7,6},{8,9},{9,8},{10,11... | collective-permute-start | bytes 196616 | tf_op jit(solution)/shard_map/ppermute | solution.py:39
  173.4 1.3 collective-permute-start.29
  174.8 3.1 %collective-permute-start.28 = (f32[32,512]{1,0:T(8,128)S(1)}, f32[32,512]{1,0:T(8,128)S(1)}, u32[]{:S(2)}, u32[]{:S(2)}) collective-permute-start(f32[32,512]{1,0:T(8,128)S(1)} %collective-permute-done.24.y_2), channel_id=1, source_target_pairs={{0,1},{1,0},{2,3},{3,2},{4,5},{5,4},{6,7},{7,6},{8,9},{9,8},{10,11... | collective-permute-start | bytes 196616 | tf_op jit(solution)/shard_map/ppermute | solution.py:39
  177.9 0.6 collective-permute-start.27
  178.5 0.3 collective-permute-done.28.z_2
  178.8 0.6 collective-permute-done.27.z_1
  179.4 6.1 %relax.3 = f32[8192,128]{1,0:T(8,128)} custom-call(s32[2]{0:T(128)S(1)} %pad_add_fusion.place, f32[32,512]{1,0:T(8,128)S(1)} %add_two.3.own, f32[32,512]{1,0:T(8,128)S(1)} %collective-permute-done.23.y_1, f32[32,512]{1,0:T(8,128)S(1)} %collective-permute-done.24.y_2, f32[32,512]{1,0:T(8,128)S(1)} %collective-permute-done.25.y_3, ...), custom_call_target="tpu_custom_call" | custom-call | flops 17179869184 | bytes 1048576 | tf_op jit(solution)/shard_map/relax/pallas_call | solution.py:444
  (43 shorter events, 0.1 us)
Async XLA Ops:
  6.5 85.2 %all-gather.2.cloned.1.call-start = ((), (), s32[]{:S(2)}) async-start(), calls=%async_computation | async-start | bytes 7077888 | tf_op jit(solution)/shard_map/all_gather | solution.py:228
  6.5 3.3 %copy-start = (f32[128,512]{1,0:T(8,128)S(1)}, f32[128,512]{1,0:T(8,128)}, u32[]{:S(2)}) copy-start(f32[128,512]{1,0:T(8,128)} %left) | copy-start | bytes 786436
  6.5 3.3 %copy-start.1 = (f32[128,512]{1,0:T(8,128)S(1)}, f32[128,512]{1,0:T(8,128)}, u32[]{:S(2)}) copy-start(f32[128,512]{1,0:T(8,128)} %right) | copy-start | bytes 786436
  6.5 3.3 %copy-start.2 = (f32[512,128]{1,0:T(8,128)S(1)}, f32[512,128]{1,0:T(8,128)}, u32[]{:S(2)}) copy-start(f32[512,128]{1,0:T(8,128)} %mixing) | copy-start | bytes 786436
  9.9 8.9 %copy-start.7 = (s32[4,128]{1,0:T(4,128)S(1)}, s32[4,128]{1,0:T(4,128)}, u32[]{:S(2)}) copy-start(s32[4,128]{1,0:T(4,128)} %param.20) | copy-start | bytes 6148
  9.9 8.9 %copy-start.8 = (s32[4,128]{1,0:T(4,128)S(1)}, s32[4,128]{1,0:T(4,128)}, u32[]{:S(2)}) copy-start(s32[4,128]{1,0:T(4,128)} %param.19) | copy-start | bytes 6148
  9.9 8.9 %copy-start.9 = (s32[4,128]{1,0:T(4,128)S(1)}, s32[4,128]{1,0:T(4,128)}, u32[]{:S(2)}) copy-start(s32[4,128]{1,0:T(4,128)} %kind.5) | copy-start | bytes 6148
  10.9 23.6 %collective-permute-start.13 = (f32[1024,128]{1,0:T(8,128)}, f32[1024,128]{1,0:T(8,128)}, u32[]{:S(2)}, u32[]{:S(2)}) collective-permute-start(f32[1024,128]{1,0:T(8,128)} %get-tuple-element.127), channel_id=1, source_target_pairs={{0,16},{16,32},{32,48},{48,64},{64,80},{80,96},{96,112},{112,128},... | collective-permute-start | bytes 1572872 | tf_op jit(solution)/shard_map/ppermute | solution.py:35
  15.2 40.8 %collective-permute-start.14 = (f32[1024,128]{1,0:T(8,128)}, f32[1024,128]{1,0:T(8,128)}, u32[]{:S(2)}, u32[]{:S(2)}) collective-permute-start(f32[1024,128]{1,0:T(8,128)} %get-tuple-element.128), channel_id=1, source_target_pairs={{0,240},{16,0},{32,16},{48,32},{64,48},{80,64},{96,80},{112,96},{1... | collective-permute-start | bytes 1572872 | tf_op jit(solution)/shard_map/ppermute | solution.py:35
  15.2 123.3 %collective-permute-start.15 = (f32[2,1024,128]{2,1,0:T(8,128)S(1)}, f32[2,1024,128]{2,1,0:T(8,128)S(1)}, u32[]{:S(2)}, u32[]{:S(2)}) collective-permute-start(f32[2,1024,128]{2,1,0:T(8,128)S(1)} %get-tuple-element.148), channel_id=1, source_target_pairs={{0,16},{16,32},{32,48},{48,64},{64,80},{80,96},{96,112},{112,128},... | collective-permute-start | bytes 3145736 | tf_op jit(solution)/shard_map/ppermute | solution.py:35
  18.8 119.7 %collective-permute-start.16 = (f32[2,1024,128]{2,1,0:T(8,128)S(1)}, f32[2,1024,128]{2,1,0:T(8,128)}, u32[]{:S(2)}, u32[]{:S(2)}) collective-permute-start(f32[2,1024,128]{2,1,0:T(8,128)S(1)} %get-tuple-element.149), channel_id=1, source_target_pairs={{0,240},{16,0},{32,16},{48,32},{64,48},{80,64},{96,80},{112,96},{1... | collective-permute-start | bytes 3145736 | tf_op jit(solution)/shard_map/ppermute | solution.py:35
  19.1 10.6 %copy-start.3 = (f32[512,2048]{1,0:T(8,128)S(1)}, f32[512,2048]{1,0:T(8,128)}, u32[]{:S(2)}) copy-start(f32[512,2048]{1,0:T(8,128)} %get-tuple-element.165.basis) | copy-start | bytes 12582916 | tf_op jit(solution)/shard_map/cond
  63.9 9.8 %collective-permute-start = (f32[128,512]{1,0:T(8,128)S(1)}, f32[128,512]{1,0:T(8,128)S(1)}, u32[]{:S(2)}, u32[]{:S(2)}) collective-permute-start(f32[128,512]{1,0:T(8,128)S(1)} %get-tuple-element.62), channel_id=1, source_target_pairs={{0,1},{1,0},{2,3},{3,2},{4,5},{5,4},{6,7},{7,6},{8,9},{9,8},{10,11... | collective-permute-start | bytes 786440 | tf_op jit(solution)/shard_map/cond/branch_1_fun/ppermute | solution.py:39
  74.3 4.9 %collective-permute-start.1 = (f32[32,512]{1,0:T(8,128)S(1)}, f32[32,512]{1,0:T(8,128)S(1)}, u32[]{:S(2)}, u32[]{:S(2)}) collective-permute-start(f32[32,512]{1,0:T(8,128)S(1)} %get-tuple-element.65), channel_id=1, source_target_pairs={{0,4},{1,5},{2,6},{3,7},{4,8},{5,9},{6,10},{7,11},{8,12},{9,13},{1... | collective-permute-start | bytes 196616 | tf_op jit(solution)/shard_map/cond/branch_1_fun/ppermute | solution.py:43
  79.2 5.0 %collective-permute-start.2 = (f32[32,512]{1,0:T(8,128)S(1)}, f32[32,512]{1,0:T(8,128)S(1)}, u32[]{:S(2)}, u32[]{:S(2)}) collective-permute-start(f32[32,512]{1,0:T(8,128)S(1)} %get-tuple-element.68), channel_id=1, source_target_pairs={{0,8},{1,9},{2,10},{3,11},{4,12},{5,13},{6,14},{7,15},{8,0},{9,1},... | collective-permute-start | bytes 196616 | tf_op jit(solution)/shard_map/cond/branch_1_fun/ppermute | solution.py:43
  84.2 3.5 %collective-permute-start.3 = (f32[32,512]{1,0:T(8,128)S(1)}, f32[32,512]{1,0:T(8,128)S(1)}, u32[]{:S(2)}, u32[]{:S(2)}) collective-permute-start(f32[32,512]{1,0:T(8,128)S(1)} %get-tuple-element.70), channel_id=1, source_target_pairs={{0,12},{1,13},{2,14},{3,15},{4,0},{5,1},{6,2},{7,3},{8,4},{9,5},{1... | collective-permute-start | bytes 196616 | tf_op jit(solution)/shard_map/cond/branch_1_fun/ppermute | solution.py:43
  88.3 3.4 %collective-permute-start.4 = (f32[32,512]{1,0:T(8,128)}, f32[32,512]{1,0:T(8,128)}, u32[]{:S(2)}, u32[]{:S(2)}) collective-permute-start(f32[32,512]{1,0:T(8,128)} %add_four.2), channel_id=1, source_target_pairs={{0,2},{1,3},{2,0},{3,1},{4,6},{5,7},{6,4},{7,5},{8,10},{9,11},{10,... | collective-permute-start | bytes 196616 | tf_op jit(solution)/shard_map/cond/branch_1_fun/ppermute | solution.py:39
  104.5 3.1 %collective-permute-start.5 = (f32[32,512]{1,0:T(8,128)S(1)}, f32[32,512]{1,0:T(8,128)S(1)}, u32[]{:S(2)}, u32[]{:S(2)}) collective-permute-start(f32[32,512]{1,0:T(8,128)S(1)} %collide.2.a), channel_id=1, source_target_pairs={{0,2},{1,3},{2,0},{3,1},{4,6},{5,7},{6,4},{7,5},{8,10},{9,11},{10,... | collective-permute-start | bytes 196616 | tf_op jit(solution)/shard_map/cond/branch_1_fun/ppermute | solution.py:39
  108.2 5.3 %collective-permute-start.6 = (f32[32,512]{1,0:T(8,128)}, f32[32,512]{1,0:T(8,128)}, u32[]{:S(2)}, u32[]{:S(2)}) collective-permute-start(f32[32,512]{1,0:T(8,128)} %add_two.2), channel_id=1, source_target_pairs={{0,4},{1,5},{2,6},{3,7},{4,8},{5,9},{6,10},{7,11},{8,12},{9,13},{1... | collective-permute-start | bytes 196616 | tf_op jit(solution)/shard_map/cond/branch_1_fun/ppermute | solution.py:43
  108.3 9.0 %collective-permute-start.9 = (f32[32,512]{1,0:T(8,128)}, f32[32,512]{1,0:T(8,128)}, u32[]{:S(2)}, u32[]{:S(2)}) collective-permute-start(f32[32,512]{1,0:T(8,128)} %add_two.2), channel_id=1, source_target_pairs={{0,1},{1,0},{2,3},{3,2},{4,5},{5,4},{6,7},{7,6},{8,9},{9,8},{10,11... | collective-permute-start | bytes 196616 | tf_op jit(solution)/shard_map/cond/branch_1_fun/ppermute | solution.py:39
  113.5 6.7 %collective-permute-start.7 = (f32[32,512]{1,0:T(8,128)}, f32[32,512]{1,0:T(8,128)}, u32[]{:S(2)}, u32[]{:S(2)}) collective-permute-start(f32[32,512]{1,0:T(8,128)} %add_two.2), channel_id=1, source_target_pairs={{0,8},{1,9},{2,10},{3,11},{4,12},{5,13},{6,14},{7,15},{8,0},{9,1},... | collective-permute-start | bytes 196616 | tf_op jit(solution)/shard_map/cond/branch_1_fun/ppermute | solution.py:43
  117.3 4.2 %collective-permute-start.10 = (f32[32,512]{1,0:T(8,128)}, f32[32,512]{1,0:T(8,128)}, u32[]{:S(2)}, u32[]{:S(2)}) collective-permute-start(f32[32,512]{1,0:T(8,128)} %collective-permute-done.6), channel_id=1, source_target_pairs={{0,1},{1,0},{2,3},{3,2},{4,5},{5,4},{6,7},{7,6},{8,9},{9,8},{10,11... | collective-permute-start | bytes 196616 | tf_op jit(solution)/shard_map/cond/branch_1_fun/ppermute | solution.py:39
  121.5 5.6 %collective-permute-start.11 = (f32[32,512]{1,0:T(8,128)}, f32[32,512]{1,0:T(8,128)}, u32[]{:S(2)}, u32[]{:S(2)}) collective-permute-start(f32[32,512]{1,0:T(8,128)} %collective-permute-done.7), channel_id=1, source_target_pairs={{0,1},{1,0},{2,3},{3,2},{4,5},{5,4},{6,7},{7,6},{8,9},{9,8},{10,11... | collective-permute-start | bytes 196616 | tf_op jit(solution)/shard_map/cond/branch_1_fun/ppermute | solution.py:39
  125.0 4.0 %collective-permute-start.8 = (f32[32,512]{1,0:T(8,128)}, f32[32,512]{1,0:T(8,128)}, u32[]{:S(2)}, u32[]{:S(2)}) collective-permute-start(f32[32,512]{1,0:T(8,128)} %add_two.2), channel_id=1, source_target_pairs={{0,12},{1,13},{2,14},{3,15},{4,0},{5,1},{6,2},{7,3},{8,4},{9,5},{1... | collective-permute-start | bytes 196616 | tf_op jit(solution)/shard_map/cond/branch_1_fun/ppermute | solution.py:43
  129.0 2.0 %collective-permute-start.12 = (f32[32,512]{1,0:T(8,128)}, f32[32,512]{1,0:T(8,128)}, u32[]{:S(2)}, u32[]{:S(2)}) collective-permute-start(f32[32,512]{1,0:T(8,128)} %collective-permute-done.8), channel_id=1, source_target_pairs={{0,1},{1,0},{2,3},{3,2},{4,5},{5,4},{6,7},{7,6},{8,9},{9,8},{10,11... | collective-permute-start | bytes 196616 | tf_op jit(solution)/shard_map/cond/branch_1_fun/ppermute | solution.py:39
  131.1 7.4 %copy-start.4 = (f32[2048,4,128]{2,1,0:T(4,128)S(1)}, f32[2048,4,128]{2,1,0:T(4,128)}, u32[]{:S(2)}) copy-start(f32[2048,4,128]{2,1,0:T(4,128)} %param.14) | copy-start | bytes 12582916
  145.1 1.6 collective-permute-start.17
  147.4 5.5 %collective-permute-start.18 = (f32[32,512]{1,0:T(8,128)S(1)}, f32[32,512]{1,0:T(8,128)S(1)}, u32[]{:S(2)}, u32[]{:S(2)}) collective-permute-start(f32[32,512]{1,0:T(8,128)S(1)} %get-tuple-element.155), channel_id=1, source_target_pairs={{0,4},{1,5},{2,6},{3,7},{4,8},{5,9},{6,10},{7,11},{8,12},{9,13},{1... | collective-permute-start | bytes 196616 | tf_op jit(solution)/shard_map/ppermute | solution.py:43
  147.4 7.4 %collective-permute-start.19 = (f32[32,512]{1,0:T(8,128)S(1)}, f32[32,512]{1,0:T(8,128)S(1)}, u32[]{:S(2)}, u32[]{:S(2)}) collective-permute-start(f32[32,512]{1,0:T(8,128)S(1)} %get-tuple-element.156), channel_id=1, source_target_pairs={{0,8},{1,9},{2,10},{3,11},{4,12},{5,13},{6,14},{7,15},{8,0},{9,1},... | collective-permute-start | bytes 196616 | tf_op jit(solution)/shard_map/ppermute | solution.py:43
  151.9 3.4 %collective-permute-start.20 = (f32[32,512]{1,0:T(8,128)S(1)}, f32[32,512]{1,0:T(8,128)S(1)}, u32[]{:S(2)}, u32[]{:S(2)}) collective-permute-start(f32[32,512]{1,0:T(8,128)S(1)} %get-tuple-element.157), channel_id=1, source_target_pairs={{0,12},{1,13},{2,14},{3,15},{4,0},{5,1},{6,2},{7,3},{8,4},{9,5},{1... | collective-permute-start | bytes 196616 | tf_op jit(solution)/shard_map/ppermute | solution.py:43
  155.3 3.2 %collective-permute-start.21 = (f32[32,512]{1,0:T(8,128)S(1)}, f32[32,512]{1,0:T(8,128)S(1)}, u32[]{:S(2)}, u32[]{:S(2)}) collective-permute-start(f32[32,512]{1,0:T(8,128)S(1)} %add_four.3.mine), channel_id=1, source_target_pairs={{0,2},{1,3},{2,0},{3,1},{4,6},{5,7},{6,4},{7,5},{8,10},{9,11},{10,... | collective-permute-start | bytes 196616 | tf_op jit(solution)/shard_map/ppermute | solution.py:39
  158.5 20.9 %copy-start.5 = (bf16[2048,512]{1,0:T(8,128)(2,1)S(1)}, bf16[2048,512]{1,0:T(8,128)(2,1)}, u32[]{:S(2)}) copy-start(bf16[2048,512]{1,0:T(8,128)(2,1)} %get-tuple-element.147.low) | copy-start | bytes 6291460
  158.5 20.9 %copy-start.6 = (bf16[2048,512]{1,0:T(8,128)(2,1)S(1)}, bf16[2048,512]{1,0:T(8,128)(2,1)}, u32[]{:S(2)}) copy-start(bf16[2048,512]{1,0:T(8,128)(2,1)} %get-tuple-element.146.high) | copy-start | bytes 6291460
  163.2 3.1 %collective-permute-start.22 = (f32[32,512]{1,0:T(8,128)S(1)}, f32[32,512]{1,0:T(8,128)S(1)}, u32[]{:S(2)}, u32[]{:S(2)}) collective-permute-start(f32[32,512]{1,0:T(8,128)S(1)} %collide.3.a), channel_id=1, source_target_pairs={{0,2},{1,3},{2,0},{3,1},{4,6},{5,7},{6,4},{7,5},{8,10},{9,11},{10,... | collective-permute-start | bytes 196616 | tf_op jit(solution)/shard_map/ppermute | solution.py:39
  166.3 7.1 %collective-permute-start.25 = (f32[32,512]{1,0:T(8,128)S(1)}, f32[32,512]{1,0:T(8,128)S(1)}, u32[]{:S(2)}, u32[]{:S(2)}) collective-permute-start(f32[32,512]{1,0:T(8,128)S(1)} %add_two.3.own), channel_id=1, source_target_pairs={{0,12},{1,13},{2,14},{3,15},{4,0},{5,1},{6,2},{7,3},{8,4},{9,5},{1... | collective-permute-start | bytes 196616 | tf_op jit(solution)/shard_map/ppermute | solution.py:43
  168.6 6.2 %collective-permute-start.24 = (f32[32,512]{1,0:T(8,128)S(1)}, f32[32,512]{1,0:T(8,128)S(1)}, u32[]{:S(2)}, u32[]{:S(2)}) collective-permute-start(f32[32,512]{1,0:T(8,128)S(1)} %add_two.3.own), channel_id=1, source_target_pairs={{0,8},{1,9},{2,10},{3,11},{4,12},{5,13},{6,14},{7,15},{8,0},{9,1},... | collective-permute-start | bytes 196616 | tf_op jit(solution)/shard_map/ppermute | solution.py:43
  168.6 9.2 %collective-permute-start.23 = (f32[32,512]{1,0:T(8,128)S(1)}, f32[32,512]{1,0:T(8,128)S(1)}, u32[]{:S(2)}, u32[]{:S(2)}) collective-permute-start(f32[32,512]{1,0:T(8,128)S(1)} %add_two.3.own), channel_id=1, source_target_pairs={{0,4},{1,5},{2,6},{3,7},{4,8},{5,9},{6,10},{7,11},{8,12},{9,13},{1... | collective-permute-start | bytes 196616 | tf_op jit(solution)/shard_map/ppermute | solution.py:43
  169.3 9.2 %collective-permute-start.26 = (f32[32,512]{1,0:T(8,128)S(1)}, f32[32,512]{1,0:T(8,128)S(1)}, u32[]{:S(2)}, u32[]{:S(2)}) collective-permute-start(f32[32,512]{1,0:T(8,128)S(1)} %add_two.3.own), channel_id=1, source_target_pairs={{0,1},{1,0},{2,3},{3,2},{4,5},{5,4},{6,7},{7,6},{8,9},{9,8},{10,11... | collective-permute-start | bytes 196616 | tf_op jit(solution)/shard_map/ppermute | solution.py:39
  173.4 5.0 %collective-permute-start.29 = (f32[32,512]{1,0:T(8,128)S(1)}, f32[32,512]{1,0:T(8,128)S(1)}, u32[]{:S(2)}, u32[]{:S(2)}) collective-permute-start(f32[32,512]{1,0:T(8,128)S(1)} %collective-permute-done.25.y_3), channel_id=1, source_target_pairs={{0,1},{1,0},{2,3},{3,2},{4,5},{5,4},{6,7},{7,6},{8,9},{9,8},{10,11... | collective-permute-start | bytes 196616 | tf_op jit(solution)/shard_map/ppermute | solution.py:39
  174.8 4.0 %collective-permute-start.28 = (f32[32,512]{1,0:T(8,128)S(1)}, f32[32,512]{1,0:T(8,128)S(1)}, u32[]{:S(2)}, u32[]{:S(2)}) collective-permute-start(f32[32,512]{1,0:T(8,128)S(1)} %collective-permute-done.24.y_2), channel_id=1, source_target_pairs={{0,1},{1,0},{2,3},{3,2},{4,5},{5,4},{6,7},{7,6},{8,9},{9,8},{10,11... | collective-permute-start | bytes 196616 | tf_op jit(solution)/shard_map/ppermute | solution.py:39
  177.9 1.5 collective-permute-start.27
Sparse Core Ops, SparseCore 0:
  11.1 46.1 all-gather.1

commit v3 on v1

--- a/solution.py
+++ b/solution.py
@@ -26,7 +26,7 @@
 MIB = 1 << 20
 UP = (0, 1, 2, 3)
 DOWN = (3, 2, 1, 0)
-EVERY = (0, 1, 2, 3)
+CELLS = COLUMNS * ROWS
 
 
 def shifted(x, by):
@@ -73,16 +73,42 @@
 
 VM = pl.BlockSpec(memory_space=pltpu.VMEM)
 SM = pl.BlockSpec(memory_space=pltpu.SMEM)
-
-
-def pack_kernel(flat, right, left):
-    upper = flat.at[pl.ds(HALF * COLUMNS, HALF * COLUMNS)]
-    right[0] = column(upper, 3, HALF)
-    right[1] = column(upper, 2, HALF)
-    right[2] = column(flat, 3, HALF)
-    left[0] = column(flat, 0, HALF)
-    left[1] = column(flat, 1, HALF)
-    left[2] = column(upper, 0, HALF)
+ANY = pl.BlockSpec(memory_space=pl.ANY)
+
+
+def pack_kernel(flat, right, left, held, right_held, left_held, arrivals, leavings):
+    steps = HALF // CHUNK
+    rows = CHUNK * COLUMNS
+    copies = []
+    for i in range(steps):
+        for half in range(2):
+            at = pl.ds((half * steps + i) * rows, rows)
+            copies.append(
+                pltpu.make_async_copy(flat.at[at], held.at[at], arrivals.at[2 * i + half])
+            )
+    for copy in copies:
+        copy.start()
+    sends = []
+    for i in range(steps):
+        lower = held.at[pl.ds(i * rows, rows)]
+        upper = held.at[pl.ds((steps + i) * rows, rows)]
+        out = pl.ds(i * CHUNK, CHUNK)
+        copies[2 * i].wait()
+        right_held[2, out, :] = column(lower, 3)
+        left_held[0, out, :] = column(lower, 0)
+        left_held[1, out, :] = column(lower, 1)
+        copies[2 * i + 1].wait()
+        right_held[0, out, :] = column(upper, 3)
+        right_held[1, out, :] = column(upper, 2)
+        left_held[2, out, :] = column(upper, 0)
+        for j, (source, target) in enumerate(((right_held, right), (left_held, left))):
+            send = pltpu.make_async_copy(
+                source.at[:, out], target.at[:, out], leavings.at[2 * i + j]
+            )
+            send.start()
+            sends.append(send)
+    for send in sends:
+        send.wait()
 
 
 def pack(flat):
@@ -90,12 +116,26 @@
     return pl.pallas_call(
         pack_kernel,
         name="pack",
-        in_specs=[VM],
-        out_specs=[VM, VM],
+        in_specs=[ANY],
+        out_specs=[ANY, ANY],
         out_shape=[out, out],
-        compiler_params=params(12),
+        scratch_shapes=[
+            pltpu.VMEM((PER_DEVICE * COLUMNS, ROWS), F32),
+            pltpu.VMEM((3, HALF, ROWS), F32),
+            pltpu.VMEM((3, HALF, ROWS), F32),
+            pltpu.SemaphoreType.DMA((2 * HALF // CHUNK,)),
+            pltpu.SemaphoreType.DMA((2 * HALF // CHUNK,)),
+        ],
+        compiler_params=params(58),
         cost_estimate=cost(1 << 20, 8 * MIB),
     )(flat)
+
+
+def staged(stage, operands):
+    shapes = jax.eval_shape(stage, *operands)
+    blank = lambda *_: jax.tree.map(lambda x: jnp.zeros(x.shape, x.dtype), shapes)
+    taken = lax.optimization_barrier(jnp.array(True))
+    return lax.cond(taken, stage, blank, *operands)
 
 
 def local_kernel(speed, dist, kind, tables, out):
@@ -200,12 +240,25 @@
     out[256:] = mixing[...].T
 
 
-def split_kernel(given, high, low):
-    for which in range(3):
-        high[which], low[which] = halves(given[which * 128 : (which + 1) * 128])
-
-
-def gathered_factors(left, right, mixing):
+def join_kernel(own, before, after, across_top, across_rest, out):
+    out[0] = own[...]
+    out[1] = before[...]
+    out[2] = after[...]
+    out[3, :192] = across_top[...]
+    out[3, 192:] = across_rest[...]
+
+
+def split_kernel(mine, theirs, high, low):
+    for i, source in enumerate((mine, theirs)):
+        for j in range(4):
+            rows = pl.ds((4 * i + j) * 128, 128)
+            for which in range(3):
+                top, rest = halves(source[j, which * 128 : (which + 1) * 128])
+                high[which, rows, :] = top
+                low[which, rows, :] = rest
+
+
+def gathered_factors(_, left, right, mixing):
     own = pl.pallas_call(
         stack_kernel,
         name="stack_factors",
@@ -215,64 +268,82 @@
         compiler_params=params(3),
         cost_estimate=cost(1 << 20, 2 * MIB),
     )(left, right, mixing)
-    groups = [[4 * y + 2 * z + c for y in range(4) for c in range(2)] for z in range(2)]
-    every = lax.all_gather(own, "vel", axis=0, tiled=True, axis_index_groups=groups)
+    before, after = along_y(own, 1), along_y(own, -1)
+    across_top, across_rest = along_y(before[:192], 1), along_y(after[192:], -1)
+    mine = pl.pallas_call(
+        join_kernel,
+        name="join_factors",
+        in_specs=[VM] * 5,
+        out_specs=VM,
+        out_shape=jax.ShapeDtypeStruct((4, 384, MOMENTS), F32),
+        compiler_params=params(8),
+        cost_estimate=cost(1 << 20, 6 * MIB),
+    )(own, before, after, across_top, across_rest)
+    return mine, exchanged(mine, 1)
+
+
+def split_factors(mine, theirs):
     out = jax.ShapeDtypeStruct((3, RANKS, MOMENTS), BF16)
-    spec = pl.BlockSpec((3, 128, MOMENTS), lambda i: (0, i, 0))
     return pl.pallas_call(
         split_kernel,
         name="split_factors",
-        grid=(RANKS // 128,),
-        in_specs=[pl.BlockSpec((384, MOMENTS), lambda i: (i, 0))],
-        out_specs=[spec, spec],
+        in_specs=[VM] * 2,
+        out_specs=[VM] * 2,
         out_shape=[out, out],
-        compiler_params=params(6),
+        compiler_params=params(16),
         cost_estimate=cost(1 << 24, 12 * MIB),
-    )(every)
+    )(mine, theirs)
 
 
 def moments_kernel(
-    columns, speed, place, lower, upper, part_lower, part_upper, from_left, from_right, kind,
-    high_lower, low_lower, high_upper, low_upper, moved, kept, sent, total,
+    speed, place, dist, part, from_left, from_right, kind, high, low, moved, kept, sent, total
 ):
     step = pl.program_id(0)
     courant = speed[0]
     slope = 0.5 * (1.0 - courant)
-
-    def half(dist, part, out, order, behind, behind_two, ahead):
+    across = pl.ds(pl.multiple_of(step * CHUNK, CHUNK), CHUNK)
+
+    def half(which, order, behind, behind_two, ahead):
+        first_line = pl.multiple_of(which * HALF + step * CHUNK, CHUNK)
+        lines = pl.ds(first_line, CHUNK)
         fluid = [courant * (1 - kind[x : x + 1, :]).astype(F32) for x in order]
-        first, second = column(dist, order[0]), column(dist, order[1])
+        first, second, third, fourth = (
+            dist[pl.ds(first_line * COLUMNS + x, CHUNK, stride=COLUMNS), :] for x in order
+        )
+        face_in = behind + slope * minmod(behind - behind_two, first - behind)
         face_0 = first + slope * minmod(first - behind, second - first)
-        values = {order[2]: part[order[2]]}
-        values[order[1]] = part[order[1]] + fluid[1] * face_0
-        if order[0] in columns:
-            third, fourth = column(dist, order[2]), column(dist, order[3])
-            face_in = behind + slope * minmod(behind - behind_two, first - behind)
-            face_3 = fourth + slope * minmod(fourth - third, ahead - fourth)
-            values[order[0]] = part[order[0]] - fluid[0] * (face_0 - face_in)
-            values[order[3]] = part[order[3]] - fluid[3] * face_3
-        values = [values[x] for x in columns]
-        for i, value in enumerate(values):
-            moved[out, i] = value
-        return halves(jnp.concatenate(values, axis=1))
+        face_3 = fourth + slope * minmod(fourth - third, ahead - fourth)
+        values = {
+            order[0]: part[order[0], lines, :] - fluid[0] * (face_0 - face_in),
+            order[1]: part[order[1], lines, :] + fluid[1] * face_0,
+            order[2]: part[order[2], lines, :],
+            order[3]: part[order[3], lines, :] - fluid[3] * face_3,
+        }
+        for x in range(COLUMNS):
+            moved[x, lines, :] = values[x]
+        return halves(jnp.concatenate([values[x] for x in range(COLUMNS)], axis=1))
 
     @pl.when(step == 0)
     def _():
         total[...] = jnp.zeros_like(total)
 
-    top, rest = half(lower, part_lower, 0, DOWN, from_right[0], from_right[1], from_left[2])
-    added = total[...] + dot(high_lower[...], top)
-    added = added + dot(high_lower[...], rest)
-    added = added + dot(low_lower[...], top)
-    top, rest = half(upper, part_upper, 1, UP, from_left[0], from_left[1], from_right[2])
-    added = added + dot(high_upper[...], top)
-    added = added + dot(high_upper[...], rest)
-    added = added + dot(low_upper[...], top)
+    left, right = from_left, from_right
+    added = total[...]
+    ends = (
+        (DOWN, right[0, across, :], right[1, across, :], left[2, across, :]),
+        (UP, left[0, across, :], left[1, across, :], right[2, across, :]),
+    )
+    for which, end in enumerate(ends):
+        top, rest = half(which, *end)
+        lines = pl.ds(pl.multiple_of(which * HALF + step * CHUNK, CHUNK), CHUNK)
+        added = added + dot(high[:, lines], top)
+        added = added + dot(high[:, lines], rest)
+        added = added + dot(low[:, lines], top)
     total[...] = added
 
     @pl.when(step == pl.num_programs(0) - 1)
     def _():
-        count = total.shape[1] // 2
+        count = CELLS // 2
         core = place[0]
         first = total[:, :count].T
         second = total[:, count:].T
@@ -280,41 +351,19 @@
         sent[...] = jnp.where(core == 0, second, first)
 
 
-def moments_part(columns, speed, place, flat, part, from_left, from_right, kind, high, low):
-    steps = HALF // CHUNK
-    rows = CHUNK * COLUMNS
-    count = len(columns)
-    lower = pl.BlockSpec((COLUMNS, CHUNK, ROWS), lambda i: (0, i, 0))
-    upper = pl.BlockSpec((COLUMNS, CHUNK, ROWS), lambda i: (0, i + steps, 0))
-    halo = pl.BlockSpec((3, CHUNK, ROWS), lambda i: (0, i, 0))
-    basis_lower = pl.BlockSpec((MOMENTS, CHUNK), lambda i: (0, i))
-    basis_upper = pl.BlockSpec((MOMENTS, CHUNK), lambda i: (0, i + steps))
-    piece = jax.ShapeDtypeStruct((count * ROWS // 2, MOMENTS), F32)
-    return pl.pallas_call(
-        functools.partial(moments_kernel, columns),
+def moments_part(speed, place, flat, part, from_left, from_right, kind, high, low):
+    piece = jax.ShapeDtypeStruct((CELLS // 2, MOMENTS), F32)
+    return pl.pallas_call(
+        moments_kernel,
         name="faces_and_moments",
-        grid=(steps,),
-        in_specs=[
-            SM,
-            SM,
-            pl.BlockSpec((rows, ROWS), lambda i: (i, 0)),
-            pl.BlockSpec((rows, ROWS), lambda i: (i + steps, 0)),
-            lower,
-            upper,
-            halo,
-            halo,
-            VM,
-            basis_lower,
-            basis_lower,
-            basis_upper,
-            basis_upper,
-        ],
-        out_specs=[pl.BlockSpec((2, count, CHUNK, ROWS), lambda i: (0, 0, i, 0)), VM, VM],
-        out_shape=[jax.ShapeDtypeStruct((2, count, HALF, ROWS), F32), piece, piece],
-        scratch_shapes=[pltpu.VMEM((MOMENTS, count * ROWS), F32)],
-        compiler_params=params(18),
+        grid=(HALF // CHUNK,),
+        in_specs=[SM, SM] + [VM] * 7,
+        out_specs=[VM] * 3,
+        out_shape=[jax.ShapeDtypeStruct((COLUMNS, PER_DEVICE, ROWS), F32), piece, piece],
+        scratch_shapes=[pltpu.VMEM((MOMENTS, CELLS), F32)],
+        compiler_params=params(26),
         cost_estimate=cost(8 << 30, 20 * MIB),
-    )(speed, place, flat, flat, part, part, from_left, from_right, kind, high, low, high, low)
+    )(speed, place, flat, part, from_left, from_right, kind, high, low)
 
 
 def small_call(kernel, name, count, shape, operands, smem=0, mib=3):
@@ -372,8 +421,8 @@
 
 
 def relax_kernel(
-    columns, place, own, y_1, y_2, y_3, other, z_1, z_2, z_3, kind, moved,
-    high, low, out, gathered, turned_high, turned_low,
+    place, own, y_1, y_2, y_3, other, z_1, z_2, z_3, kind, moved, high, low,
+    out, gathered, turned_high, turned_low,
 ):
     step = pl.program_id(0)
     size = own.shape[0]
@@ -387,40 +436,31 @@
                 gathered[pl.ds(pl.multiple_of(at * size, size), size), :] = piece[...]
         turned_high[...], turned_low[...] = halves(gathered[...].T)
 
-    gain = dot(high[...], turned_high[...])
-    gain = gain + dot(high[...], turned_low[...])
-    gain = gain + dot(low[...], turned_high[...])
-    for i, x in enumerate(columns):
+    lines = pl.ds(pl.multiple_of(step * CHUNK, CHUNK), CHUNK)
+    gain = dot(high[lines, :], turned_high[...])
+    gain = gain + dot(high[lines, :], turned_low[...])
+    gain = gain + dot(low[lines, :], turned_high[...])
+    for x in range(COLUMNS):
         fluid = HALF_STEP * (1 - kind[x : x + 1, :]).astype(F32)
         out[pl.ds(x, CHUNK, stride=COLUMNS), :] = (
-            moved[0, i] + fluid * gain[:, i * ROWS : (i + 1) * ROWS]
+            moved[x, lines, :] + fluid * gain[:, x * ROWS : (x + 1) * ROWS]
         )
 
 
-def relax(columns, place, pieces, kind, moved, high, low):
-    steps = PER_DEVICE // CHUNK
-    half = steps // 2
-    count = len(columns)
-    turned = pl.BlockSpec((CHUNK, MOMENTS), lambda i: (i, 0))
-    return pl.pallas_call(
-        functools.partial(relax_kernel, columns),
+def relax(place, pieces, kind, moved, high, low):
+    return pl.pallas_call(
+        relax_kernel,
         name="relax",
-        grid=(steps,),
-        in_specs=[SM]
-        + [VM] * 9
-        + [
-            pl.BlockSpec((1, count, CHUNK, ROWS), lambda i: (i // half, 0, i % half, 0)),
-            turned,
-            turned,
-        ],
+        grid=(PER_DEVICE // CHUNK,),
+        in_specs=[SM] + [VM] * 12,
         out_specs=pl.BlockSpec((CHUNK * COLUMNS, ROWS), lambda i: (i, 0)),
         out_shape=jax.ShapeDtypeStruct((PER_DEVICE * COLUMNS, ROWS), F32),
         scratch_shapes=[
-            pltpu.VMEM((count * ROWS, MOMENTS), F32),
-            pltpu.VMEM((MOMENTS, count * ROWS), BF16),
-            pltpu.VMEM((MOMENTS, count * ROWS), BF16),
+            pltpu.VMEM((CELLS, MOMENTS), F32),
+            pltpu.VMEM((MOMENTS, CELLS), BF16),
+            pltpu.VMEM((MOMENTS, CELLS), BF16),
         ],
-        compiler_params=params(14),
+        compiler_params=params(20),
         cost_estimate=cost(8 << 30, 16 * MIB),
     )(place, *pieces, kind, moved, high, low)
 
@@ -434,19 +474,19 @@
     from_left = shifted(to_right, 1)
     from_right = shifted(to_left, -1)
 
-    given = (left_factor, right_factor, mixing)
-    _, (left_factor, right_factor, mixing) = lax.optimization_barrier((to_left, given))
-    factors = gathered_factors(left_factor, right_factor, mixing)
+    given = (to_left[0, :8], left_factor, right_factor, mixing)
+    factors = staged(gathered_factors, given)
     high, low, turned_high, turned_low = split_basis(basis)
     part = local_part(speed, flat, cell_kind, row_tables(next_cell, prev_cell))
+    factors = split_factors(*factors)
     halo = (from_left, from_right)
     (from_left, from_right), factors = lax.optimization_barrier((halo, factors))
 
     moved, kept, sent = moments_part(
-        EVERY, speed, place, flat, part, from_left, from_right, cell_kind, high, low
+        speed, place, flat, part, from_left, from_right, cell_kind, high, low
     )
     pieces = collision_part(place, kept, sent, *factors)
-    out = relax(EVERY, place, pieces, cell_kind, moved, turned_high, turned_low)
+    out = relax(place, pieces, cell_kind, moved, turned_high, turned_low)
     return out.reshape(dist.shape)
 
 

time: 151 us -> 130 us (0.86)
  local copies, waits for them, and re-layouts: 17.1 us -> 2.59 us
  between operations: 13.6 us -> 0.15 us
  starting transfers between devices: 32.1 us -> 41.5 us
  waiting for transfers between devices: 56.5 us -> 49.9 us
  Pallas kernels: 31.2 us -> 35.6 us
    ppermute x6 -> x10, waiting for transfers between devices: 4.99 us -> 30.5 us  [along_y(): return lax.ppermute(x, 'vel', [(i, (i + 4 * by) % 16) for i in range(16)])]
    all_gather x1 -> x0, waiting for transfers between devices: 19.8 us -> none  [gathered_factors(): lax.all_gather(own, 'vel', axis=0, tiled=True, axis_index_groups=groups)]
    ppermute x2, waiting for transfers between devices: 24.5 us -> 6.49 us  [shifted(): return lax.ppermute(x, 'cells', [(i, (i + by) % size) for i in range(size)])]
    unnamed x38 -> x12, local copies, waits for them, and re-layouts: 17.1 us -> 2.53 us
    ppermute x6 -> x10, starting transfers between devices: 8.03 us -> 14.4 us  [along_y(): return lax.ppermute(x, 'vel', [(i, (i + 4 * by) % 16) for i in range(16)])]
    ppermute x7 -> x8, waiting for transfers between devices: 7.24 us -> 12.9 us  [exchanged(): return lax.ppermute(x, 'vel', [(i, i ^ bit) for i in range(16)])]
    pallas_call x4 -> x5, Pallas kernels: 17.6 us -> 21.9 us  [the longest x1 7.06 us: relax(): pl.pallas_call(relax_kernel, name='relax', grid=(PER_DEVICE // CHUNK,), i...]
    ppermute x7 -> x8, starting transfers between devices: 14.8 us -> 17.9 us  [exchanged(): return lax.ppermute(x, 'vel', [(i, i ^ bit) for i in range(16)])]
  transfers between devices with their start and end apart: 16 -> 20, of which waited for: 9 -> 11; matrix products, arithmetic and copies ran while one was open for 0% -> 0% of each run, Pallas kernels for 8% -> 13%
where the time goes in v3:
time: 130 us
  waiting for transfers between devices  49.9 us (38%)
  starting transfers between devices  41.5 us (32%)
  Pallas kernels  35.6 us (27%)
  local copies, waits for them, and re-layouts  2.59 us (2%)
    ppermute x10, waiting for transfers between devices, along_y(): return lax.ppermute(x, 'vel', [(i, (i + 4 * by) % 16) for i in range(16)])  30.5 us
    ppermute x8, starting transfers between devices, exchanged(): return lax.ppermute(x, 'vel', [(i, i ^ bit) for i in range(16)])  17.9 us
    ppermute x10, starting transfers between devices, along_y(): return lax.ppermute(x, 'vel', [(i, (i + 4 * by) % 16) for i in range(16)])  14.4 us
    ppermute x8, waiting for transfers between devices, exchanged(): return lax.ppermute(x, 'vel', [(i, i ^ bit) for i in range(16)])  12.9 us
    ppermute x2, starting transfers between devices, shifted(): return lax.ppermute(x, 'cells', [(i, (i + by) % size) for i in range(size)])  9.21 us
    pallas_call x1, Pallas kernels, local_part(): pl.pallas_call(local_kernel, name='local_transport', grid=(steps,), in_sp...  7.59 us
    pallas_call x1, Pallas kernels, relax(): pl.pallas_call(relax_kernel, name='relax', grid=(PER_DEVICE // CHUNK,), i...  7.06 us
    ppermute x2, waiting for transfers between devices, shifted(): return lax.ppermute(x, 'cells', [(i, (i + by) % size) for i in range(size)])  6.49 us
  transfers between devices with their start and end apart: 20, of which 11 were waited for; matrix products, arithmetic and copies ran while one was open for 0% of the time, Pallas kernels for 13%

profile of v3, /device:TPU:1, one launch (start us, length us, event | category | flops | bytes accessed | tf_op | source)
XLA Modules:
  0.0 130.1 jit_solution(16533377508293441872)
XLA Ops:
  0.0 3.3 %pack.1 = (f32[3,1024,128]{2,1,0:T(8,128)}, f32[3,1024,128]{2,1,0:T(8,128)}) custom-call(f32[8192,128]{1,0:T(8,128)} %bitcast.9), custom_call_target="tpu_custom_call" | custom-call | flops 1048576 | bytes 8388608 | tf_op jit(solution)/shard_map/pack/pallas_call | solution.py:116
  3.3 3.9 %collective-permute-start.5 = (f32[3,1024,128]{2,1,0:T(8,128)}, f32[3,1024,128]{2,1,0:T(8,128)S(1)}, u32[]{:S(2)}, u32[]{:S(2)}) collective-permute-start(f32[3,1024,128]{2,1,0:T(8,128)} %get-tuple-element.35), channel_id=1, source_target_pairs={{0,16},{16,32},{32,48},{48,64},{64,80},{80,96},{96,112},{112,128},... | collective-permute-start | bytes 4718600 | tf_op jit(solution)/shard_map/ppermute | solution.py:34
  7.2 5.3 %collective-permute-start.6 = (f32[3,1024,128]{2,1,0:T(8,128)}, f32[3,1024,128]{2,1,0:T(8,128)S(1)}, u32[]{:S(2)}, u32[]{:S(2)}) collective-permute-start(f32[3,1024,128]{2,1,0:T(8,128)} %get-tuple-element.36), channel_id=1, source_target_pairs={{0,240},{16,0},{32,16},{48,32},{64,48},{80,64},{96,80},{112,96},{1... | collective-permute-start | bytes 4718600 | tf_op jit(solution)/shard_map/ppermute | solution.py:34
  12.6 0.0 copy-done.3
  12.6 43.8 %conditional.1 = (f32[4,384,512]{2,1,0:T(8,128)}, f32[4,384,512]{2,1,0:T(8,128)}) conditional(s32[]{:T(128)} %convert_element_type.15, () %tuple.14, (f32[128,512]{1,0:T(8,128)S(1)}, f32[128,512]{1,0:T(8,128)}, f32[512,128]{1,0:T(8,128)}) %tuple.21), branch_computations={%region_0.1_spmd, %region_1.2_spmd} | conditional | flops 2097152 | bytes 31981784 | solution.py:138
  12.6 1.2 stack_factors.1.own
  13.8 2.8 %collective-permute-start.1 = (f32[384,512]{1,0:T(8,128)S(1)}, f32[384,512]{1,0:T(8,128)S(1)}, u32[]{:S(2)}, u32[]{:S(2)}) collective-permute-start(f32[384,512]{1,0:T(8,128)S(1)} %stack_factors.1.own), channel_id=1, source_target_pairs={{0,12},{1,13},{2,14},{3,15},{4,0},{5,1},{6,2},{7,3},{8,4},{9,5},{1... | collective-permute-start | bytes 2359304 | tf_op jit(solution)/shard_map/cond/branch_1_fun/ppermute | solution.py:42
  16.6 0.0 collective-permute-start
  16.6 15.9 %collective-permute-done.1.after = f32[384,512]{1,0:T(8,128)S(1)} collective-permute-done((f32[384,512]{1,0:T(8,128)S(1)}, f32[384,512]{1,0:T(8,128)S(1)}, u32[]{:S(2)}, u32[]{:S(2)}) %collective-permute-start.1) | collective-permute-done | bytes 786464 | tf_op jit(solution)/shard_map/cond/branch_1_fun/ppermute | solution.py:42
  32.5 3.5 %collective-permute-start.3 = (f32[192,512]{1,0:T(8,128)S(1)}, f32[192,512]{1,0:T(8,128)S(1)}, u32[]{:S(2)}, u32[]{:S(2)}) collective-permute-start(f32[192,512]{1,0:T(8,128)S(1)} %slice.7), channel_id=1, source_target_pairs={{0,12},{1,13},{2,14},{3,15},{4,0},{5,1},{6,2},{7,3},{8,4},{9,5},{1... | collective-permute-start | bytes 1179656 | tf_op jit(solution)/shard_map/cond/branch_1_fun/ppermute | solution.py:42
  36.0 0.0 collective-permute-done.before
  36.0 0.1 collective-permute-start.2
  36.1 6.4 %collective-permute-done.3.across_rest = f32[192,512]{1,0:T(8,128)S(1)} collective-permute-done((f32[192,512]{1,0:T(8,128)S(1)}, f32[192,512]{1,0:T(8,128)S(1)}, u32[]{:S(2)}, u32[]{:S(2)}) %collective-permute-start.3) | collective-permute-done | bytes 393248 | tf_op jit(solution)/shard_map/cond/branch_1_fun/ppermute | solution.py:42
  42.5 3.2 %collective-permute-done.2.across_top = f32[192,512]{1,0:T(8,128)S(1)} collective-permute-done((f32[192,512]{1,0:T(8,128)S(1)}, f32[192,512]{1,0:T(8,128)S(1)}, u32[]{:S(2)}, u32[]{:S(2)}) %collective-permute-start.2) | collective-permute-done | bytes 393248 | tf_op jit(solution)/shard_map/cond/branch_1_fun/ppermute | solution.py:42
  45.8 1.9 %join_factors.1 = f32[4,384,512]{2,1,0:T(8,128)} custom-call(f32[384,512]{1,0:T(8,128)S(1)} %stack_factors.1.own, f32[384,512]{1,0:T(8,128)S(1)} %collective-permute-done.before, f32[384,512]{1,0:T(8,128)S(1)} %collective-permute-done.1.after, f32[192,512]{1,0:T(8,128)S(1)} %collective-permute-done.2.across_top, ...), custom_call_target="tpu_custom_call" | custom-call | flops 1048576 | bytes 6291456 | tf_op jit(solution)/shard_map/cond/branch_1_fun/join_factors/pallas_call | solution.py:273
  47.6 3.1 %collective-permute-start.4 = (f32[4,384,512]{2,1,0:T(8,128)}, f32[4,384,512]{2,1,0:T(8,128)}, u32[]{:S(2)}, u32[]{:S(2)}) collective-permute-start(f32[4,384,512]{2,1,0:T(8,128)} %join_factors.1), channel_id=1, source_target_pairs={{0,1},{1,0},{2,3},{3,2},{4,5},{5,4},{6,7},{7,6},{8,9},{9,8},{10,11... | collective-permute-start | bytes 9437192 | tf_op jit(solution)/shard_map/cond/branch_1_fun/ppermute | solution.py:38
  50.7 5.6 %collective-permute-done.4 = f32[4,384,512]{2,1,0:T(8,128)} collective-permute-done((f32[4,384,512]{2,1,0:T(8,128)}, f32[4,384,512]{2,1,0:T(8,128)}, u32[]{:S(2)}, u32[]{:S(2)}) %collective-permute-start.4) | collective-permute-done | bytes 3145760 | tf_op jit(solution)/shard_map/cond/branch_1_fun/ppermute | solution.py:38
  56.3 2.2 %copy-done = f32[512,2048]{1,0:T(8,128)S(1)} copy-done((f32[512,2048]{1,0:T(8,128)S(1)}, f32[512,2048]{1,0:T(8,128)}, u32[]{:S(2)}) %copy-start) | copy-done | bytes 4194328
  58.5 2.5 %split_basis.1 = (bf16[512,2048]{1,0:T(8,128)(2,1)S(1)}, bf16[512,2048]{1,0:T(8,128)(2,1)S(1)}, bf16[2048,512]{1,0:T(8,128)(2,1)S(1)}, bf16[2048,512]{1,0:T(8,128)(2,1)S(1)}) custom-call(f32[512,2048]{1,0:T(8,128)S(1)} %copy-done), custom_call_target="tpu_custom_call" | custom-call | flops 16777216 | bytes 12582912 | tf_op jit(solution)/shard_map/split_basis/pallas_call | solution.py:224
  61.1 0.0 copy-start.4
  61.1 0.0 copy-start.5
  61.1 0.0 copy-start.1
  61.1 4.0 %split_factors.1 = (bf16[3,1024,512]{2,1,0:T(8,128)(2,1)S(1)}, bf16[3,1024,512]{2,1,0:T(8,128)(2,1)S(1)}) custom-call(f32[4,384,512]{2,1,0:T(8,128)} %get-tuple-element.37.mine, f32[4,384,512]{2,1,0:T(8,128)} %get-tuple-element.38.theirs), custom_call_target="tpu_custom_call" | custom-call | flops 16777216 | bytes 12582912 | tf_op jit(solution)/shard_map/split_factors/pallas_call | solution.py:287
  65.1 0.0 copy-start.2
  65.1 0.1 pad_add_fusion.place
  65.2 0.0 copy-done.5
  65.2 0.1 fusion
  65.2 0.1 maximum_bitcast_fusion
  65.3 0.1 pad_maximum_fusion.tables
  65.4 0.0 copy-done.1
  65.4 0.3 copy-done.2
  65.8 7.6 %local_transport.1.part = f32[4,2048,128]{2,1,0:T(8,128)S(1)} custom-call(f32[1]{0:T(128)} %bitcast.2.speed, f32[8192,128]{1,0:T(8,128)S(1)} %bitcast.10, s32[4,128]{1,0:T(4,128)S(1)} %copy-done.2, bf16[2,4,256,256]{3,2,1,0:T(8,128)(2,1)S(1)} %pad_maximum_fusion.tables), custom_call_target="tpu_custom_call" | custom-call | flops 4294967296 | bytes 10485760 | tf_op jit(solution)/shard_map/local_transport/pallas_call | solution.py:186
  73.4 0.0 collective-permute-done.5.from_left
  73.4 6.5 %collective-permute-done.6.from_right = f32[3,1024,128]{2,1,0:T(8,128)S(1)} collective-permute-done((f32[3,1024,128]{2,1,0:T(8,128)}, f32[3,1024,128]{2,1,0:T(8,128)S(1)}, u32[]{:S(2)}, u32[]{:S(2)}) %collective-permute-start.6) | collective-permute-done | bytes 1572896 | tf_op jit(solution)/shard_map/ppermute | solution.py:34
  79.9 5.6 %faces_and_moments.1 = (f32[4,2048,128]{2,1,0:T(8,128)S(1)}, f32[256,512]{1,0:T(8,128)S(1)}, f32[256,512]{1,0:T(8,128)S(1)}) custom-call(f32[1]{0:T(128)} %bitcast.2.speed, s32[2]{0:T(128)S(1)} %pad_add_fusion.place, f32[8192,128]{1,0:T(8,128)S(1)} %bitcast.11, f32[4,2048,128]{2,1,0:T(8,128)S(1)} %local_transport.1.part, ...), custom_call_target="tpu_custom_call" | custom-call | flops 8589934592 | bytes 20971520 | tf_op jit(solution)/shard_map/faces_and_moments/pallas_call | solution.py:356
  85.5 1.0 collective-permute-start.7
  86.6 1.5 %collective-permute-done.7.received = f32[256,512]{1,0:T(8,128)S(1)} collective-permute-done((f32[256,512]{1,0:T(8,128)S(1)}, f32[256,512]{1,0:T(8,128)S(1)}, u32[]{:S(2)}, u32[]{:S(2)}) %collective-permute-start.7) | collective-permute-done | bytes 524320 | tf_op jit(solution)/shard_map/ppermute | solution.py:38
  88.1 0.6 scatter.1
  88.7 1.4 %collective-permute-start.8 = (f32[64,512]{1,0:T(8,128)S(1)}, f32[64,512]{1,0:T(8,128)S(1)}, u32[]{:S(2)}, u32[]{:S(2)}) collective-permute-start(f32[64,512]{1,0:T(8,128)S(1)} %get-tuple-element.48), channel_id=1, source_target_pairs={{0,4},{1,5},{2,6},{3,7},{4,8},{5,9},{6,10},{7,11},{8,12},{9,13},{1... | collective-permute-start | bytes 393224 | tf_op jit(solution)/shard_map/ppermute | solution.py:42
  90.1 2.6 %collective-permute-start.9 = (f32[64,512]{1,0:T(8,128)S(1)}, f32[64,512]{1,0:T(8,128)S(1)}, u32[]{:S(2)}, u32[]{:S(2)}) collective-permute-start(f32[64,512]{1,0:T(8,128)S(1)} %get-tuple-element.49), channel_id=1, source_target_pairs={{0,8},{1,9},{2,10},{3,11},{4,12},{5,13},{6,14},{7,15},{8,0},{9,1},... | collective-permute-start | bytes 393224 | tf_op jit(solution)/shard_map/ppermute | solution.py:42
  92.7 1.1 collective-permute-start.10
  93.8 1.1 collective-permute-done.8.b
  94.9 3.9 %collective-permute-done.9.c = f32[64,512]{1,0:T(8,128)S(1)} collective-permute-done((f32[64,512]{1,0:T(8,128)S(1)}, f32[64,512]{1,0:T(8,128)S(1)}, u32[]{:S(2)}, u32[]{:S(2)}) %collective-permute-start.9) | collective-permute-done | bytes 131104 | tf_op jit(solution)/shard_map/ppermute | solution.py:42
  98.8 0.0 collective-permute-done.10.d
  98.8 1.7 %collective-permute-start.11 = (f32[64,512]{1,0:T(8,128)S(1)}, f32[64,512]{1,0:T(8,128)S(1)}, u32[]{:S(2)}, u32[]{:S(2)}) collective-permute-start(f32[64,512]{1,0:T(8,128)S(1)} %add_four.1.mine), channel_id=1, source_target_pairs={{0,2},{1,3},{2,0},{3,1},{4,6},{5,7},{6,4},{7,5},{8,10},{9,11},{10,... | collective-permute-start | bytes 393224 | tf_op jit(solution)/shard_map/ppermute | solution.py:38
  100.5 2.4 %collective-permute-done.11.theirs = f32[64,512]{1,0:T(8,128)S(1)} collective-permute-done((f32[64,512]{1,0:T(8,128)S(1)}, f32[64,512]{1,0:T(8,128)S(1)}, u32[]{:S(2)}, u32[]{:S(2)}) %collective-permute-start.11) | collective-permute-done | bytes 131104 | tf_op jit(solution)/shard_map/ppermute | solution.py:38
  102.9 1.7 %collide.1.a = f32[64,512]{1,0:T(8,128)S(1)} custom-call(f32[64,512]{1,0:T(8,128)S(1)} %add_four.1.mine, f32[64,512]{1,0:T(8,128)S(1)} %collective-permute-done.11.theirs, bf16[3,1024,512]{2,1,0:T(8,128)(2,1)S(1)} %get-tuple-element.51.high, bf16[3,1024,512]{2,1,0:T(8,128)(2,1)S(1)} %get-tuple-element.52.low), custom_call_target="tpu_custom_call" | custom-call | flops 1048576 | bytes 1048576 | tf_op jit(solution)/shard_map/collide/pallas_call | solution.py:371
  104.6 1.6 %collective-permute-start.12 = (f32[64,512]{1,0:T(8,128)S(1)}, f32[64,512]{1,0:T(8,128)S(1)}, u32[]{:S(2)}, u32[]{:S(2)}) collective-permute-start(f32[64,512]{1,0:T(8,128)S(1)} %collide.1.a), channel_id=1, source_target_pairs={{0,2},{1,3},{2,0},{3,1},{4,6},{5,7},{6,4},{7,5},{8,10},{9,11},{10,... | collective-permute-start | bytes 393224 | tf_op jit(solution)/shard_map/ppermute | solution.py:38
  106.2 2.4 %collective-permute-done.12.b = f32[64,512]{1,0:T(8,128)S(1)} collective-permute-done((f32[64,512]{1,0:T(8,128)S(1)}, f32[64,512]{1,0:T(8,128)S(1)}, u32[]{:S(2)}, u32[]{:S(2)}) %collective-permute-start.12) | collective-permute-done | bytes 131104 | tf_op jit(solution)/shard_map/ppermute | solution.py:38
  108.6 2.1 %collective-permute-start.15 = (f32[64,512]{1,0:T(8,128)S(1)}, f32[64,512]{1,0:T(8,128)S(1)}, u32[]{:S(2)}, u32[]{:S(2)}) collective-permute-start(f32[64,512]{1,0:T(8,128)S(1)} %add_two.1.own), channel_id=1, source_target_pairs={{0,12},{1,13},{2,14},{3,15},{4,0},{5,1},{6,2},{7,3},{8,4},{9,5},{1... | collective-permute-start | bytes 393224 | tf_op jit(solution)/shard_map/ppermute | solution.py:42
  110.6 0.7 collective-permute-start.14
  111.4 0.1 collective-permute-start.13
  111.5 4.4 %collective-permute-start.16 = (f32[64,512]{1,0:T(8,128)S(1)}, f32[64,512]{1,0:T(8,128)S(1)}, u32[]{:S(2)}, u32[]{:S(2)}) collective-permute-start(f32[64,512]{1,0:T(8,128)S(1)} %add_two.1.own), channel_id=1, source_target_pairs={{0,1},{1,0},{2,3},{3,2},{4,5},{5,4},{6,7},{7,6},{8,9},{9,8},{10,11... | collective-permute-start | bytes 393224 | tf_op jit(solution)/shard_map/ppermute | solution.py:38
  116.0 0.0 collective-permute-done.15.y_3
  116.0 1.0 collective-permute-start.19
  116.9 0.0 collective-permute-done.14.y_2
  116.9 3.8 %collective-permute-start.18 = (f32[64,512]{1,0:T(8,128)S(1)}, f32[64,512]{1,0:T(8,128)S(1)}, u32[]{:S(2)}, u32[]{:S(2)}) collective-permute-start(f32[64,512]{1,0:T(8,128)S(1)} %collective-permute-done.14.y_2), channel_id=1, source_target_pairs={{0,1},{1,0},{2,3},{3,2},{4,5},{5,4},{6,7},{7,6},{8,9},{9,8},{10,11... | collective-permute-start | bytes 393224 | tf_op jit(solution)/shard_map/ppermute | solution.py:38
  120.7 0.0 collective-permute-done.13.y_1
  120.7 1.3 %collective-permute-start.17 = (f32[64,512]{1,0:T(8,128)S(1)}, f32[64,512]{1,0:T(8,128)S(1)}, u32[]{:S(2)}, u32[]{:S(2)}) collective-permute-start(f32[64,512]{1,0:T(8,128)S(1)} %collective-permute-done.13.y_1), channel_id=1, source_target_pairs={{0,1},{1,0},{2,3},{3,2},{4,5},{5,4},{6,7},{7,6},{8,9},{9,8},{10,11... | collective-permute-start | bytes 393224 | tf_op jit(solution)/shard_map/ppermute | solution.py:38
  122.0 0.0 collective-permute-done.16.other
  122.0 0.0 collective-permute-done.19.z_3
  122.0 0.0 collective-permute-done.18.z_2
  122.0 1.0 collective-permute-done.17.z_1
  123.0 7.1 %relax.1 = f32[8192,128]{1,0:T(8,128)} custom-call(s32[2]{0:T(128)S(1)} %pad_add_fusion.place, f32[64,512]{1,0:T(8,128)S(1)} %add_two.1.own, f32[64,512]{1,0:T(8,128)S(1)} %collective-permute-done.13.y_1, f32[64,512]{1,0:T(8,128)S(1)} %collective-permute-done.14.y_2, f32[64,512]{1,0:T(8,128)S(1)} %collective-permute-done.15.y_3, ...), custom_call_target="tpu_custom_call" | custom-call | flops 8589934592 | bytes 16777216 | tf_op jit(solution)/shard_map/relax/pallas_call | solution.py:451
  (7 shorter events, 0.1 us)
Async XLA Ops:
  0.0 12.6 %copy-start.3 = (f32[128,512]{1,0:T(8,128)S(1)}, f32[128,512]{1,0:T(8,128)}, u32[]{:S(2)}) copy-start(f32[128,512]{1,0:T(8,128)} %param.12) | copy-start | bytes 786436
  3.3 70.0 %collective-permute-start.5 = (f32[3,1024,128]{2,1,0:T(8,128)}, f32[3,1024,128]{2,1,0:T(8,128)S(1)}, u32[]{:S(2)}, u32[]{:S(2)}) collective-permute-start(f32[3,1024,128]{2,1,0:T(8,128)} %get-tuple-element.35), channel_id=1, source_target_pairs={{0,16},{16,32},{32,48},{48,64},{64,80},{80,96},{96,112},{112,128},... | collective-permute-start | bytes 4718600 | tf_op jit(solution)/shard_map/ppermute | solution.py:34
  7.2 72.6 %collective-permute-start.6 = (f32[3,1024,128]{2,1,0:T(8,128)}, f32[3,1024,128]{2,1,0:T(8,128)S(1)}, u32[]{:S(2)}, u32[]{:S(2)}) collective-permute-start(f32[3,1024,128]{2,1,0:T(8,128)} %get-tuple-element.36), channel_id=1, source_target_pairs={{0,240},{16,0},{32,16},{48,32},{64,48},{80,64},{96,80},{112,96},{1... | collective-permute-start | bytes 4718600 | tf_op jit(solution)/shard_map/ppermute | solution.py:34
  13.8 18.7 %collective-permute-start.1 = (f32[384,512]{1,0:T(8,128)S(1)}, f32[384,512]{1,0:T(8,128)S(1)}, u32[]{:S(2)}, u32[]{:S(2)}) collective-permute-start(f32[384,512]{1,0:T(8,128)S(1)} %stack_factors.1.own), channel_id=1, source_target_pairs={{0,12},{1,13},{2,14},{3,15},{4,0},{5,1},{6,2},{7,3},{8,4},{9,5},{1... | collective-permute-start | bytes 2359304 | tf_op jit(solution)/shard_map/cond/branch_1_fun/ppermute | solution.py:42
  16.6 19.4 %collective-permute-start = (f32[384,512]{1,0:T(8,128)S(1)}, f32[384,512]{1,0:T(8,128)S(1)}, u32[]{:S(2)}, u32[]{:S(2)}) collective-permute-start(f32[384,512]{1,0:T(8,128)S(1)} %stack_factors.1.own), channel_id=1, source_target_pairs={{0,4},{1,5},{2,6},{3,7},{4,8},{5,9},{6,10},{7,11},{8,12},{9,13},{1... | collective-permute-start | bytes 2359304 | tf_op jit(solution)/shard_map/cond/branch_1_fun/ppermute | solution.py:42
  32.5 10.0 %collective-permute-start.3 = (f32[192,512]{1,0:T(8,128)S(1)}, f32[192,512]{1,0:T(8,128)S(1)}, u32[]{:S(2)}, u32[]{:S(2)}) collective-permute-start(f32[192,512]{1,0:T(8,128)S(1)} %slice.7), channel_id=1, source_target_pairs={{0,12},{1,13},{2,14},{3,15},{4,0},{5,1},{6,2},{7,3},{8,4},{9,5},{1... | collective-permute-start | bytes 1179656 | tf_op jit(solution)/shard_map/cond/branch_1_fun/ppermute | solution.py:42
  36.0 9.8 %collective-permute-start.2 = (f32[192,512]{1,0:T(8,128)S(1)}, f32[192,512]{1,0:T(8,128)S(1)}, u32[]{:S(2)}, u32[]{:S(2)}) collective-permute-start(f32[192,512]{1,0:T(8,128)S(1)} %slice.6), channel_id=1, source_target_pairs={{0,4},{1,5},{2,6},{3,7},{4,8},{5,9},{6,10},{7,11},{8,12},{9,13},{1... | collective-permute-start | bytes 1179656 | tf_op jit(solution)/shard_map/cond/branch_1_fun/ppermute | solution.py:42
  47.6 8.7 %collective-permute-start.4 = (f32[4,384,512]{2,1,0:T(8,128)}, f32[4,384,512]{2,1,0:T(8,128)}, u32[]{:S(2)}, u32[]{:S(2)}) collective-permute-start(f32[4,384,512]{2,1,0:T(8,128)} %join_factors.1), channel_id=1, source_target_pairs={{0,1},{1,0},{2,3},{3,2},{4,5},{5,4},{6,7},{7,6},{8,9},{9,8},{10,11... | collective-permute-start | bytes 9437192 | tf_op jit(solution)/shard_map/cond/branch_1_fun/ppermute | solution.py:38
  56.3 2.2 %copy-start = (f32[512,2048]{1,0:T(8,128)S(1)}, f32[512,2048]{1,0:T(8,128)}, u32[]{:S(2)}) copy-start(f32[512,2048]{1,0:T(8,128)} %basis.1) | copy-start | bytes 12582916
  61.1 4.1 %copy-start.4 = (s32[4,128]{1,0:T(4,128)S(1)}, s32[4,128]{1,0:T(4,128)}, u32[]{:S(2)}) copy-start(s32[4,128]{1,0:T(4,128)} %param.16) | copy-start | bytes 6148
  61.1 4.1 %copy-start.5 = (s32[4,128]{1,0:T(4,128)S(1)}, s32[4,128]{1,0:T(4,128)}, u32[]{:S(2)}) copy-start(s32[4,128]{1,0:T(4,128)} %param.15) | copy-start | bytes 6148
  61.1 4.4 %copy-start.1 = (f32[2048,4,128]{2,1,0:T(4,128)S(1)}, f32[2048,4,128]{2,1,0:T(4,128)}, u32[]{:S(2)}) copy-start(f32[2048,4,128]{2,1,0:T(4,128)} %param.10) | copy-start | bytes 12582916
  65.1 0.7 copy-start.2
  85.5 2.6 %collective-permute-start.7 = (f32[256,512]{1,0:T(8,128)S(1)}, f32[256,512]{1,0:T(8,128)S(1)}, u32[]{:S(2)}, u32[]{:S(2)}) collective-permute-start(f32[256,512]{1,0:T(8,128)S(1)} %get-tuple-element.46), channel_id=1, source_target_pairs={{0,1},{1,0},{2,3},{3,2},{4,5},{5,4},{6,7},{7,6},{8,9},{9,8},{10,11... | collective-permute-start | bytes 1572872 | tf_op jit(solution)/shard_map/ppermute | solution.py:38
  88.7 6.1 %collective-permute-start.8 = (f32[64,512]{1,0:T(8,128)S(1)}, f32[64,512]{1,0:T(8,128)S(1)}, u32[]{:S(2)}, u32[]{:S(2)}) collective-permute-start(f32[64,512]{1,0:T(8,128)S(1)} %get-tuple-element.48), channel_id=1, source_target_pairs={{0,4},{1,5},{2,6},{3,7},{4,8},{5,9},{6,10},{7,11},{8,12},{9,13},{1... | collective-permute-start | bytes 393224 | tf_op jit(solution)/shard_map/ppermute | solution.py:42
  90.1 8.7 %collective-permute-start.9 = (f32[64,512]{1,0:T(8,128)S(1)}, f32[64,512]{1,0:T(8,128)S(1)}, u32[]{:S(2)}, u32[]{:S(2)}) collective-permute-start(f32[64,512]{1,0:T(8,128)S(1)} %get-tuple-element.49), channel_id=1, source_target_pairs={{0,8},{1,9},{2,10},{3,11},{4,12},{5,13},{6,14},{7,15},{8,0},{9,1},... | collective-permute-start | bytes 393224 | tf_op jit(solution)/shard_map/ppermute | solution.py:42
  92.7 6.1 %collective-permute-start.10 = (f32[64,512]{1,0:T(8,128)S(1)}, f32[64,512]{1,0:T(8,128)S(1)}, u32[]{:S(2)}, u32[]{:S(2)}) collective-permute-start(f32[64,512]{1,0:T(8,128)S(1)} %get-tuple-element.50), channel_id=1, source_target_pairs={{0,12},{1,13},{2,14},{3,15},{4,0},{5,1},{6,2},{7,3},{8,4},{9,5},{1... | collective-permute-start | bytes 393224 | tf_op jit(solution)/shard_map/ppermute | solution.py:42
  98.8 4.1 %collective-permute-start.11 = (f32[64,512]{1,0:T(8,128)S(1)}, f32[64,512]{1,0:T(8,128)S(1)}, u32[]{:S(2)}, u32[]{:S(2)}) collective-permute-start(f32[64,512]{1,0:T(8,128)S(1)} %add_four.1.mine), channel_id=1, source_target_pairs={{0,2},{1,3},{2,0},{3,1},{4,6},{5,7},{6,4},{7,5},{8,10},{9,11},{10,... | collective-permute-start | bytes 393224 | tf_op jit(solution)/shard_map/ppermute | solution.py:38
  104.6 3.9 %collective-permute-start.12 = (f32[64,512]{1,0:T(8,128)S(1)}, f32[64,512]{1,0:T(8,128)S(1)}, u32[]{:S(2)}, u32[]{:S(2)}) collective-permute-start(f32[64,512]{1,0:T(8,128)S(1)} %collide.1.a), channel_id=1, source_target_pairs={{0,2},{1,3},{2,0},{3,1},{4,6},{5,7},{6,4},{7,5},{8,10},{9,11},{10,... | collective-permute-start | bytes 393224 | tf_op jit(solution)/shard_map/ppermute | solution.py:38
  108.6 7.4 %collective-permute-start.15 = (f32[64,512]{1,0:T(8,128)S(1)}, f32[64,512]{1,0:T(8,128)S(1)}, u32[]{:S(2)}, u32[]{:S(2)}) collective-permute-start(f32[64,512]{1,0:T(8,128)S(1)} %add_two.1.own), channel_id=1, source_target_pairs={{0,12},{1,13},{2,14},{3,15},{4,0},{5,1},{6,2},{7,3},{8,4},{9,5},{1... | collective-permute-start | bytes 393224 | tf_op jit(solution)/shard_map/ppermute | solution.py:42
  110.6 6.3 %collective-permute-start.14 = (f32[64,512]{1,0:T(8,128)S(1)}, f32[64,512]{1,0:T(8,128)S(1)}, u32[]{:S(2)}, u32[]{:S(2)}) collective-permute-start(f32[64,512]{1,0:T(8,128)S(1)} %add_two.1.own), channel_id=1, source_target_pairs={{0,8},{1,9},{2,10},{3,11},{4,12},{5,13},{6,14},{7,15},{8,0},{9,1},... | collective-permute-start | bytes 393224 | tf_op jit(solution)/shard_map/ppermute | solution.py:42
  111.4 9.3 %collective-permute-start.13 = (f32[64,512]{1,0:T(8,128)S(1)}, f32[64,512]{1,0:T(8,128)S(1)}, u32[]{:S(2)}, u32[]{:S(2)}) collective-permute-start(f32[64,512]{1,0:T(8,128)S(1)} %add_two.1.own), channel_id=1, source_target_pairs={{0,4},{1,5},{2,6},{3,7},{4,8},{5,9},{6,10},{7,11},{8,12},{9,13},{1... | collective-permute-start | bytes 393224 | tf_op jit(solution)/shard_map/ppermute | solution.py:42
  111.5 10.5 %collective-permute-start.16 = (f32[64,512]{1,0:T(8,128)S(1)}, f32[64,512]{1,0:T(8,128)S(1)}, u32[]{:S(2)}, u32[]{:S(2)}) collective-permute-start(f32[64,512]{1,0:T(8,128)S(1)} %add_two.1.own), channel_id=1, source_target_pairs={{0,1},{1,0},{2,3},{3,2},{4,5},{5,4},{6,7},{7,6},{8,9},{9,8},{10,11... | collective-permute-start | bytes 393224 | tf_op jit(solution)/shard_map/ppermute | solution.py:38
  116.0 6.1 %collective-permute-start.19 = (f32[64,512]{1,0:T(8,128)S(1)}, f32[64,512]{1,0:T(8,128)S(1)}, u32[]{:S(2)}, u32[]{:S(2)}) collective-permute-start(f32[64,512]{1,0:T(8,128)S(1)} %collective-permute-done.15.y_3), channel_id=1, source_target_pairs={{0,1},{1,0},{2,3},{3,2},{4,5},{5,4},{6,7},{7,6},{8,9},{9,8},{10,11... | collective-permute-start | bytes 393224 | tf_op jit(solution)/shard_map/ppermute | solution.py:38
  116.9 5.1 %collective-permute-start.18 = (f32[64,512]{1,0:T(8,128)S(1)}, f32[64,512]{1,0:T(8,128)S(1)}, u32[]{:S(2)}, u32[]{:S(2)}) collective-permute-start(f32[64,512]{1,0:T(8,128)S(1)} %collective-permute-done.14.y_2), channel_id=1, source_target_pairs={{0,1},{1,0},{2,3},{3,2},{4,5},{5,4},{6,7},{7,6},{8,9},{9,8},{10,11... | collective-permute-start | bytes 393224 | tf_op jit(solution)/shard_map/ppermute | solution.py:38
  120.7 2.3 %collective-permute-start.17 = (f32[64,512]{1,0:T(8,128)S(1)}, f32[64,512]{1,0:T(8,128)S(1)}, u32[]{:S(2)}, u32[]{:S(2)}) collective-permute-start(f32[64,512]{1,0:T(8,128)S(1)} %collective-permute-done.13.y_1), channel_id=1, source_target_pairs={{0,1},{1,0},{2,3},{3,2},{4,5},{5,4},{6,7},{7,6},{8,9},{9,8},{10,11... | collective-permute-start | bytes 393224 | tf_op jit(solution)/shard_map/ppermute | solution.py:38

commit v4 on v3

--- a/solution.py
+++ b/solution.py
@@ -19,6 +19,8 @@
 PER_DEVICE = 2048
 HALF = PER_DEVICE // 2
 CHUNK = 256
+CHUNK_M = 512
+CHUNK_R = 256
 MOMENTS = 512
 RANKS = 1024
 F32 = jnp.float32
@@ -138,7 +140,7 @@
     return lax.cond(taken, stage, blank, *operands)
 
 
-def local_kernel(speed, dist, kind, tables, out):
+def local_kernel(speed, dist, kind, tables, out, ends):
     step = pl.program_id(0)
     in_upper = step >= HALF // CHUNK
     line = lax.broadcasted_iota(jnp.int32, (CHUNK, ROWS), 0) + step * CHUNK
@@ -166,6 +168,10 @@
         out[order[1]] = here[1] - fluid[1] * (change[1] + face_1)
         out[order[2]] = here[2] - fluid[2] * (change[2] + (face_2 - face_1))
         out[order[3]] = here[3] - fluid[3] * (change[3] - face_2)
+        ends[0] = here[0]
+        ends[1] = here[1] - here[0]
+        ends[2] = here[3]
+        ends[3] = here[3] - here[2]
 
     @pl.when(in_upper)
     def _():
@@ -193,9 +199,9 @@
             VM,
             pl.BlockSpec((1, COLUMNS, 2 * ROWS, 2 * ROWS), lambda i: (against(i), 0, 0, 0)),
         ],
-        out_specs=pl.BlockSpec((COLUMNS, CHUNK, ROWS), lambda i: (0, i, 0)),
-        out_shape=jax.ShapeDtypeStruct((COLUMNS, PER_DEVICE, ROWS), F32),
-        compiler_params=params(12),
+        out_specs=[pl.BlockSpec((COLUMNS, CHUNK, ROWS), lambda i: (0, i, 0))] * 2,
+        out_shape=[jax.ShapeDtypeStruct((COLUMNS, PER_DEVICE, ROWS), F32)] * 2,
+        compiler_params=params(14),
         cost_estimate=cost(4 << 30, 10 * MIB),
     )(speed, flat, kind, tables)
 
@@ -219,14 +225,21 @@
 
 def split_basis(basis):
     width = 256
+    half = HALF // width
+    run = CHUNK_M // width
+
+    def paired(i):
+        return (i % half) // run * (2 * run) + i // half * run + i % run
+
     flat = pl.BlockSpec((MOMENTS, width), lambda i: (0, i))
+    ordered = pl.BlockSpec((MOMENTS, width), lambda i: (0, paired(i)))
     turned = pl.BlockSpec((width, MOMENTS), lambda i: (i, 0))
     return pl.pallas_call(
         basis_kernel,
         name="split_basis",
         grid=(PER_DEVICE // width,),
         in_specs=[flat],
-        out_specs=[flat, flat, turned, turned],
+        out_specs=[ordered, ordered, turned, turned],
         out_shape=[jax.ShapeDtypeStruct((MOMENTS, PER_DEVICE), BF16)] * 2
         + [jax.ShapeDtypeStruct((PER_DEVICE, MOMENTS), BF16)] * 2,
         compiler_params=params(8),
@@ -295,24 +308,45 @@
     )(mine, theirs)
 
 
-def moments_kernel(
-    speed, place, dist, part, from_left, from_right, kind, high, low, moved, kept, sent, total
+def share_of_moments(high, low, values, total, out):
+    step = pl.program_id(0)
+
+    @pl.when(step == 0)
+    def _():
+        total[...] = jnp.zeros_like(total)
+
+    top, rest = halves(values)
+    lines = pl.ds(pl.multiple_of(step * (2 * CHUNK_M), 2 * CHUNK_M), 2 * CHUNK_M)
+    added = total[...] + dot(high[:, lines], top)
+    added = added + dot(high[:, lines], rest)
+    added = added + dot(low[:, lines], top)
+    total[...] = added
+
+    @pl.when(step == pl.num_programs(0) - 1)
+    def _():
+        out[...] = total[...].T
+
+
+def lines_of(which):
+    step = pl.program_id(0)
+    return pl.ds(pl.multiple_of(which * HALF + step * CHUNK_M, CHUNK_M), CHUNK_M)
+
+
+def faces_kernel(
+    speed, place, ends, part, from_left, from_right, kind, high, low, moved, sent, total
 ):
-    step = pl.program_id(0)
     courant = speed[0]
     slope = 0.5 * (1.0 - courant)
-    across = pl.ds(pl.multiple_of(step * CHUNK, CHUNK), CHUNK)
+    first_core = place[0] == 0
 
     def half(which, order, behind, behind_two, ahead):
-        first_line = pl.multiple_of(which * HALF + step * CHUNK, CHUNK)
-        lines = pl.ds(first_line, CHUNK)
+        lines = lines_of(which)
         fluid = [courant * (1 - kind[x : x + 1, :]).astype(F32) for x in order]
-        first, second, third, fourth = (
-            dist[pl.ds(first_line * COLUMNS + x, CHUNK, stride=COLUMNS), :] for x in order
-        )
-        face_in = behind + slope * minmod(behind - behind_two, first - behind)
-        face_0 = first + slope * minmod(first - behind, second - first)
-        face_3 = fourth + slope * minmod(fourth - third, ahead - fourth)
+        first, forward, fourth, back = (ends[i, lines, :] for i in range(4))
+        step_in = first - behind
+        face_in = behind + slope * minmod(behind - behind_two, step_in)
+        face_0 = first + slope * minmod(step_in, forward)
+        face_3 = fourth + slope * minmod(back, ahead - fourth)
         values = {
             order[0]: part[order[0], lines, :] - fluid[0] * (face_0 - face_in),
             order[1]: part[order[1], lines, :] + fluid[1] * face_0,
@@ -321,49 +355,50 @@
         }
         for x in range(COLUMNS):
             moved[x, lines, :] = values[x]
-        return halves(jnp.concatenate([values[x] for x in range(COLUMNS)], axis=1))
-
-    @pl.when(step == 0)
-    def _():
-        total[...] = jnp.zeros_like(total)
-
-    left, right = from_left, from_right
-    added = total[...]
-    ends = (
-        (DOWN, right[0, across, :], right[1, across, :], left[2, across, :]),
-        (UP, left[0, across, :], left[1, across, :], right[2, across, :]),
-    )
-    for which, end in enumerate(ends):
-        top, rest = half(which, *end)
-        lines = pl.ds(pl.multiple_of(which * HALF + step * CHUNK, CHUNK), CHUNK)
-        added = added + dot(high[:, lines], top)
-        added = added + dot(high[:, lines], rest)
-        added = added + dot(low[:, lines], top)
-    total[...] = added
-
-    @pl.when(step == pl.num_programs(0) - 1)
-    def _():
-        count = CELLS // 2
-        core = place[0]
-        first = total[:, :count].T
-        second = total[:, count:].T
-        kept[...] = jnp.where(core == 0, first, second)
-        sent[...] = jnp.where(core == 0, second, first)
-
-
-def moments_part(speed, place, flat, part, from_left, from_right, kind, high, low):
+        pair = [jnp.where(first_core, values[2 + i], values[i]) for i in range(2)]
+        return jnp.concatenate(pair, axis=1)
+
+    left, right, at = from_left, from_right, lines_of(0)
+    lower = half(0, DOWN, right[0, at, :], right[1, at, :], left[2, at, :])
+    upper = half(1, UP, left[0, at, :], left[1, at, :], right[2, at, :])
+    share_of_moments(high, low, jnp.concatenate([lower, upper], axis=0), total, sent)
+
+
+def moments_kernel(place, moved, high, low, kept, total):
+    own = 2 * place[0]
+    values = [
+        jnp.concatenate([moved[own + i, lines_of(which), :] for i in range(2)], axis=1)
+        for which in range(2)
+    ]
+    share_of_moments(high, low, jnp.concatenate(values, axis=0), total, kept)
+
+
+def moments_part(speed, place, ends, part, from_left, from_right, kind, high, low):
     piece = jax.ShapeDtypeStruct((CELLS // 2, MOMENTS), F32)
-    return pl.pallas_call(
+    scratch = [pltpu.VMEM((MOMENTS, CELLS // 2), F32)]
+    moved, sent = pl.pallas_call(
+        faces_kernel,
+        name="faces_and_moments",
+        grid=(HALF // CHUNK_M,),
+        in_specs=[SM, SM] + [VM] * 7,
+        out_specs=[VM] * 2,
+        out_shape=[jax.ShapeDtypeStruct((COLUMNS, PER_DEVICE, ROWS), F32), piece],
+        scratch_shapes=scratch,
+        compiler_params=params(8),
+        cost_estimate=cost(4 << 30, 18 * MIB),
+    )(speed, place, ends, part, from_left, from_right, kind, high, low)
+    kept = pl.pallas_call(
         moments_kernel,
-        name="faces_and_moments",
-        grid=(HALF // CHUNK,),
-        in_specs=[SM, SM] + [VM] * 7,
-        out_specs=[VM] * 3,
-        out_shape=[jax.ShapeDtypeStruct((COLUMNS, PER_DEVICE, ROWS), F32), piece, piece],
-        scratch_shapes=[pltpu.VMEM((MOMENTS, CELLS), F32)],
-        compiler_params=params(26),
-        cost_estimate=cost(8 << 30, 20 * MIB),
-    )(speed, place, flat, part, from_left, from_right, kind, high, low)
+        name="own_moments",
+        grid=(HALF // CHUNK_M,),
+        in_specs=[SM] + [VM] * 3,
+        out_specs=VM,
+        out_shape=piece,
+        scratch_shapes=scratch,
+        compiler_params=params(6),
+        cost_estimate=cost(4 << 30, 8 * MIB),
+    )(place, moved, high, low)
+    return moved, kept, sent
 
 
 def small_call(kernel, name, count, shape, operands, smem=0, mib=3):
@@ -414,55 +449,64 @@
     arrived = [along_y(piece, away + 1) for away, piece in enumerate(others)]
     summed = small_call(add_four_kernel, "add_four", 1, shape, (own, *arrived))
     operands = (summed, exchanged(summed, 2), factor_high, factor_low)
-    share = small_call(collision_kernel, "collide", 1, shape, operands, mib=10)
+    share = small_call(collision_kernel, "collide", 1, shape, operands, mib=4)
     whole = small_call(add_two_kernel, "add_two", 1, shape, (share, exchanged(share, 2)))
     pieces = [whole] + [along_y(whole, away) for away in (1, 2, 3)]
-    return pieces + [exchanged(piece, 1) for piece in pieces]
+    return pieces, [exchanged(piece, 1) for piece in pieces]
 
 
 def relax_kernel(
-    place, own, y_1, y_2, y_3, other, z_1, z_2, z_3, kind, moved, high, low,
-    out, gathered, turned_high, turned_low,
+    other, place, own, y_1, y_2, y_3, kind, moved, high, low, *rest
 ):
+    *finished, out, gathered, turned_high, turned_low = rest
     step = pl.program_id(0)
     size = own.shape[0]
 
     @pl.when(step == 0)
     def _():
-        pieces = (((own, y_1, y_2, y_3), place[0]), ((other, z_1, z_2, z_3), 1 - place[0]))
-        for group, core in pieces:
-            for away, piece in enumerate(group):
-                at = core * 4 + (place[1] + (4 - away)) % 4
-                gathered[pl.ds(pl.multiple_of(at * size, size), size), :] = piece[...]
+        for away, piece in enumerate((own, y_1, y_2, y_3)):
+            at = pl.multiple_of((place[1] + (4 - away)) % 4 * size, size)
+            gathered[pl.ds(at, size), :] = piece[...]
         turned_high[...], turned_low[...] = halves(gathered[...].T)
 
-    lines = pl.ds(pl.multiple_of(step * CHUNK, CHUNK), CHUNK)
+    lines = pl.ds(pl.multiple_of(step * CHUNK_R, CHUNK_R), CHUNK_R)
     gain = dot(high[lines, :], turned_high[...])
     gain = gain + dot(high[lines, :], turned_low[...])
     gain = gain + dot(low[lines, :], turned_high[...])
-    for x in range(COLUMNS):
-        fluid = HALF_STEP * (1 - kind[x : x + 1, :]).astype(F32)
-        out[pl.ds(x, CHUNK, stride=COLUMNS), :] = (
-            moved[x, lines, :] + fluid * gain[:, x * ROWS : (x + 1) * ROWS]
-        )
-
-
-def relax(place, pieces, kind, moved, high, low):
+    mine = 2 * place[0]
+    here = 2 - mine if other else mine
+    for i in range(2):
+        fluid = HALF_STEP * (1 - kind[pl.ds(here + i, 1), :]).astype(F32)
+        value = moved[here + i, lines, :] + fluid * gain[:, i * ROWS : (i + 1) * ROWS]
+        if other:
+            out[pl.ds(here + i, CHUNK_R, stride=COLUMNS), :] = value
+            done = finished[0][i, lines, :]
+            out[pl.ds(mine + i, CHUNK_R, stride=COLUMNS), :] = done
+        else:
+            out[i, lines, :] = value
+
+
+def relax(place, pieces, kind, moved, high, low, finished=()):
+    if finished:
+        out_spec = pl.BlockSpec((CHUNK_R * COLUMNS, ROWS), lambda i: (i, 0))
+        shape = (PER_DEVICE * COLUMNS, ROWS)
+    else:
+        out_spec, shape = VM, (2, PER_DEVICE, ROWS)
     return pl.pallas_call(
-        relax_kernel,
-        name="relax",
-        grid=(PER_DEVICE // CHUNK,),
-        in_specs=[SM] + [VM] * 12,
-        out_specs=pl.BlockSpec((CHUNK * COLUMNS, ROWS), lambda i: (i, 0)),
-        out_shape=jax.ShapeDtypeStruct((PER_DEVICE * COLUMNS, ROWS), F32),
+        functools.partial(relax_kernel, bool(finished)),
+        name="relax_other" if finished else "relax_own",
+        grid=(PER_DEVICE // CHUNK_R,),
+        in_specs=[SM] + [VM] * (8 + len(finished)),
+        out_specs=out_spec,
+        out_shape=jax.ShapeDtypeStruct(shape, F32),
         scratch_shapes=[
-            pltpu.VMEM((CELLS, MOMENTS), F32),
-            pltpu.VMEM((MOMENTS, CELLS), BF16),
-            pltpu.VMEM((MOMENTS, CELLS), BF16),
+            pltpu.VMEM((CELLS // 2, MOMENTS), F32),
+            pltpu.VMEM((MOMENTS, CELLS // 2), BF16),
+            pltpu.VMEM((MOMENTS, CELLS // 2), BF16),
         ],
-        compiler_params=params(20),
-        cost_estimate=cost(8 << 30, 16 * MIB),
-    )(place, *pieces, kind, moved, high, low)
+        compiler_params=params(8),
+        cost_estimate=cost(4 << 30, 12 * MIB),
+    )(place, *pieces, kind, moved, high, low, *finished)
 
 
 def on_device(dist, basis, left_factor, right_factor, mixing, next_cell, prev_cell, cell_kind):
@@ -477,16 +521,17 @@
     given = (to_left[0, :8], left_factor, right_factor, mixing)
     factors = staged(gathered_factors, given)
     high, low, turned_high, turned_low = split_basis(basis)
-    part = local_part(speed, flat, cell_kind, row_tables(next_cell, prev_cell))
+    part, ends = local_part(speed, flat, cell_kind, row_tables(next_cell, prev_cell))
     factors = split_factors(*factors)
     halo = (from_left, from_right)
     (from_left, from_right), factors = lax.optimization_barrier((halo, factors))
 
     moved, kept, sent = moments_part(
-        speed, place, flat, part, from_left, from_right, cell_kind, high, low
+        speed, place, ends, part, from_left, from_right, cell_kind, high, low
     )
-    pieces = collision_part(place, kept, sent, *factors)
-    out = relax(place, pieces, cell_kind, moved, turned_high, turned_low)
+    pieces, others = collision_part(place, kept, sent, *factors)
+    finished = relax(place, pieces, cell_kind, moved, turned_high, turned_low)
+    out = relax(place, others, cell_kind, moved, turned_high, turned_low, (finished,))
     return out.reshape(dist.shape)
 
 

time: 130 us -> 133 us (1.023)
  Pallas kernels: 35.6 us -> 40.6 us
  waiting for transfers between devices: 49.9 us -> 47.8 us
    pallas_call x2 -> x4, Pallas kernels: 12.7 us -> 17 us  [the longest x2 10.1 us: relax(): pl.pallas_call(functools.partial(relax_kernel, bool(finished)), name='rel...]
    ppermute x8, waiting for transfers between devices: 12.9 us -> 11.1 us  [exchanged(): return lax.ppermute(x, 'vel', [(i, i ^ bit) for i in range(16)])]
  transfers between devices with their start and end apart: 20 -> 20, of which waited for: 11 -> 9; matrix products, arithmetic and copies ran while one was open for 0% -> 0% of each run, Pallas kernels for 13% -> 19%
where the time goes in v4:
time: 133 us; the launch traced here: 132 us
  waiting for transfers between devices  47.8 us (36%)
  starting transfers between devices  40.9 us (31%)
  Pallas kernels  40.6 us (31%)
  local copies, waits for them, and re-layouts  2.61 us (2%)
    ppermute x10, waiting for transfers between devices, along_y(): return lax.ppermute(x, 'vel', [(i, (i + 4 * by) % 16) for i in range(16)])  30.9 us
    ppermute x8, starting transfers between devices, exchanged(): return lax.ppermute(x, 'vel', [(i, i ^ bit) for i in range(16)])  17.2 us
    ppermute x10, starting transfers between devices, along_y(): return lax.ppermute(x, 'vel', [(i, (i + 4 * by) % 16) for i in range(16)])  14.5 us
    ppermute x8, waiting for transfers between devices, exchanged(): return lax.ppermute(x, 'vel', [(i, i ^ bit) for i in range(16)])  11.1 us
    pallas_call x2, Pallas kernels, relax(): pl.pallas_call(functools.partial(relax_kernel, bool(finished)), name='rel...  10.1 us
    ppermute x2, starting transfers between devices, shifted(): return lax.ppermute(x, 'cells', [(i, (i + by) % size) for i in range(size)])  9.21 us
    pallas_call x1, Pallas kernels, local_part(): pl.pallas_call(local_kernel, name='local_transport', grid=(steps,), in_sp...  8 us
    ppermute x2, waiting for transfers between devices, shifted(): return lax.ppermute(x, 'cells', [(i, (i + by) % size) for i in range(size)])  5.74 us
  transfers between devices with their start and end apart: 20, of which 9 were waited for; matrix products, arithmetic and copies ran while one was open for 0% of the time, Pallas kernels for 19%

profile of v4, /device:TPU:1, one launch (start us, length us, event | category | flops | bytes accessed | tf_op | source)
XLA Modules:
  0.0 132.4 jit_solution(1637514142755059337)
XLA Ops:
  0.0 3.3 %pack.1 = (f32[3,1024,128]{2,1,0:T(8,128)}, f32[3,1024,128]{2,1,0:T(8,128)}) custom-call(f32[8192,128]{1,0:T(8,128)} %bitcast.9), custom_call_target="tpu_custom_call" | custom-call | flops 1048576 | bytes 8388608 | tf_op jit(solution)/shard_map/pack/pallas_call | solution.py:118
  3.3 3.9 %collective-permute-start.5 = (f32[3,1024,128]{2,1,0:T(8,128)}, f32[3,1024,128]{2,1,0:T(8,128)S(1)}, u32[]{:S(2)}, u32[]{:S(2)}) collective-permute-start(f32[3,1024,128]{2,1,0:T(8,128)} %get-tuple-element.38), channel_id=1, source_target_pairs={{0,16},{16,32},{32,48},{48,64},{64,80},{80,96},{96,112},{112,128},... | collective-permute-start | bytes 4718600 | tf_op jit(solution)/shard_map/ppermute | solution.py:36
  7.2 5.3 %collective-permute-start.6 = (f32[3,1024,128]{2,1,0:T(8,128)}, f32[3,1024,128]{2,1,0:T(8,128)S(1)}, u32[]{:S(2)}, u32[]{:S(2)}) collective-permute-start(f32[3,1024,128]{2,1,0:T(8,128)} %get-tuple-element.39), channel_id=1, source_target_pairs={{0,240},{16,0},{32,16},{48,32},{64,48},{80,64},{96,80},{112,96},{1... | collective-permute-start | bytes 4718600 | tf_op jit(solution)/shard_map/ppermute | solution.py:36
  12.5 43.8 %conditional.1 = (f32[4,384,512]{2,1,0:T(8,128)}, f32[4,384,512]{2,1,0:T(8,128)}) conditional(s32[]{:T(128)} %convert_element_type.15, () %tuple.14, (f32[128,512]{1,0:T(8,128)S(1)}, f32[128,512]{1,0:T(8,128)}, f32[512,128]{1,0:T(8,128)}) %tuple.21), branch_computations={%region_0.1_spmd, %region_1.2_spmd} | conditional | flops 2097152 | bytes 31981784 | solution.py:140
  12.5 1.2 stack_factors.1.own
  13.7 2.8 %collective-permute-start.1 = (f32[384,512]{1,0:T(8,128)S(1)}, f32[384,512]{1,0:T(8,128)S(1)}, u32[]{:S(2)}, u32[]{:S(2)}) collective-permute-start(f32[384,512]{1,0:T(8,128)S(1)} %stack_factors.1.own), channel_id=1, source_target_pairs={{0,12},{1,13},{2,14},{3,15},{4,0},{5,1},{6,2},{7,3},{8,4},{9,5},{1... | collective-permute-start | bytes 2359304 | tf_op jit(solution)/shard_map/cond/branch_1_fun/ppermute | solution.py:44
  16.5 0.0 collective-permute-start
  16.5 15.9 %collective-permute-done.1.after = f32[384,512]{1,0:T(8,128)S(1)} collective-permute-done((f32[384,512]{1,0:T(8,128)S(1)}, f32[384,512]{1,0:T(8,128)S(1)}, u32[]{:S(2)}, u32[]{:S(2)}) %collective-permute-start.1) | collective-permute-done | bytes 786464 | tf_op jit(solution)/shard_map/cond/branch_1_fun/ppermute | solution.py:44
  32.4 3.5 %collective-permute-start.3 = (f32[192,512]{1,0:T(8,128)S(1)}, f32[192,512]{1,0:T(8,128)S(1)}, u32[]{:S(2)}, u32[]{:S(2)}) collective-permute-start(f32[192,512]{1,0:T(8,128)S(1)} %slice.7), channel_id=1, source_target_pairs={{0,12},{1,13},{2,14},{3,15},{4,0},{5,1},{6,2},{7,3},{8,4},{9,5},{1... | collective-permute-start | bytes 1179656 | tf_op jit(solution)/shard_map/cond/branch_1_fun/ppermute | solution.py:44
  35.9 0.0 collective-permute-done.before
  36.0 0.1 collective-permute-start.2
  36.1 6.4 %collective-permute-done.3.across_rest = f32[192,512]{1,0:T(8,128)S(1)} collective-permute-done((f32[192,512]{1,0:T(8,128)S(1)}, f32[192,512]{1,0:T(8,128)S(1)}, u32[]{:S(2)}, u32[]{:S(2)}) %collective-permute-start.3) | collective-permute-done | bytes 393248 | tf_op jit(solution)/shard_map/cond/branch_1_fun/ppermute | solution.py:44
  42.5 3.2 %collective-permute-done.2.across_top = f32[192,512]{1,0:T(8,128)S(1)} collective-permute-done((f32[192,512]{1,0:T(8,128)S(1)}, f32[192,512]{1,0:T(8,128)S(1)}, u32[]{:S(2)}, u32[]{:S(2)}) %collective-permute-start.2) | collective-permute-done | bytes 393248 | tf_op jit(solution)/shard_map/cond/branch_1_fun/ppermute | solution.py:44
  45.7 1.9 %join_factors.1 = f32[4,384,512]{2,1,0:T(8,128)} custom-call(f32[384,512]{1,0:T(8,128)S(1)} %stack_factors.1.own, f32[384,512]{1,0:T(8,128)S(1)} %collective-permute-done.before, f32[384,512]{1,0:T(8,128)S(1)} %collective-permute-done.1.after, f32[192,512]{1,0:T(8,128)S(1)} %collective-permute-done.2.across_top, ...), custom_call_target="tpu_custom_call" | custom-call | flops 1048576 | bytes 6291456 | tf_op jit(solution)/shard_map/cond/branch_1_fun/join_factors/pallas_call | solution.py:286
  47.6 3.1 %collective-permute-start.4 = (f32[4,384,512]{2,1,0:T(8,128)}, f32[4,384,512]{2,1,0:T(8,128)}, u32[]{:S(2)}, u32[]{:S(2)}) collective-permute-start(f32[4,384,512]{2,1,0:T(8,128)} %join_factors.1), channel_id=1, source_target_pairs={{0,1},{1,0},{2,3},{3,2},{4,5},{5,4},{6,7},{7,6},{8,9},{9,8},{10,11... | collective-permute-start | bytes 9437192 | tf_op jit(solution)/shard_map/cond/branch_1_fun/ppermute | solution.py:40
  50.7 5.6 %collective-permute-done.4 = f32[4,384,512]{2,1,0:T(8,128)} collective-permute-done((f32[4,384,512]{2,1,0:T(8,128)}, f32[4,384,512]{2,1,0:T(8,128)}, u32[]{:S(2)}, u32[]{:S(2)}) %collective-permute-start.4) | collective-permute-done | bytes 3145760 | tf_op jit(solution)/shard_map/cond/branch_1_fun/ppermute | solution.py:40
  56.3 2.2 %copy-done = f32[512,2048]{1,0:T(8,128)S(1)} copy-done((f32[512,2048]{1,0:T(8,128)S(1)}, f32[512,2048]{1,0:T(8,128)}, u32[]{:S(2)}) %copy-start) | copy-done | bytes 4194328
  58.5 2.9 %split_basis.1 = (bf16[512,2048]{1,0:T(8,128)(2,1)S(1)}, bf16[512,2048]{1,0:T(8,128)(2,1)S(1)}, bf16[2048,512]{1,0:T(8,128)(2,1)S(1)}, bf16[2048,512]{1,0:T(8,128)(2,1)S(1)}) custom-call(f32[512,2048]{1,0:T(8,128)S(1)} %copy-done), custom_call_target="tpu_custom_call" | custom-call | flops 16777216 | bytes 12582912 | tf_op jit(solution)/shard_map/split_basis/pallas_call | solution.py:237
  61.4 0.0 copy-start.4
  61.4 0.0 copy-start.5
  61.4 0.0 copy-start.1
  61.4 4.0 %split_factors.1 = (bf16[3,1024,512]{2,1,0:T(8,128)(2,1)S(1)}, bf16[3,1024,512]{2,1,0:T(8,128)(2,1)S(1)}) custom-call(f32[4,384,512]{2,1,0:T(8,128)} %get-tuple-element.40.mine, f32[4,384,512]{2,1,0:T(8,128)} %get-tuple-element.41.theirs), custom_call_target="tpu_custom_call" | custom-call | flops 16777216 | bytes 12582912 | tf_op jit(solution)/shard_map/split_factors/pallas_call | solution.py:300
  65.4 0.0 copy-start.2
  65.4 0.1 pad_add_fusion.place
  65.5 0.0 copy-done.5
  65.5 0.1 fusion
  65.5 0.1 maximum_bitcast_fusion
  65.6 0.1 pad_maximum_fusion.tables
  65.7 0.3 copy-done.2
  66.1 8.0 %local_transport.1 = (f32[4,2048,128]{2,1,0:T(8,128)S(1)}, f32[4,2048,128]{2,1,0:T(8,128)S(1)}) custom-call(f32[1]{0:T(128)} %bitcast.2.speed, f32[8192,128]{1,0:T(8,128)S(1)} %bitcast.10, s32[4,128]{1,0:T(4,128)S(1)} %copy-done.2, bf16[2,4,256,256]{3,2,1,0:T(8,128)(2,1)S(1)} %pad_maximum_fusion.tables), custom_call_target="tpu_custom_call" | custom-call | flops 4294967296 | bytes 10485760 | tf_op jit(solution)/shard_map/local_transport/pallas_call | solution.py:192
  74.1 0.0 collective-permute-done.5.from_left
  74.1 5.7 %collective-permute-done.6.from_right = f32[3,1024,128]{2,1,0:T(8,128)S(1)} collective-permute-done((f32[3,1024,128]{2,1,0:T(8,128)}, f32[3,1024,128]{2,1,0:T(8,128)S(1)}, u32[]{:S(2)}, u32[]{:S(2)}) %collective-permute-start.6) | collective-permute-done | bytes 1572896 | tf_op jit(solution)/shard_map/ppermute | solution.py:36
  79.8 4.0 %faces_and_moments.1 = (f32[4,2048,128]{2,1,0:T(8,128)S(1)}, f32[256,512]{1,0:T(8,128)S(1)}) custom-call(f32[1]{0:T(128)} %bitcast.2.speed, s32[2]{0:T(128)S(1)} %pad_add_fusion.place, f32[4,2048,128]{2,1,0:T(8,128)S(1)} %get-tuple-element.36.ends, f32[4,2048,128]{2,1,0:T(8,128)S(1)} %get-tuple-element.37.part, ...), custom_call_target="tpu_custom_call" | custom-call | flops 4294967296 | bytes 18874368 | tf_op jit(solution)/shard_map/faces_and_moments/pallas_call | solution.py:379
  83.8 1.1 collective-permute-start.7
  84.9 2.9 %own_moments.1.kept = f32[256,512]{1,0:T(8,128)S(1)} custom-call(s32[2]{0:T(128)S(1)} %pad_add_fusion.place, f32[4,2048,128]{2,1,0:T(8,128)S(1)} %get-tuple-element.48.moved, bf16[512,2048]{1,0:T(8,128)(2,1)S(1)} %get-tuple-element.46.high, bf16[512,2048]{1,0:T(8,128)(2,1)S(1)} %get-tuple-element.47.low), custom_call_target="tpu_custom_call" | custom-call | flops 4294967296 | bytes 8388608 | tf_op jit(solution)/shard_map/own_moments/pallas_call | solution.py:390
  87.8 0.0 collective-permute-done.7.received
  87.8 0.6 scatter.1
  88.4 1.6 %collective-permute-start.8 = (f32[64,512]{1,0:T(8,128)S(1)}, f32[64,512]{1,0:T(8,128)S(1)}, u32[]{:S(2)}, u32[]{:S(2)}) collective-permute-start(f32[64,512]{1,0:T(8,128)S(1)} %get-tuple-element.51), channel_id=1, source_target_pairs={{0,4},{1,5},{2,6},{3,7},{4,8},{5,9},{6,10},{7,11},{8,12},{9,13},{1... | collective-permute-start | bytes 393224 | tf_op jit(solution)/shard_map/ppermute | solution.py:44
  89.9 2.6 %collective-permute-start.9 = (f32[64,512]{1,0:T(8,128)S(1)}, f32[64,512]{1,0:T(8,128)S(1)}, u32[]{:S(2)}, u32[]{:S(2)}) collective-permute-start(f32[64,512]{1,0:T(8,128)S(1)} %get-tuple-element.52), channel_id=1, source_target_pairs={{0,8},{1,9},{2,10},{3,11},{4,12},{5,13},{6,14},{7,15},{8,0},{9,1},... | collective-permute-start | bytes 393224 | tf_op jit(solution)/shard_map/ppermute | solution.py:44
  92.6 1.1 collective-permute-start.10
  93.6 1.5 %collective-permute-done.8.b = f32[64,512]{1,0:T(8,128)S(1)} collective-permute-done((f32[64,512]{1,0:T(8,128)S(1)}, f32[64,512]{1,0:T(8,128)S(1)}, u32[]{:S(2)}, u32[]{:S(2)}) %collective-permute-start.8) | collective-permute-done | bytes 131104 | tf_op jit(solution)/shard_map/ppermute | solution.py:44
  95.1 3.9 %collective-permute-done.9.c = f32[64,512]{1,0:T(8,128)S(1)} collective-permute-done((f32[64,512]{1,0:T(8,128)S(1)}, f32[64,512]{1,0:T(8,128)S(1)}, u32[]{:S(2)}, u32[]{:S(2)}) %collective-permute-start.9) | collective-permute-done | bytes 131104 | tf_op jit(solution)/shard_map/ppermute | solution.py:44
  99.0 0.0 collective-permute-done.10.d
  99.0 1.7 %collective-permute-start.11 = (f32[64,512]{1,0:T(8,128)S(1)}, f32[64,512]{1,0:T(8,128)S(1)}, u32[]{:S(2)}, u32[]{:S(2)}) collective-permute-start(f32[64,512]{1,0:T(8,128)S(1)} %add_four.1.mine), channel_id=1, source_target_pairs={{0,2},{1,3},{2,0},{3,1},{4,6},{5,7},{6,4},{7,5},{8,10},{9,11},{10,... | collective-permute-start | bytes 393224 | tf_op jit(solution)/shard_map/ppermute | solution.py:40
  100.8 2.9 %collective-permute-done.11.theirs = f32[64,512]{1,0:T(8,128)S(1)} collective-permute-done((f32[64,512]{1,0:T(8,128)S(1)}, f32[64,512]{1,0:T(8,128)S(1)}, u32[]{:S(2)}, u32[]{:S(2)}) %collective-permute-start.11) | collective-permute-done | bytes 131104 | tf_op jit(solution)/shard_map/ppermute | solution.py:40
  103.7 1.7 %collide.1.a = f32[64,512]{1,0:T(8,128)S(1)} custom-call(f32[64,512]{1,0:T(8,128)S(1)} %add_four.1.mine, f32[64,512]{1,0:T(8,128)S(1)} %collective-permute-done.11.theirs, bf16[3,1024,512]{2,1,0:T(8,128)(2,1)S(1)} %get-tuple-element.54.high, bf16[3,1024,512]{2,1,0:T(8,128)(2,1)S(1)} %get-tuple-element.55.low), custom_call_target="tpu_custom_call" | custom-call | flops 1048576 | bytes 1048576 | tf_op jit(solution)/shard_map/collide/pallas_call | solution.py:406
  105.5 1.4 %collective-permute-start.12 = (f32[64,512]{1,0:T(8,128)S(1)}, f32[64,512]{1,0:T(8,128)S(1)}, u32[]{:S(2)}, u32[]{:S(2)}) collective-permute-start(f32[64,512]{1,0:T(8,128)S(1)} %collide.1.a), channel_id=1, source_target_pairs={{0,2},{1,3},{2,0},{3,1},{4,6},{5,7},{6,4},{7,5},{8,10},{9,11},{10,... | collective-permute-start | bytes 393224 | tf_op jit(solution)/shard_map/ppermute | solution.py:40
  106.8 2.6 %collective-permute-done.12.b = f32[64,512]{1,0:T(8,128)S(1)} collective-permute-done((f32[64,512]{1,0:T(8,128)S(1)}, f32[64,512]{1,0:T(8,128)S(1)}, u32[]{:S(2)}, u32[]{:S(2)}) %collective-permute-start.12) | collective-permute-done | bytes 131104 | tf_op jit(solution)/shard_map/ppermute | solution.py:40
  109.4 2.1 %collective-permute-start.18 = (f32[64,512]{1,0:T(8,128)S(1)}, f32[64,512]{1,0:T(8,128)S(1)}, u32[]{:S(2)}, u32[]{:S(2)}) collective-permute-start(f32[64,512]{1,0:T(8,128)S(1)} %add_two.1.own), channel_id=1, source_target_pairs={{0,12},{1,13},{2,14},{3,15},{4,0},{5,1},{6,2},{7,3},{8,4},{9,5},{1... | collective-permute-start | bytes 393224 | tf_op jit(solution)/shard_map/ppermute | solution.py:44
  111.5 0.0 collective-permute-start.16
  111.5 0.7 collective-permute-start.14
  112.2 3.6 %collective-permute-start.13 = (f32[64,512]{1,0:T(8,128)S(1)}, f32[64,512]{1,0:T(8,128)S(1)}, u32[]{:S(2)}, u32[]{:S(2)}) collective-permute-start(f32[64,512]{1,0:T(8,128)S(1)} %add_two.1.own), channel_id=1, source_target_pairs={{0,1},{1,0},{2,3},{3,2},{4,5},{5,4},{6,7},{7,6},{8,9},{9,8},{10,11... | collective-permute-start | bytes 393224 | tf_op jit(solution)/shard_map/ppermute | solution.py:40
  115.8 0.0 collective-permute-done.18.y_3
  115.8 2.5 %collective-permute-start.19 = (f32[64,512]{1,0:T(8,128)S(1)}, f32[64,512]{1,0:T(8,128)S(1)}, u32[]{:S(2)}, u32[]{:S(2)}) collective-permute-start(f32[64,512]{1,0:T(8,128)S(1)} %collective-permute-done.18.y_3), channel_id=1, source_target_pairs={{0,1},{1,0},{2,3},{3,2},{4,5},{5,4},{6,7},{7,6},{8,9},{9,8},{10,11... | collective-permute-start | bytes 393224 | tf_op jit(solution)/shard_map/ppermute | solution.py:40
  118.3 0.0 collective-permute-done.16.y_2
  118.3 2.6 %collective-permute-start.17 = (f32[64,512]{1,0:T(8,128)S(1)}, f32[64,512]{1,0:T(8,128)S(1)}, u32[]{:S(2)}, u32[]{:S(2)}) collective-permute-start(f32[64,512]{1,0:T(8,128)S(1)} %collective-permute-done.16.y_2), channel_id=1, source_target_pairs={{0,1},{1,0},{2,3},{3,2},{4,5},{5,4},{6,7},{7,6},{8,9},{9,8},{10,11... | collective-permute-start | bytes 393224 | tf_op jit(solution)/shard_map/ppermute | solution.py:40
  120.9 0.0 collective-permute-done.14.y_1
  120.9 1.3 collective-permute-start.15
  122.2 3.9 %relax_own.1.rest_0_ = f32[2,2048,128]{2,1,0:T(8,128)S(1)} custom-call(s32[2]{0:T(128)S(1)} %pad_add_fusion.place, f32[64,512]{1,0:T(8,128)S(1)} %add_two.1.own, f32[64,512]{1,0:T(8,128)S(1)} %collective-permute-done.14.y_1, f32[64,512]{1,0:T(8,128)S(1)} %collective-permute-done.16.y_2, f32[64,512]{1,0:T(8,128)S(1)} %collective-permute-done.18.y_3, ...), custom_call_target="tpu_custom_call" | custom-call | flops 4294967296 | bytes 12582912 | tf_op jit(solution)/shard_map/relax_own/pallas_call | solution.py:495
  126.2 0.0 collective-permute-done.13.own
  126.2 0.0 collective-permute-done.19.y_3
  126.2 0.0 collective-permute-done.17.y_2
  126.2 0.0 collective-permute-done.15.y_1
  126.2 6.2 %relax_other.1 = f32[8192,128]{1,0:T(8,128)} custom-call(s32[2]{0:T(128)S(1)} %pad_add_fusion.place, f32[64,512]{1,0:T(8,128)S(1)} %collective-permute-done.13.own, f32[64,512]{1,0:T(8,128)S(1)} %collective-permute-done.15.y_1, f32[64,512]{1,0:T(8,128)S(1)} %collective-permute-done.17.y_2, f32[64,512]{1,0:T(8,128)S(1)} %collective-permute-done.19.y_3, ...), custom_call_target="tpu_custom_call" | custom-call | flops 4294967296 | bytes 12582912 | tf_op jit(solution)/shard_map/relax_other/pallas_call | solution.py:495
  (9 shorter events, 0.1 us)
Async XLA Ops:
  0.0 12.5 %copy-start.3 = (f32[128,512]{1,0:T(8,128)S(1)}, f32[128,512]{1,0:T(8,128)}, u32[]{:S(2)}) copy-start(f32[128,512]{1,0:T(8,128)} %param.12) | copy-start | bytes 786436
  3.3 70.8 %collective-permute-start.5 = (f32[3,1024,128]{2,1,0:T(8,128)}, f32[3,1024,128]{2,1,0:T(8,128)S(1)}, u32[]{:S(2)}, u32[]{:S(2)}) collective-permute-start(f32[3,1024,128]{2,1,0:T(8,128)} %get-tuple-element.38), channel_id=1, source_target_pairs={{0,16},{16,32},{32,48},{48,64},{64,80},{80,96},{96,112},{112,128},... | collective-permute-start | bytes 4718600 | tf_op jit(solution)/shard_map/ppermute | solution.py:36
  7.2 72.6 %collective-permute-start.6 = (f32[3,1024,128]{2,1,0:T(8,128)}, f32[3,1024,128]{2,1,0:T(8,128)S(1)}, u32[]{:S(2)}, u32[]{:S(2)}) collective-permute-start(f32[3,1024,128]{2,1,0:T(8,128)} %get-tuple-element.39), channel_id=1, source_target_pairs={{0,240},{16,0},{32,16},{48,32},{64,48},{80,64},{96,80},{112,96},{1... | collective-permute-start | bytes 4718600 | tf_op jit(solution)/shard_map/ppermute | solution.py:36
  13.7 18.7 %collective-permute-start.1 = (f32[384,512]{1,0:T(8,128)S(1)}, f32[384,512]{1,0:T(8,128)S(1)}, u32[]{:S(2)}, u32[]{:S(2)}) collective-permute-start(f32[384,512]{1,0:T(8,128)S(1)} %stack_factors.1.own), channel_id=1, source_target_pairs={{0,12},{1,13},{2,14},{3,15},{4,0},{5,1},{6,2},{7,3},{8,4},{9,5},{1... | collective-permute-start | bytes 2359304 | tf_op jit(solution)/shard_map/cond/branch_1_fun/ppermute | solution.py:44
  16.5 19.4 %collective-permute-start = (f32[384,512]{1,0:T(8,128)S(1)}, f32[384,512]{1,0:T(8,128)S(1)}, u32[]{:S(2)}, u32[]{:S(2)}) collective-permute-start(f32[384,512]{1,0:T(8,128)S(1)} %stack_factors.1.own), channel_id=1, source_target_pairs={{0,4},{1,5},{2,6},{3,7},{4,8},{5,9},{6,10},{7,11},{8,12},{9,13},{1... | collective-permute-start | bytes 2359304 | tf_op jit(solution)/shard_map/cond/branch_1_fun/ppermute | solution.py:44
  32.4 10.0 %collective-permute-start.3 = (f32[192,512]{1,0:T(8,128)S(1)}, f32[192,512]{1,0:T(8,128)S(1)}, u32[]{:S(2)}, u32[]{:S(2)}) collective-permute-start(f32[192,512]{1,0:T(8,128)S(1)} %slice.7), channel_id=1, source_target_pairs={{0,12},{1,13},{2,14},{3,15},{4,0},{5,1},{6,2},{7,3},{8,4},{9,5},{1... | collective-permute-start | bytes 1179656 | tf_op jit(solution)/shard_map/cond/branch_1_fun/ppermute | solution.py:44
  36.0 9.8 %collective-permute-start.2 = (f32[192,512]{1,0:T(8,128)S(1)}, f32[192,512]{1,0:T(8,128)S(1)}, u32[]{:S(2)}, u32[]{:S(2)}) collective-permute-start(f32[192,512]{1,0:T(8,128)S(1)} %slice.6), channel_id=1, source_target_pairs={{0,4},{1,5},{2,6},{3,7},{4,8},{5,9},{6,10},{7,11},{8,12},{9,13},{1... | collective-permute-start | bytes 1179656 | tf_op jit(solution)/shard_map/cond/branch_1_fun/ppermute | solution.py:44
  47.6 8.7 %collective-permute-start.4 = (f32[4,384,512]{2,1,0:T(8,128)}, f32[4,384,512]{2,1,0:T(8,128)}, u32[]{:S(2)}, u32[]{:S(2)}) collective-permute-start(f32[4,384,512]{2,1,0:T(8,128)} %join_factors.1), channel_id=1, source_target_pairs={{0,1},{1,0},{2,3},{3,2},{4,5},{5,4},{6,7},{7,6},{8,9},{9,8},{10,11... | collective-permute-start | bytes 9437192 | tf_op jit(solution)/shard_map/cond/branch_1_fun/ppermute | solution.py:40
  56.3 2.2 %copy-start = (f32[512,2048]{1,0:T(8,128)S(1)}, f32[512,2048]{1,0:T(8,128)}, u32[]{:S(2)}) copy-start(f32[512,2048]{1,0:T(8,128)} %basis.1) | copy-start | bytes 12582916
  61.4 4.1 %copy-start.4 = (s32[4,128]{1,0:T(4,128)S(1)}, s32[4,128]{1,0:T(4,128)}, u32[]{:S(2)}) copy-start(s32[4,128]{1,0:T(4,128)} %param.16) | copy-start | bytes 6148
  61.4 4.1 %copy-start.5 = (s32[4,128]{1,0:T(4,128)S(1)}, s32[4,128]{1,0:T(4,128)}, u32[]{:S(2)}) copy-start(s32[4,128]{1,0:T(4,128)} %param.15) | copy-start | bytes 6148
  61.4 4.3 %copy-start.1 = (f32[2048,4,128]{2,1,0:T(4,128)S(1)}, f32[2048,4,128]{2,1,0:T(4,128)}, u32[]{:S(2)}) copy-start(f32[2048,4,128]{2,1,0:T(4,128)} %param.10) | copy-start | bytes 12582916
  65.4 0.7 copy-start.2
  83.8 4.0 %collective-permute-start.7 = (f32[256,512]{1,0:T(8,128)S(1)}, f32[256,512]{1,0:T(8,128)S(1)}, u32[]{:S(2)}, u32[]{:S(2)}) collective-permute-start(f32[256,512]{1,0:T(8,128)S(1)} %get-tuple-element.49), channel_id=1, source_target_pairs={{0,1},{1,0},{2,3},{3,2},{4,5},{5,4},{6,7},{7,6},{8,9},{9,8},{10,11... | collective-permute-start | bytes 1572872 | tf_op jit(solution)/shard_map/ppermute | solution.py:40
  88.4 6.7 %collective-permute-start.8 = (f32[64,512]{1,0:T(8,128)S(1)}, f32[64,512]{1,0:T(8,128)S(1)}, u32[]{:S(2)}, u32[]{:S(2)}) collective-permute-start(f32[64,512]{1,0:T(8,128)S(1)} %get-tuple-element.51), channel_id=1, source_target_pairs={{0,4},{1,5},{2,6},{3,7},{4,8},{5,9},{6,10},{7,11},{8,12},{9,13},{1... | collective-permute-start | bytes 393224 | tf_op jit(solution)/shard_map/ppermute | solution.py:44
  89.9 9.1 %collective-permute-start.9 = (f32[64,512]{1,0:T(8,128)S(1)}, f32[64,512]{1,0:T(8,128)S(1)}, u32[]{:S(2)}, u32[]{:S(2)}) collective-permute-start(f32[64,512]{1,0:T(8,128)S(1)} %get-tuple-element.52), channel_id=1, source_target_pairs={{0,8},{1,9},{2,10},{3,11},{4,12},{5,13},{6,14},{7,15},{8,0},{9,1},... | collective-permute-start | bytes 393224 | tf_op jit(solution)/shard_map/ppermute | solution.py:44
  92.6 6.4 %collective-permute-start.10 = (f32[64,512]{1,0:T(8,128)S(1)}, f32[64,512]{1,0:T(8,128)S(1)}, u32[]{:S(2)}, u32[]{:S(2)}) collective-permute-start(f32[64,512]{1,0:T(8,128)S(1)} %get-tuple-element.53), channel_id=1, source_target_pairs={{0,12},{1,13},{2,14},{3,15},{4,0},{5,1},{6,2},{7,3},{8,4},{9,5},{1... | collective-permute-start | bytes 393224 | tf_op jit(solution)/shard_map/ppermute | solution.py:44
  99.0 4.7 %collective-permute-start.11 = (f32[64,512]{1,0:T(8,128)S(1)}, f32[64,512]{1,0:T(8,128)S(1)}, u32[]{:S(2)}, u32[]{:S(2)}) collective-permute-start(f32[64,512]{1,0:T(8,128)S(1)} %add_four.1.mine), channel_id=1, source_target_pairs={{0,2},{1,3},{2,0},{3,1},{4,6},{5,7},{6,4},{7,5},{8,10},{9,11},{10,... | collective-permute-start | bytes 393224 | tf_op jit(solution)/shard_map/ppermute | solution.py:40
  105.5 3.9 %collective-permute-start.12 = (f32[64,512]{1,0:T(8,128)S(1)}, f32[64,512]{1,0:T(8,128)S(1)}, u32[]{:S(2)}, u32[]{:S(2)}) collective-permute-start(f32[64,512]{1,0:T(8,128)S(1)} %collide.1.a), channel_id=1, source_target_pairs={{0,2},{1,3},{2,0},{3,1},{4,6},{5,7},{6,4},{7,5},{8,10},{9,11},{10,... | collective-permute-start | bytes 393224 | tf_op jit(solution)/shard_map/ppermute | solution.py:40
  109.4 6.4 %collective-permute-start.18 = (f32[64,512]{1,0:T(8,128)S(1)}, f32[64,512]{1,0:T(8,128)S(1)}, u32[]{:S(2)}, u32[]{:S(2)}) collective-permute-start(f32[64,512]{1,0:T(8,128)S(1)} %add_two.1.own), channel_id=1, source_target_pairs={{0,12},{1,13},{2,14},{3,15},{4,0},{5,1},{6,2},{7,3},{8,4},{9,5},{1... | collective-permute-start | bytes 393224 | tf_op jit(solution)/shard_map/ppermute | solution.py:44
  111.5 6.8 %collective-permute-start.16 = (f32[64,512]{1,0:T(8,128)S(1)}, f32[64,512]{1,0:T(8,128)S(1)}, u32[]{:S(2)}, u32[]{:S(2)}) collective-permute-start(f32[64,512]{1,0:T(8,128)S(1)} %add_two.1.own), channel_id=1, source_target_pairs={{0,8},{1,9},{2,10},{3,11},{4,12},{5,13},{6,14},{7,15},{8,0},{9,1},... | collective-permute-start | bytes 393224 | tf_op jit(solution)/shard_map/ppermute | solution.py:44
  111.5 9.4 %collective-permute-start.14 = (f32[64,512]{1,0:T(8,128)S(1)}, f32[64,512]{1,0:T(8,128)S(1)}, u32[]{:S(2)}, u32[]{:S(2)}) collective-permute-start(f32[64,512]{1,0:T(8,128)S(1)} %add_two.1.own), channel_id=1, source_target_pairs={{0,4},{1,5},{2,6},{3,7},{4,8},{5,9},{6,10},{7,11},{8,12},{9,13},{1... | collective-permute-start | bytes 393224 | tf_op jit(solution)/shard_map/ppermute | solution.py:44
  112.2 14.0 %collective-permute-start.13 = (f32[64,512]{1,0:T(8,128)S(1)}, f32[64,512]{1,0:T(8,128)S(1)}, u32[]{:S(2)}, u32[]{:S(2)}) collective-permute-start(f32[64,512]{1,0:T(8,128)S(1)} %add_two.1.own), channel_id=1, source_target_pairs={{0,1},{1,0},{2,3},{3,2},{4,5},{5,4},{6,7},{7,6},{8,9},{9,8},{10,11... | collective-permute-start | bytes 393224 | tf_op jit(solution)/shard_map/ppermute | solution.py:40
  115.8 10.4 %collective-permute-start.19 = (f32[64,512]{1,0:T(8,128)S(1)}, f32[64,512]{1,0:T(8,128)S(1)}, u32[]{:S(2)}, u32[]{:S(2)}) collective-permute-start(f32[64,512]{1,0:T(8,128)S(1)} %collective-permute-done.18.y_3), channel_id=1, source_target_pairs={{0,1},{1,0},{2,3},{3,2},{4,5},{5,4},{6,7},{7,6},{8,9},{9,8},{10,11... | collective-permute-start | bytes 393224 | tf_op jit(solution)/shard_map/ppermute | solution.py:40
  118.3 7.9 %collective-permute-start.17 = (f32[64,512]{1,0:T(8,128)S(1)}, f32[64,512]{1,0:T(8,128)S(1)}, u32[]{:S(2)}, u32[]{:S(2)}) collective-permute-start(f32[64,512]{1,0:T(8,128)S(1)} %collective-permute-done.16.y_2), channel_id=1, source_target_pairs={{0,1},{1,0},{2,3},{3,2},{4,5},{5,4},{6,7},{7,6},{8,9},{9,8},{10,11... | collective-permute-start | bytes 393224 | tf_op jit(solution)/shard_map/ppermute | solution.py:40
  120.9 5.3 %collective-permute-start.15 = (f32[64,512]{1,0:T(8,128)S(1)}, f32[64,512]{1,0:T(8,128)S(1)}, u32[]{:S(2)}, u32[]{:S(2)}) collective-permute-start(f32[64,512]{1,0:T(8,128)S(1)} %collective-permute-done.14.y_1), channel_id=1, source_target_pairs={{0,1},{1,0},{2,3},{3,2},{4,5},{5,4},{6,7},{7,6},{8,9},{9,8},{10,11... | collective-permute-start | bytes 393224 | tf_op jit(solution)/shard_map/ppermute | solution.py:40

commit v5 on v4

--- a/solution.py
+++ b/solution.py
@@ -19,8 +19,8 @@
 PER_DEVICE = 2048
 HALF = PER_DEVICE // 2
 CHUNK = 256
-CHUNK_M = 512
-CHUNK_R = 256
+CHUNK_M = 1024
+CHUNK_R = 1024
 MOMENTS = 512
 RANKS = 1024
 F32 = jnp.float32
@@ -452,61 +452,52 @@
     share = small_call(collision_kernel, "collide", 1, shape, operands, mib=4)
     whole = small_call(add_two_kernel, "add_two", 1, shape, (share, exchanged(share, 2)))
     pieces = [whole] + [along_y(whole, away) for away in (1, 2, 3)]
-    return pieces, [exchanged(piece, 1) for piece in pieces]
+    return pieces + [exchanged(piece, 1) for piece in pieces]
 
 
 def relax_kernel(
-    other, place, own, y_1, y_2, y_3, kind, moved, high, low, *rest
+    place, own, y_1, y_2, y_3, other, z_1, z_2, z_3, kind, moved, high, low,
+    out, gathered, turned_high, turned_low,
 ):
-    *finished, out, gathered, turned_high, turned_low = rest
     step = pl.program_id(0)
     size = own.shape[0]
 
     @pl.when(step == 0)
     def _():
-        for away, piece in enumerate((own, y_1, y_2, y_3)):
-            at = pl.multiple_of((place[1] + (4 - away)) % 4 * size, size)
-            gathered[pl.ds(at, size), :] = piece[...]
+        pieces = (((own, y_1, y_2, y_3), place[0]), ((other, z_1, z_2, z_3), 1 - place[0]))
+        for group, core in pieces:
+            for away, piece in enumerate(group):
+                at = core * 4 + (place[1] + (4 - away)) % 4
+                gathered[pl.ds(pl.multiple_of(at * size, size), size), :] = piece[...]
         turned_high[...], turned_low[...] = halves(gathered[...].T)
 
     lines = pl.ds(pl.multiple_of(step * CHUNK_R, CHUNK_R), CHUNK_R)
     gain = dot(high[lines, :], turned_high[...])
     gain = gain + dot(high[lines, :], turned_low[...])
     gain = gain + dot(low[lines, :], turned_high[...])
-    mine = 2 * place[0]
-    here = 2 - mine if other else mine
-    for i in range(2):
-        fluid = HALF_STEP * (1 - kind[pl.ds(here + i, 1), :]).astype(F32)
-        value = moved[here + i, lines, :] + fluid * gain[:, i * ROWS : (i + 1) * ROWS]
-        if other:
-            out[pl.ds(here + i, CHUNK_R, stride=COLUMNS), :] = value
-            done = finished[0][i, lines, :]
-            out[pl.ds(mine + i, CHUNK_R, stride=COLUMNS), :] = done
-        else:
-            out[i, lines, :] = value
-
-
-def relax(place, pieces, kind, moved, high, low, finished=()):
-    if finished:
-        out_spec = pl.BlockSpec((CHUNK_R * COLUMNS, ROWS), lambda i: (i, 0))
-        shape = (PER_DEVICE * COLUMNS, ROWS)
-    else:
-        out_spec, shape = VM, (2, PER_DEVICE, ROWS)
+    for x in range(COLUMNS):
+        fluid = HALF_STEP * (1 - kind[x : x + 1, :]).astype(F32)
+        out[pl.ds(x, CHUNK_R, stride=COLUMNS), :] = (
+            moved[x, lines, :] + fluid * gain[:, x * ROWS : (x + 1) * ROWS]
+        )
+
+
+def relax(place, pieces, kind, moved, high, low):
     return pl.pallas_call(
-        functools.partial(relax_kernel, bool(finished)),
-        name="relax_other" if finished else "relax_own",
+        relax_kernel,
+        name="relax",
         grid=(PER_DEVICE // CHUNK_R,),
-        in_specs=[SM] + [VM] * (8 + len(finished)),
-        out_specs=out_spec,
-        out_shape=jax.ShapeDtypeStruct(shape, F32),
+        in_specs=[SM] + [VM] * 12,
+        out_specs=pl.BlockSpec((CHUNK_R * COLUMNS, ROWS), lambda i: (i, 0)),
+        out_shape=jax.ShapeDtypeStruct((PER_DEVICE * COLUMNS, ROWS), F32),
         scratch_shapes=[
-            pltpu.VMEM((CELLS // 2, MOMENTS), F32),
-            pltpu.VMEM((MOMENTS, CELLS // 2), BF16),
-            pltpu.VMEM((MOMENTS, CELLS // 2), BF16),
+            pltpu.VMEM((CELLS, MOMENTS), F32),
+            pltpu.VMEM((MOMENTS, CELLS), BF16),
+            pltpu.VMEM((MOMENTS, CELLS), BF16),
         ],
-        compiler_params=params(8),
-        cost_estimate=cost(4 << 30, 12 * MIB),
-    )(place, *pieces, kind, moved, high, low, *finished)
+        compiler_params=params(14),
+        cost_estimate=cost(8 << 30, 16 * MIB),
+    )(place, *pieces, kind, moved, high, low)
 
 
 def on_device(dist, basis, left_factor, right_factor, mixing, next_cell, prev_cell, cell_kind):
@@ -529,9 +520,8 @@
     moved, kept, sent = moments_part(
         speed, place, ends, part, from_left, from_right, cell_kind, high, low
     )
-    pieces, others = collision_part(place, kept, sent, *factors)
-    finished = relax(place, pieces, cell_kind, moved, turned_high, turned_low)
-    out = relax(place, others, cell_kind, moved, turned_high, turned_low, (finished,))
+    pieces = collision_part(place, kept, sent, *factors)
+    out = relax(place, pieces, cell_kind, moved, turned_high, turned_low)
     return out.reshape(dist.shape)
 
 

time: 133 us -> 128 us (0.962)
  Pallas kernels: 40.6 us -> 35.2 us
    pallas_call x2 -> x1, Pallas kernels: 10.1 us -> 5.89 us  [relax(): pl.pallas_call(relax_kernel, name='relax', grid=(PER_DEVICE // CHUNK_R,),...]
  transfers between devices with their start and end apart: 20 -> 20, of which waited for: 9 -> 10; matrix products, arithmetic and copies ran while one was open for 0% -> 0% of each run, Pallas kernels for 19% -> 16%
where the time goes in v5:
time: 128 us
  waiting for transfers between devices  48.9 us (38%)
  starting transfers between devices  40.9 us (32%)
  Pallas kernels  35.2 us (28%)
  local copies, waits for them, and re-layouts  2.61 us (2%)
    ppermute x10, waiting for transfers between devices, along_y(): return lax.ppermute(x, 'vel', [(i, (i + 4 * by) % 16) for i in range(16)])  31 us
    ppermute x8, starting transfers between devices, exchanged(): return lax.ppermute(x, 'vel', [(i, i ^ bit) for i in range(16)])  17.4 us
    ppermute x10, starting transfers between devices, along_y(): return lax.ppermute(x, 'vel', [(i, (i + 4 * by) % 16) for i in range(16)])  14.3 us
    ppermute x8, waiting for transfers between devices, exchanged(): return lax.ppermute(x, 'vel', [(i, i ^ bit) for i in range(16)])  12.1 us
    ppermute x2, starting transfers between devices, shifted(): return lax.ppermute(x, 'cells', [(i, (i + by) % size) for i in range(size)])  9.21 us
    pallas_call x1, Pallas kernels, local_part(): pl.pallas_call(local_kernel, name='local_transport', grid=(steps,), in_sp...  8 us
    pallas_call x1, Pallas kernels, relax(): pl.pallas_call(relax_kernel, name='relax', grid=(PER_DEVICE // CHUNK_R,),...  5.89 us
    ppermute x2, waiting for transfers between devices, shifted(): return lax.ppermute(x, 'cells', [(i, (i + by) % size) for i in range(size)])  5.77 us
  transfers between devices with their start and end apart: 20, of which 10 were waited for; matrix products, arithmetic and copies ran while one was open for 0% of the time, Pallas kernels for 16%

profile of v5, /device:TPU:1, one launch (start us, length us, event | category | flops | bytes accessed | tf_op | source)
XLA Modules:
  0.0 128.0 jit_solution(13200088235274153073)
XLA Ops:
  0.0 3.3 %pack.1 = (f32[3,1024,128]{2,1,0:T(8,128)}, f32[3,1024,128]{2,1,0:T(8,128)}) custom-call(f32[8192,128]{1,0:T(8,128)} %bitcast.9), custom_call_target="tpu_custom_call" | custom-call | flops 1048576 | bytes 8388608 | tf_op jit(solution)/shard_map/pack/pallas_call | solution.py:118
  3.3 3.9 %collective-permute-start.5 = (f32[3,1024,128]{2,1,0:T(8,128)}, f32[3,1024,128]{2,1,0:T(8,128)S(1)}, u32[]{:S(2)}, u32[]{:S(2)}) collective-permute-start(f32[3,1024,128]{2,1,0:T(8,128)} %get-tuple-element.38), channel_id=1, source_target_pairs={{0,16},{16,32},{32,48},{48,64},{64,80},{80,96},{96,112},{112,128},... | collective-permute-start | bytes 4718600 | tf_op jit(solution)/shard_map/ppermute | solution.py:36
  7.2 5.3 %collective-permute-start.6 = (f32[3,1024,128]{2,1,0:T(8,128)}, f32[3,1024,128]{2,1,0:T(8,128)S(1)}, u32[]{:S(2)}, u32[]{:S(2)}) collective-permute-start(f32[3,1024,128]{2,1,0:T(8,128)} %get-tuple-element.39), channel_id=1, source_target_pairs={{0,240},{16,0},{32,16},{48,32},{64,48},{80,64},{96,80},{112,96},{1... | collective-permute-start | bytes 4718600 | tf_op jit(solution)/shard_map/ppermute | solution.py:36
  12.5 0.0 copy-done.3
  12.5 43.8 %conditional.1 = (f32[4,384,512]{2,1,0:T(8,128)}, f32[4,384,512]{2,1,0:T(8,128)}) conditional(s32[]{:T(128)} %convert_element_type.15, () %tuple.14, (f32[128,512]{1,0:T(8,128)S(1)}, f32[128,512]{1,0:T(8,128)}, f32[512,128]{1,0:T(8,128)}) %tuple.21), branch_computations={%region_0.1_spmd, %region_1.2_spmd} | conditional | flops 2097152 | bytes 31981784 | solution.py:140
  12.5 1.2 stack_factors.1.own
  13.7 2.8 %collective-permute-start.1 = (f32[384,512]{1,0:T(8,128)S(1)}, f32[384,512]{1,0:T(8,128)S(1)}, u32[]{:S(2)}, u32[]{:S(2)}) collective-permute-start(f32[384,512]{1,0:T(8,128)S(1)} %stack_factors.1.own), channel_id=1, source_target_pairs={{0,12},{1,13},{2,14},{3,15},{4,0},{5,1},{6,2},{7,3},{8,4},{9,5},{1... | collective-permute-start | bytes 2359304 | tf_op jit(solution)/shard_map/cond/branch_1_fun/ppermute | solution.py:44
  16.5 0.0 collective-permute-start
  16.5 15.9 %collective-permute-done.1.after = f32[384,512]{1,0:T(8,128)S(1)} collective-permute-done((f32[384,512]{1,0:T(8,128)S(1)}, f32[384,512]{1,0:T(8,128)S(1)}, u32[]{:S(2)}, u32[]{:S(2)}) %collective-permute-start.1) | collective-permute-done | bytes 786464 | tf_op jit(solution)/shard_map/cond/branch_1_fun/ppermute | solution.py:44
  32.4 3.5 %collective-permute-start.3 = (f32[192,512]{1,0:T(8,128)S(1)}, f32[192,512]{1,0:T(8,128)S(1)}, u32[]{:S(2)}, u32[]{:S(2)}) collective-permute-start(f32[192,512]{1,0:T(8,128)S(1)} %slice.7), channel_id=1, source_target_pairs={{0,12},{1,13},{2,14},{3,15},{4,0},{5,1},{6,2},{7,3},{8,4},{9,5},{1... | collective-permute-start | bytes 1179656 | tf_op jit(solution)/shard_map/cond/branch_1_fun/ppermute | solution.py:44
  35.9 0.0 collective-permute-done.before
  36.0 0.1 collective-permute-start.2
  36.1 6.4 %collective-permute-done.3.across_rest = f32[192,512]{1,0:T(8,128)S(1)} collective-permute-done((f32[192,512]{1,0:T(8,128)S(1)}, f32[192,512]{1,0:T(8,128)S(1)}, u32[]{:S(2)}, u32[]{:S(2)}) %collective-permute-start.3) | collective-permute-done | bytes 393248 | tf_op jit(solution)/shard_map/cond/branch_1_fun/ppermute | solution.py:44
  42.5 3.2 %collective-permute-done.2.across_top = f32[192,512]{1,0:T(8,128)S(1)} collective-permute-done((f32[192,512]{1,0:T(8,128)S(1)}, f32[192,512]{1,0:T(8,128)S(1)}, u32[]{:S(2)}, u32[]{:S(2)}) %collective-permute-start.2) | collective-permute-done | bytes 393248 | tf_op jit(solution)/shard_map/cond/branch_1_fun/ppermute | solution.py:44
  45.7 1.9 %join_factors.1 = f32[4,384,512]{2,1,0:T(8,128)} custom-call(f32[384,512]{1,0:T(8,128)S(1)} %stack_factors.1.own, f32[384,512]{1,0:T(8,128)S(1)} %collective-permute-done.before, f32[384,512]{1,0:T(8,128)S(1)} %collective-permute-done.1.after, f32[192,512]{1,0:T(8,128)S(1)} %collective-permute-done.2.across_top, ...), custom_call_target="tpu_custom_call" | custom-call | flops 1048576 | bytes 6291456 | tf_op jit(solution)/shard_map/cond/branch_1_fun/join_factors/pallas_call | solution.py:286
  47.6 3.1 %collective-permute-start.4 = (f32[4,384,512]{2,1,0:T(8,128)}, f32[4,384,512]{2,1,0:T(8,128)}, u32[]{:S(2)}, u32[]{:S(2)}) collective-permute-start(f32[4,384,512]{2,1,0:T(8,128)} %join_factors.1), channel_id=1, source_target_pairs={{0,1},{1,0},{2,3},{3,2},{4,5},{5,4},{6,7},{7,6},{8,9},{9,8},{10,11... | collective-permute-start | bytes 9437192 | tf_op jit(solution)/shard_map/cond/branch_1_fun/ppermute | solution.py:40
  50.7 5.6 %collective-permute-done.4 = f32[4,384,512]{2,1,0:T(8,128)} collective-permute-done((f32[4,384,512]{2,1,0:T(8,128)}, f32[4,384,512]{2,1,0:T(8,128)}, u32[]{:S(2)}, u32[]{:S(2)}) %collective-permute-start.4) | collective-permute-done | bytes 3145760 | tf_op jit(solution)/shard_map/cond/branch_1_fun/ppermute | solution.py:40
  56.3 2.2 %copy-done = f32[512,2048]{1,0:T(8,128)S(1)} copy-done((f32[512,2048]{1,0:T(8,128)S(1)}, f32[512,2048]{1,0:T(8,128)}, u32[]{:S(2)}) %copy-start) | copy-done | bytes 4194328
  58.5 2.9 %split_basis.1 = (bf16[512,2048]{1,0:T(8,128)(2,1)S(1)}, bf16[512,2048]{1,0:T(8,128)(2,1)S(1)}, bf16[2048,512]{1,0:T(8,128)(2,1)S(1)}, bf16[2048,512]{1,0:T(8,128)(2,1)S(1)}) custom-call(f32[512,2048]{1,0:T(8,128)S(1)} %copy-done), custom_call_target="tpu_custom_call" | custom-call | flops 16777216 | bytes 12582912 | tf_op jit(solution)/shard_map/split_basis/pallas_call | solution.py:237
  61.3 0.0 copy-start.4
  61.3 0.0 copy-start.5
  61.4 0.0 copy-start.1
  61.4 4.0 %split_factors.1 = (bf16[3,1024,512]{2,1,0:T(8,128)(2,1)S(1)}, bf16[3,1024,512]{2,1,0:T(8,128)(2,1)S(1)}) custom-call(f32[4,384,512]{2,1,0:T(8,128)} %get-tuple-element.40.mine, f32[4,384,512]{2,1,0:T(8,128)} %get-tuple-element.41.theirs), custom_call_target="tpu_custom_call" | custom-call | flops 16777216 | bytes 12582912 | tf_op jit(solution)/shard_map/split_factors/pallas_call | solution.py:300
  65.3 0.0 copy-start.2
  65.3 0.1 pad_add_fusion.place
  65.4 0.0 copy-done.4
  65.4 0.1 fusion
  65.5 0.1 maximum_bitcast_fusion
  65.6 0.1 pad_maximum_fusion.tables
  65.7 0.3 copy-done.2
  66.0 8.0 %local_transport.1 = (f32[4,2048,128]{2,1,0:T(8,128)S(1)}, f32[4,2048,128]{2,1,0:T(8,128)S(1)}) custom-call(f32[1]{0:T(128)} %bitcast.2.speed, f32[8192,128]{1,0:T(8,128)S(1)} %bitcast.10, s32[4,128]{1,0:T(4,128)S(1)} %copy-done.2, bf16[2,4,256,256]{3,2,1,0:T(8,128)(2,1)S(1)} %pad_maximum_fusion.tables), custom_call_target="tpu_custom_call" | custom-call | flops 4294967296 | bytes 10485760 | tf_op jit(solution)/shard_map/local_transport/pallas_call | solution.py:192
  74.0 0.0 collective-permute-done.5.from_left
  74.1 5.8 %collective-permute-done.6.from_right = f32[3,1024,128]{2,1,0:T(8,128)S(1)} collective-permute-done((f32[3,1024,128]{2,1,0:T(8,128)}, f32[3,1024,128]{2,1,0:T(8,128)S(1)}, u32[]{:S(2)}, u32[]{:S(2)}) %collective-permute-start.6) | collective-permute-done | bytes 1572896 | tf_op jit(solution)/shard_map/ppermute | solution.py:36
  79.8 3.3 %faces_and_moments.1 = (f32[4,2048,128]{2,1,0:T(8,128)S(1)}, f32[256,512]{1,0:T(8,128)S(1)}) custom-call(f32[1]{0:T(128)} %bitcast.2.speed, s32[2]{0:T(128)S(1)} %pad_add_fusion.place, f32[4,2048,128]{2,1,0:T(8,128)S(1)} %get-tuple-element.36.ends, f32[4,2048,128]{2,1,0:T(8,128)S(1)} %get-tuple-element.37.part, ...), custom_call_target="tpu_custom_call" | custom-call | flops 4294967296 | bytes 18874368 | tf_op jit(solution)/shard_map/faces_and_moments/pallas_call | solution.py:379
  83.1 1.2 collective-permute-start.7
  84.4 2.4 %own_moments.1.kept = f32[256,512]{1,0:T(8,128)S(1)} custom-call(s32[2]{0:T(128)S(1)} %pad_add_fusion.place, f32[4,2048,128]{2,1,0:T(8,128)S(1)} %get-tuple-element.48.moved, bf16[512,2048]{1,0:T(8,128)(2,1)S(1)} %get-tuple-element.46.high, bf16[512,2048]{1,0:T(8,128)(2,1)S(1)} %get-tuple-element.47.low), custom_call_target="tpu_custom_call" | custom-call | flops 4294967296 | bytes 8388608 | tf_op jit(solution)/shard_map/own_moments/pallas_call | solution.py:390
  86.8 0.0 collective-permute-done.7.received
  86.8 0.6 scatter.1
  87.4 1.4 %collective-permute-start.8 = (f32[64,512]{1,0:T(8,128)S(1)}, f32[64,512]{1,0:T(8,128)S(1)}, u32[]{:S(2)}, u32[]{:S(2)}) collective-permute-start(f32[64,512]{1,0:T(8,128)S(1)} %get-tuple-element.51), channel_id=1, source_target_pairs={{0,4},{1,5},{2,6},{3,7},{4,8},{5,9},{6,10},{7,11},{8,12},{9,13},{1... | collective-permute-start | bytes 393224 | tf_op jit(solution)/shard_map/ppermute | solution.py:44
  88.8 2.6 %collective-permute-start.9 = (f32[64,512]{1,0:T(8,128)S(1)}, f32[64,512]{1,0:T(8,128)S(1)}, u32[]{:S(2)}, u32[]{:S(2)}) collective-permute-start(f32[64,512]{1,0:T(8,128)S(1)} %get-tuple-element.52), channel_id=1, source_target_pairs={{0,8},{1,9},{2,10},{3,11},{4,12},{5,13},{6,14},{7,15},{8,0},{9,1},... | collective-permute-start | bytes 393224 | tf_op jit(solution)/shard_map/ppermute | solution.py:44
  91.4 1.1 collective-permute-start.10
  92.5 1.5 %collective-permute-done.8.b = f32[64,512]{1,0:T(8,128)S(1)} collective-permute-done((f32[64,512]{1,0:T(8,128)S(1)}, f32[64,512]{1,0:T(8,128)S(1)}, u32[]{:S(2)}, u32[]{:S(2)}) %collective-permute-start.8) | collective-permute-done | bytes 131104 | tf_op jit(solution)/shard_map/ppermute | solution.py:44
  93.9 3.9 %collective-permute-done.9.c = f32[64,512]{1,0:T(8,128)S(1)} collective-permute-done((f32[64,512]{1,0:T(8,128)S(1)}, f32[64,512]{1,0:T(8,128)S(1)}, u32[]{:S(2)}, u32[]{:S(2)}) %collective-permute-start.9) | collective-permute-done | bytes 131104 | tf_op jit(solution)/shard_map/ppermute | solution.py:44
  97.9 0.0 collective-permute-done.10.d
  97.9 1.7 %collective-permute-start.11 = (f32[64,512]{1,0:T(8,128)S(1)}, f32[64,512]{1,0:T(8,128)S(1)}, u32[]{:S(2)}, u32[]{:S(2)}) collective-permute-start(f32[64,512]{1,0:T(8,128)S(1)} %add_four.1.mine), channel_id=1, source_target_pairs={{0,2},{1,3},{2,0},{3,1},{4,6},{5,7},{6,4},{7,5},{8,10},{9,11},{10,... | collective-permute-start | bytes 393224 | tf_op jit(solution)/shard_map/ppermute | solution.py:40
  99.6 3.0 %collective-permute-done.11.theirs = f32[64,512]{1,0:T(8,128)S(1)} collective-permute-done((f32[64,512]{1,0:T(8,128)S(1)}, f32[64,512]{1,0:T(8,128)S(1)}, u32[]{:S(2)}, u32[]{:S(2)}) %collective-permute-start.11) | collective-permute-done | bytes 131104 | tf_op jit(solution)/shard_map/ppermute | solution.py:40
  102.6 1.7 %collide.1.a = f32[64,512]{1,0:T(8,128)S(1)} custom-call(f32[64,512]{1,0:T(8,128)S(1)} %add_four.1.mine, f32[64,512]{1,0:T(8,128)S(1)} %collective-permute-done.11.theirs, bf16[3,1024,512]{2,1,0:T(8,128)(2,1)S(1)} %get-tuple-element.54.high, bf16[3,1024,512]{2,1,0:T(8,128)(2,1)S(1)} %get-tuple-element.55.low), custom_call_target="tpu_custom_call" | custom-call | flops 1048576 | bytes 1048576 | tf_op jit(solution)/shard_map/collide/pallas_call | solution.py:406
  104.4 1.3 %collective-permute-start.12 = (f32[64,512]{1,0:T(8,128)S(1)}, f32[64,512]{1,0:T(8,128)S(1)}, u32[]{:S(2)}, u32[]{:S(2)}) collective-permute-start(f32[64,512]{1,0:T(8,128)S(1)} %collide.1.a), channel_id=1, source_target_pairs={{0,2},{1,3},{2,0},{3,1},{4,6},{5,7},{6,4},{7,5},{8,10},{9,11},{10,... | collective-permute-start | bytes 393224 | tf_op jit(solution)/shard_map/ppermute | solution.py:40
  105.7 2.6 %collective-permute-done.12.b = f32[64,512]{1,0:T(8,128)S(1)} collective-permute-done((f32[64,512]{1,0:T(8,128)S(1)}, f32[64,512]{1,0:T(8,128)S(1)}, u32[]{:S(2)}, u32[]{:S(2)}) %collective-permute-start.12) | collective-permute-done | bytes 131104 | tf_op jit(solution)/shard_map/ppermute | solution.py:40
  108.3 2.1 %collective-permute-start.15 = (f32[64,512]{1,0:T(8,128)S(1)}, f32[64,512]{1,0:T(8,128)S(1)}, u32[]{:S(2)}, u32[]{:S(2)}) collective-permute-start(f32[64,512]{1,0:T(8,128)S(1)} %add_two.1.own), channel_id=1, source_target_pairs={{0,12},{1,13},{2,14},{3,15},{4,0},{5,1},{6,2},{7,3},{8,4},{9,5},{1... | collective-permute-start | bytes 393224 | tf_op jit(solution)/shard_map/ppermute | solution.py:44
  110.4 0.0 collective-permute-start.14
  110.4 0.7 collective-permute-start.13
  111.1 3.6 %collective-permute-start.16 = (f32[64,512]{1,0:T(8,128)S(1)}, f32[64,512]{1,0:T(8,128)S(1)}, u32[]{:S(2)}, u32[]{:S(2)}) collective-permute-start(f32[64,512]{1,0:T(8,128)S(1)} %add_two.1.own), channel_id=1, source_target_pairs={{0,1},{1,0},{2,3},{3,2},{4,5},{5,4},{6,7},{7,6},{8,9},{9,8},{10,11... | collective-permute-start | bytes 393224 | tf_op jit(solution)/shard_map/ppermute | solution.py:40
  114.7 0.0 collective-permute-done.15.y_3
  114.7 2.5 %collective-permute-start.19 = (f32[64,512]{1,0:T(8,128)S(1)}, f32[64,512]{1,0:T(8,128)S(1)}, u32[]{:S(2)}, u32[]{:S(2)}) collective-permute-start(f32[64,512]{1,0:T(8,128)S(1)} %collective-permute-done.15.y_3), channel_id=1, source_target_pairs={{0,1},{1,0},{2,3},{3,2},{4,5},{5,4},{6,7},{7,6},{8,9},{9,8},{10,11... | collective-permute-start | bytes 393224 | tf_op jit(solution)/shard_map/ppermute | solution.py:40
  117.2 0.0 collective-permute-done.14.y_2
  117.2 2.6 %collective-permute-start.18 = (f32[64,512]{1,0:T(8,128)S(1)}, f32[64,512]{1,0:T(8,128)S(1)}, u32[]{:S(2)}, u32[]{:S(2)}) collective-permute-start(f32[64,512]{1,0:T(8,128)S(1)} %collective-permute-done.14.y_2), channel_id=1, source_target_pairs={{0,1},{1,0},{2,3},{3,2},{4,5},{5,4},{6,7},{7,6},{8,9},{9,8},{10,11... | collective-permute-start | bytes 393224 | tf_op jit(solution)/shard_map/ppermute | solution.py:40
  119.8 0.0 collective-permute-done.13.y_1
  119.8 1.3 %collective-permute-start.17 = (f32[64,512]{1,0:T(8,128)S(1)}, f32[64,512]{1,0:T(8,128)S(1)}, u32[]{:S(2)}, u32[]{:S(2)}) collective-permute-start(f32[64,512]{1,0:T(8,128)S(1)} %collective-permute-done.13.y_1), channel_id=1, source_target_pairs={{0,1},{1,0},{2,3},{3,2},{4,5},{5,4},{6,7},{7,6},{8,9},{9,8},{10,11... | collective-permute-start | bytes 393224 | tf_op jit(solution)/shard_map/ppermute | solution.py:40
  121.1 0.0 collective-permute-done.16.other
  121.1 0.0 collective-permute-done.19.z_3
  121.1 0.0 collective-permute-done.18.z_2
  121.1 1.0 collective-permute-done.17.z_1
  122.1 5.9 %relax.1 = f32[8192,128]{1,0:T(8,128)} custom-call(s32[2]{0:T(128)S(1)} %pad_add_fusion.place, f32[64,512]{1,0:T(8,128)S(1)} %add_two.1.own, f32[64,512]{1,0:T(8,128)S(1)} %collective-permute-done.13.y_1, f32[64,512]{1,0:T(8,128)S(1)} %collective-permute-done.14.y_2, f32[64,512]{1,0:T(8,128)S(1)} %collective-permute-done.15.y_3, ...), custom_call_target="tpu_custom_call" | custom-call | flops 8589934592 | bytes 16777216 | tf_op jit(solution)/shard_map/relax/pallas_call | solution.py:486
  (8 shorter events, 0.1 us)
Async XLA Ops:
  0.0 12.5 %copy-start.3 = (f32[128,512]{1,0:T(8,128)S(1)}, f32[128,512]{1,0:T(8,128)}, u32[]{:S(2)}) copy-start(f32[128,512]{1,0:T(8,128)} %param.12) | copy-start | bytes 786436
  3.3 70.8 %collective-permute-start.5 = (f32[3,1024,128]{2,1,0:T(8,128)}, f32[3,1024,128]{2,1,0:T(8,128)S(1)}, u32[]{:S(2)}, u32[]{:S(2)}) collective-permute-start(f32[3,1024,128]{2,1,0:T(8,128)} %get-tuple-element.38), channel_id=1, source_target_pairs={{0,16},{16,32},{32,48},{48,64},{64,80},{80,96},{96,112},{112,128},... | collective-permute-start | bytes 4718600 | tf_op jit(solution)/shard_map/ppermute | solution.py:36
  7.2 72.6 %collective-permute-start.6 = (f32[3,1024,128]{2,1,0:T(8,128)}, f32[3,1024,128]{2,1,0:T(8,128)S(1)}, u32[]{:S(2)}, u32[]{:S(2)}) collective-permute-start(f32[3,1024,128]{2,1,0:T(8,128)} %get-tuple-element.39), channel_id=1, source_target_pairs={{0,240},{16,0},{32,16},{48,32},{64,48},{80,64},{96,80},{112,96},{1... | collective-permute-start | bytes 4718600 | tf_op jit(solution)/shard_map/ppermute | solution.py:36
  13.7 18.7 %collective-permute-start.1 = (f32[384,512]{1,0:T(8,128)S(1)}, f32[384,512]{1,0:T(8,128)S(1)}, u32[]{:S(2)}, u32[]{:S(2)}) collective-permute-start(f32[384,512]{1,0:T(8,128)S(1)} %stack_factors.1.own), channel_id=1, source_target_pairs={{0,12},{1,13},{2,14},{3,15},{4,0},{5,1},{6,2},{7,3},{8,4},{9,5},{1... | collective-permute-start | bytes 2359304 | tf_op jit(solution)/shard_map/cond/branch_1_fun/ppermute | solution.py:44
  16.5 19.4 %collective-permute-start = (f32[384,512]{1,0:T(8,128)S(1)}, f32[384,512]{1,0:T(8,128)S(1)}, u32[]{:S(2)}, u32[]{:S(2)}) collective-permute-start(f32[384,512]{1,0:T(8,128)S(1)} %stack_factors.1.own), channel_id=1, source_target_pairs={{0,4},{1,5},{2,6},{3,7},{4,8},{5,9},{6,10},{7,11},{8,12},{9,13},{1... | collective-permute-start | bytes 2359304 | tf_op jit(solution)/shard_map/cond/branch_1_fun/ppermute | solution.py:44
  32.4 10.0 %collective-permute-start.3 = (f32[192,512]{1,0:T(8,128)S(1)}, f32[192,512]{1,0:T(8,128)S(1)}, u32[]{:S(2)}, u32[]{:S(2)}) collective-permute-start(f32[192,512]{1,0:T(8,128)S(1)} %slice.7), channel_id=1, source_target_pairs={{0,12},{1,13},{2,14},{3,15},{4,0},{5,1},{6,2},{7,3},{8,4},{9,5},{1... | collective-permute-start | bytes 1179656 | tf_op jit(solution)/shard_map/cond/branch_1_fun/ppermute | solution.py:44
  36.0 9.8 %collective-permute-start.2 = (f32[192,512]{1,0:T(8,128)S(1)}, f32[192,512]{1,0:T(8,128)S(1)}, u32[]{:S(2)}, u32[]{:S(2)}) collective-permute-start(f32[192,512]{1,0:T(8,128)S(1)} %slice.6), channel_id=1, source_target_pairs={{0,4},{1,5},{2,6},{3,7},{4,8},{5,9},{6,10},{7,11},{8,12},{9,13},{1... | collective-permute-start | bytes 1179656 | tf_op jit(solution)/shard_map/cond/branch_1_fun/ppermute | solution.py:44
  47.6 8.7 %collective-permute-start.4 = (f32[4,384,512]{2,1,0:T(8,128)}, f32[4,384,512]{2,1,0:T(8,128)}, u32[]{:S(2)}, u32[]{:S(2)}) collective-permute-start(f32[4,384,512]{2,1,0:T(8,128)} %join_factors.1), channel_id=1, source_target_pairs={{0,1},{1,0},{2,3},{3,2},{4,5},{5,4},{6,7},{7,6},{8,9},{9,8},{10,11... | collective-permute-start | bytes 9437192 | tf_op jit(solution)/shard_map/cond/branch_1_fun/ppermute | solution.py:40
  56.3 2.2 %copy-start = (f32[512,2048]{1,0:T(8,128)S(1)}, f32[512,2048]{1,0:T(8,128)}, u32[]{:S(2)}) copy-start(f32[512,2048]{1,0:T(8,128)} %basis.1) | copy-start | bytes 12582916
  61.3 4.1 %copy-start.4 = (s32[4,128]{1,0:T(4,128)S(1)}, s32[4,128]{1,0:T(4,128)}, u32[]{:S(2)}) copy-start(s32[4,128]{1,0:T(4,128)} %param.16) | copy-start | bytes 6148
  61.3 4.1 %copy-start.5 = (s32[4,128]{1,0:T(4,128)S(1)}, s32[4,128]{1,0:T(4,128)}, u32[]{:S(2)}) copy-start(s32[4,128]{1,0:T(4,128)} %param.15) | copy-start | bytes 6148
  61.4 4.3 %copy-start.1 = (f32[2048,4,128]{2,1,0:T(4,128)S(1)}, f32[2048,4,128]{2,1,0:T(4,128)}, u32[]{:S(2)}) copy-start(f32[2048,4,128]{2,1,0:T(4,128)} %param.10) | copy-start | bytes 12582916
  65.3 0.7 copy-start.2
  83.1 3.6 %collective-permute-start.7 = (f32[256,512]{1,0:T(8,128)S(1)}, f32[256,512]{1,0:T(8,128)S(1)}, u32[]{:S(2)}, u32[]{:S(2)}) collective-permute-start(f32[256,512]{1,0:T(8,128)S(1)} %get-tuple-element.49), channel_id=1, source_target_pairs={{0,1},{1,0},{2,3},{3,2},{4,5},{5,4},{6,7},{7,6},{8,9},{9,8},{10,11... | collective-permute-start | bytes 1572872 | tf_op jit(solution)/shard_map/ppermute | solution.py:40
  87.4 6.5 %collective-permute-start.8 = (f32[64,512]{1,0:T(8,128)S(1)}, f32[64,512]{1,0:T(8,128)S(1)}, u32[]{:S(2)}, u32[]{:S(2)}) collective-permute-start(f32[64,512]{1,0:T(8,128)S(1)} %get-tuple-element.51), channel_id=1, source_target_pairs={{0,4},{1,5},{2,6},{3,7},{4,8},{5,9},{6,10},{7,11},{8,12},{9,13},{1... | collective-permute-start | bytes 393224 | tf_op jit(solution)/shard_map/ppermute | solution.py:44
  88.8 9.1 %collective-permute-start.9 = (f32[64,512]{1,0:T(8,128)S(1)}, f32[64,512]{1,0:T(8,128)S(1)}, u32[]{:S(2)}, u32[]{:S(2)}) collective-permute-start(f32[64,512]{1,0:T(8,128)S(1)} %get-tuple-element.52), channel_id=1, source_target_pairs={{0,8},{1,9},{2,10},{3,11},{4,12},{5,13},{6,14},{7,15},{8,0},{9,1},... | collective-permute-start | bytes 393224 | tf_op jit(solution)/shard_map/ppermute | solution.py:44
  91.4 6.5 %collective-permute-start.10 = (f32[64,512]{1,0:T(8,128)S(1)}, f32[64,512]{1,0:T(8,128)S(1)}, u32[]{:S(2)}, u32[]{:S(2)}) collective-permute-start(f32[64,512]{1,0:T(8,128)S(1)} %get-tuple-element.53), channel_id=1, source_target_pairs={{0,12},{1,13},{2,14},{3,15},{4,0},{5,1},{6,2},{7,3},{8,4},{9,5},{1... | collective-permute-start | bytes 393224 | tf_op jit(solution)/shard_map/ppermute | solution.py:44
  97.9 4.7 %collective-permute-start.11 = (f32[64,512]{1,0:T(8,128)S(1)}, f32[64,512]{1,0:T(8,128)S(1)}, u32[]{:S(2)}, u32[]{:S(2)}) collective-permute-start(f32[64,512]{1,0:T(8,128)S(1)} %add_four.1.mine), channel_id=1, source_target_pairs={{0,2},{1,3},{2,0},{3,1},{4,6},{5,7},{6,4},{7,5},{8,10},{9,11},{10,... | collective-permute-start | bytes 393224 | tf_op jit(solution)/shard_map/ppermute | solution.py:40
  104.4 3.9 %collective-permute-start.12 = (f32[64,512]{1,0:T(8,128)S(1)}, f32[64,512]{1,0:T(8,128)S(1)}, u32[]{:S(2)}, u32[]{:S(2)}) collective-permute-start(f32[64,512]{1,0:T(8,128)S(1)} %collide.1.a), channel_id=1, source_target_pairs={{0,2},{1,3},{2,0},{3,1},{4,6},{5,7},{6,4},{7,5},{8,10},{9,11},{10,... | collective-permute-start | bytes 393224 | tf_op jit(solution)/shard_map/ppermute | solution.py:40
  108.3 6.4 %collective-permute-start.15 = (f32[64,512]{1,0:T(8,128)S(1)}, f32[64,512]{1,0:T(8,128)S(1)}, u32[]{:S(2)}, u32[]{:S(2)}) collective-permute-start(f32[64,512]{1,0:T(8,128)S(1)} %add_two.1.own), channel_id=1, source_target_pairs={{0,12},{1,13},{2,14},{3,15},{4,0},{5,1},{6,2},{7,3},{8,4},{9,5},{1... | collective-permute-start | bytes 393224 | tf_op jit(solution)/shard_map/ppermute | solution.py:44
  110.4 6.7 %collective-permute-start.14 = (f32[64,512]{1,0:T(8,128)S(1)}, f32[64,512]{1,0:T(8,128)S(1)}, u32[]{:S(2)}, u32[]{:S(2)}) collective-permute-start(f32[64,512]{1,0:T(8,128)S(1)} %add_two.1.own), channel_id=1, source_target_pairs={{0,8},{1,9},{2,10},{3,11},{4,12},{5,13},{6,14},{7,15},{8,0},{9,1},... | collective-permute-start | bytes 393224 | tf_op jit(solution)/shard_map/ppermute | solution.py:44
  110.4 9.4 %collective-permute-start.13 = (f32[64,512]{1,0:T(8,128)S(1)}, f32[64,512]{1,0:T(8,128)S(1)}, u32[]{:S(2)}, u32[]{:S(2)}) collective-permute-start(f32[64,512]{1,0:T(8,128)S(1)} %add_two.1.own), channel_id=1, source_target_pairs={{0,4},{1,5},{2,6},{3,7},{4,8},{5,9},{6,10},{7,11},{8,12},{9,13},{1... | collective-permute-start | bytes 393224 | tf_op jit(solution)/shard_map/ppermute | solution.py:44
  111.1 10.0 %collective-permute-start.16 = (f32[64,512]{1,0:T(8,128)S(1)}, f32[64,512]{1,0:T(8,128)S(1)}, u32[]{:S(2)}, u32[]{:S(2)}) collective-permute-start(f32[64,512]{1,0:T(8,128)S(1)} %add_two.1.own), channel_id=1, source_target_pairs={{0,1},{1,0},{2,3},{3,2},{4,5},{5,4},{6,7},{7,6},{8,9},{9,8},{10,11... | collective-permute-start | bytes 393224 | tf_op jit(solution)/shard_map/ppermute | solution.py:40
  114.7 6.5 %collective-permute-start.19 = (f32[64,512]{1,0:T(8,128)S(1)}, f32[64,512]{1,0:T(8,128)S(1)}, u32[]{:S(2)}, u32[]{:S(2)}) collective-permute-start(f32[64,512]{1,0:T(8,128)S(1)} %collective-permute-done.15.y_3), channel_id=1, source_target_pairs={{0,1},{1,0},{2,3},{3,2},{4,5},{5,4},{6,7},{7,6},{8,9},{9,8},{10,11... | collective-permute-start | bytes 393224 | tf_op jit(solution)/shard_map/ppermute | solution.py:40
  117.2 4.0 %collective-permute-start.18 = (f32[64,512]{1,0:T(8,128)S(1)}, f32[64,512]{1,0:T(8,128)S(1)}, u32[]{:S(2)}, u32[]{:S(2)}) collective-permute-start(f32[64,512]{1,0:T(8,128)S(1)} %collective-permute-done.14.y_2), channel_id=1, source_target_pairs={{0,1},{1,0},{2,3},{3,2},{4,5},{5,4},{6,7},{7,6},{8,9},{9,8},{10,11... | collective-permute-start | bytes 393224 | tf_op jit(solution)/shard_map/ppermute | solution.py:40
  119.8 2.3 %collective-permute-start.17 = (f32[64,512]{1,0:T(8,128)S(1)}, f32[64,512]{1,0:T(8,128)S(1)}, u32[]{:S(2)}, u32[]{:S(2)}) collective-permute-start(f32[64,512]{1,0:T(8,128)S(1)} %collective-permute-done.13.y_1), channel_id=1, source_target_pairs={{0,1},{1,0},{2,3},{3,2},{4,5},{5,4},{6,7},{7,6},{8,9},{9,8},{10,11... | collective-permute-start | bytes 393224 | tf_op jit(solution)/shard_map/ppermute | solution.py:40

commit v6 on v5

--- a/solution.py
+++ b/solution.py
@@ -421,42 +421,47 @@
         out[...] = kept[pl.ds(at, size), :] + received[pl.ds(at, size), :]
 
 
-def add_four_kernel(a, b, c, d, out):
-    out[...] = (a[...] + b[...]) + (c[...] + d[...])
-
-
-def add_two_kernel(a, b, out):
-    out[...] = a[...] + b[...]
-
-
-def collision_kernel(mine, theirs, high, low, out):
-    size = out.shape[0]
-
+def add_four_kernel(a, b, c, d, upper, lower):
+    total = (a[...] + b[...]) + (c[...] + d[...])
+    upper[...], lower[...] = total[:32], total[32:]
+
+
+def add_two_kernel(a, b, c, d, out):
+    out[:32] = a[...] + c[...]
+    out[32:] = b[...] + d[...]
+
+
+def collision_kernel(mine_a, mine_b, theirs_a, theirs_b, high, low, upper, lower):
     def times(values, which, product):
         top, rest = halves(values)
         both = product(jnp.concatenate([top, rest], axis=0), high[which])
-        return both[:size] + (both[size:] + product(top, low[which]))
-
-    moments = mine[...] + theirs[...]
+        return both[:64] + (both[64:] + product(top, low[which]))
+
+    parts = [mine_a[...] + theirs_a[...], mine_b[...] + theirs_b[...]]
+    moments = jnp.concatenate(parts, axis=0)
     terms = times(moments, 0, dot_nt) * times(moments, 1, dot_nt)
-    out[...] = times(terms, 2, dot)
+    result = times(terms, 2, dot)
+    upper[...], lower[...] = result[:32], result[32:]
 
 
 def collision_part(place, kept, sent, factor_high, factor_low):
-    shape = (kept.shape[0] // 4, MOMENTS)
+    shape, half = (64, MOMENTS), (32, MOMENTS)
     operands = (place, kept, exchanged(sent, 1))
-    own, *others = small_call(scatter_kernel, "scatter", 4, shape, operands, 1)
-    arrived = [along_y(piece, away + 1) for away, piece in enumerate(others)]
-    summed = small_call(add_four_kernel, "add_four", 1, shape, (own, *arrived))
-    operands = (summed, exchanged(summed, 2), factor_high, factor_low)
-    share = small_call(collision_kernel, "collide", 1, shape, operands, mib=4)
-    whole = small_call(add_two_kernel, "add_two", 1, shape, (share, exchanged(share, 2)))
-    pieces = [whole] + [along_y(whole, away) for away in (1, 2, 3)]
+    own, to_one, to_two, to_three = small_call(scatter_kernel, "scatter", 4, shape, operands, 1)
+    arrived = (along_y(to_two, 2), along_y(to_three, 3), along_y(to_one, 1))
+    mine = small_call(add_four_kernel, "add_four", 2, half, (own, *arrived))
+    theirs = [exchanged(piece, 2) for piece in mine]
+    operands = (*mine, *theirs, factor_high, factor_low)
+    mine = small_call(collision_kernel, "collide", 2, half, operands, mib=4)
+    theirs = [exchanged(piece, 2) for piece in mine]
+    whole = small_call(add_two_kernel, "add_two", 1, shape, (*mine, *theirs))
+    y_2, y_1, y_3 = (along_y(whole, away) for away in (2, 1, 3))
+    pieces = [whole, y_1, y_3, y_2]
     return pieces + [exchanged(piece, 1) for piece in pieces]
 
 
 def relax_kernel(
-    place, own, y_1, y_2, y_3, other, z_1, z_2, z_3, kind, moved, high, low,
+    place, own, y_1, y_3, y_2, other, z_1, z_3, z_2, kind, moved, high, low,
     out, gathered, turned_high, turned_low,
 ):
     step = pl.program_id(0)

time: 128 us -> 129 us (level)
    ppermute x8 -> x10, starting transfers between devices: 17.4 us -> 16.5 us  [exchanged(): return lax.ppermute(x, 'vel', [(i, i ^ bit) for i in range(16)])]
    ppermute x8 -> x10, waiting for transfers between devices: 12.1 us -> 12.6 us  [exchanged(): return lax.ppermute(x, 'vel', [(i, i ^ bit) for i in range(16)])]
  transfers between devices with their start and end apart: 20 -> 22, of which waited for: 10 -> 12; matrix products, arithmetic and copies ran while one was open for 0% -> 0% of each run, Pallas kernels for 16% -> 16%
where the time goes in v6:
time: 129 us
  waiting for transfers between devices  49.4 us (38%)
  starting transfers between devices  41.1 us (32%)
  Pallas kernels  35.1 us (27%)
  local copies, waits for them, and re-layouts  2.61 us (2%)
    ppermute x10, waiting for transfers between devices, along_y(): return lax.ppermute(x, 'vel', [(i, (i + 4 * by) % 16) for i in range(16)])  31 us
    ppermute x10, starting transfers between devices, exchanged(): return lax.ppermute(x, 'vel', [(i, i ^ bit) for i in range(16)])  16.5 us
    ppermute x10, starting transfers between devices, along_y(): return lax.ppermute(x, 'vel', [(i, (i + 4 * by) % 16) for i in range(16)])  15.4 us
    ppermute x10, waiting for transfers between devices, exchanged(): return lax.ppermute(x, 'vel', [(i, i ^ bit) for i in range(16)])  12.6 us
    ppermute x2, starting transfers between devices, shifted(): return lax.ppermute(x, 'cells', [(i, (i + by) % size) for i in range(size)])  9.21 us
    pallas_call x1, Pallas kernels, local_part(): pl.pallas_call(local_kernel, name='local_transport', grid=(steps,), in_sp...  8 us
    pallas_call x1, Pallas kernels, relax(): pl.pallas_call(relax_kernel, name='relax', grid=(PER_DEVICE // CHUNK_R,),...  5.89 us
    ppermute x2, waiting for transfers between devices, shifted(): return lax.ppermute(x, 'cells', [(i, (i + by) % size) for i in range(size)])  5.77 us
  transfers between devices with their start and end apart: 22, of which 12 were waited for; matrix products, arithmetic and copies ran while one was open for 0% of the time, Pallas kernels for 16%

profile of v6, /device:TPU:1, one launch (start us, length us, event | category | flops | bytes accessed | tf_op | source)
XLA Modules:
  0.0 128.7 jit_solution(10296417492956205826)
XLA Ops:
  0.0 3.3 %pack.1 = (f32[3,1024,128]{2,1,0:T(8,128)}, f32[3,1024,128]{2,1,0:T(8,128)}) custom-call(f32[8192,128]{1,0:T(8,128)} %bitcast.9), custom_call_target="tpu_custom_call" | custom-call | flops 1048576 | bytes 8388608 | tf_op jit(solution)/shard_map/pack/pallas_call | solution.py:118
  3.3 3.9 %collective-permute-start.5 = (f32[3,1024,128]{2,1,0:T(8,128)}, f32[3,1024,128]{2,1,0:T(8,128)S(1)}, u32[]{:S(2)}, u32[]{:S(2)}) collective-permute-start(f32[3,1024,128]{2,1,0:T(8,128)} %get-tuple-element.42), channel_id=1, source_target_pairs={{0,16},{16,32},{32,48},{48,64},{64,80},{80,96},{96,112},{112,128},... | collective-permute-start | bytes 4718600 | tf_op jit(solution)/shard_map/ppermute | solution.py:36
  7.2 5.3 %collective-permute-start.6 = (f32[3,1024,128]{2,1,0:T(8,128)}, f32[3,1024,128]{2,1,0:T(8,128)S(1)}, u32[]{:S(2)}, u32[]{:S(2)}) collective-permute-start(f32[3,1024,128]{2,1,0:T(8,128)} %get-tuple-element.43), channel_id=1, source_target_pairs={{0,240},{16,0},{32,16},{48,32},{64,48},{80,64},{96,80},{112,96},{1... | collective-permute-start | bytes 4718600 | tf_op jit(solution)/shard_map/ppermute | solution.py:36
  12.5 43.8 %conditional.1 = (f32[4,384,512]{2,1,0:T(8,128)}, f32[4,384,512]{2,1,0:T(8,128)}) conditional(s32[]{:T(128)} %convert_element_type.15, () %tuple.14, (f32[128,512]{1,0:T(8,128)S(1)}, f32[128,512]{1,0:T(8,128)}, f32[512,128]{1,0:T(8,128)}) %tuple.21), branch_computations={%region_0.1_spmd, %region_1.2_spmd} | conditional | flops 2097152 | bytes 31981784 | solution.py:140
  12.5 1.2 stack_factors.1.own
  13.7 2.8 %collective-permute-start.1 = (f32[384,512]{1,0:T(8,128)S(1)}, f32[384,512]{1,0:T(8,128)S(1)}, u32[]{:S(2)}, u32[]{:S(2)}) collective-permute-start(f32[384,512]{1,0:T(8,128)S(1)} %stack_factors.1.own), channel_id=1, source_target_pairs={{0,12},{1,13},{2,14},{3,15},{4,0},{5,1},{6,2},{7,3},{8,4},{9,5},{1... | collective-permute-start | bytes 2359304 | tf_op jit(solution)/shard_map/cond/branch_1_fun/ppermute | solution.py:44
  16.5 0.0 collective-permute-start
  16.5 15.9 %collective-permute-done.1.after = f32[384,512]{1,0:T(8,128)S(1)} collective-permute-done((f32[384,512]{1,0:T(8,128)S(1)}, f32[384,512]{1,0:T(8,128)S(1)}, u32[]{:S(2)}, u32[]{:S(2)}) %collective-permute-start.1) | collective-permute-done | bytes 786464 | tf_op jit(solution)/shard_map/cond/branch_1_fun/ppermute | solution.py:44
  32.4 3.5 %collective-permute-start.3 = (f32[192,512]{1,0:T(8,128)S(1)}, f32[192,512]{1,0:T(8,128)S(1)}, u32[]{:S(2)}, u32[]{:S(2)}) collective-permute-start(f32[192,512]{1,0:T(8,128)S(1)} %slice.7), channel_id=1, source_target_pairs={{0,12},{1,13},{2,14},{3,15},{4,0},{5,1},{6,2},{7,3},{8,4},{9,5},{1... | collective-permute-start | bytes 1179656 | tf_op jit(solution)/shard_map/cond/branch_1_fun/ppermute | solution.py:44
  35.9 0.0 collective-permute-done.before
  36.0 0.1 collective-permute-start.2
  36.1 6.4 %collective-permute-done.3.across_rest = f32[192,512]{1,0:T(8,128)S(1)} collective-permute-done((f32[192,512]{1,0:T(8,128)S(1)}, f32[192,512]{1,0:T(8,128)S(1)}, u32[]{:S(2)}, u32[]{:S(2)}) %collective-permute-start.3) | collective-permute-done | bytes 393248 | tf_op jit(solution)/shard_map/cond/branch_1_fun/ppermute | solution.py:44
  42.5 3.2 %collective-permute-done.2.across_top = f32[192,512]{1,0:T(8,128)S(1)} collective-permute-done((f32[192,512]{1,0:T(8,128)S(1)}, f32[192,512]{1,0:T(8,128)S(1)}, u32[]{:S(2)}, u32[]{:S(2)}) %collective-permute-start.2) | collective-permute-done | bytes 393248 | tf_op jit(solution)/shard_map/cond/branch_1_fun/ppermute | solution.py:44
  45.7 1.9 %join_factors.1 = f32[4,384,512]{2,1,0:T(8,128)} custom-call(f32[384,512]{1,0:T(8,128)S(1)} %stack_factors.1.own, f32[384,512]{1,0:T(8,128)S(1)} %collective-permute-done.before, f32[384,512]{1,0:T(8,128)S(1)} %collective-permute-done.1.after, f32[192,512]{1,0:T(8,128)S(1)} %collective-permute-done.2.across_top, ...), custom_call_target="tpu_custom_call" | custom-call | flops 1048576 | bytes 6291456 | tf_op jit(solution)/shard_map/cond/branch_1_fun/join_factors/pallas_call | solution.py:286
  47.6 3.1 %collective-permute-start.4 = (f32[4,384,512]{2,1,0:T(8,128)}, f32[4,384,512]{2,1,0:T(8,128)}, u32[]{:S(2)}, u32[]{:S(2)}) collective-permute-start(f32[4,384,512]{2,1,0:T(8,128)} %join_factors.1), channel_id=1, source_target_pairs={{0,1},{1,0},{2,3},{3,2},{4,5},{5,4},{6,7},{7,6},{8,9},{9,8},{10,11... | collective-permute-start | bytes 9437192 | tf_op jit(solution)/shard_map/cond/branch_1_fun/ppermute | solution.py:40
  50.7 5.6 %collective-permute-done.4 = f32[4,384,512]{2,1,0:T(8,128)} collective-permute-done((f32[4,384,512]{2,1,0:T(8,128)}, f32[4,384,512]{2,1,0:T(8,128)}, u32[]{:S(2)}, u32[]{:S(2)}) %collective-permute-start.4) | collective-permute-done | bytes 3145760 | tf_op jit(solution)/shard_map/cond/branch_1_fun/ppermute | solution.py:40
  56.3 2.2 %copy-done = f32[512,2048]{1,0:T(8,128)S(1)} copy-done((f32[512,2048]{1,0:T(8,128)S(1)}, f32[512,2048]{1,0:T(8,128)}, u32[]{:S(2)}) %copy-start) | copy-done | bytes 4194328
  58.5 2.9 %split_basis.1 = (bf16[512,2048]{1,0:T(8,128)(2,1)S(1)}, bf16[512,2048]{1,0:T(8,128)(2,1)S(1)}, bf16[2048,512]{1,0:T(8,128)(2,1)S(1)}, bf16[2048,512]{1,0:T(8,128)(2,1)S(1)}) custom-call(f32[512,2048]{1,0:T(8,128)S(1)} %copy-done), custom_call_target="tpu_custom_call" | custom-call | flops 16777216 | bytes 12582912 | tf_op jit(solution)/shard_map/split_basis/pallas_call | solution.py:237
  61.3 0.0 copy-start.4
  61.3 0.0 copy-start.5
  61.4 0.0 copy-start.1
  61.4 4.0 %split_factors.1 = (bf16[3,1024,512]{2,1,0:T(8,128)(2,1)S(1)}, bf16[3,1024,512]{2,1,0:T(8,128)(2,1)S(1)}) custom-call(f32[4,384,512]{2,1,0:T(8,128)} %get-tuple-element.44.mine, f32[4,384,512]{2,1,0:T(8,128)} %get-tuple-element.45.theirs), custom_call_target="tpu_custom_call" | custom-call | flops 16777216 | bytes 12582912 | tf_op jit(solution)/shard_map/split_factors/pallas_call | solution.py:300
  65.3 0.0 copy-start.2
  65.3 0.1 pad_add_fusion.place
  65.4 0.1 fusion
  65.5 0.1 maximum_bitcast_fusion
  65.6 0.1 pad_maximum_fusion.tables
  65.7 0.3 copy-done.2
  66.0 8.0 %local_transport.1 = (f32[4,2048,128]{2,1,0:T(8,128)S(1)}, f32[4,2048,128]{2,1,0:T(8,128)S(1)}) custom-call(f32[1]{0:T(128)} %bitcast.2.speed, f32[8192,128]{1,0:T(8,128)S(1)} %bitcast.10, s32[4,128]{1,0:T(4,128)S(1)} %copy-done.2, bf16[2,4,256,256]{3,2,1,0:T(8,128)(2,1)S(1)} %pad_maximum_fusion.tables), custom_call_target="tpu_custom_call" | custom-call | flops 4294967296 | bytes 10485760 | tf_op jit(solution)/shard_map/local_transport/pallas_call | solution.py:192
  74.0 0.0 collective-permute-done.5.from_left
  74.1 5.8 %collective-permute-done.6.from_right = f32[3,1024,128]{2,1,0:T(8,128)S(1)} collective-permute-done((f32[3,1024,128]{2,1,0:T(8,128)}, f32[3,1024,128]{2,1,0:T(8,128)S(1)}, u32[]{:S(2)}, u32[]{:S(2)}) %collective-permute-start.6) | collective-permute-done | bytes 1572896 | tf_op jit(solution)/shard_map/ppermute | solution.py:36
  79.8 3.3 %faces_and_moments.1 = (f32[4,2048,128]{2,1,0:T(8,128)S(1)}, f32[256,512]{1,0:T(8,128)S(1)}) custom-call(f32[1]{0:T(128)} %bitcast.2.speed, s32[2]{0:T(128)S(1)} %pad_add_fusion.place, f32[4,2048,128]{2,1,0:T(8,128)S(1)} %get-tuple-element.40.ends, f32[4,2048,128]{2,1,0:T(8,128)S(1)} %get-tuple-element.41.part, ...), custom_call_target="tpu_custom_call" | custom-call | flops 4294967296 | bytes 18874368 | tf_op jit(solution)/shard_map/faces_and_moments/pallas_call | solution.py:379
  83.1 1.2 collective-permute-start.7
  84.4 2.4 %own_moments.1.kept = f32[256,512]{1,0:T(8,128)S(1)} custom-call(s32[2]{0:T(128)S(1)} %pad_add_fusion.place, f32[4,2048,128]{2,1,0:T(8,128)S(1)} %get-tuple-element.52.moved, bf16[512,2048]{1,0:T(8,128)(2,1)S(1)} %get-tuple-element.50.high, bf16[512,2048]{1,0:T(8,128)(2,1)S(1)} %get-tuple-element.51.low), custom_call_target="tpu_custom_call" | custom-call | flops 4294967296 | bytes 8388608 | tf_op jit(solution)/shard_map/own_moments/pallas_call | solution.py:390
  86.8 0.0 collective-permute-done.7.received
  86.8 0.6 scatter.1
  87.4 3.0 %collective-permute-start.8 = (f32[64,512]{1,0:T(8,128)S(1)}, f32[64,512]{1,0:T(8,128)S(1)}, u32[]{:S(2)}, u32[]{:S(2)}) collective-permute-start(f32[64,512]{1,0:T(8,128)S(1)} %get-tuple-element.55), channel_id=1, source_target_pairs={{0,8},{1,9},{2,10},{3,11},{4,12},{5,13},{6,14},{7,15},{8,0},{9,1},... | collective-permute-start | bytes 393224 | tf_op jit(solution)/shard_map/ppermute | solution.py:44
  90.4 0.8 collective-permute-start.9
  91.2 0.7 collective-permute-start.10
  91.9 2.2 %collective-permute-done.8.b = f32[64,512]{1,0:T(8,128)S(1)} collective-permute-done((f32[64,512]{1,0:T(8,128)S(1)}, f32[64,512]{1,0:T(8,128)S(1)}, u32[]{:S(2)}, u32[]{:S(2)}) %collective-permute-start.8) | collective-permute-done | bytes 131104 | tf_op jit(solution)/shard_map/ppermute | solution.py:44
  94.1 3.2 %collective-permute-done.9.c = f32[64,512]{1,0:T(8,128)S(1)} collective-permute-done((f32[64,512]{1,0:T(8,128)S(1)}, f32[64,512]{1,0:T(8,128)S(1)}, u32[]{:S(2)}, u32[]{:S(2)}) %collective-permute-start.9) | collective-permute-done | bytes 131104 | tf_op jit(solution)/shard_map/ppermute | solution.py:44
  97.3 0.0 collective-permute-done.10.d
  97.3 1.7 %collective-permute-start.11 = (f32[32,512]{1,0:T(8,128)S(1)}, f32[32,512]{1,0:T(8,128)S(1)}, u32[]{:S(2)}, u32[]{:S(2)}) collective-permute-start(f32[32,512]{1,0:T(8,128)S(1)} %get-tuple-element.58.mine_a), channel_id=1, source_target_pairs={{0,2},{1,3},{2,0},{3,1},{4,6},{5,7},{6,4},{7,5},{8,10},{9,11},{10,... | collective-permute-start | bytes 196616 | tf_op jit(solution)/shard_map/ppermute | solution.py:40
  99.1 0.1 collective-permute-start.12
  99.2 1.6 %collective-permute-done.11.theirs_a = f32[32,512]{1,0:T(8,128)S(1)} collective-permute-done((f32[32,512]{1,0:T(8,128)S(1)}, f32[32,512]{1,0:T(8,128)S(1)}, u32[]{:S(2)}, u32[]{:S(2)}) %collective-permute-start.11) | collective-permute-done | bytes 65568 | tf_op jit(solution)/shard_map/ppermute | solution.py:40
  100.7 2.1 %collective-permute-done.12.theirs_b = f32[32,512]{1,0:T(8,128)S(1)} collective-permute-done((f32[32,512]{1,0:T(8,128)S(1)}, f32[32,512]{1,0:T(8,128)S(1)}, u32[]{:S(2)}, u32[]{:S(2)}) %collective-permute-start.12) | collective-permute-done | bytes 65568 | tf_op jit(solution)/shard_map/ppermute | solution.py:40
  102.8 1.7 %collide.1 = (f32[32,512]{1,0:T(8,128)S(1)}, f32[32,512]{1,0:T(8,128)S(1)}) custom-call(f32[32,512]{1,0:T(8,128)S(1)} %get-tuple-element.58.mine_a, f32[32,512]{1,0:T(8,128)S(1)} %get-tuple-element.59.mine_b, f32[32,512]{1,0:T(8,128)S(1)} %collective-permute-done.11.theirs_a, f32[32,512]{1,0:T(8,128)S(1)} %collective-permute-done.12.theirs_b, ...), custom_call_target="tpu_custom_call" | custom-call | flops 1048576 | bytes 1048576 | tf_op jit(solution)/shard_map/collide/pallas_call | solution.py:406
  104.6 0.1 collective-permute-start.13
  104.7 1.4 %collective-permute-start.14 = (f32[32,512]{1,0:T(8,128)S(1)}, f32[32,512]{1,0:T(8,128)S(1)}, u32[]{:S(2)}, u32[]{:S(2)}) collective-permute-start(f32[32,512]{1,0:T(8,128)S(1)} %get-tuple-element.63.b), channel_id=1, source_target_pairs={{0,2},{1,3},{2,0},{3,1},{4,6},{5,7},{6,4},{7,5},{8,10},{9,11},{10,... | collective-permute-start | bytes 196616 | tf_op jit(solution)/shard_map/ppermute | solution.py:40
  106.1 1.6 %collective-permute-done.13.c = f32[32,512]{1,0:T(8,128)S(1)} collective-permute-done((f32[32,512]{1,0:T(8,128)S(1)}, f32[32,512]{1,0:T(8,128)S(1)}, u32[]{:S(2)}, u32[]{:S(2)}) %collective-permute-start.13) | collective-permute-done | bytes 65568 | tf_op jit(solution)/shard_map/ppermute | solution.py:40
  107.8 0.7 collective-permute-done.14.d
  108.5 3.0 %collective-permute-start.17 = (f32[64,512]{1,0:T(8,128)S(1)}, f32[64,512]{1,0:T(8,128)S(1)}, u32[]{:S(2)}, u32[]{:S(2)}) collective-permute-start(f32[64,512]{1,0:T(8,128)S(1)} %add_two.1.own), channel_id=1, source_target_pairs={{0,8},{1,9},{2,10},{3,11},{4,12},{5,13},{6,14},{7,15},{8,0},{9,1},... | collective-permute-start | bytes 393224 | tf_op jit(solution)/shard_map/ppermute | solution.py:44
  111.5 0.7 collective-permute-start.16
  112.2 0.8 collective-permute-start.15
  113.0 3.6 %collective-permute-start.18 = (f32[64,512]{1,0:T(8,128)S(1)}, f32[64,512]{1,0:T(8,128)S(1)}, u32[]{:S(2)}, u32[]{:S(2)}) collective-permute-start(f32[64,512]{1,0:T(8,128)S(1)} %add_two.1.own), channel_id=1, source_target_pairs={{0,1},{1,0},{2,3},{3,2},{4,5},{5,4},{6,7},{7,6},{8,9},{9,8},{10,11... | collective-permute-start | bytes 393224 | tf_op jit(solution)/shard_map/ppermute | solution.py:40
  116.6 0.0 collective-permute-done.17.y_2
  116.6 1.7 %collective-permute-start.21 = (f32[64,512]{1,0:T(8,128)S(1)}, f32[64,512]{1,0:T(8,128)S(1)}, u32[]{:S(2)}, u32[]{:S(2)}) collective-permute-start(f32[64,512]{1,0:T(8,128)S(1)} %collective-permute-done.17.y_2), channel_id=1, source_target_pairs={{0,1},{1,0},{2,3},{3,2},{4,5},{5,4},{6,7},{7,6},{8,9},{9,8},{10,11... | collective-permute-start | bytes 393224 | tf_op jit(solution)/shard_map/ppermute | solution.py:40
  118.3 0.0 collective-permute-done.16.y_3
  118.3 1.3 %collective-permute-start.20 = (f32[64,512]{1,0:T(8,128)S(1)}, f32[64,512]{1,0:T(8,128)S(1)}, u32[]{:S(2)}, u32[]{:S(2)}) collective-permute-start(f32[64,512]{1,0:T(8,128)S(1)} %collective-permute-done.16.y_3), channel_id=1, source_target_pairs={{0,1},{1,0},{2,3},{3,2},{4,5},{5,4},{6,7},{7,6},{8,9},{9,8},{10,11... | collective-permute-start | bytes 393224 | tf_op jit(solution)/shard_map/ppermute | solution.py:40
  119.6 0.0 collective-permute-done.15.y_1
  119.6 2.2 %collective-permute-start.19 = (f32[64,512]{1,0:T(8,128)S(1)}, f32[64,512]{1,0:T(8,128)S(1)}, u32[]{:S(2)}, u32[]{:S(2)}) collective-permute-start(f32[64,512]{1,0:T(8,128)S(1)} %collective-permute-done.15.y_1), channel_id=1, source_target_pairs={{0,1},{1,0},{2,3},{3,2},{4,5},{5,4},{6,7},{7,6},{8,9},{9,8},{10,11... | collective-permute-start | bytes 393224 | tf_op jit(solution)/shard_map/ppermute | solution.py:40
  121.9 0.0 collective-permute-done.18.other
  121.9 1.0 collective-permute-done.19.z_1
  122.8 5.9 %relax.1 = f32[8192,128]{1,0:T(8,128)} custom-call(s32[2]{0:T(128)S(1)} %pad_add_fusion.place, f32[64,512]{1,0:T(8,128)S(1)} %add_two.1.own, f32[64,512]{1,0:T(8,128)S(1)} %collective-permute-done.15.y_1, f32[64,512]{1,0:T(8,128)S(1)} %collective-permute-done.16.y_3, f32[64,512]{1,0:T(8,128)S(1)} %collective-permute-done.17.y_2, ...), custom_call_target="tpu_custom_call" | custom-call | flops 8589934592 | bytes 16777216 | tf_op jit(solution)/shard_map/relax/pallas_call | solution.py:491
  (12 shorter events, 0.1 us)
Async XLA Ops:
  0.0 12.5 %copy-start.3 = (f32[128,512]{1,0:T(8,128)S(1)}, f32[128,512]{1,0:T(8,128)}, u32[]{:S(2)}) copy-start(f32[128,512]{1,0:T(8,128)} %param.12) | copy-start | bytes 786436
  3.3 70.8 %collective-permute-start.5 = (f32[3,1024,128]{2,1,0:T(8,128)}, f32[3,1024,128]{2,1,0:T(8,128)S(1)}, u32[]{:S(2)}, u32[]{:S(2)}) collective-permute-start(f32[3,1024,128]{2,1,0:T(8,128)} %get-tuple-element.42), channel_id=1, source_target_pairs={{0,16},{16,32},{32,48},{48,64},{64,80},{80,96},{96,112},{112,128},... | collective-permute-start | bytes 4718600 | tf_op jit(solution)/shard_map/ppermute | solution.py:36
  7.2 72.6 %collective-permute-start.6 = (f32[3,1024,128]{2,1,0:T(8,128)}, f32[3,1024,128]{2,1,0:T(8,128)S(1)}, u32[]{:S(2)}, u32[]{:S(2)}) collective-permute-start(f32[3,1024,128]{2,1,0:T(8,128)} %get-tuple-element.43), channel_id=1, source_target_pairs={{0,240},{16,0},{32,16},{48,32},{64,48},{80,64},{96,80},{112,96},{1... | collective-permute-start | bytes 4718600 | tf_op jit(solution)/shard_map/ppermute | solution.py:36
  13.7 18.7 %collective-permute-start.1 = (f32[384,512]{1,0:T(8,128)S(1)}, f32[384,512]{1,0:T(8,128)S(1)}, u32[]{:S(2)}, u32[]{:S(2)}) collective-permute-start(f32[384,512]{1,0:T(8,128)S(1)} %stack_factors.1.own), channel_id=1, source_target_pairs={{0,12},{1,13},{2,14},{3,15},{4,0},{5,1},{6,2},{7,3},{8,4},{9,5},{1... | collective-permute-start | bytes 2359304 | tf_op jit(solution)/shard_map/cond/branch_1_fun/ppermute | solution.py:44
  16.5 19.4 %collective-permute-start = (f32[384,512]{1,0:T(8,128)S(1)}, f32[384,512]{1,0:T(8,128)S(1)}, u32[]{:S(2)}, u32[]{:S(2)}) collective-permute-start(f32[384,512]{1,0:T(8,128)S(1)} %stack_factors.1.own), channel_id=1, source_target_pairs={{0,4},{1,5},{2,6},{3,7},{4,8},{5,9},{6,10},{7,11},{8,12},{9,13},{1... | collective-permute-start | bytes 2359304 | tf_op jit(solution)/shard_map/cond/branch_1_fun/ppermute | solution.py:44
  32.4 10.0 %collective-permute-start.3 = (f32[192,512]{1,0:T(8,128)S(1)}, f32[192,512]{1,0:T(8,128)S(1)}, u32[]{:S(2)}, u32[]{:S(2)}) collective-permute-start(f32[192,512]{1,0:T(8,128)S(1)} %slice.7), channel_id=1, source_target_pairs={{0,12},{1,13},{2,14},{3,15},{4,0},{5,1},{6,2},{7,3},{8,4},{9,5},{1... | collective-permute-start | bytes 1179656 | tf_op jit(solution)/shard_map/cond/branch_1_fun/ppermute | solution.py:44
  36.0 9.8 %collective-permute-start.2 = (f32[192,512]{1,0:T(8,128)S(1)}, f32[192,512]{1,0:T(8,128)S(1)}, u32[]{:S(2)}, u32[]{:S(2)}) collective-permute-start(f32[192,512]{1,0:T(8,128)S(1)} %slice.6), channel_id=1, source_target_pairs={{0,4},{1,5},{2,6},{3,7},{4,8},{5,9},{6,10},{7,11},{8,12},{9,13},{1... | collective-permute-start | bytes 1179656 | tf_op jit(solution)/shard_map/cond/branch_1_fun/ppermute | solution.py:44
  47.6 8.7 %collective-permute-start.4 = (f32[4,384,512]{2,1,0:T(8,128)}, f32[4,384,512]{2,1,0:T(8,128)}, u32[]{:S(2)}, u32[]{:S(2)}) collective-permute-start(f32[4,384,512]{2,1,0:T(8,128)} %join_factors.1), channel_id=1, source_target_pairs={{0,1},{1,0},{2,3},{3,2},{4,5},{5,4},{6,7},{7,6},{8,9},{9,8},{10,11... | collective-permute-start | bytes 9437192 | tf_op jit(solution)/shard_map/cond/branch_1_fun/ppermute | solution.py:40
  56.3 2.2 %copy-start = (f32[512,2048]{1,0:T(8,128)S(1)}, f32[512,2048]{1,0:T(8,128)}, u32[]{:S(2)}) copy-start(f32[512,2048]{1,0:T(8,128)} %basis.1) | copy-start | bytes 12582916
  61.3 4.1 %copy-start.4 = (s32[4,128]{1,0:T(4,128)S(1)}, s32[4,128]{1,0:T(4,128)}, u32[]{:S(2)}) copy-start(s32[4,128]{1,0:T(4,128)} %param.16) | copy-start | bytes 6148
  61.3 4.1 %copy-start.5 = (s32[4,128]{1,0:T(4,128)S(1)}, s32[4,128]{1,0:T(4,128)}, u32[]{:S(2)}) copy-start(s32[4,128]{1,0:T(4,128)} %param.15) | copy-start | bytes 6148
  61.4 4.3 %copy-start.1 = (f32[2048,4,128]{2,1,0:T(4,128)S(1)}, f32[2048,4,128]{2,1,0:T(4,128)}, u32[]{:S(2)}) copy-start(f32[2048,4,128]{2,1,0:T(4,128)} %param.10) | copy-start | bytes 12582916
  65.3 0.7 copy-start.2
  83.1 3.6 %collective-permute-start.7 = (f32[256,512]{1,0:T(8,128)S(1)}, f32[256,512]{1,0:T(8,128)S(1)}, u32[]{:S(2)}, u32[]{:S(2)}) collective-permute-start(f32[256,512]{1,0:T(8,128)S(1)} %get-tuple-element.53), channel_id=1, source_target_pairs={{0,1},{1,0},{2,3},{3,2},{4,5},{5,4},{6,7},{7,6},{8,9},{9,8},{10,11... | collective-permute-start | bytes 1572872 | tf_op jit(solution)/shard_map/ppermute | solution.py:40
  87.4 6.7 %collective-permute-start.8 = (f32[64,512]{1,0:T(8,128)S(1)}, f32[64,512]{1,0:T(8,128)S(1)}, u32[]{:S(2)}, u32[]{:S(2)}) collective-permute-start(f32[64,512]{1,0:T(8,128)S(1)} %get-tuple-element.55), channel_id=1, source_target_pairs={{0,8},{1,9},{2,10},{3,11},{4,12},{5,13},{6,14},{7,15},{8,0},{9,1},... | collective-permute-start | bytes 393224 | tf_op jit(solution)/shard_map/ppermute | solution.py:44
  90.4 6.9 %collective-permute-start.9 = (f32[64,512]{1,0:T(8,128)S(1)}, f32[64,512]{1,0:T(8,128)S(1)}, u32[]{:S(2)}, u32[]{:S(2)}) collective-permute-start(f32[64,512]{1,0:T(8,128)S(1)} %get-tuple-element.56), channel_id=1, source_target_pairs={{0,12},{1,13},{2,14},{3,15},{4,0},{5,1},{6,2},{7,3},{8,4},{9,5},{1... | collective-permute-start | bytes 393224 | tf_op jit(solution)/shard_map/ppermute | solution.py:44
  91.2 6.1 %collective-permute-start.10 = (f32[64,512]{1,0:T(8,128)S(1)}, f32[64,512]{1,0:T(8,128)S(1)}, u32[]{:S(2)}, u32[]{:S(2)}) collective-permute-start(f32[64,512]{1,0:T(8,128)S(1)} %get-tuple-element.57), channel_id=1, source_target_pairs={{0,4},{1,5},{2,6},{3,7},{4,8},{5,9},{6,10},{7,11},{8,12},{9,13},{1... | collective-permute-start | bytes 393224 | tf_op jit(solution)/shard_map/ppermute | solution.py:44
  97.3 3.4 %collective-permute-start.11 = (f32[32,512]{1,0:T(8,128)S(1)}, f32[32,512]{1,0:T(8,128)S(1)}, u32[]{:S(2)}, u32[]{:S(2)}) collective-permute-start(f32[32,512]{1,0:T(8,128)S(1)} %get-tuple-element.58.mine_a), channel_id=1, source_target_pairs={{0,2},{1,3},{2,0},{3,1},{4,6},{5,7},{6,4},{7,5},{8,10},{9,11},{10,... | collective-permute-start | bytes 196616 | tf_op jit(solution)/shard_map/ppermute | solution.py:40
  99.1 3.8 %collective-permute-start.12 = (f32[32,512]{1,0:T(8,128)S(1)}, f32[32,512]{1,0:T(8,128)S(1)}, u32[]{:S(2)}, u32[]{:S(2)}) collective-permute-start(f32[32,512]{1,0:T(8,128)S(1)} %get-tuple-element.59.mine_b), channel_id=1, source_target_pairs={{0,2},{1,3},{2,0},{3,1},{4,6},{5,7},{6,4},{7,5},{8,10},{9,11},{10,... | collective-permute-start | bytes 196616 | tf_op jit(solution)/shard_map/ppermute | solution.py:40
  104.6 3.2 %collective-permute-start.13 = (f32[32,512]{1,0:T(8,128)S(1)}, f32[32,512]{1,0:T(8,128)S(1)}, u32[]{:S(2)}, u32[]{:S(2)}) collective-permute-start(f32[32,512]{1,0:T(8,128)S(1)} %get-tuple-element.62.a), channel_id=1, source_target_pairs={{0,2},{1,3},{2,0},{3,1},{4,6},{5,7},{6,4},{7,5},{8,10},{9,11},{10,... | collective-permute-start | bytes 196616 | tf_op jit(solution)/shard_map/ppermute | solution.py:40
  104.7 3.8 %collective-permute-start.14 = (f32[32,512]{1,0:T(8,128)S(1)}, f32[32,512]{1,0:T(8,128)S(1)}, u32[]{:S(2)}, u32[]{:S(2)}) collective-permute-start(f32[32,512]{1,0:T(8,128)S(1)} %get-tuple-element.63.b), channel_id=1, source_target_pairs={{0,2},{1,3},{2,0},{3,1},{4,6},{5,7},{6,4},{7,5},{8,10},{9,11},{10,... | collective-permute-start | bytes 196616 | tf_op jit(solution)/shard_map/ppermute | solution.py:40
  108.5 8.1 %collective-permute-start.17 = (f32[64,512]{1,0:T(8,128)S(1)}, f32[64,512]{1,0:T(8,128)S(1)}, u32[]{:S(2)}, u32[]{:S(2)}) collective-permute-start(f32[64,512]{1,0:T(8,128)S(1)} %add_two.1.own), channel_id=1, source_target_pairs={{0,8},{1,9},{2,10},{3,11},{4,12},{5,13},{6,14},{7,15},{8,0},{9,1},... | collective-permute-start | bytes 393224 | tf_op jit(solution)/shard_map/ppermute | solution.py:44
  111.5 6.8 %collective-permute-start.16 = (f32[64,512]{1,0:T(8,128)S(1)}, f32[64,512]{1,0:T(8,128)S(1)}, u32[]{:S(2)}, u32[]{:S(2)}) collective-permute-start(f32[64,512]{1,0:T(8,128)S(1)} %add_two.1.own), channel_id=1, source_target_pairs={{0,12},{1,13},{2,14},{3,15},{4,0},{5,1},{6,2},{7,3},{8,4},{9,5},{1... | collective-permute-start | bytes 393224 | tf_op jit(solution)/shard_map/ppermute | solution.py:44
  112.2 7.4 %collective-permute-start.15 = (f32[64,512]{1,0:T(8,128)S(1)}, f32[64,512]{1,0:T(8,128)S(1)}, u32[]{:S(2)}, u32[]{:S(2)}) collective-permute-start(f32[64,512]{1,0:T(8,128)S(1)} %add_two.1.own), channel_id=1, source_target_pairs={{0,4},{1,5},{2,6},{3,7},{4,8},{5,9},{6,10},{7,11},{8,12},{9,13},{1... | collective-permute-start | bytes 393224 | tf_op jit(solution)/shard_map/ppermute | solution.py:44
  113.0 8.8 %collective-permute-start.18 = (f32[64,512]{1,0:T(8,128)S(1)}, f32[64,512]{1,0:T(8,128)S(1)}, u32[]{:S(2)}, u32[]{:S(2)}) collective-permute-start(f32[64,512]{1,0:T(8,128)S(1)} %add_two.1.own), channel_id=1, source_target_pairs={{0,1},{1,0},{2,3},{3,2},{4,5},{5,4},{6,7},{7,6},{8,9},{9,8},{10,11... | collective-permute-start | bytes 393224 | tf_op jit(solution)/shard_map/ppermute | solution.py:40
  116.6 5.2 %collective-permute-start.21 = (f32[64,512]{1,0:T(8,128)S(1)}, f32[64,512]{1,0:T(8,128)S(1)}, u32[]{:S(2)}, u32[]{:S(2)}) collective-permute-start(f32[64,512]{1,0:T(8,128)S(1)} %collective-permute-done.17.y_2), channel_id=1, source_target_pairs={{0,1},{1,0},{2,3},{3,2},{4,5},{5,4},{6,7},{7,6},{8,9},{9,8},{10,11... | collective-permute-start | bytes 393224 | tf_op jit(solution)/shard_map/ppermute | solution.py:40
  118.3 3.5 %collective-permute-start.20 = (f32[64,512]{1,0:T(8,128)S(1)}, f32[64,512]{1,0:T(8,128)S(1)}, u32[]{:S(2)}, u32[]{:S(2)}) collective-permute-start(f32[64,512]{1,0:T(8,128)S(1)} %collective-permute-done.16.y_3), channel_id=1, source_target_pairs={{0,1},{1,0},{2,3},{3,2},{4,5},{5,4},{6,7},{7,6},{8,9},{9,8},{10,11... | collective-permute-start | bytes 393224 | tf_op jit(solution)/shard_map/ppermute | solution.py:40
  119.6 3.2 %collective-permute-start.19 = (f32[64,512]{1,0:T(8,128)S(1)}, f32[64,512]{1,0:T(8,128)S(1)}, u32[]{:S(2)}, u32[]{:S(2)}) collective-permute-start(f32[64,512]{1,0:T(8,128)S(1)} %collective-permute-done.15.y_1), channel_id=1, source_target_pairs={{0,1},{1,0},{2,3},{3,2},{4,5},{5,4},{6,7},{7,6},{8,9},{9,8},{10,11... | collective-permute-start | bytes 393224 | tf_op jit(solution)/shard_map/ppermute | solution.py:40

commit v7 on v5

--- a/solution.py
+++ b/solution.py
@@ -20,7 +20,6 @@
 HALF = PER_DEVICE // 2
 CHUNK = 256
 CHUNK_M = 1024
-CHUNK_R = 1024
 MOMENTS = 512
 RANKS = 1024
 F32 = jnp.float32
@@ -445,8 +444,8 @@
 def collision_part(place, kept, sent, factor_high, factor_low):
     shape = (kept.shape[0] // 4, MOMENTS)
     operands = (place, kept, exchanged(sent, 1))
-    own, *others = small_call(scatter_kernel, "scatter", 4, shape, operands, 1)
-    arrived = [along_y(piece, away + 1) for away, piece in enumerate(others)]
+    own, to_one, to_two, to_three = small_call(scatter_kernel, "scatter", 4, shape, operands, 1)
+    arrived = (along_y(to_two, 2), along_y(to_three, 3), along_y(to_one, 1))
     summed = small_call(add_four_kernel, "add_four", 1, shape, (own, *arrived))
     operands = (summed, exchanged(summed, 2), factor_high, factor_low)
     share = small_call(collision_kernel, "collide", 1, shape, operands, mib=4)
@@ -457,45 +456,61 @@
 
 def relax_kernel(
     place, own, y_1, y_2, y_3, other, z_1, z_2, z_3, kind, moved, high, low,
-    out, gathered, turned_high, turned_low,
+    out, gathered, turned_high, turned_low, held, leavings,
 ):
-    step = pl.program_id(0)
     size = own.shape[0]
-
-    @pl.when(step == 0)
-    def _():
-        pieces = (((own, y_1, y_2, y_3), place[0]), ((other, z_1, z_2, z_3), 1 - place[0]))
-        for group, core in pieces:
-            for away, piece in enumerate(group):
-                at = core * 4 + (place[1] + (4 - away)) % 4
-                gathered[pl.ds(pl.multiple_of(at * size, size), size), :] = piece[...]
-        turned_high[...], turned_low[...] = halves(gathered[...].T)
-
-    lines = pl.ds(pl.multiple_of(step * CHUNK_R, CHUNK_R), CHUNK_R)
-    gain = dot(high[lines, :], turned_high[...])
-    gain = gain + dot(high[lines, :], turned_low[...])
-    gain = gain + dot(low[lines, :], turned_high[...])
-    for x in range(COLUMNS):
-        fluid = HALF_STEP * (1 - kind[x : x + 1, :]).astype(F32)
-        out[pl.ds(x, CHUNK_R, stride=COLUMNS), :] = (
-            moved[x, lines, :] + fluid * gain[:, x * ROWS : (x + 1) * ROWS]
-        )
+    pieces = (((own, y_1, y_2, y_3), place[0]), ((other, z_1, z_2, z_3), 1 - place[0]))
+    for group, core in pieces:
+        for away, piece in enumerate(group):
+            at = core * 4 + (place[1] + (4 - away)) % 4
+            gathered[pl.ds(pl.multiple_of(at * size, size), size), :] = piece[...]
+    turned_high[...], turned_low[...] = halves(gathered[...].T)
+    fluid = [HALF_STEP * (1 - kind[x : x + 1, :]).astype(F32) for x in range(COLUMNS)]
+    sends = []
+    start = 0
+    for count in (1024, 512, 256, 256):
+        lines = pl.ds(start, count)
+        gains = []
+        for core in range(2):
+            cells = slice(core * 2 * ROWS, (core + 1) * 2 * ROWS)
+            gain = dot(high[lines, :], turned_high[:, cells])
+            gain = gain + dot(high[lines, :], turned_low[:, cells])
+            gains.append(gain + dot(low[lines, :], turned_high[:, cells]))
+        for part in range(count // CHUNK):
+            first = start + part * CHUNK
+            for x in range(COLUMNS):
+                gain = gains[x // 2][
+                    part * CHUNK : (part + 1) * CHUNK, x % 2 * ROWS : (x % 2 + 1) * ROWS
+                ]
+                held[pl.ds(COLUMNS * first + x, CHUNK, stride=COLUMNS), :] = (
+                    moved[x, pl.ds(first, CHUNK), :] + fluid[x] * gain
+                )
+            rows = pl.ds(COLUMNS * first, COLUMNS * CHUNK)
+            send = pltpu.make_async_copy(
+                held.at[rows], out.at[rows], leavings.at[first // CHUNK]
+            )
+            send.start()
+            sends.append(send)
+        start += count
+    for send in sends:
+        send.wait()
 
 
 def relax(place, pieces, kind, moved, high, low):
     return pl.pallas_call(
         relax_kernel,
         name="relax",
-        grid=(PER_DEVICE // CHUNK_R,),
         in_specs=[SM] + [VM] * 12,
-        out_specs=pl.BlockSpec((CHUNK_R * COLUMNS, ROWS), lambda i: (i, 0)),
+        out_specs=ANY,
         out_shape=jax.ShapeDtypeStruct((PER_DEVICE * COLUMNS, ROWS), F32),
         scratch_shapes=[
             pltpu.VMEM((CELLS, MOMENTS), F32),
             pltpu.VMEM((MOMENTS, CELLS), BF16),
             pltpu.VMEM((MOMENTS, CELLS), BF16),
+            pltpu.VMEM((PER_DEVICE * COLUMNS, ROWS), F32),
+            pltpu.SemaphoreType.DMA((PER_DEVICE // CHUNK,)),
         ],
-        compiler_params=params(14),
+        compiler_params=params(22),
         cost_estimate=cost(8 << 30, 16 * MIB),
     )(place, *pieces, kind, moved, high, low)
 

time: 128 us -> 128 us (level)
  no operation moved by 1% of the time
where the time goes in v7:
time: 128 us
  waiting for transfers between devices  48.8 us (38%)
  starting transfers between devices  41.1 us (32%)
  Pallas kernels  34.5 us (27%)
  local copies, waits for them, and re-layouts  2.61 us (2%)
    ppermute x10, waiting for transfers between devices, along_y(): return lax.ppermute(x, 'vel', [(i, (i + 4 * by) % 16) for i in range(16)])  31 us
    ppermute x8, starting transfers between devices, exchanged(): return lax.ppermute(x, 'vel', [(i, i ^ bit) for i in range(16)])  16.6 us
    ppermute x10, starting transfers between devices, along_y(): return lax.ppermute(x, 'vel', [(i, (i + 4 * by) % 16) for i in range(16)])  15.2 us
    ppermute x8, waiting for transfers between devices, exchanged(): return lax.ppermute(x, 'vel', [(i, i ^ bit) for i in range(16)])  12.1 us
    ppermute x2, starting transfers between devices, shifted(): return lax.ppermute(x, 'cells', [(i, (i + by) % size) for i in range(size)])  9.21 us
    pallas_call x1, Pallas kernels, local_part(): pl.pallas_call(local_kernel, name='local_transport', grid=(steps,), in_sp...  7.99 us
    ppermute x2, waiting for transfers between devices, shifted(): return lax.ppermute(x, 'cells', [(i, (i + by) % size) for i in range(size)])  5.78 us
    pallas_call x1, Pallas kernels, relax(): pl.pallas_call(relax_kernel, name='relax', in_specs=[SM] + [VM] * 12, out...  5.1 us
  transfers between devices with their start and end apart: 20, of which 10 were waited for; matrix products, arithmetic and copies ran while one was open for 0% of the time, Pallas kernels for 16%

profile of v7, /device:TPU:1, one launch (start us, length us, event | category | flops | bytes accessed | tf_op | source)
XLA Modules:
  0.0 127.7 jit_solution(6969064712041256857)
XLA Ops:
  0.0 3.3 %pack.1 = (f32[3,1024,128]{2,1,0:T(8,128)}, f32[3,1024,128]{2,1,0:T(8,128)}) custom-call(f32[8192,128]{1,0:T(8,128)} %bitcast.9), custom_call_target="tpu_custom_call" | custom-call | flops 1048576 | bytes 8388608 | tf_op jit(solution)/shard_map/pack/pallas_call | solution.py:117
  3.3 3.9 %collective-permute-start.5 = (f32[3,1024,128]{2,1,0:T(8,128)}, f32[3,1024,128]{2,1,0:T(8,128)S(1)}, u32[]{:S(2)}, u32[]{:S(2)}) collective-permute-start(f32[3,1024,128]{2,1,0:T(8,128)} %get-tuple-element.38), channel_id=1, source_target_pairs={{0,16},{16,32},{32,48},{48,64},{64,80},{80,96},{96,112},{112,128},... | collective-permute-start | bytes 4718600 | tf_op jit(solution)/shard_map/ppermute | solution.py:35
  7.2 5.3 %collective-permute-start.6 = (f32[3,1024,128]{2,1,0:T(8,128)}, f32[3,1024,128]{2,1,0:T(8,128)S(1)}, u32[]{:S(2)}, u32[]{:S(2)}) collective-permute-start(f32[3,1024,128]{2,1,0:T(8,128)} %get-tuple-element.39), channel_id=1, source_target_pairs={{0,240},{16,0},{32,16},{48,32},{64,48},{80,64},{96,80},{112,96},{1... | collective-permute-start | bytes 4718600 | tf_op jit(solution)/shard_map/ppermute | solution.py:35
  12.5 0.0 copy-done.3
  12.5 43.8 %conditional.1 = (f32[4,384,512]{2,1,0:T(8,128)}, f32[4,384,512]{2,1,0:T(8,128)}) conditional(s32[]{:T(128)} %convert_element_type.15, () %tuple.14, (f32[128,512]{1,0:T(8,128)S(1)}, f32[128,512]{1,0:T(8,128)}, f32[512,128]{1,0:T(8,128)}) %tuple.21), branch_computations={%region_0.1_spmd, %region_1.2_spmd} | conditional | flops 2097152 | bytes 31981784 | solution.py:139
  12.5 1.2 stack_factors.1.own
  13.7 2.8 %collective-permute-start.1 = (f32[384,512]{1,0:T(8,128)S(1)}, f32[384,512]{1,0:T(8,128)S(1)}, u32[]{:S(2)}, u32[]{:S(2)}) collective-permute-start(f32[384,512]{1,0:T(8,128)S(1)} %stack_factors.1.own), channel_id=1, source_target_pairs={{0,12},{1,13},{2,14},{3,15},{4,0},{5,1},{6,2},{7,3},{8,4},{9,5},{1... | collective-permute-start | bytes 2359304 | tf_op jit(solution)/shard_map/cond/branch_1_fun/ppermute | solution.py:43
  16.5 0.0 collective-permute-start
  16.5 15.9 %collective-permute-done.1.after = f32[384,512]{1,0:T(8,128)S(1)} collective-permute-done((f32[384,512]{1,0:T(8,128)S(1)}, f32[384,512]{1,0:T(8,128)S(1)}, u32[]{:S(2)}, u32[]{:S(2)}) %collective-permute-start.1) | collective-permute-done | bytes 786464 | tf_op jit(solution)/shard_map/cond/branch_1_fun/ppermute | solution.py:43
  32.4 3.5 %collective-permute-start.3 = (f32[192,512]{1,0:T(8,128)S(1)}, f32[192,512]{1,0:T(8,128)S(1)}, u32[]{:S(2)}, u32[]{:S(2)}) collective-permute-start(f32[192,512]{1,0:T(8,128)S(1)} %slice.7), channel_id=1, source_target_pairs={{0,12},{1,13},{2,14},{3,15},{4,0},{5,1},{6,2},{7,3},{8,4},{9,5},{1... | collective-permute-start | bytes 1179656 | tf_op jit(solution)/shard_map/cond/branch_1_fun/ppermute | solution.py:43
  35.9 0.0 collective-permute-done.before
  36.0 0.1 collective-permute-start.2
  36.1 6.4 %collective-permute-done.3.across_rest = f32[192,512]{1,0:T(8,128)S(1)} collective-permute-done((f32[192,512]{1,0:T(8,128)S(1)}, f32[192,512]{1,0:T(8,128)S(1)}, u32[]{:S(2)}, u32[]{:S(2)}) %collective-permute-start.3) | collective-permute-done | bytes 393248 | tf_op jit(solution)/shard_map/cond/branch_1_fun/ppermute | solution.py:43
  42.5 3.2 %collective-permute-done.2.across_top = f32[192,512]{1,0:T(8,128)S(1)} collective-permute-done((f32[192,512]{1,0:T(8,128)S(1)}, f32[192,512]{1,0:T(8,128)S(1)}, u32[]{:S(2)}, u32[]{:S(2)}) %collective-permute-start.2) | collective-permute-done | bytes 393248 | tf_op jit(solution)/shard_map/cond/branch_1_fun/ppermute | solution.py:43
  45.7 1.9 %join_factors.1 = f32[4,384,512]{2,1,0:T(8,128)} custom-call(f32[384,512]{1,0:T(8,128)S(1)} %stack_factors.1.own, f32[384,512]{1,0:T(8,128)S(1)} %collective-permute-done.before, f32[384,512]{1,0:T(8,128)S(1)} %collective-permute-done.1.after, f32[192,512]{1,0:T(8,128)S(1)} %collective-permute-done.2.across_top, ...), custom_call_target="tpu_custom_call" | custom-call | flops 1048576 | bytes 6291456 | tf_op jit(solution)/shard_map/cond/branch_1_fun/join_factors/pallas_call | solution.py:285
  47.6 3.1 %collective-permute-start.4 = (f32[4,384,512]{2,1,0:T(8,128)}, f32[4,384,512]{2,1,0:T(8,128)}, u32[]{:S(2)}, u32[]{:S(2)}) collective-permute-start(f32[4,384,512]{2,1,0:T(8,128)} %join_factors.1), channel_id=1, source_target_pairs={{0,1},{1,0},{2,3},{3,2},{4,5},{5,4},{6,7},{7,6},{8,9},{9,8},{10,11... | collective-permute-start | bytes 9437192 | tf_op jit(solution)/shard_map/cond/branch_1_fun/ppermute | solution.py:39
  50.7 5.6 %collective-permute-done.4 = f32[4,384,512]{2,1,0:T(8,128)} collective-permute-done((f32[4,384,512]{2,1,0:T(8,128)}, f32[4,384,512]{2,1,0:T(8,128)}, u32[]{:S(2)}, u32[]{:S(2)}) %collective-permute-start.4) | collective-permute-done | bytes 3145760 | tf_op jit(solution)/shard_map/cond/branch_1_fun/ppermute | solution.py:39
  56.3 2.2 %copy-done = f32[512,2048]{1,0:T(8,128)S(1)} copy-done((f32[512,2048]{1,0:T(8,128)S(1)}, f32[512,2048]{1,0:T(8,128)}, u32[]{:S(2)}) %copy-start) | copy-done | bytes 4194328
  58.5 2.9 %split_basis.1 = (bf16[512,2048]{1,0:T(8,128)(2,1)S(1)}, bf16[512,2048]{1,0:T(8,128)(2,1)S(1)}, bf16[2048,512]{1,0:T(8,128)(2,1)S(1)}, bf16[2048,512]{1,0:T(8,128)(2,1)S(1)}) custom-call(f32[512,2048]{1,0:T(8,128)S(1)} %copy-done), custom_call_target="tpu_custom_call" | custom-call | flops 16777216 | bytes 12582912 | tf_op jit(solution)/shard_map/split_basis/pallas_call | solution.py:236
  61.3 0.0 copy-start.4
  61.3 0.0 copy-start.5
  61.4 0.0 copy-start.1
  61.4 4.0 %split_factors.1 = (bf16[3,1024,512]{2,1,0:T(8,128)(2,1)S(1)}, bf16[3,1024,512]{2,1,0:T(8,128)(2,1)S(1)}) custom-call(f32[4,384,512]{2,1,0:T(8,128)} %get-tuple-element.40.mine, f32[4,384,512]{2,1,0:T(8,128)} %get-tuple-element.41.theirs), custom_call_target="tpu_custom_call" | custom-call | flops 16777216 | bytes 12582912 | tf_op jit(solution)/shard_map/split_factors/pallas_call | solution.py:299
  65.3 0.0 copy-start.2
  65.3 0.1 pad_add_fusion.place
  65.4 0.0 copy-done.4
  65.4 0.1 fusion
  65.5 0.1 maximum_bitcast_fusion
  65.6 0.1 pad_maximum_fusion.tables
  65.7 0.3 copy-done.2
  66.0 8.0 %local_transport.1 = (f32[4,2048,128]{2,1,0:T(8,128)S(1)}, f32[4,2048,128]{2,1,0:T(8,128)S(1)}) custom-call(f32[1]{0:T(128)} %bitcast.2.speed, f32[8192,128]{1,0:T(8,128)S(1)} %bitcast.10, s32[4,128]{1,0:T(4,128)S(1)} %copy-done.2, bf16[2,4,256,256]{3,2,1,0:T(8,128)(2,1)S(1)} %pad_maximum_fusion.tables), custom_call_target="tpu_custom_call" | custom-call | flops 4294967296 | bytes 10485760 | tf_op jit(solution)/shard_map/local_transport/pallas_call | solution.py:191
  74.0 0.0 collective-permute-done.5.from_left
  74.0 5.8 %collective-permute-done.6.from_right = f32[3,1024,128]{2,1,0:T(8,128)S(1)} collective-permute-done((f32[3,1024,128]{2,1,0:T(8,128)}, f32[3,1024,128]{2,1,0:T(8,128)S(1)}, u32[]{:S(2)}, u32[]{:S(2)}) %collective-permute-start.6) | collective-permute-done | bytes 1572896 | tf_op jit(solution)/shard_map/ppermute | solution.py:35
  79.8 3.4 %faces_and_moments.1 = (f32[4,2048,128]{2,1,0:T(8,128)S(1)}, f32[256,512]{1,0:T(8,128)S(1)}) custom-call(f32[1]{0:T(128)} %bitcast.2.speed, s32[2]{0:T(128)S(1)} %pad_add_fusion.place, f32[4,2048,128]{2,1,0:T(8,128)S(1)} %get-tuple-element.36.ends, f32[4,2048,128]{2,1,0:T(8,128)S(1)} %get-tuple-element.37.part, ...), custom_call_target="tpu_custom_call" | custom-call | flops 4294967296 | bytes 18874368 | tf_op jit(solution)/shard_map/faces_and_moments/pallas_call | solution.py:378
  83.2 1.2 collective-permute-start.7
  84.5 2.5 %own_moments.1.kept = f32[256,512]{1,0:T(8,128)S(1)} custom-call(s32[2]{0:T(128)S(1)} %pad_add_fusion.place, f32[4,2048,128]{2,1,0:T(8,128)S(1)} %get-tuple-element.48.moved, bf16[512,2048]{1,0:T(8,128)(2,1)S(1)} %get-tuple-element.46.high, bf16[512,2048]{1,0:T(8,128)(2,1)S(1)} %get-tuple-element.47.low), custom_call_target="tpu_custom_call" | custom-call | flops 4294967296 | bytes 8388608 | tf_op jit(solution)/shard_map/own_moments/pallas_call | solution.py:389
  86.9 0.0 collective-permute-done.7.received
  86.9 0.6 scatter.1
  87.5 3.0 %collective-permute-start.8 = (f32[64,512]{1,0:T(8,128)S(1)}, f32[64,512]{1,0:T(8,128)S(1)}, u32[]{:S(2)}, u32[]{:S(2)}) collective-permute-start(f32[64,512]{1,0:T(8,128)S(1)} %get-tuple-element.51), channel_id=1, source_target_pairs={{0,8},{1,9},{2,10},{3,11},{4,12},{5,13},{6,14},{7,15},{8,0},{9,1},... | collective-permute-start | bytes 393224 | tf_op jit(solution)/shard_map/ppermute | solution.py:43
  90.5 0.8 collective-permute-start.9
  91.3 0.7 collective-permute-start.10
  92.0 2.2 %collective-permute-done.8.b = f32[64,512]{1,0:T(8,128)S(1)} collective-permute-done((f32[64,512]{1,0:T(8,128)S(1)}, f32[64,512]{1,0:T(8,128)S(1)}, u32[]{:S(2)}, u32[]{:S(2)}) %collective-permute-start.8) | collective-permute-done | bytes 131104 | tf_op jit(solution)/shard_map/ppermute | solution.py:43
  94.3 3.2 %collective-permute-done.9.c = f32[64,512]{1,0:T(8,128)S(1)} collective-permute-done((f32[64,512]{1,0:T(8,128)S(1)}, f32[64,512]{1,0:T(8,128)S(1)}, u32[]{:S(2)}, u32[]{:S(2)}) %collective-permute-start.9) | collective-permute-done | bytes 131104 | tf_op jit(solution)/shard_map/ppermute | solution.py:43
  97.4 0.0 collective-permute-done.10.d
  97.5 1.7 %collective-permute-start.11 = (f32[64,512]{1,0:T(8,128)S(1)}, f32[64,512]{1,0:T(8,128)S(1)}, u32[]{:S(2)}, u32[]{:S(2)}) collective-permute-start(f32[64,512]{1,0:T(8,128)S(1)} %add_four.1.mine), channel_id=1, source_target_pairs={{0,2},{1,3},{2,0},{3,1},{4,6},{5,7},{6,4},{7,5},{8,10},{9,11},{10,... | collective-permute-start | bytes 393224 | tf_op jit(solution)/shard_map/ppermute | solution.py:39
  99.2 2.7 %collective-permute-done.11.theirs = f32[64,512]{1,0:T(8,128)S(1)} collective-permute-done((f32[64,512]{1,0:T(8,128)S(1)}, f32[64,512]{1,0:T(8,128)S(1)}, u32[]{:S(2)}, u32[]{:S(2)}) %collective-permute-start.11) | collective-permute-done | bytes 131104 | tf_op jit(solution)/shard_map/ppermute | solution.py:39
  101.9 1.8 %collide.1.a = f32[64,512]{1,0:T(8,128)S(1)} custom-call(f32[64,512]{1,0:T(8,128)S(1)} %add_four.1.mine, f32[64,512]{1,0:T(8,128)S(1)} %collective-permute-done.11.theirs, bf16[3,1024,512]{2,1,0:T(8,128)(2,1)S(1)} %get-tuple-element.54.high, bf16[3,1024,512]{2,1,0:T(8,128)(2,1)S(1)} %get-tuple-element.55.low), custom_call_target="tpu_custom_call" | custom-call | flops 1048576 | bytes 1048576 | tf_op jit(solution)/shard_map/collide/pallas_call | solution.py:405
  103.7 1.2 collective-permute-start.12
  104.9 2.7 %collective-permute-done.12.b = f32[64,512]{1,0:T(8,128)S(1)} collective-permute-done((f32[64,512]{1,0:T(8,128)S(1)}, f32[64,512]{1,0:T(8,128)S(1)}, u32[]{:S(2)}, u32[]{:S(2)}) %collective-permute-start.12) | collective-permute-done | bytes 131104 | tf_op jit(solution)/shard_map/ppermute | solution.py:39
  107.6 3.4 %collective-permute-start.15 = (f32[64,512]{1,0:T(8,128)S(1)}, f32[64,512]{1,0:T(8,128)S(1)}, u32[]{:S(2)}, u32[]{:S(2)}) collective-permute-start(f32[64,512]{1,0:T(8,128)S(1)} %add_two.1.own), channel_id=1, source_target_pairs={{0,12},{1,13},{2,14},{3,15},{4,0},{5,1},{6,2},{7,3},{8,4},{9,5},{1... | collective-permute-start | bytes 393224 | tf_op jit(solution)/shard_map/ppermute | solution.py:43
  111.0 0.2 collective-permute-start.14
  111.2 0.8 collective-permute-start.13
  112.0 3.1 %collective-permute-start.16 = (f32[64,512]{1,0:T(8,128)S(1)}, f32[64,512]{1,0:T(8,128)S(1)}, u32[]{:S(2)}, u32[]{:S(2)}) collective-permute-start(f32[64,512]{1,0:T(8,128)S(1)} %add_two.1.own), channel_id=1, source_target_pairs={{0,1},{1,0},{2,3},{3,2},{4,5},{5,4},{6,7},{7,6},{8,9},{9,8},{10,11... | collective-permute-start | bytes 393224 | tf_op jit(solution)/shard_map/ppermute | solution.py:39
  115.1 0.0 collective-permute-done.15.y_3
  115.1 2.5 %collective-permute-start.19 = (f32[64,512]{1,0:T(8,128)S(1)}, f32[64,512]{1,0:T(8,128)S(1)}, u32[]{:S(2)}, u32[]{:S(2)}) collective-permute-start(f32[64,512]{1,0:T(8,128)S(1)} %collective-permute-done.15.y_3), channel_id=1, source_target_pairs={{0,1},{1,0},{2,3},{3,2},{4,5},{5,4},{6,7},{7,6},{8,9},{9,8},{10,11... | collective-permute-start | bytes 393224 | tf_op jit(solution)/shard_map/ppermute | solution.py:39
  117.6 0.0 collective-permute-done.14.y_2
  117.6 2.5 %collective-permute-start.18 = (f32[64,512]{1,0:T(8,128)S(1)}, f32[64,512]{1,0:T(8,128)S(1)}, u32[]{:S(2)}, u32[]{:S(2)}) collective-permute-start(f32[64,512]{1,0:T(8,128)S(1)} %collective-permute-done.14.y_2), channel_id=1, source_target_pairs={{0,1},{1,0},{2,3},{3,2},{4,5},{5,4},{6,7},{7,6},{8,9},{9,8},{10,11... | collective-permute-start | bytes 393224 | tf_op jit(solution)/shard_map/ppermute | solution.py:39
  120.1 0.0 collective-permute-done.13.y_1
  120.1 1.3 %collective-permute-start.17 = (f32[64,512]{1,0:T(8,128)S(1)}, f32[64,512]{1,0:T(8,128)S(1)}, u32[]{:S(2)}, u32[]{:S(2)}) collective-permute-start(f32[64,512]{1,0:T(8,128)S(1)} %collective-permute-done.13.y_1), channel_id=1, source_target_pairs={{0,1},{1,0},{2,3},{3,2},{4,5},{5,4},{6,7},{7,6},{8,9},{9,8},{10,11... | collective-permute-start | bytes 393224 | tf_op jit(solution)/shard_map/ppermute | solution.py:39
  121.4 0.0 collective-permute-done.16.other
  121.4 0.0 collective-permute-done.19.z_3
  121.4 0.0 collective-permute-done.18.z_2
  121.4 1.0 collective-permute-done.17.z_1
  122.4 5.1 %relax.1 = f32[8192,128]{1,0:T(8,128)} custom-call(s32[2]{0:T(128)S(1)} %pad_add_fusion.place, f32[64,512]{1,0:T(8,128)S(1)} %add_two.1.own, f32[64,512]{1,0:T(8,128)S(1)} %collective-permute-done.13.y_1, f32[64,512]{1,0:T(8,128)S(1)} %collective-permute-done.14.y_2, f32[64,512]{1,0:T(8,128)S(1)} %collective-permute-done.15.y_3, ...), custom_call_target="tpu_custom_call" | custom-call | flops 8589934592 | bytes 16777216 | tf_op jit(solution)/shard_map/relax/pallas_call | solution.py:500
  (8 shorter events, 0.1 us)
Async XLA Ops:
  0.0 12.5 %copy-start.3 = (f32[128,512]{1,0:T(8,128)S(1)}, f32[128,512]{1,0:T(8,128)}, u32[]{:S(2)}) copy-start(f32[128,512]{1,0:T(8,128)} %param.12) | copy-start | bytes 786436
  3.3 70.7 %collective-permute-start.5 = (f32[3,1024,128]{2,1,0:T(8,128)}, f32[3,1024,128]{2,1,0:T(8,128)S(1)}, u32[]{:S(2)}, u32[]{:S(2)}) collective-permute-start(f32[3,1024,128]{2,1,0:T(8,128)} %get-tuple-element.38), channel_id=1, source_target_pairs={{0,16},{16,32},{32,48},{48,64},{64,80},{80,96},{96,112},{112,128},... | collective-permute-start | bytes 4718600 | tf_op jit(solution)/shard_map/ppermute | solution.py:35
  7.2 72.6 %collective-permute-start.6 = (f32[3,1024,128]{2,1,0:T(8,128)}, f32[3,1024,128]{2,1,0:T(8,128)S(1)}, u32[]{:S(2)}, u32[]{:S(2)}) collective-permute-start(f32[3,1024,128]{2,1,0:T(8,128)} %get-tuple-element.39), channel_id=1, source_target_pairs={{0,240},{16,0},{32,16},{48,32},{64,48},{80,64},{96,80},{112,96},{1... | collective-permute-start | bytes 4718600 | tf_op jit(solution)/shard_map/ppermute | solution.py:35
  13.7 18.7 %collective-permute-start.1 = (f32[384,512]{1,0:T(8,128)S(1)}, f32[384,512]{1,0:T(8,128)S(1)}, u32[]{:S(2)}, u32[]{:S(2)}) collective-permute-start(f32[384,512]{1,0:T(8,128)S(1)} %stack_factors.1.own), channel_id=1, source_target_pairs={{0,12},{1,13},{2,14},{3,15},{4,0},{5,1},{6,2},{7,3},{8,4},{9,5},{1... | collective-permute-start | bytes 2359304 | tf_op jit(solution)/shard_map/cond/branch_1_fun/ppermute | solution.py:43
  16.5 19.4 %collective-permute-start = (f32[384,512]{1,0:T(8,128)S(1)}, f32[384,512]{1,0:T(8,128)S(1)}, u32[]{:S(2)}, u32[]{:S(2)}) collective-permute-start(f32[384,512]{1,0:T(8,128)S(1)} %stack_factors.1.own), channel_id=1, source_target_pairs={{0,4},{1,5},{2,6},{3,7},{4,8},{5,9},{6,10},{7,11},{8,12},{9,13},{1... | collective-permute-start | bytes 2359304 | tf_op jit(solution)/shard_map/cond/branch_1_fun/ppermute | solution.py:43
  32.4 10.0 %collective-permute-start.3 = (f32[192,512]{1,0:T(8,128)S(1)}, f32[192,512]{1,0:T(8,128)S(1)}, u32[]{:S(2)}, u32[]{:S(2)}) collective-permute-start(f32[192,512]{1,0:T(8,128)S(1)} %slice.7), channel_id=1, source_target_pairs={{0,12},{1,13},{2,14},{3,15},{4,0},{5,1},{6,2},{7,3},{8,4},{9,5},{1... | collective-permute-start | bytes 1179656 | tf_op jit(solution)/shard_map/cond/branch_1_fun/ppermute | solution.py:43
  36.0 9.8 %collective-permute-start.2 = (f32[192,512]{1,0:T(8,128)S(1)}, f32[192,512]{1,0:T(8,128)S(1)}, u32[]{:S(2)}, u32[]{:S(2)}) collective-permute-start(f32[192,512]{1,0:T(8,128)S(1)} %slice.6), channel_id=1, source_target_pairs={{0,4},{1,5},{2,6},{3,7},{4,8},{5,9},{6,10},{7,11},{8,12},{9,13},{1... | collective-permute-start | bytes 1179656 | tf_op jit(solution)/shard_map/cond/branch_1_fun/ppermute | solution.py:43
  47.6 8.7 %collective-permute-start.4 = (f32[4,384,512]{2,1,0:T(8,128)}, f32[4,384,512]{2,1,0:T(8,128)}, u32[]{:S(2)}, u32[]{:S(2)}) collective-permute-start(f32[4,384,512]{2,1,0:T(8,128)} %join_factors.1), channel_id=1, source_target_pairs={{0,1},{1,0},{2,3},{3,2},{4,5},{5,4},{6,7},{7,6},{8,9},{9,8},{10,11... | collective-permute-start | bytes 9437192 | tf_op jit(solution)/shard_map/cond/branch_1_fun/ppermute | solution.py:39
  56.3 2.2 %copy-start = (f32[512,2048]{1,0:T(8,128)S(1)}, f32[512,2048]{1,0:T(8,128)}, u32[]{:S(2)}) copy-start(f32[512,2048]{1,0:T(8,128)} %basis.1) | copy-start | bytes 12582916
  61.3 4.1 %copy-start.4 = (s32[4,128]{1,0:T(4,128)S(1)}, s32[4,128]{1,0:T(4,128)}, u32[]{:S(2)}) copy-start(s32[4,128]{1,0:T(4,128)} %param.16) | copy-start | bytes 6148
  61.3 4.1 %copy-start.5 = (s32[4,128]{1,0:T(4,128)S(1)}, s32[4,128]{1,0:T(4,128)}, u32[]{:S(2)}) copy-start(s32[4,128]{1,0:T(4,128)} %param.15) | copy-start | bytes 6148
  61.4 4.3 %copy-start.1 = (f32[2048,4,128]{2,1,0:T(4,128)S(1)}, f32[2048,4,128]{2,1,0:T(4,128)}, u32[]{:S(2)}) copy-start(f32[2048,4,128]{2,1,0:T(4,128)} %param.10) | copy-start | bytes 12582916
  65.3 0.7 copy-start.2
  83.2 3.7 %collective-permute-start.7 = (f32[256,512]{1,0:T(8,128)S(1)}, f32[256,512]{1,0:T(8,128)S(1)}, u32[]{:S(2)}, u32[]{:S(2)}) collective-permute-start(f32[256,512]{1,0:T(8,128)S(1)} %get-tuple-element.49), channel_id=1, source_target_pairs={{0,1},{1,0},{2,3},{3,2},{4,5},{5,4},{6,7},{7,6},{8,9},{9,8},{10,11... | collective-permute-start | bytes 1572872 | tf_op jit(solution)/shard_map/ppermute | solution.py:39
  87.5 6.7 %collective-permute-start.8 = (f32[64,512]{1,0:T(8,128)S(1)}, f32[64,512]{1,0:T(8,128)S(1)}, u32[]{:S(2)}, u32[]{:S(2)}) collective-permute-start(f32[64,512]{1,0:T(8,128)S(1)} %get-tuple-element.51), channel_id=1, source_target_pairs={{0,8},{1,9},{2,10},{3,11},{4,12},{5,13},{6,14},{7,15},{8,0},{9,1},... | collective-permute-start | bytes 393224 | tf_op jit(solution)/shard_map/ppermute | solution.py:43
  90.5 6.9 %collective-permute-start.9 = (f32[64,512]{1,0:T(8,128)S(1)}, f32[64,512]{1,0:T(8,128)S(1)}, u32[]{:S(2)}, u32[]{:S(2)}) collective-permute-start(f32[64,512]{1,0:T(8,128)S(1)} %get-tuple-element.52), channel_id=1, source_target_pairs={{0,12},{1,13},{2,14},{3,15},{4,0},{5,1},{6,2},{7,3},{8,4},{9,5},{1... | collective-permute-start | bytes 393224 | tf_op jit(solution)/shard_map/ppermute | solution.py:43
  91.3 6.1 %collective-permute-start.10 = (f32[64,512]{1,0:T(8,128)S(1)}, f32[64,512]{1,0:T(8,128)S(1)}, u32[]{:S(2)}, u32[]{:S(2)}) collective-permute-start(f32[64,512]{1,0:T(8,128)S(1)} %get-tuple-element.53), channel_id=1, source_target_pairs={{0,4},{1,5},{2,6},{3,7},{4,8},{5,9},{6,10},{7,11},{8,12},{9,13},{1... | collective-permute-start | bytes 393224 | tf_op jit(solution)/shard_map/ppermute | solution.py:43
  97.5 4.4 %collective-permute-start.11 = (f32[64,512]{1,0:T(8,128)S(1)}, f32[64,512]{1,0:T(8,128)S(1)}, u32[]{:S(2)}, u32[]{:S(2)}) collective-permute-start(f32[64,512]{1,0:T(8,128)S(1)} %add_four.1.mine), channel_id=1, source_target_pairs={{0,2},{1,3},{2,0},{3,1},{4,6},{5,7},{6,4},{7,5},{8,10},{9,11},{10,... | collective-permute-start | bytes 393224 | tf_op jit(solution)/shard_map/ppermute | solution.py:39
  103.7 3.9 %collective-permute-start.12 = (f32[64,512]{1,0:T(8,128)S(1)}, f32[64,512]{1,0:T(8,128)S(1)}, u32[]{:S(2)}, u32[]{:S(2)}) collective-permute-start(f32[64,512]{1,0:T(8,128)S(1)} %collide.1.a), channel_id=1, source_target_pairs={{0,2},{1,3},{2,0},{3,1},{4,6},{5,7},{6,4},{7,5},{8,10},{9,11},{10,... | collective-permute-start | bytes 393224 | tf_op jit(solution)/shard_map/ppermute | solution.py:39
  107.6 7.5 %collective-permute-start.15 = (f32[64,512]{1,0:T(8,128)S(1)}, f32[64,512]{1,0:T(8,128)S(1)}, u32[]{:S(2)}, u32[]{:S(2)}) collective-permute-start(f32[64,512]{1,0:T(8,128)S(1)} %add_two.1.own), channel_id=1, source_target_pairs={{0,12},{1,13},{2,14},{3,15},{4,0},{5,1},{6,2},{7,3},{8,4},{9,5},{1... | collective-permute-start | bytes 393224 | tf_op jit(solution)/shard_map/ppermute | solution.py:43
  111.0 6.6 %collective-permute-start.14 = (f32[64,512]{1,0:T(8,128)S(1)}, f32[64,512]{1,0:T(8,128)S(1)}, u32[]{:S(2)}, u32[]{:S(2)}) collective-permute-start(f32[64,512]{1,0:T(8,128)S(1)} %add_two.1.own), channel_id=1, source_target_pairs={{0,8},{1,9},{2,10},{3,11},{4,12},{5,13},{6,14},{7,15},{8,0},{9,1},... | collective-permute-start | bytes 393224 | tf_op jit(solution)/shard_map/ppermute | solution.py:43
  111.2 8.9 %collective-permute-start.13 = (f32[64,512]{1,0:T(8,128)S(1)}, f32[64,512]{1,0:T(8,128)S(1)}, u32[]{:S(2)}, u32[]{:S(2)}) collective-permute-start(f32[64,512]{1,0:T(8,128)S(1)} %add_two.1.own), channel_id=1, source_target_pairs={{0,4},{1,5},{2,6},{3,7},{4,8},{5,9},{6,10},{7,11},{8,12},{9,13},{1... | collective-permute-start | bytes 393224 | tf_op jit(solution)/shard_map/ppermute | solution.py:43
  112.0 9.4 %collective-permute-start.16 = (f32[64,512]{1,0:T(8,128)S(1)}, f32[64,512]{1,0:T(8,128)S(1)}, u32[]{:S(2)}, u32[]{:S(2)}) collective-permute-start(f32[64,512]{1,0:T(8,128)S(1)} %add_two.1.own), channel_id=1, source_target_pairs={{0,1},{1,0},{2,3},{3,2},{4,5},{5,4},{6,7},{7,6},{8,9},{9,8},{10,11... | collective-permute-start | bytes 393224 | tf_op jit(solution)/shard_map/ppermute | solution.py:39
  115.1 6.3 %collective-permute-start.19 = (f32[64,512]{1,0:T(8,128)S(1)}, f32[64,512]{1,0:T(8,128)S(1)}, u32[]{:S(2)}, u32[]{:S(2)}) collective-permute-start(f32[64,512]{1,0:T(8,128)S(1)} %collective-permute-done.15.y_3), channel_id=1, source_target_pairs={{0,1},{1,0},{2,3},{3,2},{4,5},{5,4},{6,7},{7,6},{8,9},{9,8},{10,11... | collective-permute-start | bytes 393224 | tf_op jit(solution)/shard_map/ppermute | solution.py:39
  117.6 3.8 %collective-permute-start.18 = (f32[64,512]{1,0:T(8,128)S(1)}, f32[64,512]{1,0:T(8,128)S(1)}, u32[]{:S(2)}, u32[]{:S(2)}) collective-permute-start(f32[64,512]{1,0:T(8,128)S(1)} %collective-permute-done.14.y_2), channel_id=1, source_target_pairs={{0,1},{1,0},{2,3},{3,2},{4,5},{5,4},{6,7},{7,6},{8,9},{9,8},{10,11... | collective-permute-start | bytes 393224 | tf_op jit(solution)/shard_map/ppermute | solution.py:39
  120.1 2.3 %collective-permute-start.17 = (f32[64,512]{1,0:T(8,128)S(1)}, f32[64,512]{1,0:T(8,128)S(1)}, u32[]{:S(2)}, u32[]{:S(2)}) collective-permute-start(f32[64,512]{1,0:T(8,128)S(1)} %collective-permute-done.13.y_1), channel_id=1, source_target_pairs={{0,1},{1,0},{2,3},{3,2},{4,5},{5,4},{6,7},{7,6},{8,9},{9,8},{10,11... | collective-permute-start | bytes 393224 | tf_op jit(solution)/shard_map/ppermute | solution.py:39

commit v8 on v7

--- a/solution.py
+++ b/solution.py
@@ -456,15 +456,15 @@
 
 def relax_kernel(
     place, own, y_1, y_2, y_3, other, z_1, z_2, z_3, kind, moved, high, low,
-    out, gathered, turned_high, turned_low, held, leavings,
+    out, gathered_high, gathered_low, held, leavings,
 ):
     size = own.shape[0]
     pieces = (((own, y_1, y_2, y_3), place[0]), ((other, z_1, z_2, z_3), 1 - place[0]))
     for group, core in pieces:
         for away, piece in enumerate(group):
             at = core * 4 + (place[1] + (4 - away)) % 4
-            gathered[pl.ds(pl.multiple_of(at * size, size), size), :] = piece[...]
-    turned_high[...], turned_low[...] = halves(gathered[...].T)
+            rows = pl.ds(pl.multiple_of(at * size, size), size)
+            gathered_high[rows, :], gathered_low[rows, :] = halves(piece[...])
     fluid = [HALF_STEP * (1 - kind[x : x + 1, :]).astype(F32) for x in range(COLUMNS)]
     sends = []
     start = 0
@@ -473,9 +473,9 @@
         gains = []
         for core in range(2):
             cells = slice(core * 2 * ROWS, (core + 1) * 2 * ROWS)
-            gain = dot(high[lines, :], turned_high[:, cells])
-            gain = gain + dot(high[lines, :], turned_low[:, cells])
-            gains.append(gain + dot(low[lines, :], turned_high[:, cells]))
+            gain = dot_nt(high[lines, :], gathered_high[cells, :])
+            gain = gain + dot_nt(high[lines, :], gathered_low[cells, :])
+            gains.append(gain + dot_nt(low[lines, :], gathered_high[cells, :]))
         for part in range(count // CHUNK):
             first = start + part * CHUNK
             for x in range(COLUMNS):
@@ -504,9 +504,8 @@
         out_specs=ANY,
         out_shape=jax.ShapeDtypeStruct((PER_DEVICE * COLUMNS, ROWS), F32),
         scratch_shapes=[
-            pltpu.VMEM((CELLS, MOMENTS), F32),
-            pltpu.VMEM((MOMENTS, CELLS), BF16),
-            pltpu.VMEM((MOMENTS, CELLS), BF16),
+            pltpu.VMEM((CELLS, MOMENTS), BF16),
+            pltpu.VMEM((CELLS, MOMENTS), BF16),
             pltpu.VMEM((PER_DEVICE * COLUMNS, ROWS), F32),
             pltpu.SemaphoreType.DMA((PER_DEVICE // CHUNK,)),
         ],
@@ -521,16 +520,16 @@
     speed = ((MIDDLE - owner.astype(F32)) * STEP * RATIO_X).reshape(1)
     flat = dist.reshape(PER_DEVICE * COLUMNS, ROWS)
     to_right, to_left = pack(flat)
+    from_right = shifted(to_left, -1)
     from_left = shifted(to_right, 1)
-    from_right = shifted(to_left, -1)
 
     given = (to_left[0, :8], left_factor, right_factor, mixing)
     factors = staged(gathered_factors, given)
     high, low, turned_high, turned_low = split_basis(basis)
     part, ends = local_part(speed, flat, cell_kind, row_tables(next_cell, prev_cell))
     factors = split_factors(*factors)
-    halo = (from_left, from_right)
-    (from_left, from_right), factors = lax.optimization_barrier((halo, factors))
+    halo = (from_right, from_left)
+    (from_right, from_left), factors = lax.optimization_barrier((halo, factors))
 
     moved, kept, sent = moments_part(
         speed, place, ends, part, from_left, from_right, cell_kind, high, low

time: 128 us -> 133 us (1.039)
  waiting for transfers between devices: 48.8 us -> 53.7 us
    ppermute x2, waiting for transfers between devices: 5.78 us -> 10.4 us  [shifted(): return lax.ppermute(x, 'cells', [(i, (i + by) % size) for i in range(size)])]
  transfers between devices with their start and end apart: 20 -> 20, of which waited for: 10 -> 11; matrix products, arithmetic and copies ran while one was open for 0% -> 0% of each run, Pallas kernels for 16% -> 15%
where the time goes in v8:
time: 133 us
  waiting for transfers between devices  53.7 us (40%)
  starting transfers between devices  41.8 us (31%)
  Pallas kernels  34.4 us (26%)
  local copies, waits for them, and re-layouts  2.61 us (2%)
    ppermute x10, waiting for transfers between devices, along_y(): return lax.ppermute(x, 'vel', [(i, (i + 4 * by) % 16) for i in range(16)])  31 us
    ppermute x8, starting transfers between devices, exchanged(): return lax.ppermute(x, 'vel', [(i, i ^ bit) for i in range(16)])  17.5 us
    ppermute x10, starting transfers between devices, along_y(): return lax.ppermute(x, 'vel', [(i, (i + 4 * by) % 16) for i in range(16)])  15.2 us
    ppermute x8, waiting for transfers between devices, exchanged(): return lax.ppermute(x, 'vel', [(i, i ^ bit) for i in range(16)])  12.3 us
    ppermute x2, waiting for transfers between devices, shifted(): return lax.ppermute(x, 'cells', [(i, (i + by) % size) for i in range(size)])  10.4 us
    ppermute x2, starting transfers between devices, shifted(): return lax.ppermute(x, 'cells', [(i, (i + by) % size) for i in range(size)])  9.12 us
    pallas_call x1, Pallas kernels, local_part(): pl.pallas_call(local_kernel, name='local_transport', grid=(steps,), in_sp...  7.99 us
    pallas_call x1, Pallas kernels, relax(): pl.pallas_call(relax_kernel, name='relax', in_specs=[SM] + [VM] * 12, out...  4.98 us
  transfers between devices with their start and end apart: 20, of which 11 were waited for; matrix products, arithmetic and copies ran while one was open for 0% of the time, Pallas kernels for 15%

profile of v8, /device:TPU:1, one launch (start us, length us, event | category | flops | bytes accessed | tf_op | source)
XLA Modules:
  0.0 133.2 jit_solution(6339873572916363723)
XLA Ops:
  0.0 3.3 %pack.1 = (f32[3,1024,128]{2,1,0:T(8,128)}, f32[3,1024,128]{2,1,0:T(8,128)}) custom-call(f32[8192,128]{1,0:T(8,128)} %bitcast.9), custom_call_target="tpu_custom_call" | custom-call | flops 1048576 | bytes 8388608 | tf_op jit(solution)/shard_map/pack/pallas_call | solution.py:117
  3.3 9.1 %collective-permute-start.5 = (f32[3,1024,128]{2,1,0:T(8,128)}, f32[3,1024,128]{2,1,0:T(8,128)S(1)}, u32[]{:S(2)}, u32[]{:S(2)}) collective-permute-start(f32[3,1024,128]{2,1,0:T(8,128)} %get-tuple-element.38), channel_id=1, source_target_pairs={{0,240},{16,0},{32,16},{48,32},{64,48},{80,64},{96,80},{112,96},{1... | collective-permute-start | bytes 4718600 | tf_op jit(solution)/shard_map/ppermute | solution.py:35
  12.4 0.0 collective-permute-start.6
  12.4 0.0 copy-done.3
  12.4 43.8 %conditional.1 = (f32[4,384,512]{2,1,0:T(8,128)}, f32[4,384,512]{2,1,0:T(8,128)}) conditional(s32[]{:T(128)} %convert_element_type.15, () %tuple.14, (f32[128,512]{1,0:T(8,128)S(1)}, f32[128,512]{1,0:T(8,128)}, f32[512,128]{1,0:T(8,128)}) %tuple.21), branch_computations={%region_0.1_spmd, %region_1.2_spmd} | conditional | flops 2097152 | bytes 31981784 | solution.py:139
  12.4 1.2 stack_factors.1.own
  13.6 2.8 %collective-permute-start.1 = (f32[384,512]{1,0:T(8,128)S(1)}, f32[384,512]{1,0:T(8,128)S(1)}, u32[]{:S(2)}, u32[]{:S(2)}) collective-permute-start(f32[384,512]{1,0:T(8,128)S(1)} %stack_factors.1.own), channel_id=1, source_target_pairs={{0,12},{1,13},{2,14},{3,15},{4,0},{5,1},{6,2},{7,3},{8,4},{9,5},{1... | collective-permute-start | bytes 2359304 | tf_op jit(solution)/shard_map/cond/branch_1_fun/ppermute | solution.py:43
  16.4 0.0 collective-permute-start
  16.4 15.9 %collective-permute-done.1.after = f32[384,512]{1,0:T(8,128)S(1)} collective-permute-done((f32[384,512]{1,0:T(8,128)S(1)}, f32[384,512]{1,0:T(8,128)S(1)}, u32[]{:S(2)}, u32[]{:S(2)}) %collective-permute-start.1) | collective-permute-done | bytes 786464 | tf_op jit(solution)/shard_map/cond/branch_1_fun/ppermute | solution.py:43
  32.4 3.5 %collective-permute-start.3 = (f32[192,512]{1,0:T(8,128)S(1)}, f32[192,512]{1,0:T(8,128)S(1)}, u32[]{:S(2)}, u32[]{:S(2)}) collective-permute-start(f32[192,512]{1,0:T(8,128)S(1)} %slice.7), channel_id=1, source_target_pairs={{0,12},{1,13},{2,14},{3,15},{4,0},{5,1},{6,2},{7,3},{8,4},{9,5},{1... | collective-permute-start | bytes 1179656 | tf_op jit(solution)/shard_map/cond/branch_1_fun/ppermute | solution.py:43
  35.8 0.0 collective-permute-done.before
  35.9 0.1 collective-permute-start.2
  36.0 6.4 %collective-permute-done.3.across_rest = f32[192,512]{1,0:T(8,128)S(1)} collective-permute-done((f32[192,512]{1,0:T(8,128)S(1)}, f32[192,512]{1,0:T(8,128)S(1)}, u32[]{:S(2)}, u32[]{:S(2)}) %collective-permute-start.3) | collective-permute-done | bytes 393248 | tf_op jit(solution)/shard_map/cond/branch_1_fun/ppermute | solution.py:43
  42.4 3.2 %collective-permute-done.2.across_top = f32[192,512]{1,0:T(8,128)S(1)} collective-permute-done((f32[192,512]{1,0:T(8,128)S(1)}, f32[192,512]{1,0:T(8,128)S(1)}, u32[]{:S(2)}, u32[]{:S(2)}) %collective-permute-start.2) | collective-permute-done | bytes 393248 | tf_op jit(solution)/shard_map/cond/branch_1_fun/ppermute | solution.py:43
  45.6 1.9 %join_factors.1 = f32[4,384,512]{2,1,0:T(8,128)} custom-call(f32[384,512]{1,0:T(8,128)S(1)} %stack_factors.1.own, f32[384,512]{1,0:T(8,128)S(1)} %collective-permute-done.before, f32[384,512]{1,0:T(8,128)S(1)} %collective-permute-done.1.after, f32[192,512]{1,0:T(8,128)S(1)} %collective-permute-done.2.across_top, ...), custom_call_target="tpu_custom_call" | custom-call | flops 1048576 | bytes 6291456 | tf_op jit(solution)/shard_map/cond/branch_1_fun/join_factors/pallas_call | solution.py:285
  47.5 3.1 %collective-permute-start.4 = (f32[4,384,512]{2,1,0:T(8,128)}, f32[4,384,512]{2,1,0:T(8,128)}, u32[]{:S(2)}, u32[]{:S(2)}) collective-permute-start(f32[4,384,512]{2,1,0:T(8,128)} %join_factors.1), channel_id=1, source_target_pairs={{0,1},{1,0},{2,3},{3,2},{4,5},{5,4},{6,7},{7,6},{8,9},{9,8},{10,11... | collective-permute-start | bytes 9437192 | tf_op jit(solution)/shard_map/cond/branch_1_fun/ppermute | solution.py:39
  50.6 5.6 %collective-permute-done.4 = f32[4,384,512]{2,1,0:T(8,128)} collective-permute-done((f32[4,384,512]{2,1,0:T(8,128)}, f32[4,384,512]{2,1,0:T(8,128)}, u32[]{:S(2)}, u32[]{:S(2)}) %collective-permute-start.4) | collective-permute-done | bytes 3145760 | tf_op jit(solution)/shard_map/cond/branch_1_fun/ppermute | solution.py:39
  56.2 2.2 %copy-done = f32[512,2048]{1,0:T(8,128)S(1)} copy-done((f32[512,2048]{1,0:T(8,128)S(1)}, f32[512,2048]{1,0:T(8,128)}, u32[]{:S(2)}) %copy-start) | copy-done | bytes 4194328
  58.4 2.9 %split_basis.1 = (bf16[512,2048]{1,0:T(8,128)(2,1)S(1)}, bf16[512,2048]{1,0:T(8,128)(2,1)S(1)}, bf16[2048,512]{1,0:T(8,128)(2,1)S(1)}, bf16[2048,512]{1,0:T(8,128)(2,1)S(1)}) custom-call(f32[512,2048]{1,0:T(8,128)S(1)} %copy-done), custom_call_target="tpu_custom_call" | custom-call | flops 16777216 | bytes 12582912 | tf_op jit(solution)/shard_map/split_basis/pallas_call | solution.py:236
  61.2 0.0 copy-start.4
  61.3 0.0 copy-start.5
  61.3 0.0 copy-start.1
  61.3 4.0 %split_factors.1 = (bf16[3,1024,512]{2,1,0:T(8,128)(2,1)S(1)}, bf16[3,1024,512]{2,1,0:T(8,128)(2,1)S(1)}) custom-call(f32[4,384,512]{2,1,0:T(8,128)} %get-tuple-element.40.mine, f32[4,384,512]{2,1,0:T(8,128)} %get-tuple-element.41.theirs), custom_call_target="tpu_custom_call" | custom-call | flops 16777216 | bytes 12582912 | tf_op jit(solution)/shard_map/split_factors/pallas_call | solution.py:299
  65.2 0.0 copy-start.2
  65.3 0.1 pad_add_fusion.place
  65.3 0.1 fusion
  65.4 0.1 maximum_bitcast_fusion
  65.5 0.1 pad_maximum_fusion.tables
  65.6 0.0 copy-done.1
  65.6 0.3 copy-done.2
  66.0 8.0 %local_transport.1 = (f32[4,2048,128]{2,1,0:T(8,128)S(1)}, f32[4,2048,128]{2,1,0:T(8,128)S(1)}) custom-call(f32[1]{0:T(128)} %bitcast.2.speed, f32[8192,128]{1,0:T(8,128)S(1)} %bitcast.10, s32[4,128]{1,0:T(4,128)S(1)} %copy-done.2, bf16[2,4,256,256]{3,2,1,0:T(8,128)(2,1)S(1)} %pad_maximum_fusion.tables), custom_call_target="tpu_custom_call" | custom-call | flops 4294967296 | bytes 10485760 | tf_op jit(solution)/shard_map/local_transport/pallas_call | solution.py:191
  74.0 5.9 %collective-permute-done.5.from_right = f32[3,1024,128]{2,1,0:T(8,128)S(1)} collective-permute-done((f32[3,1024,128]{2,1,0:T(8,128)}, f32[3,1024,128]{2,1,0:T(8,128)S(1)}, u32[]{:S(2)}, u32[]{:S(2)}) %collective-permute-start.5) | collective-permute-done | bytes 1572896 | tf_op jit(solution)/shard_map/ppermute | solution.py:35
  79.8 4.6 %collective-permute-done.6.from_left = f32[3,1024,128]{2,1,0:T(8,128)S(1)} collective-permute-done((f32[3,1024,128]{2,1,0:T(8,128)}, f32[3,1024,128]{2,1,0:T(8,128)S(1)}, u32[]{:S(2)}, u32[]{:S(2)}) %collective-permute-start.6) | collective-permute-done | bytes 1572896 | tf_op jit(solution)/shard_map/ppermute | solution.py:35
  84.4 3.4 %faces_and_moments.1 = (f32[4,2048,128]{2,1,0:T(8,128)S(1)}, f32[256,512]{1,0:T(8,128)S(1)}) custom-call(f32[1]{0:T(128)} %bitcast.2.speed, s32[2]{0:T(128)S(1)} %pad_add_fusion.place, f32[4,2048,128]{2,1,0:T(8,128)S(1)} %get-tuple-element.36.ends, f32[4,2048,128]{2,1,0:T(8,128)S(1)} %get-tuple-element.37.part, ...), custom_call_target="tpu_custom_call" | custom-call | flops 4294967296 | bytes 18874368 | tf_op jit(solution)/shard_map/faces_and_moments/pallas_call | solution.py:378
  87.8 2.2 %collective-permute-start.7 = (f32[256,512]{1,0:T(8,128)S(1)}, f32[256,512]{1,0:T(8,128)S(1)}, u32[]{:S(2)}, u32[]{:S(2)}) collective-permute-start(f32[256,512]{1,0:T(8,128)S(1)} %get-tuple-element.49), channel_id=1, source_target_pairs={{0,1},{1,0},{2,3},{3,2},{4,5},{5,4},{6,7},{7,6},{8,9},{9,8},{10,11... | collective-permute-start | bytes 1572872 | tf_op jit(solution)/shard_map/ppermute | solution.py:39
  90.0 2.5 %own_moments.1.kept = f32[256,512]{1,0:T(8,128)S(1)} custom-call(s32[2]{0:T(128)S(1)} %pad_add_fusion.place, f32[4,2048,128]{2,1,0:T(8,128)S(1)} %get-tuple-element.48.moved, bf16[512,2048]{1,0:T(8,128)(2,1)S(1)} %get-tuple-element.46.high, bf16[512,2048]{1,0:T(8,128)(2,1)S(1)} %get-tuple-element.47.low), custom_call_target="tpu_custom_call" | custom-call | flops 4294967296 | bytes 8388608 | tf_op jit(solution)/shard_map/own_moments/pallas_call | solution.py:389
  92.4 0.0 collective-permute-done.7.received
  92.4 0.6 scatter.1
  93.1 3.0 %collective-permute-start.8 = (f32[64,512]{1,0:T(8,128)S(1)}, f32[64,512]{1,0:T(8,128)S(1)}, u32[]{:S(2)}, u32[]{:S(2)}) collective-permute-start(f32[64,512]{1,0:T(8,128)S(1)} %get-tuple-element.51), channel_id=1, source_target_pairs={{0,8},{1,9},{2,10},{3,11},{4,12},{5,13},{6,14},{7,15},{8,0},{9,1},... | collective-permute-start | bytes 393224 | tf_op jit(solution)/shard_map/ppermute | solution.py:43
  96.1 0.8 collective-permute-start.9
  96.8 0.7 collective-permute-start.10
  97.5 2.2 %collective-permute-done.8.b = f32[64,512]{1,0:T(8,128)S(1)} collective-permute-done((f32[64,512]{1,0:T(8,128)S(1)}, f32[64,512]{1,0:T(8,128)S(1)}, u32[]{:S(2)}, u32[]{:S(2)}) %collective-permute-start.8) | collective-permute-done | bytes 131104 | tf_op jit(solution)/shard_map/ppermute | solution.py:43
  99.8 3.2 %collective-permute-done.9.c = f32[64,512]{1,0:T(8,128)S(1)} collective-permute-done((f32[64,512]{1,0:T(8,128)S(1)}, f32[64,512]{1,0:T(8,128)S(1)}, u32[]{:S(2)}, u32[]{:S(2)}) %collective-permute-start.9) | collective-permute-done | bytes 131104 | tf_op jit(solution)/shard_map/ppermute | solution.py:43
  102.9 0.0 collective-permute-done.10.d
  103.0 1.9 %collective-permute-start.11 = (f32[64,512]{1,0:T(8,128)S(1)}, f32[64,512]{1,0:T(8,128)S(1)}, u32[]{:S(2)}, u32[]{:S(2)}) collective-permute-start(f32[64,512]{1,0:T(8,128)S(1)} %add_four.1.mine), channel_id=1, source_target_pairs={{0,2},{1,3},{2,0},{3,1},{4,6},{5,7},{6,4},{7,5},{8,10},{9,11},{10,... | collective-permute-start | bytes 393224 | tf_op jit(solution)/shard_map/ppermute | solution.py:39
  104.9 2.8 %collective-permute-done.11.theirs = f32[64,512]{1,0:T(8,128)S(1)} collective-permute-done((f32[64,512]{1,0:T(8,128)S(1)}, f32[64,512]{1,0:T(8,128)S(1)}, u32[]{:S(2)}, u32[]{:S(2)}) %collective-permute-start.11) | collective-permute-done | bytes 131104 | tf_op jit(solution)/shard_map/ppermute | solution.py:39
  107.7 1.8 %collide.1.a = f32[64,512]{1,0:T(8,128)S(1)} custom-call(f32[64,512]{1,0:T(8,128)S(1)} %add_four.1.mine, f32[64,512]{1,0:T(8,128)S(1)} %collective-permute-done.11.theirs, bf16[3,1024,512]{2,1,0:T(8,128)(2,1)S(1)} %get-tuple-element.54.high, bf16[3,1024,512]{2,1,0:T(8,128)(2,1)S(1)} %get-tuple-element.55.low), custom_call_target="tpu_custom_call" | custom-call | flops 1048576 | bytes 1048576 | tf_op jit(solution)/shard_map/collide/pallas_call | solution.py:405
  109.5 1.0 collective-permute-start.12
  110.5 2.9 %collective-permute-done.12.b = f32[64,512]{1,0:T(8,128)S(1)} collective-permute-done((f32[64,512]{1,0:T(8,128)S(1)}, f32[64,512]{1,0:T(8,128)S(1)}, u32[]{:S(2)}, u32[]{:S(2)}) %collective-permute-start.12) | collective-permute-done | bytes 131104 | tf_op jit(solution)/shard_map/ppermute | solution.py:39
  113.4 3.4 %collective-permute-start.15 = (f32[64,512]{1,0:T(8,128)S(1)}, f32[64,512]{1,0:T(8,128)S(1)}, u32[]{:S(2)}, u32[]{:S(2)}) collective-permute-start(f32[64,512]{1,0:T(8,128)S(1)} %add_two.1.own), channel_id=1, source_target_pairs={{0,12},{1,13},{2,14},{3,15},{4,0},{5,1},{6,2},{7,3},{8,4},{9,5},{1... | collective-permute-start | bytes 393224 | tf_op jit(solution)/shard_map/ppermute | solution.py:43
  116.8 0.2 collective-permute-start.14
  117.0 0.8 collective-permute-start.13
  117.8 3.0 %collective-permute-start.16 = (f32[64,512]{1,0:T(8,128)S(1)}, f32[64,512]{1,0:T(8,128)S(1)}, u32[]{:S(2)}, u32[]{:S(2)}) collective-permute-start(f32[64,512]{1,0:T(8,128)S(1)} %add_two.1.own), channel_id=1, source_target_pairs={{0,1},{1,0},{2,3},{3,2},{4,5},{5,4},{6,7},{7,6},{8,9},{9,8},{10,11... | collective-permute-start | bytes 393224 | tf_op jit(solution)/shard_map/ppermute | solution.py:39
  120.8 0.0 collective-permute-done.15.y_3
  120.8 2.7 %collective-permute-start.19 = (f32[64,512]{1,0:T(8,128)S(1)}, f32[64,512]{1,0:T(8,128)S(1)}, u32[]{:S(2)}, u32[]{:S(2)}) collective-permute-start(f32[64,512]{1,0:T(8,128)S(1)} %collective-permute-done.15.y_3), channel_id=1, source_target_pairs={{0,1},{1,0},{2,3},{3,2},{4,5},{5,4},{6,7},{7,6},{8,9},{9,8},{10,11... | collective-permute-start | bytes 393224 | tf_op jit(solution)/shard_map/ppermute | solution.py:39
  123.4 0.0 collective-permute-done.14.y_2
  123.4 2.3 %collective-permute-start.18 = (f32[64,512]{1,0:T(8,128)S(1)}, f32[64,512]{1,0:T(8,128)S(1)}, u32[]{:S(2)}, u32[]{:S(2)}) collective-permute-start(f32[64,512]{1,0:T(8,128)S(1)} %collective-permute-done.14.y_2), channel_id=1, source_target_pairs={{0,1},{1,0},{2,3},{3,2},{4,5},{5,4},{6,7},{7,6},{8,9},{9,8},{10,11... | collective-permute-start | bytes 393224 | tf_op jit(solution)/shard_map/ppermute | solution.py:39
  125.8 0.0 collective-permute-done.13.y_1
  125.8 1.3 collective-permute-start.17
  127.1 0.0 collective-permute-done.16.other
  127.1 0.0 collective-permute-done.19.z_3
  127.1 0.0 collective-permute-done.18.z_2
  127.1 1.0 collective-permute-done.17.z_1
  128.1 5.0 %relax.1 = f32[8192,128]{1,0:T(8,128)} custom-call(s32[2]{0:T(128)S(1)} %pad_add_fusion.place, f32[64,512]{1,0:T(8,128)S(1)} %add_two.1.own, f32[64,512]{1,0:T(8,128)S(1)} %collective-permute-done.13.y_1, f32[64,512]{1,0:T(8,128)S(1)} %collective-permute-done.14.y_2, f32[64,512]{1,0:T(8,128)S(1)} %collective-permute-done.15.y_3, ...), custom_call_target="tpu_custom_call" | custom-call | flops 8589934592 | bytes 16777216 | tf_op jit(solution)/shard_map/relax/pallas_call | solution.py:500
  (8 shorter events, 0.1 us)
Async XLA Ops:
  0.0 12.4 %copy-start.3 = (f32[128,512]{1,0:T(8,128)S(1)}, f32[128,512]{1,0:T(8,128)}, u32[]{:S(2)}) copy-start(f32[128,512]{1,0:T(8,128)} %param.12) | copy-start | bytes 786436
  3.3 76.5 %collective-permute-start.5 = (f32[3,1024,128]{2,1,0:T(8,128)}, f32[3,1024,128]{2,1,0:T(8,128)S(1)}, u32[]{:S(2)}, u32[]{:S(2)}) collective-permute-start(f32[3,1024,128]{2,1,0:T(8,128)} %get-tuple-element.38), channel_id=1, source_target_pairs={{0,240},{16,0},{32,16},{48,32},{64,48},{80,64},{96,80},{112,96},{1... | collective-permute-start | bytes 4718600 | tf_op jit(solution)/shard_map/ppermute | solution.py:35
  12.4 71.9 %collective-permute-start.6 = (f32[3,1024,128]{2,1,0:T(8,128)}, f32[3,1024,128]{2,1,0:T(8,128)S(1)}, u32[]{:S(2)}, u32[]{:S(2)}) collective-permute-start(f32[3,1024,128]{2,1,0:T(8,128)} %get-tuple-element.39), channel_id=1, source_target_pairs={{0,16},{16,32},{32,48},{48,64},{64,80},{80,96},{96,112},{112,128},... | collective-permute-start | bytes 4718600 | tf_op jit(solution)/shard_map/ppermute | solution.py:35
  13.6 18.7 %collective-permute-start.1 = (f32[384,512]{1,0:T(8,128)S(1)}, f32[384,512]{1,0:T(8,128)S(1)}, u32[]{:S(2)}, u32[]{:S(2)}) collective-permute-start(f32[384,512]{1,0:T(8,128)S(1)} %stack_factors.1.own), channel_id=1, source_target_pairs={{0,12},{1,13},{2,14},{3,15},{4,0},{5,1},{6,2},{7,3},{8,4},{9,5},{1... | collective-permute-start | bytes 2359304 | tf_op jit(solution)/shard_map/cond/branch_1_fun/ppermute | solution.py:43
  16.4 19.4 %collective-permute-start = (f32[384,512]{1,0:T(8,128)S(1)}, f32[384,512]{1,0:T(8,128)S(1)}, u32[]{:S(2)}, u32[]{:S(2)}) collective-permute-start(f32[384,512]{1,0:T(8,128)S(1)} %stack_factors.1.own), channel_id=1, source_target_pairs={{0,4},{1,5},{2,6},{3,7},{4,8},{5,9},{6,10},{7,11},{8,12},{9,13},{1... | collective-permute-start | bytes 2359304 | tf_op jit(solution)/shard_map/cond/branch_1_fun/ppermute | solution.py:43
  32.4 10.0 %collective-permute-start.3 = (f32[192,512]{1,0:T(8,128)S(1)}, f32[192,512]{1,0:T(8,128)S(1)}, u32[]{:S(2)}, u32[]{:S(2)}) collective-permute-start(f32[192,512]{1,0:T(8,128)S(1)} %slice.7), channel_id=1, source_target_pairs={{0,12},{1,13},{2,14},{3,15},{4,0},{5,1},{6,2},{7,3},{8,4},{9,5},{1... | collective-permute-start | bytes 1179656 | tf_op jit(solution)/shard_map/cond/branch_1_fun/ppermute | solution.py:43
  35.9 9.8 %collective-permute-start.2 = (f32[192,512]{1,0:T(8,128)S(1)}, f32[192,512]{1,0:T(8,128)S(1)}, u32[]{:S(2)}, u32[]{:S(2)}) collective-permute-start(f32[192,512]{1,0:T(8,128)S(1)} %slice.6), channel_id=1, source_target_pairs={{0,4},{1,5},{2,6},{3,7},{4,8},{5,9},{6,10},{7,11},{8,12},{9,13},{1... | collective-permute-start | bytes 1179656 | tf_op jit(solution)/shard_map/cond/branch_1_fun/ppermute | solution.py:43
  47.5 8.7 %collective-permute-start.4 = (f32[4,384,512]{2,1,0:T(8,128)}, f32[4,384,512]{2,1,0:T(8,128)}, u32[]{:S(2)}, u32[]{:S(2)}) collective-permute-start(f32[4,384,512]{2,1,0:T(8,128)} %join_factors.1), channel_id=1, source_target_pairs={{0,1},{1,0},{2,3},{3,2},{4,5},{5,4},{6,7},{7,6},{8,9},{9,8},{10,11... | collective-permute-start | bytes 9437192 | tf_op jit(solution)/shard_map/cond/branch_1_fun/ppermute | solution.py:39
  56.2 2.2 %copy-start = (f32[512,2048]{1,0:T(8,128)S(1)}, f32[512,2048]{1,0:T(8,128)}, u32[]{:S(2)}) copy-start(f32[512,2048]{1,0:T(8,128)} %basis.1) | copy-start | bytes 12582916
  61.2 4.1 %copy-start.4 = (s32[4,128]{1,0:T(4,128)S(1)}, s32[4,128]{1,0:T(4,128)}, u32[]{:S(2)}) copy-start(s32[4,128]{1,0:T(4,128)} %param.16) | copy-start | bytes 6148
  61.3 4.1 %copy-start.5 = (s32[4,128]{1,0:T(4,128)S(1)}, s32[4,128]{1,0:T(4,128)}, u32[]{:S(2)}) copy-start(s32[4,128]{1,0:T(4,128)} %param.15) | copy-start | bytes 6148
  61.3 4.3 %copy-start.1 = (f32[2048,4,128]{2,1,0:T(4,128)S(1)}, f32[2048,4,128]{2,1,0:T(4,128)}, u32[]{:S(2)}) copy-start(f32[2048,4,128]{2,1,0:T(4,128)} %param.10) | copy-start | bytes 12582916
  65.2 0.7 copy-start.2
  87.8 4.7 %collective-permute-start.7 = (f32[256,512]{1,0:T(8,128)S(1)}, f32[256,512]{1,0:T(8,128)S(1)}, u32[]{:S(2)}, u32[]{:S(2)}) collective-permute-start(f32[256,512]{1,0:T(8,128)S(1)} %get-tuple-element.49), channel_id=1, source_target_pairs={{0,1},{1,0},{2,3},{3,2},{4,5},{5,4},{6,7},{7,6},{8,9},{9,8},{10,11... | collective-permute-start | bytes 1572872 | tf_op jit(solution)/shard_map/ppermute | solution.py:39
  93.1 6.7 %collective-permute-start.8 = (f32[64,512]{1,0:T(8,128)S(1)}, f32[64,512]{1,0:T(8,128)S(1)}, u32[]{:S(2)}, u32[]{:S(2)}) collective-permute-start(f32[64,512]{1,0:T(8,128)S(1)} %get-tuple-element.51), channel_id=1, source_target_pairs={{0,8},{1,9},{2,10},{3,11},{4,12},{5,13},{6,14},{7,15},{8,0},{9,1},... | collective-permute-start | bytes 393224 | tf_op jit(solution)/shard_map/ppermute | solution.py:43
  96.1 6.9 %collective-permute-start.9 = (f32[64,512]{1,0:T(8,128)S(1)}, f32[64,512]{1,0:T(8,128)S(1)}, u32[]{:S(2)}, u32[]{:S(2)}) collective-permute-start(f32[64,512]{1,0:T(8,128)S(1)} %get-tuple-element.52), channel_id=1, source_target_pairs={{0,12},{1,13},{2,14},{3,15},{4,0},{5,1},{6,2},{7,3},{8,4},{9,5},{1... | collective-permute-start | bytes 393224 | tf_op jit(solution)/shard_map/ppermute | solution.py:43
  96.8 6.1 %collective-permute-start.10 = (f32[64,512]{1,0:T(8,128)S(1)}, f32[64,512]{1,0:T(8,128)S(1)}, u32[]{:S(2)}, u32[]{:S(2)}) collective-permute-start(f32[64,512]{1,0:T(8,128)S(1)} %get-tuple-element.53), channel_id=1, source_target_pairs={{0,4},{1,5},{2,6},{3,7},{4,8},{5,9},{6,10},{7,11},{8,12},{9,13},{1... | collective-permute-start | bytes 393224 | tf_op jit(solution)/shard_map/ppermute | solution.py:43
  103.0 4.7 %collective-permute-start.11 = (f32[64,512]{1,0:T(8,128)S(1)}, f32[64,512]{1,0:T(8,128)S(1)}, u32[]{:S(2)}, u32[]{:S(2)}) collective-permute-start(f32[64,512]{1,0:T(8,128)S(1)} %add_four.1.mine), channel_id=1, source_target_pairs={{0,2},{1,3},{2,0},{3,1},{4,6},{5,7},{6,4},{7,5},{8,10},{9,11},{10,... | collective-permute-start | bytes 393224 | tf_op jit(solution)/shard_map/ppermute | solution.py:39
  109.5 3.9 %collective-permute-start.12 = (f32[64,512]{1,0:T(8,128)S(1)}, f32[64,512]{1,0:T(8,128)S(1)}, u32[]{:S(2)}, u32[]{:S(2)}) collective-permute-start(f32[64,512]{1,0:T(8,128)S(1)} %collide.1.a), channel_id=1, source_target_pairs={{0,2},{1,3},{2,0},{3,1},{4,6},{5,7},{6,4},{7,5},{8,10},{9,11},{10,... | collective-permute-start | bytes 393224 | tf_op jit(solution)/shard_map/ppermute | solution.py:39
  113.4 7.4 %collective-permute-start.15 = (f32[64,512]{1,0:T(8,128)S(1)}, f32[64,512]{1,0:T(8,128)S(1)}, u32[]{:S(2)}, u32[]{:S(2)}) collective-permute-start(f32[64,512]{1,0:T(8,128)S(1)} %add_two.1.own), channel_id=1, source_target_pairs={{0,12},{1,13},{2,14},{3,15},{4,0},{5,1},{6,2},{7,3},{8,4},{9,5},{1... | collective-permute-start | bytes 393224 | tf_op jit(solution)/shard_map/ppermute | solution.py:43
  116.8 6.6 %collective-permute-start.14 = (f32[64,512]{1,0:T(8,128)S(1)}, f32[64,512]{1,0:T(8,128)S(1)}, u32[]{:S(2)}, u32[]{:S(2)}) collective-permute-start(f32[64,512]{1,0:T(8,128)S(1)} %add_two.1.own), channel_id=1, source_target_pairs={{0,8},{1,9},{2,10},{3,11},{4,12},{5,13},{6,14},{7,15},{8,0},{9,1},... | collective-permute-start | bytes 393224 | tf_op jit(solution)/shard_map/ppermute | solution.py:43
  117.0 8.8 %collective-permute-start.13 = (f32[64,512]{1,0:T(8,128)S(1)}, f32[64,512]{1,0:T(8,128)S(1)}, u32[]{:S(2)}, u32[]{:S(2)}) collective-permute-start(f32[64,512]{1,0:T(8,128)S(1)} %add_two.1.own), channel_id=1, source_target_pairs={{0,4},{1,5},{2,6},{3,7},{4,8},{5,9},{6,10},{7,11},{8,12},{9,13},{1... | collective-permute-start | bytes 393224 | tf_op jit(solution)/shard_map/ppermute | solution.py:43
  117.8 9.3 %collective-permute-start.16 = (f32[64,512]{1,0:T(8,128)S(1)}, f32[64,512]{1,0:T(8,128)S(1)}, u32[]{:S(2)}, u32[]{:S(2)}) collective-permute-start(f32[64,512]{1,0:T(8,128)S(1)} %add_two.1.own), channel_id=1, source_target_pairs={{0,1},{1,0},{2,3},{3,2},{4,5},{5,4},{6,7},{7,6},{8,9},{9,8},{10,11... | collective-permute-start | bytes 393224 | tf_op jit(solution)/shard_map/ppermute | solution.py:39
  120.8 6.3 %collective-permute-start.19 = (f32[64,512]{1,0:T(8,128)S(1)}, f32[64,512]{1,0:T(8,128)S(1)}, u32[]{:S(2)}, u32[]{:S(2)}) collective-permute-start(f32[64,512]{1,0:T(8,128)S(1)} %collective-permute-done.15.y_3), channel_id=1, source_target_pairs={{0,1},{1,0},{2,3},{3,2},{4,5},{5,4},{6,7},{7,6},{8,9},{9,8},{10,11... | collective-permute-start | bytes 393224 | tf_op jit(solution)/shard_map/ppermute | solution.py:39
  123.4 3.7 %collective-permute-start.18 = (f32[64,512]{1,0:T(8,128)S(1)}, f32[64,512]{1,0:T(8,128)S(1)}, u32[]{:S(2)}, u32[]{:S(2)}) collective-permute-start(f32[64,512]{1,0:T(8,128)S(1)} %collective-permute-done.14.y_2), channel_id=1, source_target_pairs={{0,1},{1,0},{2,3},{3,2},{4,5},{5,4},{6,7},{7,6},{8,9},{9,8},{10,11... | collective-permute-start | bytes 393224 | tf_op jit(solution)/shard_map/ppermute | solution.py:39
  125.8 2.3 %collective-permute-start.17 = (f32[64,512]{1,0:T(8,128)S(1)}, f32[64,512]{1,0:T(8,128)S(1)}, u32[]{:S(2)}, u32[]{:S(2)}) collective-permute-start(f32[64,512]{1,0:T(8,128)S(1)} %collective-permute-done.13.y_1), channel_id=1, source_target_pairs={{0,1},{1,0},{2,3},{3,2},{4,5},{5,4},{6,7},{7,6},{8,9},{9,8},{10,11... | collective-permute-start | bytes 393224 | tf_op jit(solution)/shard_map/ppermute | solution.py:39
